TPU v7x, 32 devices: a whole 2x2x4 slice. The times are simulated.
32 devices in a mesh: dp: 8 (over y, x, core), tensor: 4 (over z).
Axes of the slice: x: 2, y: 2, z: 4, core: 2. Of those that a mesh axis runs over, the one named last changes fastest.
Arguments:
- x_doc: bfloat16 [2, 8192, 1024], P(None, ('dp', 'tensor')), may hold values from -6 to 6
- x_query: bfloat16 [2, 1024, 1024], P(None, ('dp', 'tensor')), may hold values from -6 to 6
- doc_cot: float32 [2, 8192, 1024], P(None, ('dp', 'tensor')), may hold values from -6 to 6
- query_cot: float32 [2, 1024, 1024], P(None, ('dp', 'tensor')), may hold values from -6 to 6
- lengths: int32 [2, 8, 5], replicated, may hold values from 1 to 512, 1024 in all within a row
- positives: int32 [2, 32], P(None, 'dp'), may hold values from 0 to 31
- w_qkv: bfloat16 [3, 1024, 1024], P(None, 'dp', 'tensor'), may hold values from -0.1875 to 0.1875
- b_qkv: float32 [3, 1024], P(None, 'tensor'), may hold values from -2 to 2
- w_out: bfloat16 [1024, 1024], P('tensor', 'dp'), may hold values from -1.5 to 1.5
- b_out: float32 [1024], replicated, may hold values from -2 to 2
- gain_one: float32 [1024], replicated, may hold values from 0.5 to 1.5
- shift_one: float32 [1024], replicated, may hold values from -2 to 2
- w_in: bfloat16 [1024, 4096], P('dp', 'tensor'), may hold values from -0.1875 to 0.1875
- b_in: float32 [4096], P('tensor'), may hold values from -2 to 2
- w_back: bfloat16 [4096, 1024], P('tensor', 'dp'), may hold values from -0.125 to 0.125
- b_back: float32 [1024], replicated, may hold values from -2 to 2
- gain_two: float32 [1024], replicated, may hold values from 0.5 to 1.5
- shift_two: float32 [1024], replicated, may hold values from -2 to 2
- w_proj: bfloat16 [1024, 128], P('dp'), may hold values from -0.1875 to 0.1875
Outputs:
- y_doc: bfloat16 [2, 8192, 1024], P(None, ('dp', 'tensor'))
- y_query: bfloat16 [2, 1024, 1024], P(None, ('dp', 'tensor'))
- query_loss: float32 [2, 32], P(None, ('dp', 'tensor'))
- grad_x_doc: float32 [2, 8192, 1024], P(None, ('dp', 'tensor'))
- grad_x_query: float32 [2, 1024, 1024], P(None, ('dp', 'tensor'))
- grad_w_qkv: float32 [3, 1024, 1024], P(None, 'dp', 'tensor')
- grad_b_qkv: float32 [3, 1024], P(None, 'tensor')
- grad_w_out: float32 [1024, 1024], P('tensor', 'dp')
- grad_b_out: float32 [1024], replicated
- grad_gain_one: float32 [1024], replicated
- grad_shift_one: float32 [1024], replicated
- grad_w_in: float32 [1024, 4096], P('dp', 'tensor')
- grad_b_in: float32 [4096], P('tensor')
- grad_w_back: float32 [4096, 1024], P('tensor', 'dp')
- grad_b_back: float32 [1024], replicated
- grad_gain_two: float32 [1024], replicated
- grad_shift_two: float32 [1024], replicated
- grad_w_proj: float32 [1024, 128], P('dp')
Inputs may be any that keep to these rules, and one draw needn't show every extreme that they name: Entry s < 4 of lengths[m, r] is the length of document s packed in order in document row r of micro-batch m; entry 4 counts the padding tokens at the row's end; each row sums to 1024. positives[m, q] names document n = r * 4 + s (document s of document row r) of micro-batch m; queries are numbered by index of dp, then in order.
All inputs are finite; a program needn't handle non-finite values.
Results may differ from a plain program's by a relative error of at most 0.014.
Values may be sent and summed in bfloat16 or wider, within the bound.
A program may use at most 192 MiB of HBM per device.

v0:
```python
import math

import jax
import jax.numpy as jnp
from jax import lax
from jax.sharding import PartitionSpec as P

HEAD_WIDTH = 64
QLEN = 32


FULL_PRECISION = lax.Precision.HIGHEST
TAU = 20.0
EPS = 1e-05
LOGIT_SCALE = 2.0
MASKED = -1e30


def layer_norm(values, gain, shift):
    center = values - jnp.mean(values, axis=-1, keepdims=True)
    spread = jnp.mean(center * center, axis=-1, keepdims=True)
    return center * lax.rsqrt(spread + EPS) * gain + shift


def normalize(values):
    return values * lax.rsqrt(jnp.sum(values * values, axis=-1, keepdims=True) + 1e-06)


def gelu_exact(values):
    return jax.nn.gelu(values, approximate=False)


def rope_angle(position, width):
    half = width // 2
    rates = 10000.0 ** (-(2.0 * jnp.arange(half, dtype=jnp.float32)) / width)
    return position.astype(jnp.float32)[:, None] * rates[None, :]


def rotate(values, angle):
    half = values.shape[-1] // 2
    cosine = jnp.cos(angle)[:, None, :]
    sine = jnp.sin(angle)[:, None, :]
    first = values[..., :half]
    second = values[..., half:]
    return jnp.concatenate(
        [first * cosine - second * sine, second * cosine + first * sine], axis=-1
    )


def unrotate(grads, angle):
    half = grads.shape[-1] // 2
    cosine = jnp.cos(angle)[:, None, :]
    sine = jnp.sin(angle)[:, None, :]
    first = grads[..., :half]
    second = grads[..., half:]
    return jnp.concatenate(
        [first * cosine + second * sine, second * cosine - first * sine], axis=-1
    )


def row_layout(sizes, count):
    ends = jnp.cumsum(sizes[:-1])
    index = jnp.arange(count, dtype=jnp.int32)
    segment = jnp.sum((index[:, None] >= ends[None, :]).astype(jnp.int32), axis=1)
    starts = jnp.concatenate([jnp.zeros((1,), jnp.int32), ends])
    labels = jnp.arange(starts.shape[0], dtype=jnp.int32)
    begin = jnp.sum(jnp.where(segment[:, None] == labels[None, :], starts[None, :], 0), axis=1)
    return (segment, index - begin)


def query_losses(totals, counts, positive):
    best = (jnp.log(totals) - jnp.log(counts)[None, :]) / TAU + 1.0
    score = jnp.sum(best.reshape(-1, QLEN, best.shape[-1]), axis=1)
    logits = LOGIT_SCALE * score
    labels = jnp.arange(logits.shape[-1], dtype=jnp.int32)
    picked = jnp.sum(jnp.where(labels[None, :] == positive[:, None], logits, 0.0), axis=1)
    return jax.nn.logsumexp(logits, axis=-1) - picked


def gather_rows(first, second):
    return (
        lax.all_gather(first, "tensor", axis=0, tiled=True),
        lax.all_gather(second, "tensor", axis=0, tiled=True),
    )


def sum_rows(first, second):
    return (
        lax.psum_scatter(first, "tensor", scatter_dimension=0, tiled=True),
        lax.psum_scatter(second, "tensor", scatter_dimension=0, tiled=True),
    )


def quarter_sum(values):
    return lax.psum(values.astype(jnp.bfloat16), "tensor").astype(jnp.float32)


def attend_forward(query_matrix, key, value_matrix, row_labels, key_labels):
    rows, heads, width = query_matrix.shape
    block = min(512, rows)
    score_scale = width ** (-0.5)
    query_blocks = query_matrix.reshape(rows // block, block, heads, width)
    label_blocks = row_labels.reshape(rows // block, block)

    def one_block(pack):
        query_block, block_labels = pack
        attention_scores = (
            jnp.einsum("fio,uio->ifu", query_block, key, preferred_element_type=jnp.float32)
            * score_scale
        )
        same = block_labels[:, None] == key_labels[None, :]
        attention_scores = jnp.where(same[None], attention_scores, MASKED)
        highest = jnp.max(attention_scores, axis=-1, keepdims=True)
        powers = jnp.exp(attention_scores - highest)
        total = jnp.sum(powers, axis=-1, keepdims=True)
        attention_weights = (powers / total).astype(jnp.bfloat16)
        mixed_heads = jnp.einsum(
            "evg,geb->veb", attention_weights, value_matrix, preferred_element_type=jnp.float32
        )
        return (mixed_heads, (highest + jnp.log(total))[..., 0])

    mixed_heads, logsum = lax.map(one_block, (query_blocks, label_blocks))
    return (
        mixed_heads.reshape(rows, heads * width),
        jnp.moveaxis(logsum, 0, 1).reshape(heads, rows),
    )


def attend_backward(query_matrix, key, value_matrix, row_labels, key_labels, logsum, grad_mixed):
    rows, heads, width = query_matrix.shape
    block = min(512, rows)
    score_scale = width ** (-0.5)
    count = rows // block
    query_blocks = query_matrix.reshape(count, block, heads, width)
    label_blocks = row_labels.reshape(count, block)
    grad_blocks = grad_mixed.reshape(count, block, heads, width)
    logsum_blocks = jnp.moveaxis(logsum.reshape(heads, count, block), 1, 0)

    def one_block(carry, pack):
        key_grad, value_grad = carry
        query_block, block_labels, block_gradient, block_logsum = pack
        attention_scores = (
            jnp.einsum("fio,uio->ifu", query_block, key, preferred_element_type=jnp.float32)
            * score_scale
        )
        same = block_labels[:, None] == key_labels[None, :]
        attention_scores = jnp.where(same[None], attention_scores, MASKED)
        probabilities = jnp.exp(attention_scores - block_logsum[..., None])
        value_grad = value_grad + jnp.einsum(
            "yjo,jyb->oyb",
            probabilities.astype(jnp.bfloat16),
            block_gradient,
            preferred_element_type=jnp.float32,
        )
        prob_grad = jnp.einsum(
            "fio,uio->ifu", block_gradient, value_matrix, preferred_element_type=jnp.float32
        )
        score_grad = probabilities * (
            prob_grad - jnp.sum(probabilities * prob_grad, axis=-1, keepdims=True)
        )
        reduced_scores = score_grad.astype(jnp.bfloat16)
        query_grad = (
            jnp.einsum("evg,geb->veb", reduced_scores, key, preferred_element_type=jnp.float32)
            * score_scale
        )
        key_grad = (
            key_grad
            + jnp.einsum(
                "yjo,jyb->oyb", reduced_scores, query_block, preferred_element_type=jnp.float32
            )
            * score_scale
        )
        return ((key_grad, value_grad), query_grad)

    zeros = jnp.zeros(key.shape, jnp.float32)
    (key_grad, value_grad), query_grad = lax.scan(
        one_block, (zeros, zeros), (query_blocks, label_blocks, grad_blocks, logsum_blocks)
    )
    return (query_grad.reshape(rows, heads, width), key_grad, value_grad)


def segment_totals(query_vecs, doc_vecs, member):
    rows, length, width = doc_vecs.shape
    group = math.gcd(rows, 8)
    count = rows // group
    documents = doc_vecs.reshape(count, group, length, width)
    marks = member.reshape(count, group, length, member.shape[2])

    def one_group(carry, pack):
        block_docs, block_marks = pack
        cosines = jnp.einsum(
            "qp,glp->qgl", query_vecs, block_docs, preferred_element_type=jnp.float32
        )
        weight = jnp.exp(TAU * (cosines - 1.0))
        return (carry, jnp.einsum("qgl,gls->qgs", weight, block_marks, precision=FULL_PRECISION))

    carry, totals = lax.scan(one_group, jnp.zeros((), jnp.float32), (documents, marks))
    return jnp.moveaxis(totals, 0, 1).reshape(query_vecs.shape[0], rows, member.shape[2])


def segment_grads(query_vecs, doc_vecs, member, coef):
    rows, length, width = doc_vecs.shape
    group = math.gcd(rows, 8)
    count = rows // group
    queries = query_vecs.shape[0]
    documents = doc_vecs.reshape(count, group, length, width)
    marks = member.reshape(count, group, length, member.shape[2])
    coefs = jnp.moveaxis(coef.reshape(queries, count, group, coef.shape[2]), 1, 0)

    def one_group(carry, pack):
        block_docs, block_marks, block_coef = pack
        cosines = jnp.einsum(
            "qp,glp->qgl", query_vecs, block_docs, preferred_element_type=jnp.float32
        )
        weight = jnp.exp(TAU * (cosines - 1.0))
        spread = jnp.einsum("qgs,gls->qgl", block_coef, block_marks, precision=FULL_PRECISION)
        cosine_grad = (weight * spread).astype(jnp.bfloat16)
        carry = carry + jnp.einsum(
            "qgl,glp->qp", cosine_grad, block_docs, preferred_element_type=jnp.float32
        )
        doc_grad = jnp.einsum(
            "qgl,qp->glp", cosine_grad, query_vecs, preferred_element_type=jnp.float32
        )
        return (carry, doc_grad)

    query_grad, doc_grads = lax.scan(
        one_group, jnp.zeros((queries, width), jnp.float32), (documents, marks, coefs)
    )
    return (query_grad, doc_grads.reshape(rows, length, width))


def body(
    x_doc,
    x_query,
    doc_cot,
    query_cot,
    lengths,
    positives,
    w_qkv,
    b_qkv,
    w_out,
    b_out,
    gain_one,
    shift_one,
    w_in,
    b_in,
    w_back,
    b_back,
    gain_two,
    shift_two,
    w_proj,
):
    ways = lax.axis_size("tensor")
    column = lax.axis_index("tensor")
    rank = lax.axis_index("dp")
    groups = lax.axis_size("dp")
    full_qkv, full_out, full_in, full_back, full_proj = (
        lax.all_gather(w_qkv, "dp", axis=1, tiled=True),
        lax.all_gather(w_out, "dp", axis=1, tiled=True),
        lax.all_gather(w_in, "dp", axis=0, tiled=True),
        lax.all_gather(w_back, "dp", axis=1, tiled=True),
        lax.all_gather(w_proj, "dp", axis=0, tiled=True),
    )
    micro = x_doc.shape[0]
    doc_rows = x_doc.shape[1]
    query_rows = x_query.shape[1]
    width = x_doc.shape[2]
    local_width = full_qkv.shape[2]
    local_units = full_in.shape[1]
    proj_width = full_proj.shape[1]
    head_size = HEAD_WIDTH
    local_heads = local_width // head_size
    doc_len = doc_rows * ways
    query_len = query_rows * ways
    segments = lengths.shape[2] - 1
    query_index = jnp.arange(query_len, dtype=jnp.int32)
    query_labels = query_index // QLEN
    query_places = query_index % QLEN
    seg_labels = jnp.arange(segments, dtype=jnp.int32)
    own_queries = query_rows // QLEN
    grad_w_qkv = jnp.zeros((3, width, local_width), jnp.float32)
    grad_b_qkv = jnp.zeros((3, local_width), jnp.float32)
    grad_w_out = jnp.zeros((local_width, width), jnp.float32)
    grad_b_out = jnp.zeros((width,), jnp.float32)
    grad_gain_one = jnp.zeros((width,), jnp.float32)
    grad_shift_one = jnp.zeros((width,), jnp.float32)
    grad_w_in = jnp.zeros((width, local_units), jnp.float32)
    grad_b_in = jnp.zeros((local_units,), jnp.float32)
    grad_w_back = jnp.zeros((local_units, width), jnp.float32)
    grad_b_back = jnp.zeros((width,), jnp.float32)
    grad_gain_two = jnp.zeros((width,), jnp.float32)
    grad_shift_two = jnp.zeros((width,), jnp.float32)
    grad_proj = jnp.zeros((width, proj_width), jnp.float32)
    doc_outs, query_outs, loss_rows, doc_inputs, query_inputs = ([], [], [], [], [])
    for step in range(micro):
        sizes_all = lengths[step]
        all_labels, all_places = jax.vmap(lambda sizes: row_layout(sizes, doc_len))(sizes_all)
        doc_labels = lax.dynamic_index_in_dim(all_labels, rank, 0, keepdims=False)
        doc_places = lax.dynamic_index_in_dim(all_places, rank, 0, keepdims=False)
        angle = rope_angle(jnp.concatenate([doc_places, query_places]), head_size)
        counts = sizes_all[:, :segments].reshape(-1).astype(jnp.float32)
        picks = positives[step]
        doc_in = x_doc[step]
        query_in = x_query[step]
        whole_doc, whole_query = gather_rows(doc_in, query_in)
        rows_in = jnp.concatenate([whole_doc, whole_query], axis=0)
        total_rows = rows_in.shape[0]
        projected = [
            jnp.dot(rows_in, full_qkv[index], preferred_element_type=jnp.float32) + b_qkv[index]
            for index in range(3)
        ]
        query_rot = rotate(projected[0].reshape(total_rows, local_heads, head_size), angle).astype(
            jnp.bfloat16
        )
        key_rot = rotate(projected[1].reshape(total_rows, local_heads, head_size), angle).astype(
            jnp.bfloat16
        )
        value_low = projected[2].astype(jnp.bfloat16).reshape(total_rows, local_heads, head_size)
        mixed_doc, logsum_doc = attend_forward(
            query_rot[:doc_len], key_rot[:doc_len], value_low[:doc_len], doc_labels, doc_labels
        )
        mixed_query, logsum_query = attend_forward(
            query_rot[doc_len:], key_rot[doc_len:], value_low[doc_len:], query_labels, query_labels
        )
        mixed_heads = jnp.concatenate([mixed_doc, mixed_query], axis=0).astype(jnp.bfloat16)
        partial_value = jnp.dot(mixed_heads, full_out, preferred_element_type=jnp.float32)
        branch_doc, branch_query = sum_rows(partial_value[:doc_len], partial_value[doc_len:])
        own_in = jnp.concatenate([doc_in, query_in], axis=0).astype(jnp.float32)
        resid_one = own_in + jnp.concatenate([branch_doc, branch_query], axis=0) + b_out
        normed, norm_one_pull = jax.vjp(layer_norm, resid_one, gain_one, shift_one)
        normed_low = normed.astype(jnp.bfloat16)
        hidden_doc, hidden_query = gather_rows(normed_low[:doc_rows], normed_low[doc_rows:])
        hidden = jnp.concatenate([hidden_doc, hidden_query], axis=0)
        inner = jnp.dot(hidden, full_in, preferred_element_type=jnp.float32) + b_in
        active, gelu_pull = jax.vjp(gelu_exact, inner)
        active_low = active.astype(jnp.bfloat16)
        partial_two = jnp.dot(active_low, full_back, preferred_element_type=jnp.float32)
        update_doc, update_query = sum_rows(partial_two[:doc_len], partial_two[doc_len:])
        resid_two = normed + jnp.concatenate([update_doc, update_query], axis=0) + b_back
        output, norm_two_pull = jax.vjp(layer_norm, resid_two, gain_two, shift_two)
        output_low = output.astype(jnp.bfloat16)
        doc_outs.append(output_low[:doc_rows])
        query_outs.append(output_low[doc_rows:])
        projection = jnp.dot(output_low, full_proj, preferred_element_type=jnp.float32)
        unit, unit_pull = jax.vjp(normalize, projection)
        unit_low = unit.astype(jnp.bfloat16)
        doc_unit = unit_low[:doc_rows]
        query_unit = unit_low[doc_rows:]
        quarter_labels = lax.dynamic_slice_in_dim(all_labels, column * doc_rows, doc_rows, axis=1)
        member = (quarter_labels[:, :, None] == seg_labels[None, None, :]).astype(jnp.float32)
        documents = lax.all_gather(doc_unit, "dp", axis=0, tiled=True).reshape(
            groups, doc_rows, proj_width
        )
        queries = lax.all_gather(query_unit, "tensor", axis=0, tiled=True)
        totals = quarter_sum(segment_totals(queries, documents, member))
        losses, loss_pull = jax.vjp(
            lambda values: query_losses(values, counts, picks),
            totals.reshape(query_len, groups * segments),
        )
        (total_grad,) = loss_pull(jnp.ones_like(losses))
        query_grad_all, doc_grads = segment_grads(
            queries, documents, member, TAU * total_grad.reshape(query_len, groups, segments)
        )
        doc_grad = lax.psum_scatter(
            doc_grads.reshape(groups * doc_rows, proj_width), "dp", scatter_dimension=0, tiled=True
        )
        query_grad = lax.psum_scatter(
            query_grad_all.astype(jnp.bfloat16), "tensor", scatter_dimension=0, tiled=True
        ).astype(jnp.float32)
        loss_rows.append(lax.dynamic_slice_in_dim(losses, column * own_queries, own_queries))
        unit_grad = jnp.concatenate([doc_grad, query_grad], axis=0)
        (proj_grad,) = unit_pull(unit_grad)
        proj_low = proj_grad.astype(jnp.bfloat16)
        grad_proj = grad_proj + jnp.einsum(
            "rd,rp->dp", output_low, proj_low, preferred_element_type=jnp.float32
        )
        out_grad = jnp.concatenate([doc_cot[step], query_cot[step]], axis=0) + jnp.einsum(
            "rp,dp->rd", proj_low, full_proj, preferred_element_type=jnp.float32
        )
        resid_two_grad, gain_two_grad, shift_two_grad = norm_two_pull(out_grad)
        grad_gain_two = grad_gain_two + gain_two_grad
        grad_shift_two = grad_shift_two + shift_two_grad
        update_low = resid_two_grad.astype(jnp.bfloat16)
        grad_b_back = grad_b_back + jnp.sum(update_low.astype(jnp.float32), axis=0)
        wide_doc, wide_query = gather_rows(update_low[:doc_rows], update_low[doc_rows:])
        update_full = jnp.concatenate([wide_doc, wide_query], axis=0)
        grad_w_back = grad_w_back + jnp.einsum(
            "rf,rd->fd", active_low, update_full, preferred_element_type=jnp.float32
        )
        active_grad = jnp.einsum(
            "rd,fd->rf", update_full, full_back, preferred_element_type=jnp.float32
        )
        (inner_grad,) = gelu_pull(active_grad)
        inner_low = inner_grad.astype(jnp.bfloat16)
        grad_b_in = grad_b_in + jnp.sum(inner_low.astype(jnp.float32), axis=0)
        grad_w_in = grad_w_in + jnp.einsum(
            "rd,rf->df", hidden, inner_low, preferred_element_type=jnp.float32
        )
        hidden_part = jnp.einsum(
            "rf,df->rd", inner_low, full_in, preferred_element_type=jnp.float32
        )
        normed_doc_grad, normed_query_grad = sum_rows(hidden_part[:doc_len], hidden_part[doc_len:])
        normed_grad = jnp.concatenate([normed_doc_grad, normed_query_grad], axis=0) + resid_two_grad
        resid_one_grad, gain_one_grad, shift_one_grad = norm_one_pull(normed_grad)
        grad_gain_one = grad_gain_one + gain_one_grad
        grad_shift_one = grad_shift_one + shift_one_grad
        branch_low = resid_one_grad.astype(jnp.bfloat16)
        grad_b_out = grad_b_out + jnp.sum(branch_low.astype(jnp.float32), axis=0)
        branch_doc_grad, branch_query_grad = gather_rows(
            branch_low[:doc_rows], branch_low[doc_rows:]
        )
        branch_full = jnp.concatenate([branch_doc_grad, branch_query_grad], axis=0)
        grad_w_out = grad_w_out + jnp.einsum(
            "rc,rd->cd", mixed_heads, branch_full, preferred_element_type=jnp.float32
        )
        mixed_grad = jnp.einsum(
            "rd,cd->rc", branch_full, full_out, preferred_element_type=jnp.float32
        ).astype(jnp.bfloat16)
        mixed_grad = mixed_grad.reshape(total_rows, local_heads, head_size)
        query_doc_grad, key_doc_grad, value_doc_grad = attend_backward(
            query_rot[:doc_len],
            key_rot[:doc_len],
            value_low[:doc_len],
            doc_labels,
            doc_labels,
            logsum_doc,
            mixed_grad[:doc_len],
        )
        query_query_grad, key_query_grad, value_query_grad = attend_backward(
            query_rot[doc_len:],
            key_rot[doc_len:],
            value_low[doc_len:],
            query_labels,
            query_labels,
            logsum_query,
            mixed_grad[doc_len:],
        )
        query_rot_grad = jnp.concatenate([query_doc_grad, query_query_grad], axis=0)
        key_rot_grad = jnp.concatenate([key_doc_grad, key_query_grad], axis=0)
        value_grad = jnp.concatenate([value_doc_grad, value_query_grad], axis=0)
        pre_grads = [unrotate(query_rot_grad, angle), unrotate(key_rot_grad, angle), value_grad]
        pre_low = [item.reshape(total_rows, local_width).astype(jnp.bfloat16) for item in pre_grads]
        grad_b_qkv = grad_b_qkv + jnp.stack(
            [jnp.sum(item.astype(jnp.float32), axis=0) for item in pre_low]
        )
        grad_w_qkv = grad_w_qkv + jnp.stack(
            [
                jnp.einsum("rd,rc->dc", rows_in, item, preferred_element_type=jnp.float32)
                for item in pre_low
            ]
        )
        input_part = pre_low[0].dot(full_qkv[0].T, preferred_element_type=jnp.float32)
        input_part = input_part + jnp.einsum(
            "rc,dc->rd", pre_low[1], full_qkv[1], preferred_element_type=jnp.float32
        )
        input_part = input_part + jnp.einsum(
            "rc,dc->rd", pre_low[2], full_qkv[2], preferred_element_type=jnp.float32
        )
        input_doc, input_query = sum_rows(input_part[:doc_len], input_part[doc_len:])
        input_grad = resid_one_grad + jnp.concatenate([input_doc, input_query], axis=0)
        doc_inputs.append(input_grad[:doc_rows])
        query_inputs.append(input_grad[doc_rows:])
    out_qkv, out_out, out_in, out_back = (
        lax.psum_scatter(grad_w_qkv, "dp", scatter_dimension=1, tiled=True),
        lax.psum_scatter(grad_w_out, "dp", scatter_dimension=1, tiled=True),
        lax.psum_scatter(grad_w_in, "dp", scatter_dimension=0, tiled=True),
        lax.psum_scatter(grad_w_back, "dp", scatter_dimension=1, tiled=True),
    )
    wide_qkv = lax.dynamic_update_slice(
        jnp.zeros((3, local_width * ways), jnp.float32), grad_b_qkv, (0, column * local_width)
    )
    wide_in = lax.dynamic_update_slice(
        jnp.zeros((local_units * ways,), jnp.float32), grad_b_in, (column * local_units,)
    )
    sums = lax.psum(
        (
            wide_qkv,
            wide_in,
            grad_b_out,
            grad_gain_one,
            grad_shift_one,
            grad_b_back,
            grad_gain_two,
            grad_shift_two,
            grad_proj,
        ),
        ("dp", "tensor"),
    )
    bias_qkv = lax.dynamic_slice_in_dim(sums[0], column * local_width, local_width, axis=1)
    bias_in = lax.dynamic_slice_in_dim(sums[1], column * local_units, local_units, axis=0)
    shard_rows = width // groups
    proj_rows = lax.dynamic_slice_in_dim(sums[8], rank * shard_rows, shard_rows, axis=0)
    return (
        jnp.stack(doc_outs),
        jnp.stack(query_outs),
        jnp.stack(loss_rows),
        jnp.stack(doc_inputs),
        jnp.stack(query_inputs),
        out_qkv,
        bias_qkv,
        out_out,
        sums[2],
        sums[3],
        sums[4],
        out_in,
        bias_in,
        out_back,
        sums[5],
        sums[6],
        sums[7],
        proj_rows,
    )


def solution(mesh):
    in_specs = (
        P(None, ("dp", "tensor"), None),
        P(None, ("dp", "tensor"), None),
        P(None, ("dp", "tensor"), None),
        P(None, ("dp", "tensor"), None),
        P(),
        P(None, "dp"),
        P(None, "dp", "tensor"),
        P(None, "tensor"),
        P("tensor", "dp"),
        P(),
        P(),
        P(),
        P("dp", "tensor"),
        P("tensor"),
        P("tensor", "dp"),
        P(),
        P(),
        P(),
        P("dp", None),
    )
    out_specs = (
        P(None, ("dp", "tensor"), None),
        P(None, ("dp", "tensor"), None),
        P(None, ("dp", "tensor")),
        P(None, ("dp", "tensor"), None),
        P(None, ("dp", "tensor"), None),
        P(None, "dp", "tensor"),
        P(None, "tensor"),
        P("tensor", "dp"),
        P(),
        P(),
        P(),
        P("dp", "tensor"),
        P("tensor"),
        P("tensor", "dp"),
        P(),
        P(),
        P(),
        P("dp", None),
    )
    return jax.shard_map(body, mesh=mesh, in_specs=in_specs, out_specs=out_specs, check_vma=False)
```

profile of v0, /device:TPU:0, one launch (start us, length us, event | category | flops | bytes accessed | tf_op | source)
XLA Modules:
  0.0 1905.4 jit_solution(5464243227913904738)
XLA Ops:
  14.9 15.6 all-gather.3
  30.5 15.3 all-gather.1
  57.1 29.4 %all-gather.36.cloned.1.call-done = bf16[1,1024,1024]{2,1,0:T(8,128)(2,1)} async-done(((bf16[1,256,1024]{2,1,0:T(8,128)(2,1)}), bf16[1,1024,1024]{2,1,0:T(8,128)(2,1)}) %all-gather.36.cloned.1.call-update) | async-done | bytes 2097168 | tf_op jit(solution)/shard_map/all_gather | solution.py:82
  94.3 38.5 %all-gather.34.cloned.1.call-done = bf16[1,1024,1024]{2,1,0:T(8,128)(2,1)} async-done(((bf16[1,256,1024]{2,1,0:T(8,128)(2,1)}), bf16[1,1024,1024]{2,1,0:T(8,128)(2,1)}) %all-gather.34.cloned.1.call-update) | async-done | bytes 2097168 | tf_op jit(solution)/shard_map/all_gather | solution.py:82
  141.7 17.1 while.11
  168.9 16.1 while.10
  200.6 10.5 reduce-scatter.27.cloned.1.call-done
  211.1 77.2 %reduce-scatter.33.cloned.1.call-done = f32[256,1024]{1,0:T(8,128)} async-done(((f32[1024,1024]{1,0:T(8,128)}), f32[256,1024]{1,0:T(8,128)}) %reduce-scatter.33.cloned.1.call-update) | async-done | bytes 1048592 | tf_op jit(solution)/shard_map/reduce_scatter | solution.py:89
  288.2 79.7 %reduce-scatter.25.cloned.1.call-done = f32[256,1024]{1,0:T(8,128)} async-done(((f32[1024,1024]{1,0:T(8,128)}), f32[256,1024]{1,0:T(8,128)}) %reduce-scatter.25.cloned.1.call-update) | async-done | bytes 1048592 | tf_op jit(solution)/shard_map/reduce_scatter | solution.py:89
  376.1 16.5 all_gather.86
  392.6 16.2 all_gather.80
  408.9 17.0 all-gather.24.cloned.1.call-done
  429.7 25.3 %all-gather.20.cloned.1.call-done = bf16[1024,1024]{1,0:T(8,128)(2,1)} async-done(((bf16[128,1024]{1,0:T(8,128)(2,1)}), bf16[1024,1024]{1,0:T(8,128)(2,1)}) %all-gather.20.cloned.1.call-update) | async-done | bytes 2097168 | tf_op jit(solution)/shard_map/all_gather | solution.py:260
  455.0 16.3 multiply_convert_fusion.2
  471.3 13.8 all-gather.22.cloned.1.call-done
  493.3 39.9 %all-gather.18.cloned.1.call-done = bf16[1024,1024]{1,0:T(8,128)(2,1)} async-done(((bf16[256,1024]{1,0:T(8,128)(2,1)}), bf16[1024,1024]{1,0:T(8,128)(2,1)}) %all-gather.18.cloned.1.call-update) | async-done | bytes 2097168 | tf_op jit(solution)/shard_map/all_gather | solution.py:82
  535.5 14.3 multiply_convert_fusion.3
  579.2 77.2 %reduce-scatter.37.cloned.1.call-done = f32[256,1024]{1,0:T(8,128)} async-done(((f32[1024,1024]{1,0:T(8,128)}), f32[256,1024]{1,0:T(8,128)}) %reduce-scatter.37.cloned.1.call-update) | async-done | bytes 1048592 | tf_op jit(solution)/shard_map/reduce_scatter | solution.py:89
  656.4 79.5 %reduce-scatter.29.cloned.1.call-done = f32[256,1024]{1,0:T(8,128)} async-done(((f32[1024,1024]{1,0:T(8,128)}), f32[256,1024]{1,0:T(8,128)}) %reduce-scatter.29.cloned.1.call-update) | async-done | bytes 1048592 | tf_op jit(solution)/shard_map/reduce_scatter | solution.py:89
  752.4 13.7 all_gather.88
  775.9 13.1 all_gather.90
  793.1 19.3 %all-reduce.3 = (bf16[128,8,4]{0,2,1:T(4,128)(2,1)}, bf16[128,8,4]{0,2,1:T(4,128)(2,1)}) all-reduce(bf16[128,8,4]{0,2,1:T(4,128)(2,1)} %fusion.115, bf16[128,8,4]{0,2,1:T(4,128)(2,1)} %fusion.114), channel_id=1, replica_groups=mesh['dp'=8,'tensor'=4] {'tensor'}, use_global_device_ids=true, to_apply=%region_41.42 | all-reduce | flops 8192 | bytes 32768 | tf_op jit(solution)/shard_map/psum | solution.py:95
  848.1 13.0 reduce-scatter.55.cloned.1.call-done
  862.4 35.9 %reduce-scatter.41.cloned.1.call-done = f32[256,128]{1,0:T(8,128)} async-done(((f32[2048,128]{1,0:T(8,128)}), f32[256,128]{1,0:T(8,128)}) %reduce-scatter.41.cloned.1.call-update) | async-done | bytes 131088 | tf_op jit(solution)/shard_map/reduce_scatter | solution.py:364
  900.7 37.4 %reduce-scatter.53.cloned.1.call-done = f32[256,128]{1,0:T(8,128)} async-done(((f32[2048,128]{1,0:T(8,128)}), f32[256,128]{1,0:T(8,128)}) %reduce-scatter.53.cloned.1.call-update) | async-done | bytes 131088 | tf_op jit(solution)/shard_map/reduce_scatter | solution.py:364
  955.6 16.5 all_gather.93
  972.1 17.1 all_gather.97
  989.2 14.3 all-gather.30.cloned.1.call-done
  1019.7 31.3 %all-gather.26.cloned.1.call-done = bf16[1024,1024]{1,0:T(8,128)(2,1)} async-done(((bf16[256,1024]{1,0:T(8,128)(2,1)}), bf16[1024,1024]{1,0:T(8,128)(2,1)}) %all-gather.26.cloned.1.call-update) | async-done | bytes 2097168 | tf_op jit(solution)/shard_map/all_gather | solution.py:82
  1077.0 20.1 %reduce-scatter.47.cloned.1.call-done = f32[32,1024]{1,0:T(8,128)} async-done(((f32[128,1024]{1,0:T(8,128)}), f32[32,1024]{1,0:T(8,128)}) %reduce-scatter.47.cloned.1.call-update) | async-done | bytes 131088 | tf_op jit(solution)/shard_map/reduce_scatter | solution.py:90
  1097.1 77.2 %reduce-scatter.57.cloned.1.call-done = f32[256,1024]{1,0:T(8,128)} async-done(((f32[1024,1024]{1,0:T(8,128)}), f32[256,1024]{1,0:T(8,128)}) %reduce-scatter.57.cloned.1.call-update) | async-done | bytes 1048592 | tf_op jit(solution)/shard_map/reduce_scatter | solution.py:89
  1174.3 79.7 %reduce-scatter.45.cloned.1.call-done = f32[256,1024]{1,0:T(8,128)} async-done(((f32[1024,1024]{1,0:T(8,128)}), f32[256,1024]{1,0:T(8,128)}) %reduce-scatter.45.cloned.1.call-update) | async-done | bytes 1048592 | tf_op jit(solution)/shard_map/reduce_scatter | solution.py:89
  1270.1 16.7 all_gather.95
  1286.8 27.2 %all-gather.28.cloned.1.call-done = bf16[1024,1024]{1,0:T(8,128)(2,1)} async-done(((bf16[256,1024]{1,0:T(8,128)(2,1)}), bf16[1024,1024]{1,0:T(8,128)(2,1)}) %all-gather.28.cloned.1.call-update) | async-done | bytes 2097168 | tf_op jit(solution)/shard_map/all_gather | solution.py:82
  1324.0 60.2 %while.12 = (s32[]{:T(128)}, f32[1024,4,64]{0,2,1:T(8,128)S(1)}, f32[1024,4,64]{0,2,1:T(8,128)}, f32[2,512,4,64]{1,0,3,2:T(2,128)}, bf16[2,512,4,64]{1,3,2,0:T(8...) while((s32[]{:T(128)}, f32[1024,4,64]{0,2,1:T(8,128)S(1)}, ...), condition=%wide.region_57.58_spmd.clone, body=%wide.region_55.57_spmd.clone.sunk | while | flops 1375598592 | bytes 164694368 | solution.py:176
  1334.6 10.4 dynamic_update_slice.70
  1364.0 10.4 dynamic_update_slice.70
  1396.1 14.0 all_gather.99
  1420.5 58.4 %while.13 = (s32[]{:T(128)}, f32[1024,4,64]{0,2,1:T(8,128)S(1)}, f32[1024,4,64]{0,2,1:T(8,128)}, f32[2,512,4,64]{1,0,3,2:T(2,128)}, bf16[2,512,4,64]{1,3,2,0:T(8...) while((s32[]{:T(128)}, f32[1024,4,64]{0,2,1:T(8,128)S(1)}, ...), condition=%wide.region_72.73_spmd.clone, body=%wide.region_70.72_spmd.clone.sunk | while | flops 1375598592 | bytes 164694368 | solution.py:176
  1430.5 10.4 dynamic_update_slice.71
  1458.9 10.4 dynamic_update_slice.71
  1544.7 43.8 %all-reduce.2 = (f32[3,1024]{1,0:T(4,128)S(1)}, f32[1024]{0:T(1024)}, f32[1024]{0:T(1024)}, f32[1024]{0:T(1024)}, f32[4096]{0:T(1024)S(1)}, /*index=5*/f32[1024]{0:T(1024)}, f32[1024]{0:T(1024)}, f32[1024]{0:T(1024)}) all-reduce(f32[3,1024]{1,0:T(4,128)S(1)} %fusion.165, ...), channel_id=1, replica_groups=mesh['dp'=8,'tensor'=4] {'dp','tensor'}, use_global_device_ids=true, to_apply=%region_83.84 | all-reduce | flops 13312 | bytes 106496 | tf_op jit(solution)/shard_map/psum | solution.py:475
  1596.9 22.3 %reduce-scatter.63.cloned.1.call-done = f32[32,1024]{1,0:T(8,128)} async-done(((f32[128,1024]{1,0:T(8,128)}), f32[32,1024]{1,0:T(8,128)}) %reduce-scatter.63.cloned.1.call-update) | async-done | bytes 131088 | tf_op jit(solution)/shard_map/reduce_scatter | solution.py:90
  1619.1 77.4 %reduce-scatter.61.cloned.1.call-done = f32[256,1024]{1,0:T(8,128)} async-done(((f32[1024,1024]{1,0:T(8,128)}), f32[256,1024]{1,0:T(8,128)}) %reduce-scatter.61.cloned.1.call-update) | async-done | bytes 1048592 | tf_op jit(solution)/shard_map/reduce_scatter | solution.py:89
  1700.5 52.1 %reduce-scatter.71.cloned.1.call-done = f32[1024,128]{1,0:T(8,128)} async-done(((f32[1024,1024]{1,0:T(8,128)}), f32[1024,128]{1,0:T(8,128)}) %reduce-scatter.71.cloned.1.call-update) | async-done | bytes 524304 | tf_op jit(solution)/shard_map/reduce_scatter | solution.py:467
  1752.6 55.3 %reduce-scatter.69.cloned.1.call-done = f32[128,1024]{1,0:T(8,128)} async-done(((f32[1024,1024]{1,0:T(8,128)}), f32[128,1024]{1,0:T(8,128)}) %reduce-scatter.69.cloned.1.call-update) | async-done | bytes 524304 | tf_op jit(solution)/shard_map/reduce_scatter | solution.py:466
  1807.9 40.2 %reduce-scatter.67.cloned.1.call-done = f32[256,128]{1,0:T(8,128)} async-done(((f32[256,1024]{1,0:T(8,128)}), f32[256,128]{1,0:T(8,128)}) %reduce-scatter.67.cloned.1.call-update) | async-done | bytes 131088 | tf_op jit(solution)/shard_map/reduce_scatter | solution.py:465
  1848.0 50.4 %reduce-scatter.65.cloned.1.call-done = f32[3,128,256]{2,1,0:T(8,128)} async-done(((f32[3,1024,256]{2,1,0:T(8,128)}), f32[3,128,256]{2,1,0:T(8,128)}) %reduce-scatter.65.cloned.1.call-update) | async-done | bytes 393232 | tf_op jit(solution)/shard_map/reduce_scatter | solution.py:464
  (996 shorter events, 474.2 us)
Async XLA Ops:
  7.2 49.9 %all-gather.16.cloned.1.call-start = ((), (), s32[]{:S(2)}) async-start(), calls=%async_computation.24 | async-start | bytes 1769472 | tf_op jit(solution)/shard_map/all_gather | solution.py:258
  8.0 78.5 %all-gather.36.cloned.1.call-start = ((), (), s32[]{:S(2)}) async-start(), calls=%async_computation.59 | async-start | bytes 2621440 | tf_op jit(solution)/shard_map/all_gather | solution.py:82
  10.7 122.1 %all-gather.34.cloned.1.call-start = ((), (), s32[]{:S(2)}) async-start(), calls=%async_computation.58 | async-start | bytes 2621440 | tf_op jit(solution)/shard_map/all_gather | solution.py:82
  11.4 189.2 %reduce-scatter.35.cloned.1.call-start = ((), (), s32[]{:S(2)}) async-start(), calls=%async_computation.33 | async-start | bytes 655360 | tf_op jit(solution)/shard_map/reduce_scatter | solution.py:90
  55.8 130.7 %copy-start.61 = (bf16[256,1024]{1,0:T(8,128)(2,1)}, bf16[256,1024]{1,0:T(8,128)(2,1)S(1)}, u32[]{:S(2)}) copy-start(bf16[256,1024]{1,0:T(8,128)(2,1)S(1)} %all_gather.78) | copy-start | bytes 1572868
  167.2 43.9 %reduce-scatter.27.cloned.1.call-start = ((), (), s32[]{:S(2)}) async-start(), calls=%async_computation.26 | async-start | bytes 655360 | tf_op jit(solution)/shard_map/reduce_scatter | solution.py:90
  190.5 97.7 %reduce-scatter.33.cloned.1.call-start = ((), (), s32[]{:S(2)}) async-start(), calls=%async_computation.32 | async-start | bytes 5242880 | tf_op jit(solution)/shard_map/reduce_scatter | solution.py:89
  195.4 172.5 %reduce-scatter.25.cloned.1.call-start = ((), (), s32[]{:S(2)}) async-start(), calls=%async_computation.25 | async-start | bytes 5242880 | tf_op jit(solution)/shard_map/reduce_scatter | solution.py:89
  200.5 167.5 %copy-start.93 = (bf16[256,1024]{1,0:T(8,128)(2,1)S(1)}, bf16[256,1024]{1,0:T(8,128)(2,1)}, u32[]{:S(2)}) copy-start(bf16[256,1024]{1,0:T(8,128)(2,1)} %get-tuple-element.782) | copy-start | bytes 1572868
  200.5 167.5 %copy-start.94 = (bf16[256,1024]{1,0:T(8,128)(2,1)S(1)}, bf16[256,1024]{1,0:T(8,128)(2,1)}, u32[]{:S(2)}) copy-start(bf16[256,1024]{1,0:T(8,128)(2,1)} %get-tuple-element.783) | copy-start | bytes 1572868
  200.5 167.5 %copy-start.141 = (bf16[32,1024]{1,0:T(8,128)(2,1)S(1)}, bf16[32,1024]{1,0:T(8,128)(2,1)}, u32[]{:S(2)}) copy-start(bf16[32,1024]{1,0:T(8,128)(2,1)} %get-tuple-element.796) | copy-start | bytes 196612
  200.5 167.5 %copy-start.142 = (bf16[32,1024]{1,0:T(8,128)(2,1)S(1)}, bf16[32,1024]{1,0:T(8,128)(2,1)}, u32[]{:S(2)}) copy-start(bf16[32,1024]{1,0:T(8,128)(2,1)} %get-tuple-element.797) | copy-start | bytes 196612
  200.5 167.5 %copy-start.236 = (f32[1024]{0:T(1024)S(1)}, f32[1024]{0:T(1024)}, u32[]{:S(2)}) copy-start(f32[1024]{0:T(1024)} %param.36) | copy-start | bytes 12292
  200.5 225.4 %all-gather.24.cloned.1.call-start = ((), (), s32[]{:S(2)}) async-start(), calls=%async_computation.34 | async-start | bytes 2621440 | tf_op jit(solution)/shard_map/all_gather | solution.py:82
  373.3 81.8 %all-gather.20.cloned.1.call-start = ((), (), s32[]{:S(2)}) async-start(), calls=%async_computation.28 | async-start | bytes 2359296 | tf_op jit(solution)/shard_map/all_gather | solution.py:260
  374.0 111.1 %all-gather.22.cloned.1.call-start = ((), (), s32[]{:S(2)}) async-start(), calls=%async_computation.29 | async-start | bytes 2359296 | tf_op jit(solution)/shard_map/all_gather | solution.py:261
  374.6 158.6 %all-gather.18.cloned.1.call-start = ((), (), s32[]{:S(2)}) async-start(), calls=%async_computation.27 | async-start | bytes 2621440 | tf_op jit(solution)/shard_map/all_gather | solution.py:82
  408.9 169.8 %reduce-scatter.39.cloned.1.call-start = ((), (), s32[]{:S(2)}) async-start(), calls=%async_computation.36 | async-start | bytes 655360 | tf_op jit(solution)/shard_map/reduce_scatter | solution.py:90
  493.1 86.1 %reduce-scatter.31.cloned.1.call-start = ((), (), s32[]{:S(2)}) async-start(), calls=%async_computation.31 | async-start | bytes 655360 | tf_op jit(solution)/shard_map/reduce_scatter | solution.py:90
  555.5 100.9 %reduce-scatter.37.cloned.1.call-start = ((), (), s32[]{:S(2)}) async-start(), calls=%async_computation.35 | async-start | bytes 5242880 | tf_op jit(solution)/shard_map/reduce_scatter | solution.py:89
  560.4 175.6 %reduce-scatter.29.cloned.1.call-start = ((), (), s32[]{:S(2)}) async-start(), calls=%async_computation.30 | async-start | bytes 5242880 | tf_op jit(solution)/shard_map/reduce_scatter | solution.py:89
  565.2 282.2 %reduce-scatter.43.cloned.1.call-start = ((), (), s32[]{:S(2)}) async-start(), calls=%async_computation.38 | async-start | bytes 40960 | tf_op jit(solution)/shard_map/reduce_scatter | solution.py:367
  825.0 36.1 %reduce-scatter.55.cloned.1.call-start = ((), (), s32[]{:S(2)}) async-start(), calls=%async_computation.46 | async-start | bytes 40960 | tf_op jit(solution)/shard_map/reduce_scatter | solution.py:367
  837.7 60.7 %reduce-scatter.41.cloned.1.call-start = ((), (), s32[]{:S(2)}) async-start(), calls=%async_computation.37 | async-start | bytes 1179648 | tf_op jit(solution)/shard_map/reduce_scatter | solution.py:364
  840.1 98.0 %reduce-scatter.53.cloned.1.call-start = ((), (), s32[]{:S(2)}) async-start(), calls=%async_computation.45 | async-start | bytes 1179648 | tf_op jit(solution)/shard_map/reduce_scatter | solution.py:364
  842.6 161.0 %all-gather.30.cloned.1.call-start = ((), (), s32[]{:S(2)}) async-start(), calls=%async_computation.47 | async-start | bytes 2621440 | tf_op jit(solution)/shard_map/all_gather | solution.py:82
  950.8 100.2 %all-gather.26.cloned.1.call-start = ((), (), s32[]{:S(2)}) async-start(), calls=%async_computation.39 | async-start | bytes 2621440 | tf_op jit(solution)/shard_map/all_gather | solution.py:82
  953.8 123.1 %reduce-scatter.59.cloned.1.call-start = ((), (), s32[]{:S(2)}) async-start(), calls=%async_computation.49 | async-start | bytes 655360 | tf_op jit(solution)/shard_map/reduce_scatter | solution.py:90
  1019.4 77.6 %reduce-scatter.47.cloned.1.call-start = ((), (), s32[]{:S(2)}) async-start(), calls=%async_computation.41 | async-start | bytes 655360 | tf_op jit(solution)/shard_map/reduce_scatter | solution.py:90
  1067.0 107.3 %reduce-scatter.57.cloned.1.call-start = ((), (), s32[]{:S(2)}) async-start(), calls=%async_computation.48 | async-start | bytes 5242880 | tf_op jit(solution)/shard_map/reduce_scatter | solution.py:89
  1071.9 182.0 %reduce-scatter.45.cloned.1.call-start = ((), (), s32[]{:S(2)}) async-start(), calls=%async_computation.40 | async-start | bytes 5242880 | tf_op jit(solution)/shard_map/reduce_scatter | solution.py:89
  1076.9 177.1 %copy-start.163 = (f32[288]{0:T(512)S(1)}, f32[288]{0:T(512)}, u32[]{:S(2)}) copy-start(f32[288]{0:T(512)} %copy-done.162) | copy-start | bytes 3460
  1076.9 177.1 %copy-start.165 = (f32[288]{0:T(512)S(1)}, f32[288]{0:T(512)}, u32[]{:S(2)}) copy-start(f32[288]{0:T(512)} %copy-done.164) | copy-start | bytes 3460
  1076.9 177.1 %copy-start.169 = (f32[1024]{0:T(1024)S(1)}, f32[1024]{0:T(1024)}, u32[]{:S(2)}) copy-start(f32[1024]{0:T(1024)} %param.37) | copy-start | bytes 12292
  1076.9 177.1 %copy-start.176 = (f32[288]{0:T(512)S(1)}, f32[288]{0:T(512)}, u32[]{:S(2)}) copy-start(f32[288]{0:T(512)} %copy-done.175) | copy-start | bytes 3460
  1076.9 237.0 %all-gather.28.cloned.1.call-start = ((), (), s32[]{:S(2)}) async-start(), calls=%async_computation.42 | async-start | bytes 2621440 | tf_op jit(solution)/shard_map/all_gather | solution.py:82
  1264.0 146.2 %all-gather.32.cloned.1.call-start = ((), (), s32[]{:S(2)}) async-start(), calls=%async_computation.50 | async-start | bytes 2621440 | tf_op jit(solution)/shard_map/all_gather | solution.py:82
  1266.5 275.9 %all-reduce.6.cloned.1.call-start = ((), (), s32[]{:S(2)}) async-start(), calls=%async_computation.57 | async-start | bytes 1048576 | tf_op jit(solution)/shard_map/psum | solution.py:475
  1269.2 320.5 %reduce-scatter.51.cloned.1.call-start = ((), (), s32[]{:S(2)}) async-start(), calls=%async_computation.44 | async-start | bytes 655360 | tf_op jit(solution)/shard_map/reduce_scatter | solution.py:90
  1395.2 199.5 %reduce-scatter.49.cloned.1.call-start = ((), (), s32[]{:S(2)}) async-start(), calls=%async_computation.43 | async-start | bytes 5242880 | tf_op jit(solution)/shard_map/reduce_scatter | solution.py:89
  1418.9 200.2 %reduce-scatter.63.cloned.1.call-start = ((), (), s32[]{:S(2)}) async-start(), calls=%async_computation.52 | async-start | bytes 655360 | tf_op jit(solution)/shard_map/reduce_scatter | solution.py:90
  1490.5 206.1 %reduce-scatter.61.cloned.1.call-start = ((), (), s32[]{:S(2)}) async-start(), calls=%async_computation.51 | async-start | bytes 5242880 | tf_op jit(solution)/shard_map/reduce_scatter | solution.py:89
  1495.3 257.3 %reduce-scatter.71.cloned.1.call-start = ((), (), s32[]{:S(2)}) async-start(), calls=%async_computation.56 | async-start | bytes 4718592 | tf_op jit(solution)/shard_map/reduce_scatter | solution.py:467
  1505.5 302.4 %reduce-scatter.69.cloned.1.call-start = ((), (), s32[]{:S(2)}) async-start(), calls=%async_computation.55 | async-start | bytes 4718592 | tf_op jit(solution)/shard_map/reduce_scatter | solution.py:466
  1517.6 330.4 %reduce-scatter.67.cloned.1.call-start = ((), (), s32[]{:S(2)}) async-start(), calls=%async_computation.54 | async-start | bytes 1179648 | tf_op jit(solution)/shard_map/reduce_scatter | solution.py:465
  1526.7 371.7 %reduce-scatter.65.cloned.1.call-start = ((), (), s32[]{:S(2)}) async-start(), calls=%async_computation.53 | async-start | bytes 3538944 | tf_op jit(solution)/shard_map/reduce_scatter | solution.py:464
  1542.3 154.3 %copy-start.30 = (f32[288,1024]{1,0:T(8,128)S(1)}, f32[288,1024]{1,0:T(8,128)}, u32[]{:S(2)}) copy-start(f32[288,1024]{1,0:T(8,128)} %copy-done.29) | copy-start | bytes 3538948
  1542.3 154.3 %copy-start.207 = (f32[288]{0:T(512)S(1)}, f32[288]{0:T(512)}, u32[]{:S(2)}) copy-start(f32[288]{0:T(512)} %copy-done.206) | copy-start | bytes 3460
  (264 other events, 1950.9 us)
Sparse Core Ops, SparseCore 0:
  9.9 28.3 all-gather.15
  40.5 45.9 all-gather.35
  88.0 44.6 all-gather.33
  167.3 20.3 reduce-scatter.34
  190.7 20.3 reduce-scatter.26
  213.2 74.9 reduce-scatter.32
  290.6 77.2 reduce-scatter.24
  373.4 52.4 all-gather.23
  427.8 27.2 all-gather.19
  456.8 28.3 all-gather.21
  487.3 45.9 all-gather.17
  535.9 20.3 reduce-scatter.38
  559.2 19.9 reduce-scatter.30
  581.3 75.0 reduce-scatter.36
  658.6 77.2 reduce-scatter.28
  825.1 16.1 reduce-scatter.42
  844.0 17.0 reduce-scatter.54
  864.1 34.1 reduce-scatter.40
  902.1 35.9 reduce-scatter.52
  950.9 52.5 all-gather.29
  1005.7 45.2 all-gather.25
  1053.8 20.3 reduce-scatter.58
  1077.1 19.9 reduce-scatter.46
  1099.2 75.0 reduce-scatter.56
  1176.7 77.2 reduce-scatter.44
  1264.1 49.8 all-gather.27
  1315.9 45.2 all-gather.31
  1366.5 126.7 all-reduce.5
  1495.7 20.6 reduce-scatter.50
  1518.6 76.1 reduce-scatter.48
  1597.0 22.0 reduce-scatter.62
  1621.4 75.1 reduce-scatter.60
  1700.7 51.8 reduce-scatter.70
  1756.5 51.2 reduce-scatter.68
  1811.9 36.0 reduce-scatter.66
  1852.2 46.2 reduce-scatter.64
where the time goes:
time: 1920 us; the launch traced here: 1910 us
  waiting for transfers between devices  1130 us (59%)
  blocking collectives  258 us (13%)
  matrix products  210 us (11%)
  local copies, waits for them, and re-layouts  204 us (11%)
  other arithmetic  82.3 us (4%)
    reduce_scatter x8, waiting for transfers between devices, sum_rows(): lax.psum_scatter(first, 'tensor', scatter_dimension=0, tiled=True)  553 us
    all_gather x8, waiting for transfers between devices, gather_rows(): lax.all_gather(first, 'tensor', axis=0, tiled=True)  197 us
    all_gather x8, blocking collectives, gather_rows(): lax.all_gather(second, 'tensor', axis=0, tiled=True)  128 us
    reduce_scatter x2, waiting for transfers between devices, body(): lax.psum_scatter(doc_grads.reshape(groups * doc_rows, proj_width), 'dp',...  73.3 us
    reduce_scatter x1, waiting for transfers between devices, body(): lax.psum_scatter(grad_w_in, 'dp', scatter_dimension=0, tiled=True)  55.3 us
    unnamed x504, local copies, waits for them, and re-layouts  55.1 us
    reduce_scatter x8, waiting for transfers between devices, sum_rows(): lax.psum_scatter(second, 'tensor', scatter_dimension=0, tiled=True)  53.4 us
    reduce_scatter x1, waiting for transfers between devices, body(): lax.psum_scatter(grad_w_back, 'dp', scatter_dimension=1, tiled=True)  52.1 us
  transfers between devices with their start and end apart: 36, of which 28 were waited for; matrix products, arithmetic and copies ran while one was open for 20% of the time, Pallas kernels for 0%

commit v1 on v0

v1 whole, which is shorter than its diff:
```python
import functools

import jax
import jax.numpy as jnp
from jax import lax
from jax.experimental import pallas as pl
from jax.experimental.pallas import tpu as pltpu
from jax.sharding import PartitionSpec as P

HEAD_WIDTH = 64
QLEN = 32
FULL_PRECISION = lax.Precision.HIGHEST
TAU = 20.0
EPS = 1e-05
LOGIT_SCALE = 2.0
MASKED = -1e30
AXES = ("dp", "tensor")
BF = jnp.bfloat16
F32 = jnp.float32


def layer_norm(values, gain, shift):
    center = values - jnp.mean(values, axis=-1, keepdims=True)
    spread = jnp.mean(center * center, axis=-1, keepdims=True)
    return center * lax.rsqrt(spread + EPS) * gain + shift


def normalize(values):
    return values * lax.rsqrt(jnp.sum(values * values, axis=-1, keepdims=True) + 1e-06)


def gelu_exact(values):
    return jax.nn.gelu(values, approximate=False)


def dot_nn(a, b):
    return lax.dot_general(a, b, (((1,), (0,)), ((), ())), preferred_element_type=F32)


def dot_nt(a, b):
    return lax.dot_general(a, b, (((1,), (1,)), ((), ())), preferred_element_type=F32)


def dot_tn(a, b):
    return lax.dot_general(a, b, (((0,), (0,)), ((), ())), preferred_element_type=F32)


def half_turn(values):
    lane = lax.broadcasted_iota(jnp.int32, values.shape, 1)
    ahead = jnp.roll(values, -32, axis=1)
    behind = jnp.roll(values, 32, axis=1)
    return jnp.where(lane % HEAD_WIDTH < 32, -ahead, behind)


def attention_forward(q, k_own, v_own, k_far, v_far, col_labels, own_labels, far_labels, docs):
    rows, width = q.shape
    far = k_far.shape[0]
    block = 128
    asked = rows - docs

    def kernel(q_ref, ko_ref, vo_ref, kf_ref, vf_ref, lc_ref, lo_ref, lf_ref, o_ref):
        lane = lax.broadcasted_iota(jnp.int32, (1, 128), 1)

        def part(start, size, keys, sames):
            q_block = q_ref[pl.ds(start, size), :]
            outs = []
            for head in range(2):
                mask = (lane // HEAD_WIDTH) == head
                q_head = jnp.where(mask, q_block, jnp.zeros_like(q_block))
                scores = [
                    jnp.where(same, dot_nt(q_head, key), MASKED)
                    for (key, _), same in zip(keys, sames)
                ]
                top = functools.reduce(
                    jnp.maximum, [jnp.max(s, axis=-1, keepdims=True) for s in scores]
                )
                powers = [jnp.exp(s - top) for s in scores]
                total = functools.reduce(
                    jnp.add, [jnp.sum(p, axis=-1, keepdims=True) for p in powers]
                )
                mixed = functools.reduce(
                    jnp.add, [dot_nn(p.astype(BF), value) for p, (_, value) in zip(powers, keys)]
                )
                outs.append(mixed * (1.0 / total))
            o_ref[pl.ds(start, size), :] = jnp.where(lane < HEAD_WIDTH, outs[0], outs[1]).astype(BF)

        doc_keys = [
            (ko_ref[:docs, :], vo_ref[:docs, :]),
            (kf_ref[...], vf_ref[...]),
        ]
        for at in range(docs // block):
            labels = lc_ref[pl.ds(at * block, block), :]
            part(at * block, block, doc_keys, [labels == lo_ref[...], labels == lf_ref[...]])
        row = lax.broadcasted_iota(jnp.int32, (asked, asked), 0) // QLEN
        col = lax.broadcasted_iota(jnp.int32, (asked, asked), 1) // QLEN
        part(docs, asked, [(ko_ref[docs:, :], vo_ref[docs:, :])], [row == col])

    head_block = lambda n: pl.BlockSpec((n, 128), lambda h: (0, h))
    whole = lambda shape: pl.BlockSpec(shape, lambda h: (0, 0))
    return pl.pallas_call(
        kernel,
        grid=(width // 128,),
        in_specs=[
            head_block(rows),
            head_block(rows),
            head_block(rows),
            head_block(far),
            head_block(far),
            whole((docs, 1)),
            whole((1, docs)),
            whole((1, far)),
        ],
        out_specs=head_block(rows),
        out_shape=jax.ShapeDtypeStruct((rows, width), BF),
        compiler_params=pltpu.CompilerParams(vmem_limit_bytes=40 << 20),
        name="attend_forward",
        cost_estimate=pl.CostEstimate(
            flops=4 * rows * 2 * docs * width,
            bytes_accessed=2 * (4 * rows + 2 * far) * width,
            transcendentals=rows * 2 * docs * width // 64,
        ),
    )(q, k_own, v_own, k_far, v_far, col_labels, own_labels, far_labels)


def attention_backward(
    q, k_own, v_own, k_far, v_far, grad, col_labels, own_labels, far_labels, docs
):
    rows, width = q.shape
    far = k_far.shape[0]
    block = 128
    asked = rows - docs

    def kernel(
        q_ref, ko_ref, vo_ref, kf_ref, vf_ref, g_ref, lc_ref, lo_ref, lf_ref,
        dq_ref, dko_ref, dvo_ref, dkf_ref, dvf_ref, sums_own, sums_far,
    ):
        lane = lax.broadcasted_iota(jnp.int32, (1, 128), 1)
        sums_own[...] = jnp.zeros_like(sums_own)
        sums_far[...] = jnp.zeros_like(sums_far)

        def part(start, size, keys, sames, sums):
            q_block = q_ref[pl.ds(start, size), :]
            g_block = g_ref[pl.ds(start, size), :]
            grads = []
            for head in range(2):
                mask = (lane // HEAD_WIDTH) == head
                q_head = jnp.where(mask, q_block, jnp.zeros_like(q_block))
                g_head = jnp.where(mask, g_block, jnp.zeros_like(g_block))
                scores = [
                    jnp.where(same, dot_nt(q_head, key), MASKED)
                    for (key, _), same in zip(keys, sames)
                ]
                top = functools.reduce(
                    jnp.maximum, [jnp.max(s, axis=-1, keepdims=True) for s in scores]
                )
                powers = [jnp.exp(s - top) for s in scores]
                total = functools.reduce(
                    jnp.add, [jnp.sum(p, axis=-1, keepdims=True) for p in powers]
                )
                inverse = 1.0 / total
                g_head = (g_head.astype(F32) * inverse).astype(BF)
                pulls = [dot_nt(g_head, value) for _, value in keys]
                mean = functools.reduce(
                    jnp.add,
                    [jnp.sum(p * d, axis=-1, keepdims=True) for p, d in zip(powers, pulls)],
                ) * inverse
                turned = [(p * (d - mean)).astype(BF) for p, d in zip(powers, pulls)]
                got = functools.reduce(
                    jnp.add, [dot_nn(s, key) for s, (key, _) in zip(turned, keys)]
                )
                grads.append(got * 0.125)
                for (ref, first, count), s, p in zip(sums, turned, powers):
                    ref[0, pl.ds(first, count), :] += dot_tn(s, q_head)
                    ref[1, pl.ds(first, count), :] += dot_tn(p.astype(BF), g_head)
            dq_ref[pl.ds(start, size), :] = jnp.where(lane < HEAD_WIDTH, grads[0], grads[1])

        doc_keys = [
            (ko_ref[:docs, :], vo_ref[:docs, :]),
            (kf_ref[...], vf_ref[...]),
        ]
        for at in range(docs // block):
            labels = lc_ref[pl.ds(at * block, block), :]
            part(
                at * block,
                block,
                doc_keys,
                [labels == lo_ref[...], labels == lf_ref[...]],
                [(sums_own, 0, docs), (sums_far, 0, far)],
            )
        row = lax.broadcasted_iota(jnp.int32, (asked, asked), 0) // QLEN
        col = lax.broadcasted_iota(jnp.int32, (asked, asked), 1) // QLEN
        part(
            docs,
            asked,
            [(ko_ref[docs:, :], vo_ref[docs:, :])],
            [row == col],
            [(sums_own, docs, asked)],
        )
        dko_ref[...] = sums_own[0]
        dvo_ref[...] = sums_own[1]
        dkf_ref[...] = sums_far[0].astype(BF)
        dvf_ref[...] = sums_far[1].astype(BF)

    head_block = lambda n: pl.BlockSpec((n, 128), lambda h: (0, h))
    whole = lambda shape: pl.BlockSpec(shape, lambda h: (0, 0))
    return pl.pallas_call(
        kernel,
        grid=(width // 128,),
        in_specs=[
            head_block(rows),
            head_block(rows),
            head_block(rows),
            head_block(far),
            head_block(far),
            head_block(rows),
            whole((docs, 1)),
            whole((1, docs)),
            whole((1, far)),
        ],
        out_specs=[
            head_block(rows),
            head_block(rows),
            head_block(rows),
            head_block(far),
            head_block(far),
        ],
        out_shape=[
            jax.ShapeDtypeStruct((rows, width), F32),
            jax.ShapeDtypeStruct((rows, width), F32),
            jax.ShapeDtypeStruct((rows, width), F32),
            jax.ShapeDtypeStruct((far, width), BF),
            jax.ShapeDtypeStruct((far, width), BF),
        ],
        scratch_shapes=[pltpu.VMEM((2, rows, 128), F32), pltpu.VMEM((2, far, 128), F32)],
        compiler_params=pltpu.CompilerParams(vmem_limit_bytes=40 << 20),
        name="attend_backward",
        cost_estimate=pl.CostEstimate(
            flops=10 * rows * 2 * docs * width,
            bytes_accessed=4 * (6 * rows + 4 * far) * width,
            transcendentals=rows * 2 * docs * width // 64,
        ),
    )(q, k_own, v_own, k_far, v_far, grad, col_labels, own_labels, far_labels)


def body(
    x_doc,
    x_query,
    doc_cot,
    query_cot,
    lengths,
    positives,
    w_qkv,
    b_qkv,
    w_out,
    b_out,
    gain_one,
    shift_one,
    w_in,
    b_in,
    w_back,
    b_back,
    gain_two,
    shift_two,
    w_proj,
):
    ways = lax.axis_size("tensor")
    groups = lax.axis_size("dp")
    column = lax.axis_index("tensor")
    rank = lax.axis_index("dp")
    core = rank % 2
    chip = rank // 2
    chips = groups // 2
    micro, quarter, width = x_doc.shape
    asked = x_query.shape[1]
    segments = lengths.shape[2] - 1
    proj_width = w_proj.shape[1]
    heads_local = w_qkv.shape[2]
    units_local = w_in.shape[1]
    block = width // groups
    assert ways == 2 * micro and ways == 4

    def exchange(value, dr=0, dt=0):
        pairs = [
            (r * ways + t, (r ^ dr) * ways + (t ^ dt)) for r in range(groups) for t in range(ways)
        ]
        return lax.ppermute(value, AXES, pairs)

    chip_bits = []
    bit = 2
    while bit < groups:
        chip_bits.append(bit)
        bit *= 2

    def gather_weights(pack, reverse):
        pieces = [pack] + [exchange(pack, dt=j) for j in range(1, ways)]
        pieces = [(0, jnp.concatenate(pieces, axis=-1))]
        order = chip_bits[::-1] if reverse and len(chip_bits) == 2 else chip_bits
        for dr in order:
            pieces = pieces + [(j + dr // 2, exchange(p, dr=dr)) for j, p in pieces]
            if len(pieces) >= 4 or dr == order[-1]:
                pieces.sort(key=lambda item: item[0])
                pieces = [(0, jnp.concatenate([p for _, p in pieces], axis=-2))]
        (_, half), = pieces
        return jnp.concatenate([half, exchange(half, dr=1)], axis=-2)

    def gather_proj(pack):
        for dr in chip_bits + [1]:
            pack = jnp.concatenate([pack, exchange(pack, dr=dr)], axis=0)
        return pack

    unit_micro = column // 2
    unit_row = chip * 2 + column % 2

    def rows_in(docs, queries):
        blocks = jnp.concatenate([docs, queries], axis=1)
        got = []
        for j in range(2):
            send = jnp.where((column + j) % 2 == 0, blocks[0], blocks[1])
            pairs = []
            for r in range(groups):
                for t in range(ways):
                    m = (t + j) % 2
                    pairs.append(
                        (r * ways + t, ((r // 2) * 2 + t // 2) * ways + 2 * m + r % 2)
                    )
            got.append(lax.ppermute(send, AXES, pairs))
        first = jnp.where(unit_micro == 0, got[0], got[1])
        second = jnp.where(unit_micro == 0, got[1], got[0])
        return jnp.concatenate(
            [first[:quarter], second[:quarter], first[quarter:], second[quarter:]], axis=0
        )

    def quarters_out(first, second):
        got = []
        for j in range(2):
            send = jnp.where((unit_micro + j) % 2 == 0, first, second)
            pairs = []
            for r in range(groups):
                for t in range(ways):
                    m = t // 2
                    pairs.append(
                        (
                            r * ways + t,
                            ((r // 2) * 2 + t % 2) * ways + 2 * (r % 2) + (m + j) % 2,
                        )
                    )
            got.append(lax.ppermute(send, AXES, pairs))
        even = jnp.where(column % 2 == 0, got[0], got[1])
        odd = jnp.where(column % 2 == 0, got[1], got[0])
        return jnp.stack([even, odd])

    def rows_out(values):
        docs = 2 * quarter
        first = jnp.concatenate([values[:quarter], values[docs : docs + asked]], axis=0)
        second = jnp.concatenate([values[quarter:docs], values[docs + asked :]], axis=0)
        blocks = quarters_out(first, second)
        return blocks[:, :quarter], blocks[:, quarter:]

    place = jnp.arange(width, dtype=jnp.int32)
    step = place // block
    actual = (rank ^ (2 * (step % chips) + step // chips)) * block + place % block
    turn = (place[:, None] == actual[None, :]).astype(BF)

    pack_one = jnp.stack([w_qkv[0], w_qkv[1]])
    pack_two = jnp.stack([w_qkv[2], w_out.T])
    full_qk = gather_weights(pack_one, False)
    full_vo = gather_weights(pack_two, True)
    bias_pack = jnp.concatenate([b_qkv.reshape(-1), b_in])[None]
    biases = [bias_pack] + [exchange(bias_pack, dt=j) for j in range(1, ways)]
    bias_qkv = jnp.concatenate(
        [b[0, : 3 * heads_local].reshape(3, heads_local) for b in biases], axis=1
    )
    bias_in = jnp.concatenate([b[0, 3 * heads_local :] for b in biases])
    own_x = rows_in(x_doc, x_query)
    own_cot = rows_in(doc_cot.astype(BF), query_cot.astype(BF))
    full_in = gather_weights(w_in, False)
    full_back = gather_weights(w_back.T, True)
    full_proj = gather_proj(w_proj)
    params = jnp.stack(
        [b_out, gain_one, shift_one, b_back, gain_two, shift_two, b_out, b_out]
    )
    params = jnp.dot(params, turn.astype(F32), precision=FULL_PRECISION)
    b_out, gain_one, shift_one, b_back, gain_two, shift_two = [params[i] for i in range(6)]

    docs = 2 * quarter
    queries = 2 * asked
    rows = docs + queries
    sizes_all = lengths[unit_micro]
    sizes = sizes_all[unit_row]
    ends = jnp.cumsum(sizes[:-1])
    starts = jnp.concatenate([jnp.zeros((1,), jnp.int32), ends])

    def layout(first):
        index = first + jnp.arange(docs, dtype=jnp.int32)
        segment = jnp.sum((index[:, None] >= ends[None, :]).astype(jnp.int32), axis=1)
        labels = jnp.arange(starts.shape[0], dtype=jnp.int32)
        begin = jnp.sum(
            jnp.where(segment[:, None] == labels[None, :], starts[None, :], 0), axis=1
        )
        return segment, index - begin

    own_labels, own_places = layout(core * docs)
    far_labels, _ = layout((1 - core) * docs)
    places = jnp.concatenate([own_places, jnp.arange(queries, dtype=jnp.int32) % QLEN])
    half = HEAD_WIDTH // 2
    rates = 10000.0 ** (-(2.0 * jnp.arange(half, dtype=F32)) / HEAD_WIDTH)
    angle = places.astype(F32)[:, None] * rates[None, :]
    cosine = jnp.tile(jnp.cos(angle), (1, width // half))
    sine = jnp.tile(jnp.sin(angle), (1, width // half))

    x_low = dot_nn(own_x, turn).astype(BF)
    parts = [
        dot_nn(x_low, full_qk[0]) + bias_qkv[0],
        dot_nn(x_low, full_qk[1]) + bias_qkv[1],
        dot_nn(x_low, full_vo[0]) + bias_qkv[2],
    ]
    q_rot = (parts[0] * cosine + half_turn(parts[0]) * sine).astype(BF) * 0.125
    k_rot = (parts[1] * cosine + half_turn(parts[1]) * sine).astype(BF)
    v_low = parts[2].astype(BF)
    k_far = exchange(k_rot[:docs], dr=1)
    v_far = exchange(v_low[:docs], dr=1)
    label_args = (own_labels[:, None], own_labels[None, :], far_labels[None, :], docs)
    mixed = attention_forward(q_rot, k_rot, v_low, k_far, v_far, *label_args)
    branch = dot_nt(mixed, full_vo[1])
    resid_one = x_low.astype(F32) + branch + b_out
    normed, norm_one_pull = jax.vjp(layer_norm, resid_one, gain_one, shift_one)
    normed_low = normed.astype(BF)
    inner = dot_nn(normed_low, full_in) + bias_in
    active, gelu_pull = jax.vjp(gelu_exact, inner)
    active_low = active.astype(BF)
    resid_two = normed + dot_nt(active_low, full_back) + b_back
    output, norm_two_pull = jax.vjp(layer_norm, resid_two, gain_two, shift_two)
    output_low = output.astype(BF)
    y_doc, y_query = rows_out(dot_nt(output_low, turn).astype(BF))
    projection = dot_nn(output_low, full_proj)
    unit, unit_pull = jax.vjp(normalize, projection)
    unit_low = unit.astype(BF)

    doc_unit = unit_low[:docs]
    query_unit = unit_low[docs:]

    def bit_of(dr, dt):
        return (rank // dr) % 2 == 1 if dr else (column // dt) % 2 == 1

    def join(value, dr, dt, axis=0):
        got = exchange(value, dr=dr, dt=dt)
        on = bit_of(dr, dt)
        low = jnp.where(on, got, value)
        high = jnp.where(on, value, got)
        return jnp.concatenate([low, high], axis=axis)

    def split_sum(value, dr, dt):
        on = bit_of(dr, dt)
        size = value.shape[0] // 2
        send = jnp.where(on, value[:size], value[size:])
        keep = jnp.where(on, value[size:], value[:size])
        return keep + exchange(send.astype(BF), dr=dr, dt=dt).astype(F32)

    steps = [(1, 0), (0, 1)] + [(dr, 0) for dr in chip_bits]
    all_queries = query_unit
    for dr, dt in steps:
        all_queries = join(all_queries, dr, dt)
    picks = jnp.where(unit_micro == 0, positives[0], positives[1])[None]
    picks = join(picks, 1, 0)
    for dr in chip_bits:
        picks = join(picks, dr, 0)
    picks = picks.reshape(-1)
    seg_labels = jnp.arange(segments, dtype=jnp.int32)
    member = (own_labels[:, None] == seg_labels[None, :]).astype(F32)
    cosines = dot_nt(doc_unit, all_queries)
    weight = jnp.exp(TAU * (cosines - 1.0))
    totals = jnp.einsum("js,ji->si", member, weight, precision=FULL_PRECISION)
    totals = totals + exchange(totals, dr=1)
    for dr, dt in steps[1:]:
        totals = join(totals, dr, dt)
    counts = sizes_all[:, :segments].reshape(-1).astype(F32)
    best = (jnp.log(totals) - jnp.log(counts)[:, None]) / TAU + 1.0
    score = jnp.sum(best.reshape(best.shape[0], -1, QLEN), axis=-1)
    logits = LOGIT_SCALE * score
    documents = jnp.arange(logits.shape[0], dtype=jnp.int32)
    chosen = (documents[:, None] == picks[None, :]).astype(F32)
    peak = jnp.max(logits, axis=0, keepdims=True)
    powers = jnp.exp(logits - peak)
    mass = jnp.sum(powers, axis=0, keepdims=True)
    losses = (peak + jnp.log(mass))[0] - jnp.sum(chosen * logits, axis=0)
    logit_grad = LOGIT_SCALE * (powers / mass - chosen)
    own_grad = lax.dynamic_slice_in_dim(logit_grad, unit_row * segments, segments, axis=0)
    own_total = lax.dynamic_slice_in_dim(totals, unit_row * segments, segments, axis=0)
    coef = jnp.repeat(own_grad, QLEN, axis=1) / own_total
    spread = jnp.einsum("js,si->ji", member, coef, precision=FULL_PRECISION)
    cosine_grad = (weight * spread).astype(BF)
    doc_grad = dot_nn(cosine_grad, all_queries)
    query_grad = dot_tn(cosine_grad, doc_unit)
    for dr, dt in steps[::-1]:
        query_grad = split_sum(query_grad, dr, dt)
    own_losses = lax.dynamic_slice_in_dim(losses, unit_row * (4 * asked // QLEN) + core * 2 * (asked // QLEN), 2 * (asked // QLEN))
    per = asked // QLEN
    loss_tiles = [
        jnp.broadcast_to(own_losses[i * per : (i + 1) * per, None], (per, 128)) for i in range(2)
    ]
    loss_out = quarters_out(loss_tiles[0], loss_tiles[1])[:, :, 0]

    def reduce_weights(left, right, reverse):
        size = left.shape[1] // 2
        send = dot_tn(left[:, size:], right).astype(BF)
        got = exchange(send, dr=1)
        keep = dot_tn(left[:, :size], right) + got.astype(F32)
        order = chip_bits if reverse and len(chip_bits) == 2 else chip_bits[::-1]
        left_bits = sorted(chip_bits)
        for dr in order:
            at = left_bits.index(dr)
            inner_rows = block << at
            view = keep.reshape(-1, 2, inner_rows, keep.shape[-1])
            send = view[:, 1].reshape(-1, keep.shape[-1]).astype(BF)
            stay = view[:, 0].reshape(-1, keep.shape[-1])
            keep = stay + exchange(send, dr=dr).astype(F32)
            left_bits.remove(dr)
        size = keep.shape[1] // ways
        total = keep[:, :size]
        low = keep.astype(BF)
        for j in range(1, ways):
            total = total + exchange(low[:, j * size : (j + 1) * size], dt=j).astype(F32)
        return total

    unit_grad = jnp.concatenate([doc_grad, query_grad], axis=0)
    (proj_grad,) = unit_pull(unit_grad)
    proj_low = proj_grad.astype(BF)
    out_grad = own_cot_turned = dot_nn(own_cot, turn) + dot_nt(proj_low, full_proj)
    resid_two_grad, gain_two_grad, shift_two_grad = norm_two_pull(out_grad)
    update_low = resid_two_grad.astype(BF)
    active_grad = dot_nn(update_low, full_back)
    (inner_grad,) = gelu_pull(active_grad)
    inner_low = inner_grad.astype(BF)
    out_back = reduce_weights(update_low, active_low, True)
    out_in = reduce_weights(normed_low, inner_low, False)
    normed_grad = dot_nt(inner_low, full_in) + resid_two_grad
    resid_one_grad, gain_one_grad, shift_one_grad = norm_one_pull(normed_grad)
    branch_low = resid_one_grad.astype(BF)
    mixed_grad = dot_nn(branch_low, full_vo[1]).astype(BF)
    out_out = reduce_weights(branch_low, mixed, True)
    q_grad, k_grad, v_grad, k_give, v_give = attention_backward(
        q_rot, k_rot, v_low, k_far, v_far, mixed_grad, *label_args
    )
    pad = jnp.zeros((queries, width), F32)
    k_grad = k_grad + jnp.concatenate([exchange(k_give, dr=1).astype(F32), pad], axis=0)
    v_grad = v_grad + jnp.concatenate([exchange(v_give, dr=1).astype(F32), pad], axis=0)
    pre_low = [
        (q_grad * cosine - half_turn(q_grad) * sine).astype(BF),
        (k_grad * cosine - half_turn(k_grad) * sine).astype(BF),
        v_grad.astype(BF),
    ]
    out_qkv = jnp.stack(
        [reduce_weights(x_low, pre_low[i], i == 2) for i in range(3)]
    )
    x_grad = (
        resid_one_grad
        + dot_nt(pre_low[0], full_qk[0])
        + dot_nt(pre_low[1], full_qk[1])
        + dot_nt(pre_low[2], full_vo[0])
    )
    gx_doc, gx_query = rows_out(dot_nt(x_grad.astype(BF), turn).astype(BF))

    grad_proj = dot_tn(output_low, proj_low)
    for dr in [1] + chip_bits[::-1]:
        size = grad_proj.shape[0] // 2
        got = exchange(grad_proj[size:].astype(BF), dr=dr)
        grad_proj = grad_proj[:size] + got.astype(F32)
    for dt in (1, 2):
        grad_proj = grad_proj + exchange(grad_proj, dt=dt)

    vectors = jnp.stack(
        [
            jnp.sum(branch_low.astype(F32), axis=0),
            gain_one_grad,
            shift_one_grad,
            jnp.sum(update_low.astype(F32), axis=0),
            gain_two_grad,
            shift_two_grad,
        ]
    )
    vectors = lax.dot_general(
        vectors, turn.astype(F32), (((1,), (1,)), ((), ())), precision=FULL_PRECISION
    )
    tensor_grads = jnp.concatenate(
        [
            jnp.sum(item.astype(F32), axis=0).reshape(ways, heads_local) for item in pre_low
        ]
        + [jnp.sum(inner_low.astype(F32), axis=0).reshape(ways, units_local)],
        axis=1,
    )
    for dt in (2, 1):
        tensor_grads = tensor_grads[:dt] + exchange(tensor_grads[dt:], dt=dt)
        vectors = vectors + exchange(vectors, dt=dt)
    for dr in [1] + chip_bits:
        tensor_grads = tensor_grads + exchange(tensor_grads, dr=dr)
        vectors = vectors + exchange(vectors, dr=dr)
    tensor_grads = tensor_grads[0]
    return (
        y_doc,
        y_query,
        loss_out,
        gx_doc.astype(F32),
        gx_query.astype(F32),
        out_qkv,
        tensor_grads[: 3 * heads_local].reshape(3, heads_local),
        out_out.T,
        vectors[0],
        vectors[1],
        vectors[2],
        out_in,
        tensor_grads[3 * heads_local :],
        out_back.T,
        vectors[3],
        vectors[4],
        vectors[5],
        grad_proj,
    )


def solution(mesh):
    rows = P(None, ("dp", "tensor"), None)
    in_specs = (
        rows,
        rows,
        rows,
        rows,
        P(),
        P(None, "dp"),
        P(None, "dp", "tensor"),
        P(None, "tensor"),
        P("tensor", "dp"),
        P(),
        P(),
        P(),
        P("dp", "tensor"),
        P("tensor"),
        P("tensor", "dp"),
        P(),
        P(),
        P(),
        P("dp", None),
    )
    out_specs = (
        rows,
        rows,
        P(None, ("dp", "tensor")),
        rows,
        rows,
        P(None, "dp", "tensor"),
        P(None, "tensor"),
        P("tensor", "dp"),
        P(),
        P(),
        P(),
        P("dp", "tensor"),
        P("tensor"),
        P("tensor", "dp"),
        P(),
        P(),
        P(),
        P("dp", None),
    )
    return jax.shard_map(body, mesh=mesh, in_specs=in_specs, out_specs=out_specs, check_vma=False)
```

time: 1920 us -> 838 us (0.44)
  waiting for transfers between devices: 1130 us -> 290 us
  blocking collectives: 258 us -> 0 us
  starting transfers between devices: 2.04 us -> 146 us
  local copies, waits for them, and re-layouts: 204 us -> 82.3 us
  Pallas kernels: 0 us -> 96.3 us
  matrix products: 210 us -> 141 us
    reduce_scatter x24 -> x0, waiting for transfers between devices: 891 us -> none  [the longest x8 553 us: sum_rows(): lax.psum_scatter(first, 'tensor', scatter_dimension=0, tiled=True)]
    ppermute x0 -> x114, waiting for transfers between devices: none -> 290 us  [the longest x104 274 us: exchange(): return lax.ppermute(value, AXES, pairs)]
    all_gather x11 -> x0, waiting for transfers between devices: 237 us -> none  [the longest x8 197 us: gather_rows(): lax.all_gather(first, 'tensor', axis=0, tiled=True)]
    all_gather x14 -> x0, blocking collectives: 195 us -> none  [the longest x8 128 us: gather_rows(): lax.all_gather(second, 'tensor', axis=0, tiled=True)]
    ppermute x0 -> x114, starting transfers between devices: none -> 146 us  [the longest x104 111 us: exchange(): return lax.ppermute(value, AXES, pairs)]
    pallas_call x0 -> x2, Pallas kernels: none -> 96.3 us  [the longest x1 69 us: attention_backward(): pl.pallas_call(kernel, grid=(width // 128,), in_specs=[head_block(rows),...]
    dot_general x92 -> x37, matrix products: 210 us -> 141 us  [the longest x10 61.1 us: dot_nn(): lax.dot_general(a, b, (((1,), (0,)), ((), ())), preferred_element_type=F32)]
    psum x2 -> x0, blocking collectives: 63.1 us -> none  [the longest x1 43.8 us: body(): lax.psum((wide_qkv, wide_in, grad_b_out, grad_gain_one, grad_shift_one, g...]
  transfers between devices with their start and end apart: 36 -> 114, of which waited for: 28 -> 47; matrix products, arithmetic and copies ran while one was open for 20% -> 27% of each run, Pallas kernels for 0% -> 12%
where the time goes in v1:
time: 838 us; the launch traced here: 828 us
  waiting for transfers between devices  290 us (35%)
  starting transfers between devices  146 us (17%)
  matrix products  141 us (17%)
  Pallas kernels  96.3 us (11%)
  local copies, waits for them, and re-layouts  82.3 us (10%)
  other arithmetic  66.7 us (8%)
    ppermute x104, waiting for transfers between devices, exchange(): return lax.ppermute(value, AXES, pairs)  274 us
    ppermute x104, starting transfers between devices, exchange(): return lax.ppermute(value, AXES, pairs)  111 us
    pallas_call x1, Pallas kernels, attention_backward(): pl.pallas_call(kernel, grid=(width // 128,), in_specs=[head_block(rows),...  69 us
    dot_general x10, matrix products, dot_nn(): lax.dot_general(a, b, (((1,), (0,)), ((), ())), preferred_element_type=F32)  61.1 us
    dot_general x14, matrix products, dot_tn(): lax.dot_general(a, b, (((0,), (0,)), ((), ())), preferred_element_type=F32)  39.1 us
    dot_general x9, matrix products, dot_nt(): lax.dot_general(a, b, (((1,), (1,)), ((), ())), preferred_element_type=F32)  33.2 us
    unnamed x313, local copies, waits for them, and re-layouts  29.6 us
    pallas_call x1, Pallas kernels, attention_forward(): pl.pallas_call(kernel, grid=(width // 128,), in_specs=[head_block(rows),...  27.3 us
  transfers between devices with their start and end apart: 114, of which 47 were waited for; matrix products, arithmetic and copies ran while one was open for 27% of the time, Pallas kernels for 12%

profile of v1, /device:TPU:0, one launch (start us, length us, event | category | flops | bytes accessed | tf_op | source)
XLA Modules:
  0.0 828.4 jit_solution(3659963923496097119)
XLA Ops:
  2.8 5.0 collective-permute-start.11
  40.0 3.3 collective-permute-done.49
  43.3 3.6 collective-permute-start.14
  49.8 3.7 collective-permute-start.4
  63.0 3.7 collective-permute-start.30
  70.0 9.6 %collective-permute-done.3 = bf16[2,128,256]{2,1,0:T(8,128)(2,1)S(1)} collective-permute-done((bf16[2,128,256]{2,1,0:T(8,128)(2,1)S(1)}, bf16[2,128,256]{2,1,0:T(8,128)(2,1)S(1)}, u32[]{:S(2)}, u32[]{:S(2)}) %collective-permute-start.3) | collective-permute-done | bytes 131104 | tf_op jit(solution)/shard_map/ppermute | solution.py:286
  81.0 4.6 collective-permute-start.21
  85.7 17.8 %collective-permute-done.29 = bf16[128,1024]{0,1:T(8,128)(2,1)S(1)} collective-permute-done((bf16[128,1024]{0,1:T(8,128)(2,1)S(1)}, bf16[128,1024]{0,1:T(8,128)(2,1)S(1)}, u32[]{:S(2)}, u32[]{:S(2)}) %collective-permute-start.29) | collective-permute-done | bytes 262176 | tf_op jit(solution)/shard_map/ppermute | solution.py:286
  105.5 3.3 collective-permute-done.21
  108.8 6.0 collective-permute-start.53
  121.3 3.7 collective-permute-done.5
  129.0 18.2 %collective-permute-start.54 = (bf16[288,1024]{1,0:T(8,128)(2,1)}, bf16[288,1024]{1,0:T(8,128)(2,1)}, u32[]{:S(2)}, u32[]{:S(2)}) collective-permute-start(bf16[288,1024]{1,0:T(8,128)(2,1)} %get-tuple-element.135), channel_id=1, source_target_pairs={{0,2},{1,0},{2,6},{3,4},{4,3},{5,1},{6,7},{7,5},{8,10},{9,8},{10,1... | collective-permute-start | bytes 1769480 | tf_op jit(solution)/shard_map/ppermute | solution.py:326
  151.6 10.4 %collective-permute-done.17 = bf16[2,128,1024]{1,2,0:T(8,128)(2,1)S(1)} collective-permute-done((bf16[2,128,1024]{1,2,0:T(8,128)(2,1)S(1)}, bf16[2,128,1024]{1,2,0:T(8,128)(2,1)S(1)}, u32[]{:S(2)}, u32[]{:S(2)}) %collective-permute-start.17) | collective-permute-done | bytes 524320 | tf_op jit(solution)/shard_map/ppermute | solution.py:286
  164.6 20.0 %collective-permute-done.24 = bf16[128,4096]{1,0:T(8,128)(2,1)S(1)} collective-permute-done((bf16[128,4096]{1,0:T(8,128)(2,1)S(1)}, bf16[128,4096]{1,0:T(8,128)(2,1)S(1)}, u32[]{:S(2)}, u32[]{:S(2)}) %collective-permute-start.24) | collective-permute-done | bytes 1048608 | tf_op jit(solution)/shard_map/ppermute | solution.py:286
  187.1 19.8 %collective-permute-done.31 = bf16[128,4096]{0,1:T(8,128)(2,1)S(1)} collective-permute-done((bf16[128,4096]{0,1:T(8,128)(2,1)S(1)}, bf16[128,4096]{0,1:T(8,128)(2,1)S(1)}, u32[]{:S(2)}, u32[]{:S(2)}) %collective-permute-start.31) | collective-permute-done | bytes 1048608 | tf_op jit(solution)/shard_map/ppermute | solution.py:286
  210.8 21.3 %collective-permute-done.26 = bf16[128,4096]{1,0:T(8,128)(2,1)S(1)} collective-permute-done((bf16[128,4096]{1,0:T(8,128)(2,1)S(1)}, bf16[128,4096]{1,0:T(8,128)(2,1)S(1)}, u32[]{:S(2)}, u32[]{:S(2)}) %collective-permute-start.26) | collective-permute-done | bytes 1048608 | tf_op jit(solution)/shard_map/ppermute | solution.py:286
  236.3 9.7 %pad_maximum_fusion.1 = bf16[512,4096]{0,1:T(8,128)(2,1)} fusion(bf16[128,4096]{0,1:T(8,128)(2,1)S(1)} %collective-permute-done.33, bf16[128,4096]{0,1:T(8,128)(2,1)S(1)} %collective-permute-done.32, bf16[128,4096]{0,1:T(8,128)(2,1)S(1)} %collective-permute-done.31, bf16[128,1024]{0,1:T(8,128)(2,1)S(1)} %collective-permute-done.30, ...), kind=kLoop, calls=%fused_computation.27 | loop fusion | flops 29360128 | bytes 8388608 | tf_op jit(solution)/shard_map/concatenate | solution.py:302
  263.9 27.3 %attend_forward.1 = bf16[576,1024]{1,0:T(8,128)(2,1)S(1)} custom-call(bf16[576,1024]{1,0:T(8,128)(2,1)S(1)} %fusion.70.q_ref, bf16[576,1024]{1,0:T(8,128)(2,1)S(1)} %fusion.20.ko_ref, bf16[576,1024]{1,0:T(8,128)(2,1)S(1)} %add_convert_fusion.4.vo_ref, bf16[512,1024]{1,0:T(8,128)(2,1)S(1)} %collective-permute-done.19.kf_ref, ...), custom_call_target="tpu_custom_call" | custom-call | flops 2415919104 | bytes 6815744 | tf_op jit(solution)/shard_map/attend_forward/pallas_call | solution.py:100
  294.1 5.1 constant_dynamic-update-slice_fusion.19
  299.2 28.6 %multiply_convert_fusion = (bf16[576,4096]{1,0:T(8,128)(2,1)S(1)}, f32[576,4096]{1,0:T(8,128)}, f32[576,4096]{1,0:T(8,128)}) fusion(f32[4096]{0:T(1024)S(1)} %pad_maximum_fusion.32, bf16[576,1024]{1,0:T(8,128)(2,1)S(1)} %fusion.38, bf16[1024,4096]{1,0:T(8,128)(2,1)} %constant_dynamic-update-slice_fusion.19), kind=kOutput, calls=%fused_computation.4 | convolution fusion | flops 4987551744 | bytes 33177600 | tf_op jit(solution)/shard_map/dot_general | solution.py:37
  330.3 5.2 fusion.228
  360.9 3.6 collective-permute-done.45
  364.7 3.9 collective-permute-done.46
  371.3 5.9 collective-permute-start.35
  397.3 3.8 collective-permute-done.55
  417.7 18.0 %convert_reduce_fusion = (f32[4096]{0:T(1024)}, bf16[576,4096]{1,0:T(8,128)(2,1)}) fusion(f32[576,4096]{1,0:T(8,128)} %get-tuple-element.105, f32[576,4096]{1,0:T(8,128)} %get-tuple-element.223, f32[4096]{0:T(1024)S(1)} %copy-done.112, bf16[576,1024]{1,0:T(8,128)(2,1)} %get-tuple-element.79, bf16[1024,4096]{0,1:T(8,128)(2,1)} %copy-done.81), kind=kOutput, calls=%fused_computation.2 | convolution fusion | flops 4871942144 | bytes 33193984 | tf_op jit(solution)/shard_map/dot_general | solution.py:37
  435.7 11.0 %multiply_reduce_fusion.1 = (f32[1024]{0:T(1024)S(1)}, f32[576]{0:T(1024)S(1)}, f32[1024]{0:T(1024)S(1)}, f32[576,1024]{1,0:T(8,128)S(1)}) fusion(f32[576,1024]{1,0:T(8,128)S(1)} %copy-done.23, f32[576]{0:T(1024)S(1)} %copy-done.97, f32[576]{0:T(1024)S(1)} %broadcast_multiply_fusion.1, f32[1024]{0:T(1024)S(1)} %bitcast.282, ...), kind=kOutput, calls=%fused_computation.60 | convolution fusion | flops 4837733888 | bytes 20206592 | tf_op jit(solution)/shard_map/dot_general | solution.py:41
  446.7 5.1 convolution_convert_fusion.1
  451.8 5.2 convolution_convert_fusion
  463.3 3.4 collective-permute-start.92
  466.7 3.2 fusion.51.g_ref
  470.6 69.0 %attend_backward.1 = (f32[576,1024]{1,0:T(8,128)S(1)}, f32[576,1024]{1,0:T(8,128)S(1)}, f32[576,1024]{1,0:T(8,128)}, bf16[512,1024]{1,0:T(8,128)(2,1)}, bf16[512,1024]{1,0:T(8,128)(2,1)S(1)}) custom-call(bf16[576,1024]{1,0:T(8,128)(2,1)S(1)} %copy-done.6, bf16[576,1024]{1,0:T(8,128)(2,1)S(1)} %copy-done.3, bf16[576,1024]{1,0:T(8,128)(2,1)S(1)} %copy-done.8, ...), custom_call_target="tpu_custom_call" | custom-call | flops 6039797760 | bytes 22544384 | tf_op jit(solution)/shard_map/attend_backward/pallas_call | solution.py:206
  585.0 7.4 fusion.54
  594.6 3.4 convolution_convert_fusion.3
  611.1 16.1 %collective-permute-done.62 = bf16[288,1024]{1,0:T(8,128)(2,1)S(1)} collective-permute-done((bf16[288,1024]{1,0:T(8,128)(2,1)S(1)}, bf16[288,1024]{1,0:T(8,128)(2,1)S(1)}, u32[]{:S(2)}, u32[]{:S(2)}) %collective-permute-start.62) | collective-permute-done | bytes 589856 | tf_op jit(solution)/shard_map/ppermute | solution.py:347
  628.9 6.9 collective-permute-start.89
  638.8 3.2 collective-permute-done.91
  653.3 7.4 collective-permute-done.76
  666.2 9.8 %collective-permute-done.64 = bf16[256,1024]{1,0:T(8,128)(2,1)S(1)} collective-permute-done((bf16[256,1024]{1,0:T(8,128)(2,1)S(1)}, bf16[256,1024]{1,0:T(8,128)(2,1)S(1)}, u32[]{:S(2)}, u32[]{:S(2)}) %collective-permute-start.64) | collective-permute-done | bytes 524320 | tf_op jit(solution)/shard_map/ppermute | solution.py:286
  677.5 3.8 collective-permute-done.77
  698.6 5.6 convert_add_fusion
  708.7 5.4 convert_add_fusion.1
  715.8 33.2 %collective-permute-done.104 = bf16[256,4096]{1,0:T(8,128)(2,1)S(1)} collective-permute-done((bf16[256,4096]{1,0:T(8,128)(2,1)S(1)}, bf16[256,4096]{1,0:T(8,128)(2,1)S(1)}, u32[]{:S(2)}, u32[]{:S(2)}) %collective-permute-start.104) | collective-permute-done | bytes 2097184 | tf_op jit(solution)/shard_map/ppermute | solution.py:286
  751.2 11.8 %collective-permute-done.98 = bf16[256,4096]{1,0:T(8,128)(2,1)S(1)} collective-permute-done((bf16[256,4096]{1,0:T(8,128)(2,1)S(1)}, bf16[256,4096]{1,0:T(8,128)(2,1)S(1)}, u32[]{:S(2)}, u32[]{:S(2)}) %collective-permute-start.98) | collective-permute-done | bytes 2097184 | tf_op jit(solution)/shard_map/ppermute | solution.py:286
  764.7 16.4 %collective-permute-done.105 = bf16[128,4096]{1,0:T(8,128)(2,1)S(1)} collective-permute-done((bf16[128,4096]{1,0:T(8,128)(2,1)S(1)}, bf16[128,4096]{1,0:T(8,128)(2,1)S(1)}, u32[]{:S(2)}, u32[]{:S(2)}) %collective-permute-start.105) | collective-permute-done | bytes 1048608 | tf_op jit(solution)/shard_map/ppermute | solution.py:286
  791.2 5.9 collective-permute-done.106
  798.7 19.8 %collective-permute-done.107 = bf16[128,1024]{1,0:T(8,128)(2,1)S(1)} collective-permute-done((bf16[128,1024]{1,0:T(8,128)(2,1)S(1)}, bf16[128,1024]{1,0:T(8,128)(2,1)S(1)}, u32[]{:S(2)}, u32[]{:S(2)}) %collective-permute-start.107) | collective-permute-done | bytes 262176 | tf_op jit(solution)/shard_map/ppermute | solution.py:286
  819.7 7.6 collective-permute-done.101
  (775 shorter events, 296.4 us)
Async XLA Ops:
  2.8 44.7 %collective-permute-start.11 = (f32[1,1792]{1,0:T(1,128)}, f32[1,1792]{1,0:T(1,128)}, u32[]{:S(2)}, u32[]{:S(2)}) collective-permute-start(f32[1,1792]{1,0:T(1,128)} %broadcast_in_dim.36), channel_id=1, source_target_pairs={{0,3},{1,2},{2,1},{3,0},{4,7},{5,6},{6,5},{7,4},{8,11},{9,10},{10,... | collective-permute-start | bytes 21512 | tf_op jit(solution)/shard_map/ppermute | solution.py:286
  7.9 40.3 %collective-permute-start.10 = (f32[1,1792]{1,0:T(1,128)}, f32[1,1792]{1,0:T(1,128)}, u32[]{:S(2)}, u32[]{:S(2)}) collective-permute-start(f32[1,1792]{1,0:T(1,128)} %broadcast_in_dim.36), channel_id=1, source_target_pairs={{0,2},{1,3},{2,0},{3,1},{4,6},{5,7},{6,4},{7,5},{8,10},{9,11},{10,... | collective-permute-start | bytes 21512 | tf_op jit(solution)/shard_map/ppermute | solution.py:286
  7.9 41.9 %collective-permute-start.9 = (f32[1,1792]{1,0:T(1,128)}, f32[1,1792]{1,0:T(1,128)}, u32[]{:S(2)}, u32[]{:S(2)}) collective-permute-start(f32[1,1792]{1,0:T(1,128)} %broadcast_in_dim.36), channel_id=1, source_target_pairs={{0,1},{1,0},{2,3},{3,2},{4,5},{5,4},{6,7},{7,6},{8,9},{9,8},{10,11... | collective-permute-start | bytes 21512 | tf_op jit(solution)/shard_map/ppermute | solution.py:286
  9.7 29.2 %collective-permute-start.48 = (s32[1,4]{1,0:T(1,128)}, s32[1,4]{1,0:T(1,128)}, u32[]{:S(2)}, u32[]{:S(2)}) collective-permute-start(s32[1,4]{1,0:T(1,128)} %broadcast_select_fusion.22), channel_id=1, source_target_pairs={{0,4},{1,5},{2,6},{3,7},{4,0},{5,1},{6,2},{7,3},{8,12},{9,13},{10,... | collective-permute-start | bytes 56 | tf_op jit(solution)/shard_map/ppermute | solution.py:286
  9.7 46.6 %collective-permute-start.37 = (bf16[128,128]{1,0:T(8,128)(2,1)}, bf16[128,128]{1,0:T(8,128)(2,1)}, u32[]{:S(2)}, u32[]{:S(2)}) collective-permute-start(bf16[128,128]{1,0:T(8,128)(2,1)} %param.37), channel_id=1, source_target_pairs={{0,8},{1,9},{2,10},{3,11},{4,12},{5,13},{6,14},{7,15},{8,0},{9,1},... | collective-permute-start | bytes 98312 | tf_op jit(solution)/shard_map/ppermute | solution.py:286
  63.0 22.6 %collective-permute-start.30 = (bf16[128,1024]{0,1:T(8,128)(2,1)S(1)}, bf16[128,1024]{0,1:T(8,128)(2,1)S(1)}, u32[]{:S(2)}, u32[]{:S(2)}) collective-permute-start(bf16[128,1024]{0,1:T(8,128)(2,1)S(1)} %bitcast.269), channel_id=1, source_target_pairs={{0,3},{1,2},{2,1},{3,0},{4,7},{5,6},{6,5},{7,4},{8,11},{9,10},{10,... | collective-permute-start | bytes 786440 | tf_op jit(solution)/shard_map/ppermute | solution.py:286
  66.7 36.8 %collective-permute-start.29 = (bf16[128,1024]{0,1:T(8,128)(2,1)S(1)}, bf16[128,1024]{0,1:T(8,128)(2,1)S(1)}, u32[]{:S(2)}, u32[]{:S(2)}) collective-permute-start(bf16[128,1024]{0,1:T(8,128)(2,1)S(1)} %bitcast.270), channel_id=1, source_target_pairs={{0,2},{1,3},{2,0},{3,1},{4,6},{5,7},{6,4},{7,5},{8,10},{9,11},{10,... | collective-permute-start | bytes 786440 | tf_op jit(solution)/shard_map/ppermute | solution.py:286
  66.7 38.5 %collective-permute-start.28 = (bf16[128,1024]{0,1:T(8,128)(2,1)S(1)}, bf16[128,1024]{0,1:T(8,128)(2,1)S(1)}, u32[]{:S(2)}, u32[]{:S(2)}) collective-permute-start(bf16[128,1024]{0,1:T(8,128)(2,1)S(1)} %bitcast.271), channel_id=1, source_target_pairs={{0,1},{1,0},{2,3},{3,2},{4,5},{5,4},{6,7},{7,6},{8,9},{9,8},{10,11... | collective-permute-start | bytes 786440 | tf_op jit(solution)/shard_map/ppermute | solution.py:286
  79.6 36.0 %collective-permute-start.22 = (bf16[128,1024]{1,0:T(8,128)(2,1)}, bf16[128,1024]{1,0:T(8,128)(2,1)S(1)}, u32[]{:S(2)}, u32[]{:S(2)}) collective-permute-start(bf16[128,1024]{1,0:T(8,128)(2,1)} %param.31), channel_id=1, source_target_pairs={{0,2},{1,3},{2,0},{3,1},{4,6},{5,7},{6,4},{7,5},{8,10},{9,11},{10,... | collective-permute-start | bytes 786440 | tf_op jit(solution)/shard_map/ppermute | solution.py:286
  81.0 27.8 %collective-permute-start.21 = (bf16[128,1024]{1,0:T(8,128)(2,1)}, bf16[128,1024]{1,0:T(8,128)(2,1)S(1)}, u32[]{:S(2)}, u32[]{:S(2)}) collective-permute-start(bf16[128,1024]{1,0:T(8,128)(2,1)} %param.31), channel_id=1, source_target_pairs={{0,1},{1,0},{2,3},{3,2},{4,5},{5,4},{6,7},{7,6},{8,9},{9,8},{10,11... | collective-permute-start | bytes 786440 | tf_op jit(solution)/shard_map/ppermute | solution.py:286
  85.6 31.2 %collective-permute-start.23 = (bf16[128,1024]{1,0:T(8,128)(2,1)}, bf16[128,1024]{1,0:T(8,128)(2,1)S(1)}, u32[]{:S(2)}, u32[]{:S(2)}) collective-permute-start(bf16[128,1024]{1,0:T(8,128)(2,1)} %param.31), channel_id=1, source_target_pairs={{0,3},{1,2},{2,1},{3,0},{4,7},{5,6},{6,5},{7,4},{8,11},{9,10},{10,... | collective-permute-start | bytes 786440 | tf_op jit(solution)/shard_map/ppermute | solution.py:286
  108.8 242.3 %collective-permute-start.53 = (bf16[288,1024]{1,0:T(8,128)(2,1)}, bf16[288,1024]{1,0:T(8,128)(2,1)}, u32[]{:S(2)}, u32[]{:S(2)}) collective-permute-start(bf16[288,1024]{1,0:T(8,128)(2,1)} %get-tuple-element.134), channel_id=1, source_target_pairs={{0,0},{1,2},{2,4},{3,6},{4,1},{5,3},{6,5},{7,7},{8,8},{9,10},{10,1... | collective-permute-start | bytes 1769480 | tf_op jit(solution)/shard_map/ppermute | solution.py:326
  119.1 28.1 %collective-permute-start.15 = (bf16[2,128,1024]{1,2,0:T(8,128)(2,1)S(1)}, bf16[2,128,1024]{1,2,0:T(8,128)(2,1)S(1)}, u32[]{:S(2)}, u32[]{:S(2)}) collective-permute-start(bf16[2,128,1024]{1,2,0:T(8,128)(2,1)S(1)} %get-tuple-element.158), channel_id=1, source_target_pairs={{0,8},{1,9},{2,10},{3,11},{4,12},{5,13},{6,14},{7,15},{8,0},{9,1},... | collective-permute-start | bytes 1572872 | tf_op jit(solution)/shard_map/ppermute | solution.py:286
  120.6 28.5 %collective-permute-start.6 = (bf16[2,128,1024]{2,1,0:T(8,128)(2,1)S(1)}, bf16[2,128,1024]{2,1,0:T(8,128)(2,1)S(1)}, u32[]{:S(2)}, u32[]{:S(2)}) collective-permute-start(bf16[2,128,1024]{2,1,0:T(8,128)(2,1)S(1)} %get-tuple-element.156), channel_id=1, source_target_pairs={{0,16},{1,17},{2,18},{3,19},{4,20},{5,21},{6,22},{7,23},{8,24},{9,... | collective-permute-start | bytes 1572872 | tf_op jit(solution)/shard_map/ppermute | solution.py:286
  125.0 24.8 %collective-permute-start.7 = (bf16[2,128,1024]{2,1,0:T(8,128)(2,1)S(1)}, bf16[2,128,1024]{2,1,0:T(8,128)(2,1)S(1)}, u32[]{:S(2)}, u32[]{:S(2)}) collective-permute-start(bf16[2,128,1024]{2,1,0:T(8,128)(2,1)S(1)} %collective-permute-done.5), channel_id=1, source_target_pairs={{0,16},{1,17},{2,18},{3,19},{4,20},{5,21},{6,22},{7,23},{8,24},{9,... | collective-permute-start | bytes 1572872 | tf_op jit(solution)/shard_map/ppermute | solution.py:286
  129.0 222.1 %collective-permute-start.54 = (bf16[288,1024]{1,0:T(8,128)(2,1)}, bf16[288,1024]{1,0:T(8,128)(2,1)}, u32[]{:S(2)}, u32[]{:S(2)}) collective-permute-start(bf16[288,1024]{1,0:T(8,128)(2,1)} %get-tuple-element.135), channel_id=1, source_target_pairs={{0,2},{1,0},{2,6},{3,4},{4,3},{5,1},{6,7},{7,5},{8,10},{9,8},{10,1... | collective-permute-start | bytes 1769480 | tf_op jit(solution)/shard_map/ppermute | solution.py:326
  149.2 35.4 %collective-permute-start.24 = (bf16[128,4096]{1,0:T(8,128)(2,1)S(1)}, bf16[128,4096]{1,0:T(8,128)(2,1)S(1)}, u32[]{:S(2)}, u32[]{:S(2)}) collective-permute-start(bf16[128,4096]{1,0:T(8,128)(2,1)S(1)} %get-tuple-element.174), channel_id=1, source_target_pairs={{0,8},{1,9},{2,10},{3,11},{4,12},{5,13},{6,14},{7,15},{8,0},{9,1},... | collective-permute-start | bytes 3145736 | tf_op jit(solution)/shard_map/ppermute | solution.py:286
  149.9 57.1 %collective-permute-start.31 = (bf16[128,4096]{0,1:T(8,128)(2,1)S(1)}, bf16[128,4096]{0,1:T(8,128)(2,1)S(1)}, u32[]{:S(2)}, u32[]{:S(2)}) collective-permute-start(bf16[128,4096]{0,1:T(8,128)(2,1)S(1)} %get-tuple-element.154), channel_id=1, source_target_pairs={{0,8},{1,9},{2,10},{3,11},{4,12},{5,13},{6,14},{7,15},{8,0},{9,1},... | collective-permute-start | bytes 3145736 | tf_op jit(solution)/shard_map/ppermute | solution.py:286
  162.1 46.8 %collective-permute-start.32 = (bf16[128,4096]{0,1:T(8,128)(2,1)S(1)}, bf16[128,4096]{0,1:T(8,128)(2,1)S(1)}, u32[]{:S(2)}, u32[]{:S(2)}) collective-permute-start(bf16[128,4096]{0,1:T(8,128)(2,1)S(1)} %get-tuple-element.154), channel_id=1, source_target_pairs={{0,16},{1,17},{2,18},{3,19},{4,20},{5,21},{6,22},{7,23},{8,24},{9,... | collective-permute-start | bytes 3145736 | tf_op jit(solution)/shard_map/ppermute | solution.py:286
  184.5 25.1 %collective-permute-start.25 = (bf16[128,4096]{1,0:T(8,128)(2,1)S(1)}, bf16[128,4096]{1,0:T(8,128)(2,1)S(1)}, u32[]{:S(2)}, u32[]{:S(2)}) collective-permute-start(bf16[128,4096]{1,0:T(8,128)(2,1)S(1)} %get-tuple-element.174), channel_id=1, source_target_pairs={{0,16},{1,17},{2,18},{3,19},{4,20},{5,21},{6,22},{7,23},{8,24},{9,... | collective-permute-start | bytes 3145736 | tf_op jit(solution)/shard_map/ppermute | solution.py:286
  207.0 25.1 %collective-permute-start.26 = (bf16[128,4096]{1,0:T(8,128)(2,1)S(1)}, bf16[128,4096]{1,0:T(8,128)(2,1)S(1)}, u32[]{:S(2)}, u32[]{:S(2)}) collective-permute-start(bf16[128,4096]{1,0:T(8,128)(2,1)S(1)} %collective-permute-done.24), channel_id=1, source_target_pairs={{0,16},{1,17},{2,18},{3,19},{4,20},{5,21},{6,22},{7,23},{8,24},{9,... | collective-permute-start | bytes 3145736 | tf_op jit(solution)/shard_map/ppermute | solution.py:286
  208.9 37.2 %collective-permute-start.18 = (bf16[2,512,1024]{1,2,0:T(8,128)(2,1)S(1)}, bf16[2,512,1024]{1,2,0:T(8,128)(2,1)S(1)}, u32[]{:S(2)}, u32[]{:S(2)}) collective-permute-start(bf16[2,512,1024]{1,2,0:T(8,128)(2,1)S(1)} %pad_maximum_fusion.3), channel_id=1, source_target_pairs={{0,4},{1,5},{2,6},{3,7},{4,0},{5,1},{6,2},{7,3},{8,12},{9,13},{10,... | collective-permute-start | bytes 6291464 | tf_op jit(solution)/shard_map/ppermute | solution.py:286
  209.6 25.8 %collective-permute-start.33 = (bf16[128,4096]{0,1:T(8,128)(2,1)S(1)}, bf16[128,4096]{0,1:T(8,128)(2,1)S(1)}, u32[]{:S(2)}, u32[]{:S(2)}) collective-permute-start(bf16[128,4096]{0,1:T(8,128)(2,1)S(1)} %collective-permute-done.32), channel_id=1, source_target_pairs={{0,8},{1,9},{2,10},{3,11},{4,12},{5,13},{6,14},{7,15},{8,0},{9,1},... | collective-permute-start | bytes 3145736 | tf_op jit(solution)/shard_map/ppermute | solution.py:286
  235.4 58.7 %collective-permute-start.27 = (bf16[512,4096]{1,0:T(8,128)(2,1)}, bf16[512,4096]{1,0:T(8,128)(2,1)}, u32[]{:S(2)}, u32[]{:S(2)}) collective-permute-start(bf16[512,4096]{1,0:T(8,128)(2,1)} %pad_maximum_fusion), channel_id=1, source_target_pairs={{0,4},{1,5},{2,6},{3,7},{4,0},{5,1},{6,2},{7,3},{8,12},{9,13},{10,... | collective-permute-start | bytes 12582920 | tf_op jit(solution)/shard_map/ppermute | solution.py:286
  262.3 76.8 %collective-permute-start.50 = (s32[4,4]{1,0:T(4,128)S(1)}, s32[4,4]{1,0:T(4,128)S(1)}, u32[]{:S(2)}, u32[]{:S(2)}) collective-permute-start(s32[4,4]{1,0:T(4,128)S(1)} %copy-done.129), channel_id=1, source_target_pairs={{0,16},{1,17},{2,18},{3,19},{4,20},{5,21},{6,22},{7,23},{8,24},{9,... | collective-permute-start | bytes 200 | tf_op jit(solution)/shard_map/ppermute | solution.py:286
  263.9 63.9 %collective-permute-start.34 = (bf16[512,4096]{0,1:T(8,128)(2,1)}, bf16[512,4096]{0,1:T(8,128)(2,1)S(1)}, u32[]{:S(2)}, u32[]{:S(2)}) collective-permute-start(bf16[512,4096]{0,1:T(8,128)(2,1)} %pad_maximum_fusion.1), channel_id=1, source_target_pairs={{0,4},{1,5},{2,6},{3,7},{4,0},{5,1},{6,2},{7,3},{8,12},{9,13},{10,... | collective-permute-start | bytes 12582920 | tf_op jit(solution)/shard_map/ppermute | solution.py:286
  371.3 35.0 %collective-permute-start.36 = (bf16[288,1024]{1,0:T(8,128)(2,1)}, bf16[288,1024]{1,0:T(8,128)(2,1)}, u32[]{:S(2)}, u32[]{:S(2)}) collective-permute-start(bf16[288,1024]{1,0:T(8,128)(2,1)} %get-tuple-element.138), channel_id=1, source_target_pairs={{0,1},{1,5},{2,0},{3,4},{4,3},{5,7},{6,2},{7,6},{8,9},{9,13},{10,8... | collective-permute-start | bytes 1769480 | tf_op jit(solution)/shard_map/ppermute | solution.py:347
  371.3 35.0 %collective-permute-start.35 = (bf16[288,1024]{1,0:T(8,128)(2,1)}, bf16[288,1024]{1,0:T(8,128)(2,1)}, u32[]{:S(2)}, u32[]{:S(2)}) collective-permute-start(bf16[288,1024]{1,0:T(8,128)(2,1)} %get-tuple-element.139), channel_id=1, source_target_pairs={{0,0},{1,4},{2,1},{3,5},{4,2},{5,6},{6,3},{7,7},{8,8},{9,12},{10,9... | collective-permute-start | bytes 1769480 | tf_op jit(solution)/shard_map/ppermute | solution.py:347
  458.6 81.7 %collective-permute-start.109 = (bf16[512,128]{1,0:T(8,128)(2,1)}, bf16[512,128]{1,0:T(8,128)(2,1)S(1)}, u32[]{:S(2)}, u32[]{:S(2)}) collective-permute-start(bf16[512,128]{1,0:T(8,128)(2,1)} %slice.1039), channel_id=1, source_target_pairs={{0,4},{1,5},{2,6},{3,7},{4,0},{5,1},{6,2},{7,3},{8,12},{9,13},{10,... | collective-permute-start | bytes 393224 | tf_op jit(solution)/shard_map/ppermute | solution.py:286
  470.0 69.7 %collective-permute-start.93 = (f32[6,1024]{1,0:T(8,128)S(1)}, f32[6,1024]{1,0:T(8,128)S(1)}, u32[]{:S(2)}, u32[]{:S(2)}) collective-permute-start(f32[6,1024]{1,0:T(8,128)S(1)} %add.604), channel_id=1, source_target_pairs={{0,1},{1,0},{2,3},{3,2},{4,5},{5,4},{6,7},{7,6},{8,9},{9,8},{10,11... | collective-permute-start | bytes 73736 | tf_op jit(solution)/shard_map/ppermute | solution.py:286
  539.6 21.2 %collective-permute-start.59 = (bf16[512,1024]{1,0:T(8,128)(2,1)}, bf16[512,1024]{1,0:T(8,128)(2,1)}, u32[]{:S(2)}, u32[]{:S(2)}) collective-permute-start(bf16[512,1024]{1,0:T(8,128)(2,1)} %get-tuple-element.25), channel_id=1, source_target_pairs={{0,4},{1,5},{2,6},{3,7},{4,0},{5,1},{6,2},{7,3},{8,12},{9,13},{10,... | collective-permute-start | bytes 3145736 | tf_op jit(solution)/shard_map/ppermute | solution.py:286
  552.2 29.5 %collective-permute-start.60 = (bf16[512,1024]{1,0:T(8,128)(2,1)S(1)}, bf16[512,1024]{1,0:T(8,128)(2,1)S(1)}, u32[]{:S(2)}, u32[]{:S(2)}) collective-permute-start(bf16[512,1024]{1,0:T(8,128)(2,1)S(1)} %get-tuple-element.27), channel_id=1, source_target_pairs={{0,4},{1,5},{2,6},{3,7},{4,0},{5,1},{6,2},{7,3},{8,12},{9,13},{10,... | collective-permute-start | bytes 3145736 | tf_op jit(solution)/shard_map/ppermute | solution.py:286
  566.8 42.3 %collective-permute-start.87 = (bf16[256,1024]{1,0:T(8,128)(2,1)}, bf16[256,1024]{1,0:T(8,128)(2,1)}, u32[]{:S(2)}, u32[]{:S(2)}) collective-permute-start(bf16[256,1024]{1,0:T(8,128)(2,1)} %bitcast.70), channel_id=1, source_target_pairs={{0,8},{1,9},{2,10},{3,11},{4,12},{5,13},{6,14},{7,15},{8,0},{9,1},... | collective-permute-start | bytes 1572872 | tf_op jit(solution)/shard_map/ppermute | solution.py:286
  600.0 43.7 %collective-permute-start.75 = (bf16[512,1024]{1,0:T(8,128)(2,1)}, bf16[512,1024]{1,0:T(8,128)(2,1)}, u32[]{:S(2)}, u32[]{:S(2)}) collective-permute-start(bf16[512,1024]{1,0:T(8,128)(2,1)} %convolution_convert_fusion.3), channel_id=1, source_target_pairs={{0,4},{1,5},{2,6},{3,7},{4,0},{5,1},{6,2},{7,3},{8,12},{9,13},{10,... | collective-permute-start | bytes 3145736 | tf_op jit(solution)/shard_map/ppermute | solution.py:286
  600.1 47.4 %collective-permute-start.69 = (bf16[512,1024]{1,0:T(8,128)(2,1)}, bf16[512,1024]{1,0:T(8,128)(2,1)}, u32[]{:S(2)}, u32[]{:S(2)}) collective-permute-start(bf16[512,1024]{1,0:T(8,128)(2,1)} %convolution_convert_fusion.4), channel_id=1, source_target_pairs={{0,4},{1,5},{2,6},{3,7},{4,0},{5,1},{6,2},{7,3},{8,12},{9,13},{10,... | collective-permute-start | bytes 3145736 | tf_op jit(solution)/shard_map/ppermute | solution.py:286
  604.1 23.2 %collective-permute-start.62 = (bf16[288,1024]{1,0:T(8,128)(2,1)S(1)}, bf16[288,1024]{1,0:T(8,128)(2,1)S(1)}, u32[]{:S(2)}, u32[]{:S(2)}) collective-permute-start(bf16[288,1024]{1,0:T(8,128)(2,1)S(1)} %get-tuple-element.126), channel_id=1, source_target_pairs={{0,1},{1,5},{2,0},{3,4},{4,3},{5,7},{6,2},{7,6},{8,9},{9,13},{10,8... | collective-permute-start | bytes 1769480 | tf_op jit(solution)/shard_map/ppermute | solution.py:347
  606.7 20.5 %collective-permute-start.61 = (bf16[288,1024]{1,0:T(8,128)(2,1)S(1)}, bf16[288,1024]{1,0:T(8,128)(2,1)S(1)}, u32[]{:S(2)}, u32[]{:S(2)}) collective-permute-start(bf16[288,1024]{1,0:T(8,128)(2,1)S(1)} %get-tuple-element.127), channel_id=1, source_target_pairs={{0,0},{1,4},{2,1},{3,5},{4,2},{5,6},{6,3},{7,7},{8,8},{9,12},{10,9... | collective-permute-start | bytes 1769480 | tf_op jit(solution)/shard_map/ppermute | solution.py:347
  638.8 59.7 %collective-permute-start.103 = (bf16[512,4096]{1,0:T(8,128)(2,1)}, bf16[512,4096]{1,0:T(8,128)(2,1)}, u32[]{:S(2)}, u32[]{:S(2)}) collective-permute-start(bf16[512,4096]{1,0:T(8,128)(2,1)} %convolution_convert_fusion), channel_id=1, source_target_pairs={{0,4},{1,5},{2,6},{3,7},{4,0},{5,1},{6,2},{7,3},{8,12},{9,13},{10,... | collective-permute-start | bytes 12582920 | tf_op jit(solution)/shard_map/ppermute | solution.py:286
  642.0 64.7 %collective-permute-start.97 = (bf16[512,4096]{1,0:T(8,128)(2,1)}, bf16[512,4096]{1,0:T(8,128)(2,1)}, u32[]{:S(2)}, u32[]{:S(2)}) collective-permute-start(bf16[512,4096]{1,0:T(8,128)(2,1)} %convolution_convert_fusion.1), channel_id=1, source_target_pairs={{0,4},{1,5},{2,6},{3,7},{4,0},{5,1},{6,2},{7,3},{8,12},{9,13},{10,... | collective-permute-start | bytes 12582920 | tf_op jit(solution)/shard_map/ppermute | solution.py:286
  652.5 23.5 %collective-permute-start.64 = (bf16[256,1024]{1,0:T(8,128)(2,1)S(1)}, bf16[256,1024]{1,0:T(8,128)(2,1)S(1)}, u32[]{:S(2)}, u32[]{:S(2)}) collective-permute-start(bf16[256,1024]{1,0:T(8,128)(2,1)S(1)} %fusion.94), channel_id=1, source_target_pairs={{0,16},{1,17},{2,18},{3,19},{4,20},{5,21},{6,22},{7,23},{8,24},{9,... | collective-permute-start | bytes 1572872 | tf_op jit(solution)/shard_map/ppermute | solution.py:286
  704.4 44.6 %collective-permute-start.104 = (bf16[256,4096]{1,0:T(8,128)(2,1)S(1)}, bf16[256,4096]{1,0:T(8,128)(2,1)S(1)}, u32[]{:S(2)}, u32[]{:S(2)}) collective-permute-start(bf16[256,4096]{1,0:T(8,128)(2,1)S(1)} %bitcast.260), channel_id=1, source_target_pairs={{0,8},{1,9},{2,10},{3,11},{4,12},{5,13},{6,14},{7,15},{8,0},{9,1},... | collective-permute-start | bytes 6291464 | tf_op jit(solution)/shard_map/ppermute | solution.py:286
  714.3 48.6 %collective-permute-start.98 = (bf16[256,4096]{1,0:T(8,128)(2,1)S(1)}, bf16[256,4096]{1,0:T(8,128)(2,1)S(1)}, u32[]{:S(2)}, u32[]{:S(2)}) collective-permute-start(bf16[256,4096]{1,0:T(8,128)(2,1)S(1)} %fusion.29), channel_id=1, source_target_pairs={{0,16},{1,17},{2,18},{3,19},{4,20},{5,21},{6,22},{7,23},{8,24},{9,... | collective-permute-start | bytes 6291464 | tf_op jit(solution)/shard_map/ppermute | solution.py:286
  749.8 31.3 %collective-permute-start.105 = (bf16[128,4096]{1,0:T(8,128)(2,1)S(1)}, bf16[128,4096]{1,0:T(8,128)(2,1)S(1)}, u32[]{:S(2)}, u32[]{:S(2)}) collective-permute-start(bf16[128,4096]{1,0:T(8,128)(2,1)S(1)} %fusion.75), channel_id=1, source_target_pairs={{0,16},{1,17},{2,18},{3,19},{4,20},{5,21},{6,22},{7,23},{8,24},{9,... | collective-permute-start | bytes 3145736 | tf_op jit(solution)/shard_map/ppermute | solution.py:286
  763.8 22.4 %collective-permute-start.99 = (bf16[128,4096]{1,0:T(8,128)(2,1)S(1)}, bf16[128,4096]{1,0:T(8,128)(2,1)S(1)}, u32[]{:S(2)}, u32[]{:S(2)}) collective-permute-start(bf16[128,4096]{1,0:T(8,128)(2,1)S(1)} %fusion.74), channel_id=1, source_target_pairs={{0,8},{1,9},{2,10},{3,11},{4,12},{5,13},{6,14},{7,15},{8,0},{9,1},... | collective-permute-start | bytes 3145736 | tf_op jit(solution)/shard_map/ppermute | solution.py:286
  785.7 32.9 %collective-permute-start.107 = (bf16[128,1024]{1,0:T(8,128)(2,1)S(1)}, bf16[128,1024]{1,0:T(8,128)(2,1)S(1)}, u32[]{:S(2)}, u32[]{:S(2)}) collective-permute-start(bf16[128,1024]{1,0:T(8,128)(2,1)S(1)} %get-tuple-element.150), channel_id=1, source_target_pairs={{0,2},{1,3},{2,0},{3,1},{4,6},{5,7},{6,4},{7,5},{8,10},{9,11},{10,... | collective-permute-start | bytes 786440 | tf_op jit(solution)/shard_map/ppermute | solution.py:286
  787.4 32.3 %collective-permute-start.100 = (bf16[128,1024]{1,0:T(8,128)(2,1)}, bf16[128,1024]{1,0:T(8,128)(2,1)S(1)}, u32[]{:S(2)}, u32[]{:S(2)}) collective-permute-start(bf16[128,1024]{1,0:T(8,128)(2,1)} %get-tuple-element.151), channel_id=1, source_target_pairs={{0,1},{1,0},{2,3},{3,2},{4,5},{5,4},{6,7},{7,6},{8,9},{9,8},{10,11... | collective-permute-start | bytes 786440 | tf_op jit(solution)/shard_map/ppermute | solution.py:286
  790.2 29.5 %collective-permute-start.102 = (bf16[128,1024]{1,0:T(8,128)(2,1)}, bf16[128,1024]{1,0:T(8,128)(2,1)S(1)}, u32[]{:S(2)}, u32[]{:S(2)}) collective-permute-start(bf16[128,1024]{1,0:T(8,128)(2,1)} %get-tuple-element.152), channel_id=1, source_target_pairs={{0,3},{1,2},{2,1},{3,0},{4,7},{5,6},{6,5},{7,4},{8,11},{9,10},{10,... | collective-permute-start | bytes 786440 | tf_op jit(solution)/shard_map/ppermute | solution.py:286
  797.1 30.2 %collective-permute-start.101 = (bf16[128,1024]{1,0:T(8,128)(2,1)}, bf16[128,1024]{1,0:T(8,128)(2,1)S(1)}, u32[]{:S(2)}, u32[]{:S(2)}) collective-permute-start(bf16[128,1024]{1,0:T(8,128)(2,1)} %get-tuple-element.153), channel_id=1, source_target_pairs={{0,2},{1,3},{2,0},{3,1},{4,6},{5,7},{6,4},{7,5},{8,10},{9,11},{10,... | collective-permute-start | bytes 786440 | tf_op jit(solution)/shard_map/ppermute | solution.py:286
  (208 other events, 2804.0 us)

commit v2 on v1

--- a/solution.py
+++ b/solution.py
@@ -15,6 +15,7 @@
 LOGIT_SCALE = 2.0
 MASKED = -1e30
 AXES = ("dp", "tensor")
+MESH = pl.DeviceIdType.MESH
 BF = jnp.bfloat16
 F32 = jnp.float32
 
@@ -45,24 +46,54 @@
     return lax.dot_general(a, b, (((0,), (0,)), ((), ())), preferred_element_type=F32)
 
 
-def half_turn(values):
-    lane = lax.broadcasted_iota(jnp.int32, values.shape, 1)
-    ahead = jnp.roll(values, -32, axis=1)
-    behind = jnp.roll(values, 32, axis=1)
-    return jnp.where(lane % HEAD_WIDTH < 32, -ahead, behind)
-
-
-def attention_forward(q, k_own, v_own, k_far, v_far, col_labels, own_labels, far_labels, docs):
-    rows, width = q.shape
-    far = k_far.shape[0]
+def turned(values):
+    lane = lax.broadcasted_iota(jnp.int32, (1, 128), 1)
+    ahead = pltpu.roll(values, 96, 1)
+    behind = pltpu.roll(values, 32, 1)
+    return jnp.where(lane % HEAD_WIDTH < HEAD_WIDTH // 2, ahead, behind)
+
+
+def project_heads(x, weights, bias, cosine, sine):
+    rows, width = x.shape
+    columns = 256
+
+    def kernel(x_ref, w_ref, b_ref, c_ref, s_ref, o_ref):
+        got = dot_nn(x_ref[...], w_ref[0]) + b_ref[0]
+        for at in range(0, columns, 128):
+            piece = got[:, at : at + 128]
+            o_ref[0, :, at : at + 128] = (piece * c_ref[0] + turned(piece) * s_ref[0]).astype(BF)
+
+    return pl.pallas_call(
+        kernel,
+        grid=(3, width // columns),
+        in_specs=[
+            pl.BlockSpec((rows, width), lambda j, n: (0, 0)),
+            pl.BlockSpec((1, width, columns), lambda j, n: (j, 0, n)),
+            pl.BlockSpec((1, 1, columns), lambda j, n: (j, 0, n)),
+            pl.BlockSpec((1, rows, 128), lambda j, n: (j, 0, 0)),
+            pl.BlockSpec((1, rows, 128), lambda j, n: (j, 0, 0)),
+        ],
+        out_specs=pl.BlockSpec((1, rows, columns), lambda j, n: (j, 0, n)),
+        out_shape=jax.ShapeDtypeStruct((3, rows, width), BF),
+        compiler_params=pltpu.CompilerParams(vmem_limit_bytes=40 << 20),
+        name="project_heads",
+        cost_estimate=pl.CostEstimate(
+            flops=6 * rows * width * width, bytes_accessed=6 * width * width, transcendentals=0
+        ),
+    )(x, weights, bias[:, None, :], cosine, sine)
+
+
+def attention_forward(qkv, far_kv, col_labels, own_labels, far_labels):
+    rows, width = qkv.shape[1:]
+    docs = far_kv.shape[1]
     block = 128
     asked = rows - docs
 
-    def kernel(q_ref, ko_ref, vo_ref, kf_ref, vf_ref, lc_ref, lo_ref, lf_ref, o_ref):
+    def kernel(qkv_ref, far_ref, lc_ref, lo_ref, lf_ref, o_ref):
         lane = lax.broadcasted_iota(jnp.int32, (1, 128), 1)
 
         def part(start, size, keys, sames):
-            q_block = q_ref[pl.ds(start, size), :]
+            q_block = qkv_ref[0, pl.ds(start, size), :]
             outs = []
             for head in range(2):
                 mask = (lane // HEAD_WIDTH) == head
@@ -85,61 +116,59 @@
             o_ref[pl.ds(start, size), :] = jnp.where(lane < HEAD_WIDTH, outs[0], outs[1]).astype(BF)
 
         doc_keys = [
-            (ko_ref[:docs, :], vo_ref[:docs, :]),
-            (kf_ref[...], vf_ref[...]),
+            (qkv_ref[1, :docs, :], qkv_ref[2, :docs, :]),
+            (far_ref[0], far_ref[1]),
         ]
         for at in range(docs // block):
             labels = lc_ref[pl.ds(at * block, block), :]
             part(at * block, block, doc_keys, [labels == lo_ref[...], labels == lf_ref[...]])
         row = lax.broadcasted_iota(jnp.int32, (asked, asked), 0) // QLEN
         col = lax.broadcasted_iota(jnp.int32, (asked, asked), 1) // QLEN
-        part(docs, asked, [(ko_ref[docs:, :], vo_ref[docs:, :])], [row == col])
-
-    head_block = lambda n: pl.BlockSpec((n, 128), lambda h: (0, h))
+        part(docs, asked, [(qkv_ref[1, docs:, :], qkv_ref[2, docs:, :])], [row == col])
+
     whole = lambda shape: pl.BlockSpec(shape, lambda h: (0, 0))
     return pl.pallas_call(
         kernel,
         grid=(width // 128,),
         in_specs=[
-            head_block(rows),
-            head_block(rows),
-            head_block(rows),
-            head_block(far),
-            head_block(far),
+            pl.BlockSpec((3, rows, 128), lambda h: (0, 0, h)),
+            pl.BlockSpec((2, docs, 128), lambda h: (0, 0, h)),
             whole((docs, 1)),
             whole((1, docs)),
-            whole((1, far)),
+            whole((1, docs)),
         ],
-        out_specs=head_block(rows),
+        out_specs=pl.BlockSpec((rows, 128), lambda h: (0, h)),
         out_shape=jax.ShapeDtypeStruct((rows, width), BF),
         compiler_params=pltpu.CompilerParams(vmem_limit_bytes=40 << 20),
         name="attend_forward",
         cost_estimate=pl.CostEstimate(
-            flops=4 * rows * 2 * docs * width,
-            bytes_accessed=2 * (4 * rows + 2 * far) * width,
+            flops=32 * rows * 2 * docs * width,
+            bytes_accessed=2 * (4 * rows + 2 * docs) * width,
             transcendentals=rows * 2 * docs * width // 64,
         ),
-    )(q, k_own, v_own, k_far, v_far, col_labels, own_labels, far_labels)
+    )(qkv, far_kv, col_labels, own_labels, far_labels)
 
 
 def attention_backward(
-    q, k_own, v_own, k_far, v_far, grad, col_labels, own_labels, far_labels, docs
+    first, count, qkv, far_kv, grad, cosine, sine, far_cosine, far_sine,
+    col_labels, own_labels, far_labels,
 ):
-    rows, width = q.shape
-    far = k_far.shape[0]
+    rows = qkv.shape[1]
+    docs = far_kv.shape[1]
+    width = count * 128
     block = 128
     asked = rows - docs
 
     def kernel(
-        q_ref, ko_ref, vo_ref, kf_ref, vf_ref, g_ref, lc_ref, lo_ref, lf_ref,
-        dq_ref, dko_ref, dvo_ref, dkf_ref, dvf_ref, sums_own, sums_far,
+        qkv_ref, far_ref, g_ref, c_ref, s_ref, fc_ref, fs_ref, lc_ref, lo_ref, lf_ref,
+        dq_ref, own_ref, give_ref, sums_own, sums_far,
     ):
         lane = lax.broadcasted_iota(jnp.int32, (1, 128), 1)
         sums_own[...] = jnp.zeros_like(sums_own)
         sums_far[...] = jnp.zeros_like(sums_far)
 
         def part(start, size, keys, sames, sums):
-            q_block = q_ref[pl.ds(start, size), :]
+            q_block = qkv_ref[0, pl.ds(start, size), :]
             g_block = g_ref[pl.ds(start, size), :]
             grads = []
             for head in range(2):
@@ -164,19 +193,21 @@
                     jnp.add,
                     [jnp.sum(p * d, axis=-1, keepdims=True) for p, d in zip(powers, pulls)],
                 ) * inverse
-                turned = [(p * (d - mean)).astype(BF) for p, d in zip(powers, pulls)]
+                slopes = [(p * (d - mean)).astype(BF) for p, d in zip(powers, pulls)]
                 got = functools.reduce(
-                    jnp.add, [dot_nn(s, key) for s, (key, _) in zip(turned, keys)]
+                    jnp.add, [dot_nn(s, key) for s, (key, _) in zip(slopes, keys)]
                 )
                 grads.append(got * 0.125)
-                for (ref, first, count), s, p in zip(sums, turned, powers):
-                    ref[0, pl.ds(first, count), :] += dot_tn(s, q_head)
-                    ref[1, pl.ds(first, count), :] += dot_tn(p.astype(BF), g_head)
-            dq_ref[pl.ds(start, size), :] = jnp.where(lane < HEAD_WIDTH, grads[0], grads[1])
+                for (ref, begin, many), s, p in zip(sums, slopes, powers):
+                    ref[0, pl.ds(begin, many), :] += dot_tn(s, q_head)
+                    ref[1, pl.ds(begin, many), :] += dot_tn(p.astype(BF), g_head)
+            whole = jnp.where(lane < HEAD_WIDTH, grads[0], grads[1])
+            at = pl.ds(start, size)
+            dq_ref[at, :] = (whole * c_ref[at, :] - turned(whole) * s_ref[at, :]).astype(BF)
 
         doc_keys = [
-            (ko_ref[:docs, :], vo_ref[:docs, :]),
-            (kf_ref[...], vf_ref[...]),
+            (qkv_ref[1, :docs, :], qkv_ref[2, :docs, :]),
+            (far_ref[0], far_ref[1]),
         ]
         for at in range(docs // block):
             labels = lc_ref[pl.ds(at * block, block), :]
@@ -185,61 +216,389 @@
                 block,
                 doc_keys,
                 [labels == lo_ref[...], labels == lf_ref[...]],
-                [(sums_own, 0, docs), (sums_far, 0, far)],
+                [(sums_own, 0, docs), (sums_far, 0, docs)],
             )
         row = lax.broadcasted_iota(jnp.int32, (asked, asked), 0) // QLEN
         col = lax.broadcasted_iota(jnp.int32, (asked, asked), 1) // QLEN
         part(
             docs,
             asked,
-            [(ko_ref[docs:, :], vo_ref[docs:, :])],
+            [(qkv_ref[1, docs:, :], qkv_ref[2, docs:, :])],
             [row == col],
             [(sums_own, docs, asked)],
         )
-        dko_ref[...] = sums_own[0]
-        dvo_ref[...] = sums_own[1]
-        dkf_ref[...] = sums_far[0].astype(BF)
-        dvf_ref[...] = sums_far[1].astype(BF)
-
-    head_block = lambda n: pl.BlockSpec((n, 128), lambda h: (0, h))
+        own_ref[0] = sums_own[0] * c_ref[...] - turned(sums_own[0]) * s_ref[...]
+        own_ref[1] = sums_own[1]
+        give_ref[0] = (sums_far[0] * fc_ref[...] - turned(sums_far[0]) * fs_ref[...]).astype(BF)
+        give_ref[1] = sums_far[1].astype(BF)
+
     whole = lambda shape: pl.BlockSpec(shape, lambda h: (0, 0))
     return pl.pallas_call(
         kernel,
-        grid=(width // 128,),
+        grid=(count,),
         in_specs=[
-            head_block(rows),
-            head_block(rows),
-            head_block(rows),
-            head_block(far),
-            head_block(far),
-            head_block(rows),
+            pl.BlockSpec((3, rows, 128), lambda h: (0, 0, h + first)),
+            pl.BlockSpec((2, docs, 128), lambda h: (0, 0, h + first)),
+            pl.BlockSpec((rows, 128), lambda h: (0, h + first)),
+            whole((rows, 128)),
+            whole((rows, 128)),
+            whole((docs, 128)),
+            whole((docs, 128)),
             whole((docs, 1)),
             whole((1, docs)),
-            whole((1, far)),
+            whole((1, docs)),
         ],
         out_specs=[
-            head_block(rows),
-            head_block(rows),
-            head_block(rows),
-            head_block(far),
-            head_block(far),
+            pl.BlockSpec((rows, 128), lambda h: (0, h)),
+            pl.BlockSpec((2, rows, 128), lambda h: (0, 0, h)),
+            pl.BlockSpec((2, docs, 128), lambda h: (0, 0, h)),
         ],
         out_shape=[
-            jax.ShapeDtypeStruct((rows, width), F32),
-            jax.ShapeDtypeStruct((rows, width), F32),
-            jax.ShapeDtypeStruct((rows, width), F32),
-            jax.ShapeDtypeStruct((far, width), BF),
-            jax.ShapeDtypeStruct((far, width), BF),
+            jax.ShapeDtypeStruct((rows, width), BF),
+            jax.ShapeDtypeStruct((2, rows, width), F32),
+            jax.ShapeDtypeStruct((2, docs, width), BF),
         ],
-        scratch_shapes=[pltpu.VMEM((2, rows, 128), F32), pltpu.VMEM((2, far, 128), F32)],
+        scratch_shapes=[pltpu.VMEM((2, rows, 128), F32), pltpu.VMEM((2, docs, 128), F32)],
         compiler_params=pltpu.CompilerParams(vmem_limit_bytes=40 << 20),
         name="attend_backward",
         cost_estimate=pl.CostEstimate(
-            flops=10 * rows * 2 * docs * width,
-            bytes_accessed=4 * (6 * rows + 4 * far) * width,
+            flops=100 * rows * 2 * docs * width,
+            bytes_accessed=4 * (6 * rows + 4 * docs) * width,
             transcendentals=rows * 2 * docs * width // 64,
         ),
-    )(q, k_own, v_own, k_far, v_far, grad, col_labels, own_labels, far_labels)
+    )(
+        qkv, far_kv, grad, cosine, sine, far_cosine, far_sine, col_labels, own_labels, far_labels
+    )
+
+
+def differing(a, b, bits):
+    total = 0
+    for bit in range(bits):
+        x, y = (a // 2**bit) % 2, (b // 2**bit) % 2
+        total = total + 2**bit * (x + y - 2 * x * y)
+    return total
+
+
+def gather_kernel(x_doc, x_query, qkv, out, up, back, proj, bias, picks):
+    chips, ways = 4, 4
+    groups = 2 * chips
+    weights = [qkv, out, up, back]
+    feature_axis = [1, 1, 0, 1]
+    tensor_axis = [2, 0, 1, 0]
+    first_bits = [(2, 4), (4, 2), (2, 4), (4, 2)]
+    count = len(weights)
+    quarter, width = x_doc.shape[1:]
+    asked = x_query.shape[1]
+    docs = 2 * quarter
+    slots = 32
+
+    def place(j):
+        return (j & 1) * chips + (j >> 1)
+
+    def kernel(*refs):
+        xd_ref, xq_ref = refs[:2]
+        sources = refs[2 : 2 + count]
+        proj_ref, bias_ref, picks_ref = refs[2 + count : 5 + count]
+        x_out = refs[5 + count]
+        outs = refs[6 + count : 6 + 2 * count]
+        proj_out, bias_out, picks_out = refs[6 + 2 * count : 9 + 2 * count]
+        send_sem, recv_sem, small_send, small_recv, x_send, x_recv, local_sem = refs[9 + 2 * count :]
+        rank = lax.axis_index("dp")
+        column = lax.axis_index("tensor")
+        core = rank % 2
+        base = rank - core
+
+        def other(bit):
+            return rank + bit - 2 * bit * ((rank // bit) % 2)
+
+        barrier = pltpu.get_barrier_semaphore()
+        for dc in range(2):
+            for dt in range(4):
+                if dc + dt > 0:
+                    pl.semaphore_signal(
+                        barrier,
+                        inc=1,
+                        device_id=(base + (core + dc) % 2, (column + dt) % 4),
+                        device_id_type=MESH,
+                    )
+        for bit in (2, 4):
+            pl.semaphore_signal(
+                barrier, inc=1, device_id=(other(bit), column), device_id_type=MESH
+            )
+        pl.semaphore_wait(barrier, 9)
+
+        local = []
+
+        def keep(src, dst):
+            copy = pltpu.make_async_copy(src, dst, local_sem.at[len(local)])
+            copy.start()
+            local.append(copy)
+
+        lonely = 3 * core == column
+        x_copies = []
+        for m in range(2):
+            mine = jnp.logical_and(lonely, column // 2 == m)
+            q = column % 2
+            for kind, (ref, size, begin) in enumerate(((xd_ref, quarter, 0), (xq_ref, asked, docs))):
+                src = ref.at[m]
+                dst = x_out.at[pl.ds(pl.multiple_of(begin + q * size, 32), size), :]
+                away = pltpu.make_async_remote_copy(
+                    src_ref=src,
+                    dst_ref=dst,
+                    send_sem=x_send.at[m, kind],
+                    recv_sem=x_recv.at[q, kind],
+                    device_id=(base + column // 2, 2 * m + core),
+                    device_id_type=MESH,
+                )
+                here = pltpu.make_async_copy(src, dst, x_send.at[m, kind])
+
+                @pl.when(mine)
+                def _():
+                    here.start()
+
+                @pl.when(jnp.logical_not(mine))
+                def _():
+                    away.start()
+
+                x_copies.append((mine, here, away))
+
+        waits = []
+
+        def remote(a, slot, src, dst, to):
+            return pltpu.make_async_remote_copy(
+                src_ref=src,
+                dst_ref=dst,
+                send_sem=send_sem.at[a, slot],
+                recv_sem=recv_sem.at[a, slot],
+                device_id=to,
+                device_id_type=MESH,
+            )
+
+        def piece(a, j, source, at=None):
+            at = column if at is None else at
+            index = [slice(None)] * len(sources[a].shape)
+            size = sources[a].shape[feature_axis[a]]
+            index[feature_axis[a]] = pl.ds(place(j) * size, size)
+            size = sources[a].shape[tensor_axis[a]]
+            offset = pl.multiple_of(differing(at, source, 2) * size, size)
+            index[tensor_axis[a]] = pl.ds(offset, size)
+            return outs[a].at[tuple(index)]
+
+        def line(a, j):
+            index = [slice(None)] * len(sources[a].shape)
+            size = sources[a].shape[feature_axis[a]]
+            index[feature_axis[a]] = pl.ds(place(j) * size, size)
+            return outs[a].at[tuple(index)]
+
+        def go(copy, condition):
+            if condition is None:
+                copy.start()
+            else:
+
+                @pl.when(condition)
+                def _():
+                    copy.start()
+
+            waits.append((condition, copy))
+
+        def origin(kind):
+            if kind == 0:
+                return column, None
+            if kind <= 3:
+                return column - kind, column >= kind
+            return column + (kind - 3), column + (kind - 3) <= 3
+
+        def both(x, y):
+            if x is None:
+                return y
+            return x if y is None else jnp.logical_and(x, y)
+
+        def spread(a, kind):
+            source, there = origin(kind)
+            first, second = first_bits[a]
+            src = sources[a] if kind == 0 else piece(a, 0, source)
+            go(remote(a, 6 + kind, src, piece(a, first, source), (other(first), column)), there)
+            go(remote(a, 13 + kind, src, piece(a, second, source), (other(second), column)), there)
+
+        def along(a, kind):
+            source, there = origin(kind)
+            src = sources[a] if kind == 0 else piece(a, 0, source)
+            hops = kind if kind <= 3 else kind - 3
+            if kind <= 3 and hops < 3:
+                dst = piece(a, 0, source, column + 1)
+                go(remote(a, hops, src, dst, (rank, column + 1)), both(there, column < 3))
+            if (kind == 0 or kind > 3) and hops < 3:
+                dst = piece(a, 0, source, column - 1)
+                go(remote(a, 3 + hops, src, dst, (rank, column - 1)), both(there, column > 0))
+
+        def arrived(a, slot, dst, condition):
+            copy = remote(a, slot, dst, dst, (rank, column))
+            if condition is None:
+                copy.wait_recv()
+            else:
+
+                @pl.when(condition)
+                def _():
+                    copy.wait_recv()
+
+        def onward(a, kind):
+            source, there = origin(kind)
+            first, second = first_bits[a]
+            src = piece(a, first, source)
+            arrived(a, 6 + kind, src, there)
+            dst = piece(a, first | second, source)
+            go(remote(a, 20 + kind, src, dst, (other(second), column)), there)
+
+        small = []
+
+        def tiny(src, dst, to):
+            at = len(small)
+            copy = pltpu.make_async_remote_copy(
+                src_ref=src,
+                dst_ref=dst,
+                send_sem=small_send.at[at],
+                recv_sem=small_recv.at[at],
+                device_id=to,
+                device_id_type=MESH,
+            )
+            copy.start()
+            small.append(copy)
+            return copy
+
+        for a in range(count):
+            along(a, 0)
+            spread(a, 0)
+        for a in range(count):
+            keep(sources[a], piece(a, 0, column))
+        keep(bias_ref, bias_out.at[0])
+        for dt in range(1, 4):
+            to = differing(column, dt, 2)
+            tiny(bias_ref, bias_out.at[dt], (rank, to))
+        flat = []
+        for ref, out_ref in ((proj_ref, proj_out), (picks_ref, picks_out)):
+            keep(ref, out_ref.at[0])
+            flat.append(
+                (
+                    tiny(ref, out_ref.at[place(2)], (other(2), column)),
+                    tiny(ref, out_ref.at[place(4)], (other(4), column)),
+                    tiny(ref, out_ref.at[place(1)], (other(1), column)),
+                    out_ref,
+                )
+            )
+
+        for hops in range(1, 4):
+            for a in range(count):
+                for kind in (hops, hops + 3):
+                    source, there = origin(kind)
+                    slot = hops - 1 if kind <= 3 else 2 + hops
+                    arrived(a, slot, piece(a, 0, source), there)
+                    along(a, kind)
+                    spread(a, kind)
+            kinds = (0,) if hops == 1 else (hops - 1, hops + 2)
+            for a in range(count):
+                for kind in kinds:
+                    onward(a, kind)
+        for copy in local:
+            copy.wait()
+
+        def sibling(a, slot, j):
+            go(remote(a, slot, line(a, j), line(a, j | 1), (other(1), column)), None)
+
+        for a in range(count):
+            sibling(a, 27, 0)
+        for by_two, by_four, _, out_ref in flat:
+            by_two.wait_recv()
+            tiny(out_ref.at[place(2)], out_ref.at[place(6)], (other(4), column))
+            tiny(out_ref.at[place(2)], out_ref.at[place(3)], (other(1), column))
+            by_four.wait_recv()
+            tiny(out_ref.at[place(4)], out_ref.at[place(5)], (other(1), column))
+        for a in range(count):
+            for kind in (3, 6):
+                onward(a, kind)
+            sibling(a, 28, first_bits[a][0])
+        for n, (_, _, _, out_ref) in enumerate(flat):
+            small[9 + 3 * n].wait_recv()
+            tiny(out_ref.at[place(6)], out_ref.at[place(7)], (other(1), column))
+        for a in range(count):
+            first, second = first_bits[a]
+            for base_slot, j, slot in ((13, second, 29), (20, first | second, 30)):
+                for kind in range(7):
+                    source, there = origin(kind)
+                    arrived(a, base_slot + kind, piece(a, j, source), there)
+                sibling(a, slot, j)
+        for n, copy in enumerate(small):
+            if n not in (3, 4, 6, 7, 9, 12):
+                copy.wait_recv()
+            copy.wait_send()
+        for q in range(2):
+            mine = jnp.logical_and(lonely, column % 2 == q)
+            for kind, (size, begin) in enumerate(((quarter, 0), (asked, docs))):
+                dst = x_out.at[pl.ds(begin + q * size, size), :]
+                copy = pltpu.make_async_remote_copy(
+                    src_ref=dst,
+                    dst_ref=dst,
+                    send_sem=x_send.at[q, kind],
+                    recv_sem=x_recv.at[q, kind],
+                    device_id=(rank, column),
+                    device_id_type=MESH,
+                )
+
+                @pl.when(jnp.logical_not(mine))
+                def _():
+                    copy.wait_recv()
+
+        for mine, here, away in x_copies:
+
+            @pl.when(mine)
+            def _():
+                here.wait()
+
+            @pl.when(jnp.logical_not(mine))
+            def _():
+                away.wait_send()
+
+        for a in range(count):
+            for slot, j in ((27, 1), (28, first_bits[a][0] | 1), (29, first_bits[a][1] | 1), (30, 7)):
+                arrived(a, slot, line(a, j), None)
+        for condition, copy in waits:
+            if condition is None:
+                copy.wait_send()
+            else:
+
+                @pl.when(condition)
+                def _():
+                    copy.wait_send()
+
+    out_shape = [jax.ShapeDtypeStruct((docs + 2 * asked, width), x_doc.dtype)]
+    for w, f, t in zip(weights, feature_axis, tensor_axis):
+        shape = list(w.shape)
+        shape[f] *= groups
+        shape[t] *= ways
+        out_shape.append(jax.ShapeDtypeStruct(tuple(shape), w.dtype))
+    out_shape += [
+        jax.ShapeDtypeStruct((groups,) + proj.shape, proj.dtype),
+        jax.ShapeDtypeStruct((ways,) + bias.shape, bias.dtype),
+        jax.ShapeDtypeStruct((groups,) + picks.shape, picks.dtype),
+    ]
+    anywhere = pl.BlockSpec(memory_space=pl.ANY)
+    dma = pltpu.SemaphoreType.DMA
+    return pl.pallas_call(
+        kernel,
+        out_shape=out_shape,
+        in_specs=[anywhere] * (5 + count),
+        out_specs=[anywhere] * (4 + count),
+        scratch_shapes=[
+            dma((count, slots)),
+            dma((count, slots)),
+            dma((17,)),
+            dma((17,)),
+            dma((2, 2)),
+            dma((2, 2)),
+            dma((count + 3,)),
+        ],
+        compiler_params=pltpu.CompilerParams(collective_id=0, has_side_effects=True),
+        name="gather_weights",
+    )(x_doc, x_query, *weights, proj, bias, picks)
 
 
 def body(
@@ -361,21 +720,29 @@
     actual = (rank ^ (2 * (step % chips) + step // chips)) * block + place % block
     turn = (place[:, None] == actual[None, :]).astype(BF)
 
-    pack_one = jnp.stack([w_qkv[0], w_qkv[1]])
-    pack_two = jnp.stack([w_qkv[2], w_out.T])
-    full_qk = gather_weights(pack_one, False)
-    full_vo = gather_weights(pack_two, True)
-    bias_pack = jnp.concatenate([b_qkv.reshape(-1), b_in])[None]
-    biases = [bias_pack] + [exchange(bias_pack, dt=j) for j in range(1, ways)]
+    bias_pack = jnp.concatenate([b_qkv.reshape(-1), b_in])
+    own_picks = jnp.zeros((8, 128), jnp.int32).at[:micro, : positives.shape[1]].set(positives)
+    if chips == 4:
+        own_x, full_qkv, full_out, full_in, full_back, full_proj, biases, picks_rel = gather_kernel(
+            x_doc, x_query, w_qkv, w_out, w_in, w_back, w_proj, bias_pack.reshape(-1, 128), own_picks
+        )
+        biases = [biases[j].reshape(-1) for j in range(ways)]
+        full_proj = full_proj.reshape(width, proj_width)
+    else:
+        own_x = rows_in(x_doc, x_query)
+        full_qkv = gather_weights(w_qkv, False)
+        full_out = gather_weights(w_out.T, False).T
+        full_in = gather_weights(w_in, False)
+        full_back = gather_weights(w_back.T, False).T
+        full_proj = gather_proj(w_proj)
+        picks_rel = gather_proj(own_picks[None])
+        biases = [bias_pack] + [exchange(bias_pack[None], dt=j)[0] for j in range(1, ways)]
+    picks_rel = picks_rel[:, :micro, : positives.shape[1]].astype(F32)
+    own_cot = rows_in(doc_cot.astype(BF), query_cot.astype(BF))
     bias_qkv = jnp.concatenate(
-        [b[0, : 3 * heads_local].reshape(3, heads_local) for b in biases], axis=1
+        [b[: 3 * heads_local].reshape(3, heads_local) for b in biases], axis=1
     )
-    bias_in = jnp.concatenate([b[0, 3 * heads_local :] for b in biases])
-    own_x = rows_in(x_doc, x_query)
-    own_cot = rows_in(doc_cot.astype(BF), query_cot.astype(BF))
-    full_in = gather_weights(w_in, False)
-    full_back = gather_weights(w_back.T, True)
-    full_proj = gather_proj(w_proj)
+    bias_in = jnp.concatenate([b[3 * heads_local :] for b in biases])
     params = jnp.stack(
         [b_out, gain_one, shift_one, b_back, gain_two, shift_two, b_out, b_out]
     )
@@ -400,35 +767,34 @@
         return segment, index - begin
 
     own_labels, own_places = layout(core * docs)
-    far_labels, _ = layout((1 - core) * docs)
-    places = jnp.concatenate([own_places, jnp.arange(queries, dtype=jnp.int32) % QLEN])
+    far_labels, far_places = layout((1 - core) * docs)
+    own_places = jnp.concatenate([own_places, jnp.arange(queries, dtype=jnp.int32) % QLEN])
     half = HEAD_WIDTH // 2
     rates = 10000.0 ** (-(2.0 * jnp.arange(half, dtype=F32)) / HEAD_WIDTH)
-    angle = places.astype(F32)[:, None] * rates[None, :]
-    cosine = jnp.tile(jnp.cos(angle), (1, width // half))
-    sine = jnp.tile(jnp.sin(angle), (1, width // half))
+
+    def rotation(places):
+        angle = places.astype(F32)[:, None] * rates[None, :]
+        sine = jnp.sin(angle)
+        return jnp.tile(jnp.cos(angle), (1, 4)), jnp.concatenate([-sine, sine] * 2, axis=1)
+
+    cosine, sine = rotation(own_places)
+    far_cosine, far_sine = rotation(far_places)
+    cosines_three = jnp.stack([cosine * 0.125, cosine, jnp.ones_like(cosine)])
+    sines_three = jnp.stack([sine * 0.125, sine, jnp.zeros_like(sine)])
 
     x_low = dot_nn(own_x, turn).astype(BF)
-    parts = [
-        dot_nn(x_low, full_qk[0]) + bias_qkv[0],
-        dot_nn(x_low, full_qk[1]) + bias_qkv[1],
-        dot_nn(x_low, full_vo[0]) + bias_qkv[2],
-    ]
-    q_rot = (parts[0] * cosine + half_turn(parts[0]) * sine).astype(BF) * 0.125
-    k_rot = (parts[1] * cosine + half_turn(parts[1]) * sine).astype(BF)
-    v_low = parts[2].astype(BF)
-    k_far = exchange(k_rot[:docs], dr=1)
-    v_far = exchange(v_low[:docs], dr=1)
-    label_args = (own_labels[:, None], own_labels[None, :], far_labels[None, :], docs)
-    mixed = attention_forward(q_rot, k_rot, v_low, k_far, v_far, *label_args)
-    branch = dot_nt(mixed, full_vo[1])
+    qkv = project_heads(x_low, full_qkv, bias_qkv, cosines_three, sines_three)
+    far_kv = exchange(qkv[1:, :docs], dr=1)
+    label_args = (own_labels[:, None], own_labels[None, :], far_labels[None, :])
+    mixed = attention_forward(qkv, far_kv, *label_args)
+    branch = dot_nn(mixed, full_out)
     resid_one = x_low.astype(F32) + branch + b_out
     normed, norm_one_pull = jax.vjp(layer_norm, resid_one, gain_one, shift_one)
     normed_low = normed.astype(BF)
     inner = dot_nn(normed_low, full_in) + bias_in
     active, gelu_pull = jax.vjp(gelu_exact, inner)
     active_low = active.astype(BF)
-    resid_two = normed + dot_nt(active_low, full_back) + b_back
+    resid_two = normed + dot_nn(active_low, full_back) + b_back
     output, norm_two_pull = jax.vjp(layer_norm, resid_two, gain_two, shift_two)
     output_low = output.astype(BF)
     y_doc, y_query = rows_out(dot_nt(output_low, turn).astype(BF))
@@ -460,11 +826,11 @@
     all_queries = query_unit
     for dr, dt in steps:
         all_queries = join(all_queries, dr, dt)
-    picks = jnp.where(unit_micro == 0, positives[0], positives[1])[None]
-    picks = join(picks, 1, 0)
-    for dr in chip_bits:
-        picks = join(picks, dr, 0)
-    picks = picks.reshape(-1)
+    held = jnp.arange(groups, dtype=jnp.int32)
+    held = rank ^ (2 * (held % chips) + held // chips)
+    order = (jnp.arange(groups, dtype=jnp.int32)[:, None] == held[None, :]).astype(F32)
+    picks = jnp.where(unit_micro == 0, picks_rel[:, 0], picks_rel[:, 1])
+    picks = jnp.dot(order, picks, precision=FULL_PRECISION).astype(jnp.int32).reshape(-1)
     seg_labels = jnp.arange(segments, dtype=jnp.int32)
     member = (own_labels[:, None] == seg_labels[None, :]).astype(F32)
     cosines = dot_nt(doc_unit, all_queries)
@@ -500,27 +866,78 @@
     ]
     loss_out = quarters_out(loss_tiles[0], loss_tiles[1])[:, :, 0]
 
-    def reduce_weights(left, right, reverse):
-        size = left.shape[1] // 2
-        send = dot_tn(left[:, size:], right).astype(BF)
-        got = exchange(send, dr=1)
-        keep = dot_tn(left[:, :size], right) + got.astype(F32)
-        order = chip_bits if reverse and len(chip_bits) == 2 else chip_bits[::-1]
-        left_bits = sorted(chip_bits)
-        for dr in order:
-            at = left_bits.index(dr)
-            inner_rows = block << at
-            view = keep.reshape(-1, 2, inner_rows, keep.shape[-1])
-            send = view[:, 1].reshape(-1, keep.shape[-1]).astype(BF)
-            stay = view[:, 0].reshape(-1, keep.shape[-1])
-            keep = stay + exchange(send, dr=dr).astype(F32)
-            left_bits.remove(dr)
-        size = keep.shape[1] // ways
-        total = keep[:, :size]
-        low = keep.astype(BF)
-        for j in range(1, ways):
-            total = total + exchange(low[:, j * size : (j + 1) * size], dt=j).astype(F32)
-        return total
+    class Reduction:
+        def __init__(self, half, axis, reverse, last):
+            self.bits = chip_bits if reverse and len(chip_bits) == 2 else chip_bits[::-1]
+            self.left = sorted(chip_bits)
+            self.axis, self.last = axis, last
+            self.sends = [half(1).astype(BF)]
+            self.hops = [(1, 0)]
+            self.kept = lambda: half(0)
+            self.stage = 0
+
+        def advance(self):
+            total = self.kept()
+            for s, (dr, dt) in zip(self.sends, self.hops):
+                got = exchange(s, dr=dr, dt=dt).astype(F32)
+                total = got if total is None else total + got
+            if self.stage == len(self.bits) + 1:
+                return total
+            if self.stage < len(self.bits):
+                dr = self.bits[self.stage]
+                at = self.left.index(dr)
+                self.left.remove(dr)
+                size = block << at
+                stay, send = [
+                    jnp.concatenate(
+                        [
+                            lax.slice_in_dim(total, b, b + size, axis=self.axis)
+                            for b in range(side * size, total.shape[self.axis], 2 * size)
+                        ],
+                        axis=self.axis,
+                    )
+                    for side in (0, 1)
+                ]
+                self.sends = [send.astype(BF)]
+                self.hops = [(dr, 0)]
+            else:
+                stay, sends = self.last(total)
+                self.sends = [piece.astype(BF) for _, piece in sends]
+                self.hops = [(0, dt) for dt, _ in sends]
+            self.kept = lambda: stay
+            self.stage += 1
+            return None
+
+        def finish(self):
+            total = None
+            while total is None:
+                total = self.advance()
+            return total
+
+    def weight_sum(left, right, axis, reverse):
+        size = width // 2
+
+        def half(n):
+            if axis == 0:
+                return dot_tn(left[:, n * size : (n + 1) * size], right)
+            return dot_tn(left, right[:, n * size : (n + 1) * size])
+
+        def last(total):
+            size = total.shape[1 - axis] // ways
+            pieces = [
+                lax.slice_in_dim(total, j * size, (j + 1) * size, axis=1 - axis)
+                for j in range(ways)
+            ]
+            return pieces[0], [(j, pieces[j]) for j in range(1, ways)]
+
+        return Reduction(half, axis, reverse, last)
+
+    def after(value, reductions):
+        sends = [r.sends for r in reductions]
+        value, sends = lax.optimization_barrier((value, sends))
+        for r, s in zip(reductions, sends):
+            r.sends = s
+        return value
 
     unit_grad = jnp.concatenate([doc_grad, query_grad], axis=0)
     (proj_grad,) = unit_pull(unit_grad)
@@ -528,36 +945,80 @@
     out_grad = own_cot_turned = dot_nn(own_cot, turn) + dot_nt(proj_low, full_proj)
     resid_two_grad, gain_two_grad, shift_two_grad = norm_two_pull(out_grad)
     update_low = resid_two_grad.astype(BF)
-    active_grad = dot_nn(update_low, full_back)
+    sum_back = weight_sum(active_low, update_low, 1, True)
+    active_grad = dot_nt(update_low, full_back)
     (inner_grad,) = gelu_pull(active_grad)
     inner_low = inner_grad.astype(BF)
-    out_back = reduce_weights(update_low, active_low, True)
-    out_in = reduce_weights(normed_low, inner_low, False)
+    sum_in = weight_sum(normed_low, inner_low, 0, False)
     normed_grad = dot_nt(inner_low, full_in) + resid_two_grad
     resid_one_grad, gain_one_grad, shift_one_grad = norm_one_pull(normed_grad)
     branch_low = resid_one_grad.astype(BF)
-    mixed_grad = dot_nn(branch_low, full_vo[1]).astype(BF)
-    out_out = reduce_weights(branch_low, mixed, True)
-    q_grad, k_grad, v_grad, k_give, v_give = attention_backward(
-        q_rot, k_rot, v_low, k_far, v_far, mixed_grad, *label_args
-    )
-    pad = jnp.zeros((queries, width), F32)
-    k_grad = k_grad + jnp.concatenate([exchange(k_give, dr=1).astype(F32), pad], axis=0)
-    v_grad = v_grad + jnp.concatenate([exchange(v_give, dr=1).astype(F32), pad], axis=0)
-    pre_low = [
-        (q_grad * cosine - half_turn(q_grad) * sine).astype(BF),
-        (k_grad * cosine - half_turn(k_grad) * sine).astype(BF),
-        v_grad.astype(BF),
-    ]
-    out_qkv = jnp.stack(
-        [reduce_weights(x_low, pre_low[i], i == 2) for i in range(3)]
-    )
-    x_grad = (
-        resid_one_grad
-        + dot_nt(pre_low[0], full_qk[0])
-        + dot_nt(pre_low[1], full_qk[1])
-        + dot_nt(pre_low[2], full_vo[0])
-    )
+    mixed_grad = dot_nt(branch_low, full_out).astype(BF)
+    sum_out = weight_sum(mixed, branch_low, 1, False)
+
+    def heads_sum(rights, first_block, blocks, reverse):
+        size = width // 2
+        many = rights.shape[1] // 3 // blocks
+
+        def half(n):
+            return dot_tn(x_low[:, n * size : (n + 1) * size], rights)
+
+        def last(total):
+            stay, sends = None, []
+            for b in range(blocks):
+                piece = jnp.stack(
+                    [total[:, (j * blocks + b) * many : (j * blocks + b + 1) * many] for j in range(3)]
+                )
+                if first_block + b == 0:
+                    stay = piece
+                else:
+                    sends.append((first_block + b, piece))
+            return stay, sends
+
+        return Reduction(half, 0, reverse, last)
+
+    head_sums, head_rights = [], []
+    running = [sum_back, sum_in]
+    per_block = heads_local // 128
+    for first_block, blocks in ((0, 2), (2, 1), (3, 1)):
+        for item in running:
+            item.advance()
+        mixed_grad = after(mixed_grad, running)
+        dq, own_grads, give = attention_backward(
+            first_block * per_block,
+            blocks * per_block,
+            qkv,
+            far_kv,
+            mixed_grad,
+            cosine,
+            sine,
+            far_cosine,
+            far_sine,
+            *label_args,
+        )
+        got = exchange(give, dr=1).astype(F32)
+        rights = [dq] + [
+            jnp.concatenate([own_grads[i, :docs] + got[i], own_grads[i, docs:]], axis=0).astype(BF)
+            for i in range(2)
+        ]
+        rights = jnp.concatenate(rights, axis=1)
+        head_rights.append((blocks, rights))
+        item = heads_sum(rights, first_block, blocks, first_block > 0)
+        head_sums.append(item)
+        if first_block == 0:
+            running += [sum_out]
+        elif first_block == 2:
+            running += [head_sums[0]]
+    out_back = sum_back.finish()
+    out_in = sum_in.finish()
+    out_out = sum_out.finish()
+    out_qkv = functools.reduce(jnp.add, [item.finish() for item in head_sums])
+    x_grad = resid_one_grad
+    for j in range(3):
+        pre = jnp.concatenate(
+            [r[:, j * r.shape[1] // 3 : (j + 1) * r.shape[1] // 3] for _, r in head_rights], axis=1
+        )
+        x_grad = x_grad + dot_nt(pre, full_qkv[j])
     gx_doc, gx_query = rows_out(dot_nt(x_grad.astype(BF), turn).astype(BF))
 
     grad_proj = dot_tn(output_low, proj_low)
@@ -581,11 +1042,15 @@
     vectors = lax.dot_general(
         vectors, turn.astype(F32), (((1,), (1,)), ((), ())), precision=FULL_PRECISION
     )
+    head_bias = []
+    for blocks, r in head_rights:
+        sums = jnp.sum(r.astype(F32), axis=0).reshape(3, blocks, heads_local)
+        head_bias.append(jnp.swapaxes(sums, 0, 1).reshape(blocks, 3 * heads_local))
     tensor_grads = jnp.concatenate(
         [
-            jnp.sum(item.astype(F32), axis=0).reshape(ways, heads_local) for item in pre_low
-        ]
-        + [jnp.sum(inner_low.astype(F32), axis=0).reshape(ways, units_local)],
+            jnp.concatenate(head_bias, axis=0),
+            jnp.sum(inner_low.astype(F32), axis=0).reshape(ways, units_local),
+        ],
         axis=1,
     )
     for dt in (2, 1):
@@ -603,13 +1068,13 @@
         gx_query.astype(F32),
         out_qkv,
         tensor_grads[: 3 * heads_local].reshape(3, heads_local),
-        out_out.T,
+        out_out,
         vectors[0],
         vectors[1],
         vectors[2],
         out_in,
         tensor_grads[3 * heads_local :],
-        out_back.T,
+        out_back,
         vectors[3],
         vectors[4],
         vectors[5],

time: 838 us -> 742 us (0.89)
  waiting for transfers between devices: 290 us -> 119 us
  Pallas kernels: 96.3 us -> 242 us
  starting transfers between devices: 146 us -> 82.3 us
  local copies, waits for them, and re-layouts: 82.3 us -> 66.8 us
    ppermute x104 -> x61, waiting for transfers between devices: 274 us -> 96 us  [exchange(): return lax.ppermute(value, AXES, pairs)]
    pallas_call x2 -> x6, Pallas kernels: 96.3 us -> 242 us  [the longest x1 133 us: gather_kernel(): pl.pallas_call(kernel, out_shape=out_shape, in_specs=[anywhere] * (5 + co...]
    ppermute x104 -> x61, starting transfers between devices: 111 us -> 59.5 us  [exchange(): return lax.ppermute(value, AXES, pairs)]
    dot_general x10 -> x7, matrix products: 61.1 us -> 42.4 us  [dot_nn(): lax.dot_general(a, b, (((1,), (0,)), ((), ())), preferred_element_type=F32)]
    dot_general x9, matrix products: 33.2 us -> 48.8 us  [dot_nt(): lax.dot_general(a, b, (((1,), (1,)), ((), ())), preferred_element_type=F32)]
    ppermute x4 -> x2, starting transfers between devices: 25.9 us -> 13 us  [rows_in(): got.append(lax.ppermute(send, AXES, pairs))]
    concatenate x11 -> x9, other arithmetic: 16.6 us -> 6.2 us  [the longest x3 3.75 us: rotation(): jnp.concatenate([-sine, sine] * 2, axis=1)]
    unnamed x313 -> x292, local copies, waits for them, and re-layouts: 29.6 us -> 20 us
  transfers between devices with their start and end apart: 114 -> 69, of which waited for: 47 -> 23; matrix products, arithmetic and copies ran while one was open for 27% -> 28% of each run, Pallas kernels for 12% -> 9%
where the time goes in v2:
time: 742 us; the launch traced here: 733 us
  Pallas kernels  242 us (33%)
  matrix products  148 us (20%)
  waiting for transfers between devices  119 us (16%)
  starting transfers between devices  82.3 us (11%)
  other arithmetic  69.1 us (9%)
  local copies, waits for them, and re-layouts  66.8 us (9%)
    pallas_call x1, Pallas kernels, gather_kernel(): pl.pallas_call(kernel, out_shape=out_shape, in_specs=[anywhere] * (5 + co...  133 us
    ppermute x61, waiting for transfers between devices, exchange(): return lax.ppermute(value, AXES, pairs)  96 us
    pallas_call x3, Pallas kernels, attention_backward(): pl.pallas_call(kernel, grid=(count,), in_specs=[pl.BlockSpec((3, rows, 12...  71.7 us
    ppermute x61, starting transfers between devices, exchange(): return lax.ppermute(value, AXES, pairs)  59.5 us
    dot_general x9, matrix products, dot_nt(): lax.dot_general(a, b, (((1,), (1,)), ((), ())), preferred_element_type=F32)  48.8 us
    dot_general x14, matrix products, dot_tn(): lax.dot_general(a, b, (((0,), (0,)), ((), ())), preferred_element_type=F32)  47 us
    dot_general x7, matrix products, dot_nn(): lax.dot_general(a, b, (((1,), (0,)), ((), ())), preferred_element_type=F32)  42.4 us
    pallas_call x1, Pallas kernels, attention_forward(): pl.pallas_call(kernel, grid=(width // 128,), in_specs=[pl.BlockSpec((3, r...  27.4 us
  transfers between devices with their start and end apart: 69, of which 23 were waited for; matrix products, arithmetic and copies ran while one was open for 28% of the time, Pallas kernels for 9%

profile of v2, /device:TPU:0, one launch (start us, length us, event | category | flops | bytes accessed | tf_op | source)
XLA Modules:
  0.0 732.5 jit_solution(6035988580196298325)
XLA Ops:
  5.5 132.8 %gather_weights.1 = (bf16[576,1024]{1,0:T(8,128)(2,1)}, bf16[3,1024,1024]{2,1,0:T(8,128)(2,1)}, bf16[1024,1024]{1,0:T(8,128)(2,1)}, bf16[1024,4096]{1,0:T(8,128)...) custom-call(bf16[2,256,1024]{2,1,0:T(8,128)(2,1)} %refs_0_.1, ...), custom_call_target="tpu_custom_call" | custom-call | tf_op jit(solution)/shard_map/gather_weights/pallas_call | solution.py:585
  142.5 9.7 %project_heads.1.qkv_ref = bf16[3,576,1024]{2,1,0:T(8,128)(2,1)S(1)} custom-call(bf16[576,1024]{1,0:T(8,128)(2,1)S(1)} %fusion.30.x_ref, bf16[3,1024,1024]{2,1,0:T(8,128)(2,1)S(1)} %bitcast.181, f32[3,1,1024]{2,1,0:T(1,128)S(1)} %broadcast_in_dim.40.b_ref, f32[3,576,128]{2,1,0:T(8,128)S(1)} %maximum_maximum_fusion.1.c_ref, ...), custom_call_target="tpu_custom_call" | custom-call | flops 3623878656 | bytes 6291456 | tf_op jit(solution)/shard_map/project_heads/pallas_call | solution.py:66
  157.6 6.0 collective-permute-start.13
  163.5 7.0 collective-permute-start.14
  179.2 2.8 fusion.152
  183.0 27.4 %attend_forward.1 = bf16[576,1024]{1,0:T(8,128)(2,1)S(1)} custom-call(bf16[3,576,1024]{2,1,0:T(8,128)(2,1)S(1)} %project_heads.1.qkv_ref, bf16[2,512,1024]{2,1,0:T(8,128)(2,1)} %collective-permute-done.far_ref, s32[512,1]{1,0:T(8,128)S(1)} %copy-done.15, s32[1,512]{1,0:T(1,128)S(1)} %bitcast.172, s32[1,512]{1,0:T(1,128)S(1)} %bitcast.176), custom_call_target="tpu_custom_call" | custom-call | flops 19327352832 | bytes 6815744 | tf_op jit(solution)/shard_map/attend_forward/pallas_call | solution.py:130
  212.9 30.4 %multiply_convert_fusion = (bf16[576,4096]{1,0:T(8,128)(2,1)S(1)}, f32[576,4096]{1,0:T(8,128)}, f32[576,4096]{1,0:T(8,128)}) fusion(f32[4096]{0:T(1024)S(1)} %pad_maximum_fusion.26, bf16[576,1024]{1,0:T(8,128)(2,1)S(1)} %fusion.27, bf16[1024,4096]{1,0:T(8,128)(2,1)} %get-tuple-element.67), kind=kOutput, calls=%fused_computation.4 | convolution fusion | flops 4987551744 | bytes 33177600 | tf_op jit(solution)/shard_map/dot_general | solution.py:38
  243.4 5.4 fusion.223
  295.9 5.9 collective-permute-start.1
  312.0 2.9 multiply_convert_fusion.1
  316.8 3.7 collective-permute-done.15
  326.1 3.1 collective-permute-start.17
  337.7 2.6 multiply_reduce_fusion
  342.1 17.7 %convert_reduce_fusion = (f32[4096]{0:T(1024)}, bf16[576,4096]{1,0:T(8,128)(2,1)}) fusion(f32[576,4096]{1,0:T(8,128)} %get-tuple-element.201, f32[576,4096]{1,0:T(8,128)} %get-tuple-element.315, f32[4096]{0:T(1024)S(1)} %copy-done.120, bf16[576,1024]{1,0:T(8,128)(2,1)S(1)} %get-tuple-element.181, bf16[4096,1024]{1,0:T(8,128)(2,1)} %get-tuple-element.68), kind=kOutput, calls=%fused_computation.2 | convolution fusion | flops 4871942144 | bytes 33193984 | tf_op jit(solution)/shard_map/dot_general | solution.py:42
  359.8 7.6 %convolution_convert_fusion = bf16[512,4096]{1,0:T(8,128)(2,1)} fusion(bf16[576,4096]{1,0:T(8,128)(2,1)} %get-tuple-element.187, bf16[576,1024]{1,0:T(8,128)(2,1)S(1)} %copy-done.47), kind=kOutput, calls=%fused_computation.20 | convolution fusion | flops 2418016256 | bytes 9502720 | tf_op jit(solution)/shard_map/dot_general | solution.py:46
  367.4 10.5 %multiply_reduce_fusion.1 = (f32[1024]{0:T(1024)}, f32[576]{0:T(1024)S(1)}, f32[1024]{0:T(1024)}, f32[576,1024]{1,0:T(8,128)S(1)}) fusion(f32[576,1024]{1,0:T(8,128)S(1)} %copy-done.31, f32[576]{0:T(1024)S(1)} %copy-done.104, f32[576]{0:T(1024)S(1)} %broadcast_multiply_fusion.2, f32[1024]{0:T(1024)S(1)} %bitcast.193, ...), kind=kOutput, calls=%fused_computation.39 | convolution fusion | flops 4837733888 | bytes 20206592 | tf_op jit(solution)/shard_map/dot_general | solution.py:42
  377.9 5.6 convolution_convert_fusion.1
  388.9 2.8 fusion.6
  411.0 2.5 convolution_convert_fusion.3.g_ref
  417.9 3.8 collective-permute-done.68
  422.4 2.9 convert_add_fusion.3
  426.3 6.8 convert_add_fusion
  433.1 3.4 copy-done.29
  438.1 5.5 fusion.224
  446.2 35.1 %attend_backward.3 = (bf16[576,512]{1,0:T(8,128)(2,1)S(1)}, f32[2,576,512]{2,1,0:T(8,128)S(1)}, bf16[2,512,512]{2,1,0:T(8,128)(2,1)S(1)}) custom-call(bf16[3,576,1024]{2,1,0:T(8,128)(2,1)S(1)} %project_heads.1.qkv_ref, bf16[2,512,1024]{2,1,0:T(8,128)(2,1)} %collective-permute-done.far_ref, bf16[576,1024]{1,0:T(8,128)(2,1)S(1)} %copy-done.27, ...), custom_call_target="tpu_custom_call" | custom-call | flops 30198988800 | bytes 11272192 | tf_op jit(solution)/shard_map/attend_backward/pallas_call | solution.py:236
  487.2 2.6 convolution_convert_fusion.2
  490.8 39.3 %collective-permute-done.22 = bf16[256,4096]{1,0:T(8,128)(2,1)} collective-permute-done((bf16[256,4096]{1,0:T(8,128)(2,1)}, bf16[256,4096]{1,0:T(8,128)(2,1)}, u32[]{:S(2)}, u32[]{:S(2)}) %collective-permute-start.22) | collective-permute-done | bytes 2097184 | tf_op jit(solution)/shard_map/ppermute | solution.py:645
  530.0 3.7 slice_add_fusion
  535.7 2.5 maximum_add_fusion
  542.0 18.0 %attend_backward.4 = (bf16[576,256]{1,0:T(8,128)(2,1)S(1)}, f32[2,576,256]{2,1,0:T(8,128)S(1)}, bf16[2,512,256]{2,1,0:T(8,128)(2,1)S(1)}) custom-call(bf16[3,576,1024]{2,1,0:T(8,128)(2,1)S(1)} %project_heads.1.qkv_ref, bf16[2,512,1024]{2,1,0:T(8,128)(2,1)} %collective-permute-done.far_ref, bf16[576,1024]{1,0:T(8,128)(2,1)S(1)} %copy-done.28, ...), custom_call_target="tpu_custom_call" | custom-call | flops 15099494400 | bytes 5636096 | tf_op jit(solution)/shard_map/attend_backward/pallas_call | solution.py:236
  560.3 3.0 convert_add_fusion.2
  568.5 2.9 fusion.199
  572.3 3.5 collective-permute-done.24
  582.6 18.5 %attend_backward.5 = (bf16[576,256]{1,0:T(8,128)(2,1)S(1)}, f32[2,576,256]{2,1,0:T(8,128)S(1)}, bf16[2,512,256]{2,1,0:T(8,128)(2,1)S(1)}) custom-call(bf16[3,576,1024]{2,1,0:T(8,128)(2,1)S(1)} %copy-done.3, bf16[2,512,1024]{2,1,0:T(8,128)(2,1)} %collective-permute-done.far_ref, bf16[576,1024]{1,0:T(8,128)(2,1)S(1)} %copy-done.28, f32[576,128]{1,0:T(8,128)S(1)} %copy-done.12, ...), custom_call_target="tpu_custom_call" | custom-call | flops 15099494400 | bytes 5636096 | tf_op jit(solution)/shard_map/attend_backward/pallas_call | solution.py:236
  601.1 4.4 fusion.16
  611.3 5.0 collective-permute-done.49
  621.1 4.4 collective-permute-done.59
  625.5 5.7 collective-permute-start.51
  642.9 4.7 fusion.12
  648.4 6.7 fusion.32
  656.0 2.5 collective-permute-start.45
  658.5 2.8 convolution_convert_fusion.5
  678.6 3.1 collective-permute-done.38
  683.0 22.8 %collective-permute-done.32 = bf16[288,1024]{1,0:T(8,128)(2,1)S(1)} collective-permute-done((bf16[288,1024]{1,0:T(8,128)(2,1)}, bf16[288,1024]{1,0:T(8,128)(2,1)S(1)}, u32[]{:S(2)}, u32[]{:S(2)}) %collective-permute-start.32) | collective-permute-done | bytes 589856 | tf_op jit(solution)/shard_map/ppermute | solution.py:706
  711.8 6.2 collective-permute-done.41
  719.4 4.5 collective-permute-done.42
  724.1 2.8 collective-permute-done.35
  726.9 4.6 collective-permute-done.43
  (648 shorter events, 208.6 us)
Async XLA Ops:
  153.9 28.2 %collective-permute-start = (bf16[2,512,1024]{2,1,0:T(8,128)(2,1)}, bf16[2,512,1024]{2,1,0:T(8,128)(2,1)}, u32[]{:S(2)}, u32[]{:S(2)}) collective-permute-start(bf16[2,512,1024]{2,1,0:T(8,128)(2,1)} %slice.722), channel_id=1, source_target_pairs={{0,4},{1,5},{2,6},{3,7},{4,0},{5,1},{6,2},{7,3},{8,12},{9,13},{10,... | collective-permute-start | bytes 6291464 | tf_op jit(solution)/shard_map/ppermute | solution.py:645
  157.6 118.8 %collective-permute-start.13 = (bf16[288,1024]{1,0:T(8,128)(2,1)}, bf16[288,1024]{1,0:T(8,128)(2,1)}, u32[]{:S(2)}, u32[]{:S(2)}) collective-permute-start(bf16[288,1024]{1,0:T(8,128)(2,1)} %get-tuple-element.228), channel_id=1, source_target_pairs={{0,0},{1,2},{2,4},{3,6},{4,1},{5,3},{6,5},{7,7},{8,8},{9,10},{10,1... | collective-permute-start | bytes 1769480 | tf_op jit(solution)/shard_map/ppermute | solution.py:685
  163.5 112.8 %collective-permute-start.14 = (bf16[288,1024]{1,0:T(8,128)(2,1)}, bf16[288,1024]{1,0:T(8,128)(2,1)}, u32[]{:S(2)}, u32[]{:S(2)}) collective-permute-start(bf16[288,1024]{1,0:T(8,128)(2,1)} %get-tuple-element.229), channel_id=1, source_target_pairs={{0,2},{1,0},{2,6},{3,4},{4,3},{5,1},{6,7},{7,5},{8,10},{9,8},{10,1... | collective-permute-start | bytes 1769480 | tf_op jit(solution)/shard_map/ppermute | solution.py:685
  261.2 9.4 %collective-permute-start.4 = (bf16[128,128]{1,0:T(8,128)(2,1)}, bf16[128,128]{1,0:T(8,128)(2,1)}, u32[]{:S(2)}, u32[]{:S(2)}) collective-permute-start(bf16[128,128]{1,0:T(8,128)(2,1)} %pad_maximum_fusion.22), channel_id=1, source_target_pairs={{0,1},{1,0},{2,3},{3,2},{4,5},{5,4},{6,7},{7,6},{8,9},{9,8},{10,11... | collective-permute-start | bytes 98312 | tf_op jit(solution)/shard_map/ppermute | solution.py:645
  293.2 8.8 %collective-permute-start.10 = (f32[16,1024]{1,0:T(8,128)S(1)}, f32[16,1024]{1,0:T(8,128)S(1)}, u32[]{:S(2)}, u32[]{:S(2)}) collective-permute-start(f32[16,1024]{1,0:T(8,128)S(1)} %pad_maximum_fusion.21), channel_id=1, source_target_pairs={{0,16},{1,17},{2,18},{3,19},{4,20},{5,21},{6,22},{7,23},{8,24},{9,... | collective-permute-start | bytes 196616 | tf_op jit(solution)/shard_map/ppermute | solution.py:645
  295.9 37.4 %collective-permute-start.1 = (bf16[288,1024]{1,0:T(8,128)(2,1)}, bf16[288,1024]{1,0:T(8,128)(2,1)}, u32[]{:S(2)}, u32[]{:S(2)}) collective-permute-start(bf16[288,1024]{1,0:T(8,128)(2,1)} %get-tuple-element.233), channel_id=1, source_target_pairs={{0,0},{1,4},{2,1},{3,5},{4,2},{5,6},{6,3},{7,7},{8,8},{9,12},{10,9... | collective-permute-start | bytes 1769480 | tf_op jit(solution)/shard_map/ppermute | solution.py:706
  301.9 31.5 %collective-permute-start.2 = (bf16[288,1024]{1,0:T(8,128)(2,1)}, bf16[288,1024]{1,0:T(8,128)(2,1)}, u32[]{:S(2)}, u32[]{:S(2)}) collective-permute-start(bf16[288,1024]{1,0:T(8,128)(2,1)} %get-tuple-element.232), channel_id=1, source_target_pairs={{0,1},{1,5},{2,0},{3,4},{4,3},{5,7},{6,2},{7,6},{8,9},{9,13},{10,8... | collective-permute-start | bytes 1769480 | tf_op jit(solution)/shard_map/ppermute | solution.py:706
  320.6 5.5 collective-permute-start.16
  324.0 5.2 collective-permute-start.12
  377.8 48.4 %collective-permute-start.20 = (bf16[512,4096]{1,0:T(8,128)(2,1)}, bf16[512,4096]{1,0:T(8,128)(2,1)}, u32[]{:S(2)}, u32[]{:S(2)}) collective-permute-start(bf16[512,4096]{1,0:T(8,128)(2,1)} %convolution_convert_fusion), channel_id=1, source_target_pairs={{0,4},{1,5},{2,6},{3,7},{4,0},{5,1},{6,2},{7,3},{8,12},{9,13},{10,... | collective-permute-start | bytes 12582920 | tf_op jit(solution)/shard_map/ppermute | solution.py:645
  383.4 54.7 %collective-permute-start.19 = (bf16[4096,512]{0,1:T(8,128)(2,1)}, bf16[4096,512]{0,1:T(8,128)(2,1)}, u32[]{:S(2)}, u32[]{:S(2)}) collective-permute-start(bf16[4096,512]{0,1:T(8,128)(2,1)} %convolution_convert_fusion.1), channel_id=1, source_target_pairs={{0,4},{1,5},{2,6},{3,7},{4,0},{5,1},{6,2},{7,3},{8,12},{9,13},{10,... | collective-permute-start | bytes 12582920 | tf_op jit(solution)/shard_map/ppermute | solution.py:645
  391.7 5.2 collective-permute-start.53
  395.1 5.7 collective-permute-start.64
  403.8 18.5 %collective-permute-start.23 = (bf16[1024,512]{1,0:T(8,128)(2,1)}, bf16[1024,512]{1,0:T(8,128)(2,1)}, u32[]{:S(2)}, u32[]{:S(2)}) collective-permute-start(bf16[1024,512]{1,0:T(8,128)(2,1)} %convolution_convert_fusion.4), channel_id=1, source_target_pairs={{0,4},{1,5},{2,6},{3,7},{4,0},{5,1},{6,2},{7,3},{8,12},{9,13},{10,... | collective-permute-start | bytes 3145736 | tf_op jit(solution)/shard_map/ppermute | solution.py:645
  408.8 6.0 collective-permute-start.57
  416.5 5.2 collective-permute-start.68
  481.6 48.4 %collective-permute-start.22 = (bf16[256,4096]{1,0:T(8,128)(2,1)}, bf16[256,4096]{1,0:T(8,128)(2,1)}, u32[]{:S(2)}, u32[]{:S(2)}) collective-permute-start(bf16[256,4096]{1,0:T(8,128)(2,1)} %slice.1071), channel_id=1, source_target_pairs={{0,16},{1,17},{2,18},{3,19},{4,20},{5,21},{6,22},{7,23},{8,24},{9,... | collective-permute-start | bytes 6291464 | tf_op jit(solution)/shard_map/ppermute | solution.py:645
  482.6 52.3 %collective-permute-start.21 = (bf16[4096,256]{0,1:T(8,128)(2,1)}, bf16[4096,256]{0,1:T(8,128)(2,1)}, u32[]{:S(2)}, u32[]{:S(2)}) collective-permute-start(bf16[4096,256]{0,1:T(8,128)(2,1)} %pad_maximum_fusion), channel_id=1, source_target_pairs={{0,8},{1,9},{2,10},{3,11},{4,12},{5,13},{6,14},{7,15},{8,0},{9,1},... | collective-permute-start | bytes 6291464 | tf_op jit(solution)/shard_map/ppermute | solution.py:645
  489.8 70.5 %collective-permute-start.28 = (bf16[512,1536]{1,0:T(8,128)(2,1)}, bf16[512,1536]{1,0:T(8,128)(2,1)}, u32[]{:S(2)}, u32[]{:S(2)}) collective-permute-start(bf16[512,1536]{1,0:T(8,128)(2,1)} %convolution_convert_fusion.2), channel_id=1, source_target_pairs={{0,4},{1,5},{2,6},{3,7},{4,0},{5,1},{6,2},{7,3},{8,12},{9,13},{10,... | collective-permute-start | bytes 4718600 | tf_op jit(solution)/shard_map/ppermute | solution.py:645
  539.4 25.0 %collective-permute-start.26 = (bf16[1024,256]{1,0:T(8,128)(2,1)}, bf16[1024,256]{1,0:T(8,128)(2,1)S(1)}, u32[]{:S(2)}, u32[]{:S(2)}) collective-permute-start(bf16[1024,256]{1,0:T(8,128)(2,1)} %slice.1075), channel_id=1, source_target_pairs={{0,16},{1,17},{2,18},{3,19},{4,20},{5,21},{6,22},{7,23},{8,24},{9,... | collective-permute-start | bytes 1572872 | tf_op jit(solution)/shard_map/ppermute | solution.py:645
  540.3 28.2 %collective-permute-start.25 = (bf16[128,4096]{1,0:T(8,128)(2,1)}, bf16[128,4096]{1,0:T(8,128)(2,1)}, u32[]{:S(2)}, u32[]{:S(2)}) collective-permute-start(bf16[128,4096]{1,0:T(8,128)(2,1)} %slice.1072), channel_id=1, source_target_pairs={{0,8},{1,9},{2,10},{3,11},{4,12},{5,13},{6,14},{7,15},{8,0},{9,1},... | collective-permute-start | bytes 3145736 | tf_op jit(solution)/shard_map/ppermute | solution.py:645
  540.9 34.9 %collective-permute-start.24 = (bf16[4096,128]{0,1:T(8,128)(2,1)}, bf16[4096,128]{0,1:T(8,128)(2,1)}, u32[]{:S(2)}, u32[]{:S(2)}) collective-permute-start(bf16[4096,128]{0,1:T(8,128)(2,1)} %slice.1073), channel_id=1, source_target_pairs={{0,16},{1,17},{2,18},{3,19},{4,20},{5,21},{6,22},{7,23},{8,24},{9,... | collective-permute-start | bytes 3145736 | tf_op jit(solution)/shard_map/ppermute | solution.py:645
  568.0 65.4 %collective-permute-start.36 = (bf16[512,768]{1,0:T(8,128)(2,1)}, bf16[512,768]{1,0:T(8,128)(2,1)}, u32[]{:S(2)}, u32[]{:S(2)}) collective-permute-start(bf16[512,768]{1,0:T(8,128)(2,1)} %convolution_convert_fusion.6), channel_id=1, source_target_pairs={{0,4},{1,5},{2,6},{3,7},{4,0},{5,1},{6,2},{7,3},{8,12},{9,13},{10,... | collective-permute-start | bytes 2359304 | tf_op jit(solution)/shard_map/ppermute | solution.py:645
  577.4 28.8 %collective-permute-start.61 = (bf16[1024,128]{0,1:T(8,128)(2,1)S(1)}, bf16[1024,128]{0,1:T(8,128)(2,1)S(1)}, u32[]{:S(2)}, u32[]{:S(2)}) collective-permute-start(bf16[1024,128]{0,1:T(8,128)(2,1)S(1)} %get-tuple-element.93), channel_id=1, source_target_pairs={{0,1},{1,0},{2,3},{3,2},{4,5},{5,4},{6,7},{7,6},{8,9},{9,8},{10,11... | collective-permute-start | bytes 786440 | tf_op jit(solution)/shard_map/ppermute | solution.py:645
  579.1 29.3 %collective-permute-start.62 = (bf16[1024,128]{0,1:T(8,128)(2,1)S(1)}, bf16[1024,128]{0,1:T(8,128)(2,1)S(1)}, u32[]{:S(2)}, u32[]{:S(2)}) collective-permute-start(bf16[1024,128]{0,1:T(8,128)(2,1)S(1)} %get-tuple-element.94), channel_id=1, source_target_pairs={{0,2},{1,3},{2,0},{3,1},{4,6},{5,7},{6,4},{7,5},{8,10},{9,11},{10,... | collective-permute-start | bytes 786440 | tf_op jit(solution)/shard_map/ppermute | solution.py:645
  580.4 29.5 %collective-permute-start.63 = (bf16[1024,128]{0,1:T(8,128)(2,1)S(1)}, bf16[1024,128]{0,1:T(8,128)(2,1)S(1)}, u32[]{:S(2)}, u32[]{:S(2)}) collective-permute-start(bf16[1024,128]{0,1:T(8,128)(2,1)S(1)} %get-tuple-element.95), channel_id=1, source_target_pairs={{0,3},{1,2},{2,1},{3,0},{4,7},{5,6},{6,5},{7,4},{8,11},{9,10},{10,... | collective-permute-start | bytes 786440 | tf_op jit(solution)/shard_map/ppermute | solution.py:645
  581.9 38.3 %collective-permute-start.58 = (bf16[128,1024]{1,0:T(8,128)(2,1)}, bf16[128,1024]{1,0:T(8,128)(2,1)}, u32[]{:S(2)}, u32[]{:S(2)}) collective-permute-start(bf16[128,1024]{1,0:T(8,128)(2,1)} %get-tuple-element.90), channel_id=1, source_target_pairs={{0,1},{1,0},{2,3},{3,2},{4,5},{5,4},{6,7},{7,6},{8,9},{9,8},{10,11... | collective-permute-start | bytes 786440 | tf_op jit(solution)/shard_map/ppermute | solution.py:645
  606.2 19.3 %collective-permute-start.59 = (bf16[128,1024]{1,0:T(8,128)(2,1)}, bf16[128,1024]{1,0:T(8,128)(2,1)}, u32[]{:S(2)}, u32[]{:S(2)}) collective-permute-start(bf16[128,1024]{1,0:T(8,128)(2,1)} %get-tuple-element.91), channel_id=1, source_target_pairs={{0,2},{1,3},{2,0},{3,1},{4,6},{5,7},{6,4},{7,5},{8,10},{9,11},{10,... | collective-permute-start | bytes 786440 | tf_op jit(solution)/shard_map/ppermute | solution.py:645
  608.4 17.1 %collective-permute-start.60 = (bf16[128,1024]{1,0:T(8,128)(2,1)}, bf16[128,1024]{1,0:T(8,128)(2,1)}, u32[]{:S(2)}, u32[]{:S(2)}) collective-permute-start(bf16[128,1024]{1,0:T(8,128)(2,1)} %get-tuple-element.92), channel_id=1, source_target_pairs={{0,3},{1,2},{2,1},{3,0},{4,7},{5,6},{6,5},{7,4},{8,11},{9,10},{10,... | collective-permute-start | bytes 786440 | tf_op jit(solution)/shard_map/ppermute | solution.py:645
  609.9 6.4 collective-permute-start.49
  616.3 25.1 %collective-permute-start.30 = (bf16[2,512,256]{2,1,0:T(8,128)(2,1)S(1)}, bf16[2,512,256]{2,1,0:T(8,128)(2,1)}, u32[]{:S(2)}, u32[]{:S(2)}) collective-permute-start(bf16[2,512,256]{2,1,0:T(8,128)(2,1)S(1)} %get-tuple-element.87), channel_id=1, source_target_pairs={{0,4},{1,5},{2,6},{3,7},{4,0},{5,1},{6,2},{7,3},{8,12},{9,13},{10,... | collective-permute-start | bytes 1572872 | tf_op jit(solution)/shard_map/ppermute | solution.py:645
  620.2 54.9 %collective-permute-start.33 = (bf16[256,1536]{1,0:T(8,128)(2,1)}, bf16[256,1536]{1,0:T(8,128)(2,1)}, u32[]{:S(2)}, u32[]{:S(2)}) collective-permute-start(bf16[256,1536]{1,0:T(8,128)(2,1)} %slice.1074), channel_id=1, source_target_pairs={{0,16},{1,17},{2,18},{3,19},{4,20},{5,21},{6,22},{7,23},{8,24},{9,... | collective-permute-start | bytes 2359304 | tf_op jit(solution)/shard_map/ppermute | solution.py:645
  625.5 13.8 %collective-permute-start.50 = (bf16[256,128]{1,0:T(8,128)(2,1)S(1)}, bf16[256,128]{1,0:T(8,128)(2,1)S(1)}, u32[]{:S(2)}, u32[]{:S(2)}) collective-permute-start(bf16[256,128]{1,0:T(8,128)(2,1)S(1)} %get-tuple-element.258), channel_id=1, source_target_pairs={{0,1},{1,0},{2,3},{3,2},{4,5},{5,4},{6,7},{7,6},{8,9},{9,8},{10,11... | collective-permute-start | bytes 196616 | tf_op jit(solution)/shard_map/ppermute | solution.py:645
  625.5 14.3 %collective-permute-start.51 = (bf16[256,128]{1,0:T(8,128)(2,1)S(1)}, bf16[256,128]{1,0:T(8,128)(2,1)S(1)}, u32[]{:S(2)}, u32[]{:S(2)}) collective-permute-start(bf16[256,128]{1,0:T(8,128)(2,1)S(1)} %get-tuple-element.260), channel_id=1, source_target_pairs={{0,2},{1,3},{2,0},{3,1},{4,6},{5,7},{6,4},{7,5},{8,10},{9,11},{10,... | collective-permute-start | bytes 196616 | tf_op jit(solution)/shard_map/ppermute | solution.py:645
  633.4 6.4 collective-permute-start.52
  639.3 33.7 %collective-permute-start.37 = (bf16[256,768]{1,0:T(8,128)(2,1)}, bf16[256,768]{1,0:T(8,128)(2,1)}, u32[]{:S(2)}, u32[]{:S(2)}) collective-permute-start(bf16[256,768]{1,0:T(8,128)(2,1)} %pad_maximum_fusion.6), channel_id=1, source_target_pairs={{0,8},{1,9},{2,10},{3,11},{4,12},{5,13},{6,14},{7,15},{8,0},{9,1},... | collective-permute-start | bytes 1179656 | tf_op jit(solution)/shard_map/ppermute | solution.py:645
  648.4 6.8 collective-permute-start.44
  656.0 5.3 collective-permute-start.45
  664.2 43.9 %collective-permute-start.40 = (bf16[512,768]{1,0:T(8,128)(2,1)}, bf16[512,768]{1,0:T(8,128)(2,1)}, u32[]{:S(2)}, u32[]{:S(2)}) collective-permute-start(bf16[512,768]{1,0:T(8,128)(2,1)} %convolution_convert_fusion.5), channel_id=1, source_target_pairs={{0,4},{1,5},{2,6},{3,7},{4,0},{5,1},{6,2},{7,3},{8,12},{9,13},{10,... | collective-permute-start | bytes 2359304 | tf_op jit(solution)/shard_map/ppermute | solution.py:645
  668.7 14.4 %collective-permute-start.31 = (bf16[288,1024]{1,0:T(8,128)(2,1)}, bf16[288,1024]{1,0:T(8,128)(2,1)S(1)}, u32[]{:S(2)}, u32[]{:S(2)}) collective-permute-start(bf16[288,1024]{1,0:T(8,128)(2,1)} %get-tuple-element.219), channel_id=1, source_target_pairs={{0,0},{1,4},{2,1},{3,5},{4,2},{5,6},{6,3},{7,7},{8,8},{9,12},{10,9... | collective-permute-start | bytes 1769480 | tf_op jit(solution)/shard_map/ppermute | solution.py:706
  670.4 35.4 %collective-permute-start.32 = (bf16[288,1024]{1,0:T(8,128)(2,1)}, bf16[288,1024]{1,0:T(8,128)(2,1)S(1)}, u32[]{:S(2)}, u32[]{:S(2)}) collective-permute-start(bf16[288,1024]{1,0:T(8,128)(2,1)} %get-tuple-element.218), channel_id=1, source_target_pairs={{0,1},{1,5},{2,0},{3,4},{4,3},{5,7},{6,2},{7,6},{8,9},{9,13},{10,8... | collective-permute-start | bytes 1769480 | tf_op jit(solution)/shard_map/ppermute | solution.py:706
  674.0 7.7 %collective-permute-start.38 = (bf16[128,768]{1,0:T(8,128)(2,1)S(1)}, bf16[128,768]{1,0:T(8,128)(2,1)S(1)}, u32[]{:S(2)}, u32[]{:S(2)}) collective-permute-start(bf16[128,768]{1,0:T(8,128)(2,1)S(1)} %slice.1079), channel_id=1, source_target_pairs={{0,16},{1,17},{2,18},{3,19},{4,20},{5,21},{6,22},{7,23},{8,24},{9,... | collective-permute-start | bytes 589832 | tf_op jit(solution)/shard_map/ppermute | solution.py:645
  677.0 34.6 %collective-permute-start.34 = (bf16[128,1536]{1,0:T(8,128)(2,1)S(1)}, bf16[128,1536]{1,0:T(8,128)(2,1)S(1)}, u32[]{:S(2)}, u32[]{:S(2)}) collective-permute-start(bf16[128,1536]{1,0:T(8,128)(2,1)S(1)} %slice.1076), channel_id=1, source_target_pairs={{0,8},{1,9},{2,10},{3,11},{4,12},{5,13},{6,14},{7,15},{8,0},{9,1},... | collective-permute-start | bytes 1179656 | tf_op jit(solution)/shard_map/ppermute | solution.py:645
  681.8 42.3 %collective-permute-start.39 = (bf16[3,128,256]{2,1,0:T(8,128)(2,1)S(1)}, bf16[3,128,256]{2,1,0:T(8,128)(2,1)S(1)}, u32[]{:S(2)}, u32[]{:S(2)}) collective-permute-start(bf16[3,128,256]{2,1,0:T(8,128)(2,1)S(1)} %pad_maximum_fusion.13), channel_id=1, source_target_pairs={{0,2},{1,3},{2,0},{3,1},{4,6},{5,7},{6,4},{7,5},{8,10},{9,11},{10,... | collective-permute-start | bytes 589832 | tf_op jit(solution)/shard_map/ppermute | solution.py:645
  710.2 7.8 %collective-permute-start.41 = (bf16[256,768]{1,0:T(8,128)(2,1)S(1)}, bf16[256,768]{1,0:T(8,128)(2,1)S(1)}, u32[]{:S(2)}, u32[]{:S(2)}) collective-permute-start(bf16[256,768]{1,0:T(8,128)(2,1)S(1)} %pad_maximum_fusion.7), channel_id=1, source_target_pairs={{0,8},{1,9},{2,10},{3,11},{4,12},{5,13},{6,14},{7,15},{8,0},{9,1},... | collective-permute-start | bytes 1179656 | tf_op jit(solution)/shard_map/ppermute | solution.py:645
  718.1 5.7 collective-permute-start.42
  719.3 7.6 %collective-permute-start.35 = (bf16[3,128,256]{2,1,0:T(8,128)(2,1)S(1)}, bf16[3,128,256]{2,1,0:T(8,128)(2,1)S(1)}, u32[]{:S(2)}, u32[]{:S(2)}) collective-permute-start(bf16[3,128,256]{2,1,0:T(8,128)(2,1)S(1)} %pad_maximum_fusion.12), channel_id=1, source_target_pairs={{0,1},{1,0},{2,3},{3,2},{4,5},{5,4},{6,7},{7,6},{8,9},{9,8},{10,11... | collective-permute-start | bytes 589832 | tf_op jit(solution)/shard_map/ppermute | solution.py:645
  724.0 7.5 %collective-permute-start.43 = (bf16[3,128,256]{2,1,0:T(8,128)(2,1)S(1)}, bf16[3,128,256]{2,1,0:T(8,128)(2,1)S(1)}, u32[]{:S(2)}, u32[]{:S(2)}) collective-permute-start(bf16[3,128,256]{2,1,0:T(8,128)(2,1)S(1)} %pad_maximum_fusion.14), channel_id=1, source_target_pairs={{0,3},{1,2},{2,1},{3,0},{4,7},{5,6},{6,5},{7,4},{8,11},{9,10},{10,... | collective-permute-start | bytes 589832 | tf_op jit(solution)/shard_map/ppermute | solution.py:645
  (166 other events, 2166.6 us)

commit v3 on v2

--- a/solution.py
+++ b/solution.py
@@ -599,6 +599,670 @@
         compiler_params=pltpu.CompilerParams(collective_id=0, has_side_effects=True),
         name="gather_weights",
     )(x_doc, x_query, *weights, proj, bias, picks)
+
+
+class Around:
+    def __init__(self):
+        self.rank = lax.axis_index("dp")
+        self.column = lax.axis_index("tensor")
+        self.core = self.rank % 2
+        self.base = self.rank - self.core
+
+    def other(self, bit):
+        rank = self.rank
+        return (rank + bit - 2 * bit * ((rank // bit) % 2), self.column)
+
+    def along(self, dt):
+        return (self.rank, differing(self.column, dt, 2))
+
+    def meet(self):
+        barrier = pltpu.get_barrier_semaphore()
+        for dc in range(2):
+            for dt in range(4):
+                if dc + dt > 0:
+                    pl.semaphore_signal(
+                        barrier,
+                        inc=1,
+                        device_id=(self.base + (self.core + dc) % 2, (self.column + dt) % 4),
+                        device_id_type=MESH,
+                    )
+        for bit in (2, 4):
+            pl.semaphore_signal(
+                barrier, inc=1, device_id=self.other(bit), device_id_type=MESH
+            )
+        pl.semaphore_wait(barrier, 9)
+
+
+class Sender:
+    def __init__(self, send_sem, recv_sem):
+        self.send_sem, self.recv_sem = send_sem, recv_sem
+        self.sent = []
+
+    def __call__(self, src, dst, to):
+        at = len(self.sent)
+        copy = pltpu.make_async_remote_copy(
+            src_ref=src,
+            dst_ref=dst,
+            send_sem=self.send_sem.at[at],
+            recv_sem=self.recv_sem.at[at],
+            device_id=to,
+            device_id_type=MESH,
+        )
+        self.sent.append(copy)
+        return copy
+
+    def drain(self):
+        for copy in self.sent:
+            copy.wait_send()
+
+
+class MatrixSum:
+    def __init__(
+        self, around, send, axis, across, own, got, next_, near, far, home, local_sems, pieces
+    ):
+        self.axis, self.own, self.got, self.next, self.near = axis, own, got, next_, near
+        self.block = own.shape[axis] // 4
+        first, second = (2, 4) if across else (4, 2)
+        self.gone, self.later = ((1, 3), 2) if across else ((2, 3), 1)
+        self.cores = [send(src, dst, around.other(1)) for src, dst in far]
+        self.loads = [
+            pltpu.make_async_copy(src, dst, sem) for (src, dst), sem in zip(home, local_sems)
+        ]
+        self.firsts = [
+            send(self.at(own, n), self.at(next_, slot), around.other(first))
+            for slot, n in enumerate(self.gone)
+        ]
+        self.second = send(self.at(own, self.later), near, around.other(second))
+        self.pieces = [send(own.at[index], dst, around.along(dt)) for dt, index, dst in pieces]
+
+    def at(self, ref, n):
+        span = pl.ds(n * self.block, self.block)
+        return ref.at[span, :] if self.axis == 0 else ref.at[:, span]
+
+    def begin(self):
+        for copy in self.cores + self.loads:
+            copy.start()
+
+    def add(self, n, ref, m):
+        rows = self.block if self.axis == 0 else self.own.shape[0]
+        step = 16 if self.axis == 0 else 128
+        block = self.block
+
+        @pl.loop(0, rows // step)
+        def _(k):
+            if self.axis == 0:
+                to = (pl.ds(pl.multiple_of(n * block + k * step, step), step), slice(None))
+                fr = (pl.ds(pl.multiple_of(m * block + k * step, step), step), slice(None))
+            else:
+                at = pl.ds(pl.multiple_of(k * step, step), step)
+                to, fr = (at, pl.ds(n * block, block)), (at, pl.ds(m * block, block))
+            self.own[to] = (self.own[to].astype(F32) + ref[fr].astype(F32)).astype(BF)
+
+    def first_axis(self):
+        for load in self.loads:
+            load.wait()
+        for copy in self.cores:
+            copy.wait_recv()
+        for n, copy in zip(self.gone, self.firsts):
+            self.add(n, self.got, n)
+            copy.start()
+        for n in (self.later, 0):
+            self.add(n, self.got, n)
+
+    def second_axis(self):
+        for copy in self.firsts:
+            copy.wait_recv()
+        self.add(self.later, self.next, 1)
+        self.second.start()
+        self.add(0, self.next, 0)
+
+    def tensor(self):
+        self.second.wait_recv()
+        self.add(0, self.near, 0)
+        for copy in self.pieces:
+            copy.start()
+
+    def settle(self):
+        for copy in self.pieces:
+            copy.wait_recv()
+
+
+class SmallSum:
+    def __init__(self, around, send, got, run, bits=(1, 4, 2), tensor=(1, 2)):
+        self.got, self.run = got, run
+        tos = [around.other(bit) for bit in bits] + [around.along(dt) for dt in tensor]
+        self.copies = [send(run.at[n], got.at[n], to) for n, to in enumerate(tos)]
+
+    def begin(self, value):
+        self.run[0] = value
+        self.copies[0].start()
+
+    def hop(self, n):
+        self.copies[n].wait_recv()
+        self.run[n + 1] = self.run[n] + self.got[n]
+        if n + 1 < len(self.copies):
+            self.copies[n + 1].start()
+
+
+class ProjSum:
+    def __init__(self, around, send, ref, run, got):
+        self.ref, self.run, self.got = ref, run, got
+        rows = ref.shape[0]
+        self.half = [rows // 2, rows // 4, rows // 8]
+        starts = [0, rows // 2, 3 * rows // 4]
+        self.starts = starts
+        self.copies = [
+            send(ref.at[self.half[0] :, :], got.at[pl.ds(starts[0], self.half[0]), :], around.other(1))
+        ]
+        for n, bit in ((1, 4), (2, 2)):
+            self.copies.append(
+                send(
+                    run.at[pl.ds(self.half[n], self.half[n]), :],
+                    got.at[pl.ds(starts[n], self.half[n]), :],
+                    around.other(bit),
+                )
+            )
+        last = self.half[2]
+        self.last = last
+        base = rows
+        for n, dt in ((0, 1), (1, 2)):
+            self.copies.append(
+                send(
+                    run.at[pl.ds(rows // 2 + n * last, last), :],
+                    got.at[pl.ds(base + n * last, last), :],
+                    around.along(dt),
+                )
+            )
+
+    def begin(self):
+        self.copies[0].start()
+
+    def hop(self, n):
+        self.copies[n].wait_recv()
+        rows = self.ref.shape[0]
+        last = self.last
+        if n < 3:
+            size = self.half[n]
+            old = self.ref if n == 0 else self.run
+            total = old[:size, :] + self.got[pl.ds(self.starts[n], size), :]
+            if n < 2:
+                self.run[:size, :] = total
+            else:
+                self.run[pl.ds(rows // 2, last), :] = total
+        else:
+            at = rows // 2 + (n - 3) * last
+            got = self.got[pl.ds(rows + (n - 3) * last, last), :]
+            self.run[pl.ds(at + last, last), :] = self.run[pl.ds(at, last), :] + got
+        if n + 1 < len(self.copies):
+            self.copies[n + 1].start()
+
+    def result(self):
+        return self.run[pl.ds(self.ref.shape[0] // 2 + 2 * self.last, self.last), :]
+
+
+def finish_kernel(qkv, out, rows, tensor_sums):
+    ways = 4
+    width = qkv.shape[0]
+    half, block = width // 2, width // 8
+    share = width // ways
+    docs = rows.shape[0] // 9 * 8
+    quarter, asked = docs // 2, (rows.shape[0] - docs) // 2
+    chunk = 16
+    parts = 4
+    part = 3 * share
+
+    def kernel(
+        qkv_ref, out_ref, rows_ref, ten_ref,
+        qkv_o, out_o, doc_o, ask_o, ten_o,
+        qa, q0, q1, q2, q3, oa, o0, o1, o2, o3, gd, ga, t_got, t_run, tz,
+        send_sem, recv_sem, local_sem, row_send, row_recv,
+    ):
+        around = Around()
+        rank, column, core, base = around.rank, around.column, around.core, around.base
+        around.meet()
+        send = Sender(send_sem, recv_sem)
+        small = SmallSum(around, send, t_got, t_run, tensor=())
+        spread = [send(t_run.at[3, dt], tz.at[dt - 1], around.along(dt)) for dt in range(1, ways)]
+        across = (True, False, False, True)
+        heads, feats = [], []
+        for n in range(parts):
+            spans = [(pl.ds(j * width + n * share, share), pl.ds(j * share, share)) for j in range(3)]
+            heads.append(
+                MatrixSum(
+                    around, send, 0, across[n], qa.at[n], q0.at[n], q1.at[n], q2.at[n],
+                    [(qkv_ref.at[half:, fr], q0.at[n, :, to]) for fr, to in spans],
+                    [(qkv_ref.at[:half, fr], qa.at[n, :, to]) for fr, to in spans],
+                    [local_sem.at[3 * n + j] for j in range(3)],
+                    [
+                        (n, (slice(0, block), pl.ds(j * share, share)), q3.at[n - 1, j])
+                        for j in range(3)
+                        if n > 0
+                    ],
+                )
+            )
+        for n in range(2):
+            span = pl.ds(n * half, half)
+            feats.append(
+                MatrixSum(
+                    around, send, 1, n == 0, oa.at[n], o0.at[n], o1.at[n], o2.at[n],
+                    [(out_ref.at[span, half:], o0.at[n])],
+                    [(out_ref.at[span, :half], oa.at[n])],
+                    [local_sem.at[3 * parts + n]],
+                    [
+                        (dt, (pl.ds((dt % 2) * share, share), slice(0, block)), o3.at[dt - 1])
+                        for dt in (2 * n, 2 * n + 1)
+                        if dt > 0
+                    ],
+                )
+            )
+        items = [heads[2], heads[3], feats[1], heads[0], heads[1], feats[0]]
+        small.begin(ten_ref[...])
+        for item in items:
+            item.begin()
+
+        lonely = 3 * core == column
+        row_copies = []
+        for q in range(2):
+            own = jnp.logical_and(lonely, core == q)
+            for kind, (begin, size, buf) in enumerate(((0, quarter, gd), (docs, asked, ga))):
+                src = rows_ref.at[pl.ds(begin + q * size, size), :]
+                dst = buf.at[column // 2]
+                away = pltpu.make_async_remote_copy(
+                    src_ref=src,
+                    dst_ref=dst,
+                    send_sem=row_send.at[q, kind],
+                    recv_sem=row_recv.at[column // 2, kind],
+                    device_id=(base + column % 2, 2 * core + q),
+                    device_id_type=MESH,
+                )
+                here = pltpu.make_async_copy(src, dst, row_send.at[q, kind])
+
+                @pl.when(own)
+                def _():
+                    here.start()
+
+                @pl.when(jnp.logical_not(own))
+                def _():
+                    away.start()
+
+                row_copies.append((own, here, away))
+
+        for n in range(0, len(items) + 4, 2):
+            for item in items[n - 2 : n] if n >= 2 else []:
+                item.second_axis()
+            for item in items[n : n + 2]:
+                item.first_axis()
+            if n // 2 < 3:
+                small.hop(n // 2)
+            if n // 2 == 2:
+                for copy in spread:
+                    copy.start()
+            for m in (n - 4, n - 3):
+                if 0 <= m < len(items):
+                    items[m].tensor()
+
+        for m in range(2):
+            own = jnp.logical_and(lonely, column // 2 == m)
+            for kind, buf in enumerate((gd, ga)):
+                copy = pltpu.make_async_remote_copy(
+                    src_ref=buf.at[m],
+                    dst_ref=buf.at[m],
+                    send_sem=row_send.at[m, kind],
+                    recv_sem=row_recv.at[m, kind],
+                    device_id=(rank, column),
+                    device_id_type=MESH,
+                )
+
+                @pl.when(jnp.logical_not(own))
+                def _():
+                    copy.wait_recv()
+
+        for own, here, away in row_copies:
+
+            @pl.when(own)
+            def _():
+                here.wait()
+
+            @pl.when(jnp.logical_not(own))
+            def _():
+                away.wait_send()
+
+        for m in range(2):
+
+            @pl.loop(0, quarter // chunk)
+            def _(n):
+                at = pl.ds(pl.multiple_of(n * chunk, chunk), chunk)
+                doc_o[m, at, :] = gd[m, at, :].astype(F32)
+
+        ask_o[...] = ga[...].astype(F32)
+        for copy in spread:
+            copy.wait_recv()
+        ten_o[...] = t_run[3, 0] + tz[0] + tz[1] + tz[2]
+        for item in items:
+            item.settle()
+        for j in range(3):
+            total = qa[0, :block, pl.ds(j * share, share)].astype(F32)
+            for dt in range(ways - 1):
+                total = total + q3[dt, j].astype(F32)
+            qkv_o[j] = total
+        total = oa[0, :share, :block].astype(F32)
+        for dt in range(ways - 1):
+            total = total + o3[dt].astype(F32)
+        out_o[...] = total
+        send.drain()
+
+    def whole(x):
+        return pl.BlockSpec(x.shape, lambda: (0,) * len(x.shape))
+
+    out_shape = [
+        jax.ShapeDtypeStruct((3, block, share), F32),
+        jax.ShapeDtypeStruct((share, block), F32),
+        jax.ShapeDtypeStruct((2, quarter, width), F32),
+        jax.ShapeDtypeStruct((2, asked, width), F32),
+        jax.ShapeDtypeStruct(tensor_sums.shape[1:], F32),
+    ]
+    anywhere = pl.BlockSpec(memory_space=pl.ANY)
+    vmem = pltpu.VMEM
+    dma = pltpu.SemaphoreType.DMA
+    count = 6 + parts * 6 + 9 + 2 * 4 + 3
+    return pl.pallas_call(
+        kernel,
+        out_shape=out_shape,
+        in_specs=[anywhere] * 3 + [whole(tensor_sums)],
+        out_specs=[whole(x) for x in out_shape],
+        scratch_shapes=[
+            vmem((parts, half, part), BF),
+            vmem((parts, half, part), BF),
+            vmem((parts, 2 * block, part), BF),
+            vmem((parts, block, part), BF),
+            vmem((ways - 1, 3, block, share), BF),
+            vmem((2, half, half), BF),
+            vmem((2, half, half), BF),
+            vmem((2, half, 2 * block), BF),
+            vmem((2, half, block), BF),
+            vmem((ways - 1, share, block), BF),
+            vmem((2, quarter, width), BF),
+            vmem((2, asked, width), BF),
+            vmem((3,) + tensor_sums.shape, F32),
+            vmem((4,) + tensor_sums.shape, F32),
+            vmem((ways - 1,) + tensor_sums.shape[1:], F32),
+            dma((count,)),
+            dma((count,)),
+            dma((3 * parts + 2,)),
+            dma((2, 2)),
+            dma((2, 2)),
+        ],
+        compiler_params=pltpu.CompilerParams(
+            collective_id=1, has_side_effects=True, vmem_limit_bytes=48 << 20
+        ),
+        name="last_sums",
+    )(qkv, out, rows, tensor_sums)
+
+
+def attention_backward_kernel(
+    qkv, far_kv, grad, cosine, sine, far_cosine, far_sine, col_labels, own_labels, far_labels,
+    up, back, vectors, proj,
+):
+    rows, width = qkv.shape[1:]
+    docs = far_kv.shape[1]
+    pairs = width // 128
+    block = 128
+    asked = rows - docs
+    ways = 4
+    half, own_block = width // 2, width // 8
+    share = up.shape[1] // ways
+    assert pairs == 8
+
+    def kernel(
+        qkv_ref, far_ref, g_ref, c_ref, s_ref, fc_ref, fs_ref, lc_ref, lo_ref, lf_ref,
+        up_ref, back_ref, vec_ref, proj_ref,
+        pre_ref, bias_ref, up_o, back_o, vec_o, proj_o,
+        sums_own, sums_far, give, kept, got_kv,
+        ua, u0, u1, u2, u3, ba, b0, b1, b2, b3, v_got, v_run, p_run, p_got,
+        send_sem, recv_sem, local_sem,
+    ):
+        h = pl.program_id(0)
+        around = Around()
+        send = Sender(send_sem, recv_sem)
+        ups, backs = [], []
+        for n in range(ways):
+            span = pl.ds(n * share, share)
+            ups.append(
+                MatrixSum(
+                    around, send, 0, False, ua.at[n], u0.at[n], u1.at[n], u2.at[n],
+                    [(up_ref.at[half:, span], u0.at[n])],
+                    [(up_ref.at[:half, span], ua.at[n])],
+                    [local_sem.at[n]],
+                    [(n, (slice(0, own_block), slice(None)), u3.at[n - 1])] if n > 0 else [],
+                )
+            )
+            backs.append(
+                MatrixSum(
+                    around, send, 1, True, ba.at[n], b0.at[n], b1.at[n], b2.at[n],
+                    [(back_ref.at[span, half:], b0.at[n])],
+                    [(back_ref.at[span, :half], ba.at[n])],
+                    [local_sem.at[ways + n]],
+                    [(n, (slice(None), slice(0, own_block)), b3.at[n - 1])] if n > 0 else [],
+                )
+            )
+        couples = [(ups[n], backs[n]) for n in (2, 3, 1, 0)]
+        small = SmallSum(around, send, v_got, v_run)
+        mean_proj = ProjSum(around, send, proj_ref, p_run, p_got)
+        gives = [send(give.at[n], got_kv.at[n], around.other(1)) for n in range(pairs)]
+        lane = lax.broadcasted_iota(jnp.int32, (1, 128), 1)
+
+        def finish(n):
+            gives[n].wait_recv()
+            at = pl.ds(n * 128, 128)
+            for i in range(2):
+                low = (kept[n % 2, i, :docs, :] + got_kv[n, i].astype(F32)).astype(BF)
+                tail = kept[n % 2, i, docs:, :].astype(BF)
+                pre_ref[i + 1, :docs, at] = low
+                pre_ref[i + 1, docs:, at] = tail
+                total = jnp.sum(low.astype(F32), axis=0, keepdims=True)
+                total = total + jnp.sum(tail.astype(F32), axis=0, keepdims=True)
+                bias_ref[i + 1 : i + 2, at] = total
+
+        for step in range(pairs):
+
+            @pl.when(h == step)
+            def _(step=step):
+                if step == 0:
+                    around.meet()
+                    small.begin(vec_ref[...])
+                    mean_proj.begin()
+                    for couple in couples:
+                        for item in couple:
+                            item.begin()
+                else:
+                    if 0 <= step - 2 < 4:
+                        for item in couples[step - 2]:
+                            item.second_axis()
+                    if 0 <= step - 1 < 4:
+                        for item in couples[step - 1]:
+                            item.first_axis()
+                    if step <= 5:
+                        small.hop(step - 1)
+                        mean_proj.hop(step - 1)
+                    if 0 <= step - 3 < 4:
+                        for item in couples[step - 3]:
+                            item.tensor()
+                    finish(step - 1)
+
+        sums_own[...] = jnp.zeros_like(sums_own)
+        sums_far[...] = jnp.zeros_like(sums_far)
+
+        def part(start, size, keys, sames, sums):
+            q_block = qkv_ref[0, pl.ds(start, size), :]
+            g_block = g_ref[pl.ds(start, size), :]
+            grads = []
+            for head in range(2):
+                mask = (lane // HEAD_WIDTH) == head
+                q_head = jnp.where(mask, q_block, jnp.zeros_like(q_block))
+                g_head = jnp.where(mask, g_block, jnp.zeros_like(g_block))
+                scores = [
+                    jnp.where(same, dot_nt(q_head, key), MASKED)
+                    for (key, _), same in zip(keys, sames)
+                ]
+                top = functools.reduce(
+                    jnp.maximum, [jnp.max(s, axis=-1, keepdims=True) for s in scores]
+                )
+                powers = [jnp.exp(s - top) for s in scores]
+                total = functools.reduce(
+                    jnp.add, [jnp.sum(p, axis=-1, keepdims=True) for p in powers]
+                )
+                inverse = 1.0 / total
+                g_head = (g_head.astype(F32) * inverse).astype(BF)
+                pulls = [dot_nt(g_head, value) for _, value in keys]
+                mean = functools.reduce(
+                    jnp.add,
+                    [jnp.sum(p * d, axis=-1, keepdims=True) for p, d in zip(powers, pulls)],
+                ) * inverse
+                slopes = [(p * (d - mean)).astype(BF) for p, d in zip(powers, pulls)]
+                got = functools.reduce(
+                    jnp.add, [dot_nn(s, key) for s, (key, _) in zip(slopes, keys)]
+                )
+                grads.append(got * 0.125)
+                for (ref, begin, many), s, p in zip(sums, slopes, powers):
+                    ref[0, pl.ds(begin, many), :] += dot_tn(s, q_head)
+                    ref[1, pl.ds(begin, many), :] += dot_tn(p.astype(BF), g_head)
+            total = jnp.where(lane < HEAD_WIDTH, grads[0], grads[1])
+            at = pl.ds(start, size)
+            low = (total * c_ref[at, :] - turned(total) * s_ref[at, :]).astype(BF)
+            pre_ref[0, at, pl.ds(pl.multiple_of(h * 128, 128), 128)] = low
+            return jnp.sum(low.astype(F32), axis=0, keepdims=True)
+
+        doc_keys = [
+            (qkv_ref[1, :docs, :], qkv_ref[2, :docs, :]),
+            (far_ref[0], far_ref[1]),
+        ]
+        bias = jnp.zeros((1, 128), F32)
+        for at in range(docs // block):
+            labels = lc_ref[pl.ds(at * block, block), :]
+            bias = bias + part(
+                at * block,
+                block,
+                doc_keys,
+                [labels == lo_ref[...], labels == lf_ref[...]],
+                [(sums_own, 0, docs), (sums_far, 0, docs)],
+            )
+        row = lax.broadcasted_iota(jnp.int32, (asked, asked), 0) // QLEN
+        col = lax.broadcasted_iota(jnp.int32, (asked, asked), 1) // QLEN
+        bias = bias + part(
+            docs,
+            asked,
+            [(qkv_ref[1, docs:, :], qkv_ref[2, docs:, :])],
+            [row == col],
+            [(sums_own, docs, asked)],
+        )
+        bias_ref[0:1, pl.ds(pl.multiple_of(h * 128, 128), 128)] = bias
+        side = h % 2
+        kept[side, 0] = sums_own[0] * c_ref[...] - turned(sums_own[0]) * s_ref[...]
+        kept[side, 1] = sums_own[1]
+        give[h, 0] = (sums_far[0] * fc_ref[...] - turned(sums_far[0]) * fs_ref[...]).astype(BF)
+        give[h, 1] = sums_far[1].astype(BF)
+        for step in range(pairs):
+
+            @pl.when(h == step)
+            def _(step=step):
+                gives[step].start()
+
+        @pl.when(h == pairs - 1)
+        def _():
+            finish(pairs - 1)
+            for couple in couples:
+                for item in couple:
+                    item.settle()
+            up_o[...] = (
+                ua[0, :own_block, :].astype(F32)
+                + u3[0].astype(F32)
+                + u3[1].astype(F32)
+                + u3[2].astype(F32)
+            )
+            back_o[...] = (
+                ba[0, :, :own_block].astype(F32)
+                + b3[0].astype(F32)
+                + b3[1].astype(F32)
+                + b3[2].astype(F32)
+            )
+            vec_o[...] = v_run[5]
+            proj_o[...] = mean_proj.result()
+            send.drain()
+
+    def whole(shape):
+        return pl.BlockSpec(shape, lambda h: (0,) * len(shape))
+
+    anywhere = pl.BlockSpec(memory_space=pl.ANY)
+    vmem = pltpu.VMEM
+    dma = pltpu.SemaphoreType.DMA
+    columns = proj.shape[1]
+    out_shape = [
+        jax.ShapeDtypeStruct((3, rows, width), BF),
+        jax.ShapeDtypeStruct((8, width), F32),
+        jax.ShapeDtypeStruct((own_block, share), F32),
+        jax.ShapeDtypeStruct((share, own_block), F32),
+        jax.ShapeDtypeStruct(vectors.shape, F32),
+        jax.ShapeDtypeStruct((own_block, columns), F32),
+    ]
+    count = 2 * (ways * 4 + 3) + 5 + 5 + pairs
+    return pl.pallas_call(
+        kernel,
+        grid=(pairs,),
+        in_specs=[
+            pl.BlockSpec((3, rows, 128), lambda h: (0, 0, h)),
+            pl.BlockSpec((2, docs, 128), lambda h: (0, 0, h)),
+            pl.BlockSpec((rows, 128), lambda h: (0, h)),
+            whole((rows, 128)),
+            whole((rows, 128)),
+            whole((docs, 128)),
+            whole((docs, 128)),
+            whole((docs, 1)),
+            whole((1, docs)),
+            whole((1, docs)),
+            anywhere,
+            anywhere,
+            whole(vectors.shape),
+            whole(proj.shape),
+        ],
+        out_specs=[whole(x.shape) for x in out_shape],
+        out_shape=out_shape,
+        scratch_shapes=[
+            vmem((2, rows, 128), F32),
+            vmem((2, docs, 128), F32),
+            vmem((pairs, 2, docs, 128), BF),
+            vmem((2, 2, rows, 128), F32),
+            vmem((pairs, 2, docs, 128), BF),
+            vmem((ways, half, share), BF),
+            vmem((ways, half, share), BF),
+            vmem((ways, 2 * own_block, share), BF),
+            vmem((ways, own_block, share), BF),
+            vmem((ways - 1, own_block, share), BF),
+            vmem((ways, share, half), BF),
+            vmem((ways, share, half), BF),
+            vmem((ways, share, 2 * own_block), BF),
+            vmem((ways, share, own_block), BF),
+            vmem((ways - 1, share, own_block), BF),
+            vmem((5,) + vectors.shape, F32),
+            vmem((6,) + vectors.shape, F32),
+            vmem((width, columns), F32),
+            vmem((width + 2 * own_block, columns), F32),
+            dma((count,)),
+            dma((count,)),
+            dma((2 * ways,)),
+        ],
+        compiler_params=pltpu.CompilerParams(
+            collective_id=2, has_side_effects=True, vmem_limit_bytes=60 << 20
+        ),
+        name="attend_backward_and_sum",
+        cost_estimate=pl.CostEstimate(
+            flops=100 * rows * 2 * docs * width,
+            bytes_accessed=4 * (6 * rows + 4 * docs) * width,
+            transcendentals=rows * 2 * docs * width // 64,
+        ),
+    )(
+        qkv, far_kv, grad, cosine, sine, far_cosine, far_sine, col_labels, own_labels, far_labels,
+        up, back, vectors, proj,
+    )
 
 
 def body(
@@ -945,16 +1609,39 @@
     out_grad = own_cot_turned = dot_nn(own_cot, turn) + dot_nt(proj_low, full_proj)
     resid_two_grad, gain_two_grad, shift_two_grad = norm_two_pull(out_grad)
     update_low = resid_two_grad.astype(BF)
-    sum_back = weight_sum(active_low, update_low, 1, True)
+    whole_path = chips == 4
+    if whole_path:
+        back_grad = dot_tn(active_low, update_low).astype(BF)
+    else:
+        sum_back = weight_sum(active_low, update_low, 1, True)
     active_grad = dot_nt(update_low, full_back)
     (inner_grad,) = gelu_pull(active_grad)
     inner_low = inner_grad.astype(BF)
-    sum_in = weight_sum(normed_low, inner_low, 0, False)
+    if whole_path:
+        in_grad = dot_tn(normed_low, inner_low).astype(BF)
+    else:
+        sum_in = weight_sum(normed_low, inner_low, 0, False)
     normed_grad = dot_nt(inner_low, full_in) + resid_two_grad
     resid_one_grad, gain_one_grad, shift_one_grad = norm_one_pull(normed_grad)
     branch_low = resid_one_grad.astype(BF)
     mixed_grad = dot_nt(branch_low, full_out).astype(BF)
-    sum_out = weight_sum(mixed, branch_low, 1, False)
+    grad_proj = dot_tn(output_low, proj_low)
+    zero = jnp.zeros((width,), F32)
+    vectors = jnp.stack(
+        [
+            jnp.sum(branch_low.astype(F32), axis=0),
+            gain_one_grad,
+            shift_one_grad,
+            jnp.sum(update_low.astype(F32), axis=0),
+            gain_two_grad,
+            shift_two_grad,
+            zero,
+            zero,
+        ]
+    )
+    vectors = lax.dot_general(
+        vectors, turn.astype(F32), (((1,), (1,)), ((), ())), precision=FULL_PRECISION
+    )
 
     def heads_sum(rights, first_block, blocks, reverse):
         size = width // 2
@@ -977,16 +1664,9 @@
 
         return Reduction(half, 0, reverse, last)
 
-    head_sums, head_rights = [], []
-    running = [sum_back, sum_in]
-    per_block = heads_local // 128
-    for first_block, blocks in ((0, 2), (2, 1), (3, 1)):
-        for item in running:
-            item.advance()
-        mixed_grad = after(mixed_grad, running)
-        dq, own_grads, give = attention_backward(
-            first_block * per_block,
-            blocks * per_block,
+    inner_bias = jnp.sum(inner_low.astype(F32), axis=0).reshape(ways, units_local)
+    if whole_path:
+        pre, head_bias, out_in, out_back, vectors, grad_proj = attention_backward_kernel(
             qkv,
             far_kv,
             mixed_grad,
@@ -995,77 +1675,89 @@
             far_cosine,
             far_sine,
             *label_args,
+            in_grad,
+            back_grad,
+            vectors,
+            grad_proj,
         )
-        got = exchange(give, dr=1).astype(F32)
-        rights = [dq] + [
-            jnp.concatenate([own_grads[i, :docs] + got[i], own_grads[i, docs:]], axis=0).astype(BF)
-            for i in range(2)
-        ]
-        rights = jnp.concatenate(rights, axis=1)
-        head_rights.append((blocks, rights))
-        item = heads_sum(rights, first_block, blocks, first_block > 0)
-        head_sums.append(item)
-        if first_block == 0:
-            running += [sum_out]
-        elif first_block == 2:
-            running += [head_sums[0]]
-    out_back = sum_back.finish()
-    out_in = sum_in.finish()
-    out_out = sum_out.finish()
-    out_qkv = functools.reduce(jnp.add, [item.finish() for item in head_sums])
+        head_bias = head_bias[:3].reshape(3, ways, heads_local)
+        pre = [pre[j] for j in range(3)]
+    else:
+        head_sums, head_rights = [], []
+        running = [sum_back, sum_in]
+        per_block = heads_local // 128
+        sum_out = weight_sum(mixed, branch_low, 1, False)
+        for first_block, blocks in ((0, 2), (2, 1), (3, 1)):
+            for item in running:
+                item.advance()
+            mixed_grad = after(mixed_grad, running)
+            dq, own_grads, give = attention_backward(
+                first_block * per_block,
+                blocks * per_block,
+                qkv,
+                far_kv,
+                mixed_grad,
+                cosine,
+                sine,
+                far_cosine,
+                far_sine,
+                *label_args,
+            )
+            got = exchange(give, dr=1).astype(F32)
+            rights = [dq] + [
+                jnp.concatenate(
+                    [own_grads[i, :docs] + got[i], own_grads[i, docs:]], axis=0
+                ).astype(BF)
+                for i in range(2)
+            ]
+            head_rights.append(rights)
+            head_sums.append(
+                heads_sum(jnp.concatenate(rights, axis=1), first_block, blocks, first_block > 0)
+            )
+        out_back = sum_back.finish()
+        out_in = sum_in.finish()
+        pre = [jnp.concatenate([part[j] for part in head_rights], axis=1) for j in range(3)]
+        head_bias = jnp.stack([jnp.sum(p.astype(F32), axis=0) for p in pre])
+        head_bias = head_bias.reshape(3, ways, heads_local)
     x_grad = resid_one_grad
     for j in range(3):
-        pre = jnp.concatenate(
-            [r[:, j * r.shape[1] // 3 : (j + 1) * r.shape[1] // 3] for _, r in head_rights], axis=1
+        x_grad = x_grad + dot_nt(pre[j], full_qkv[j])
+    x_grad = dot_nt(x_grad.astype(BF), turn).astype(BF)
+    tensor_grads = jnp.concatenate(
+        [jnp.swapaxes(head_bias, 0, 1).reshape(ways, 3 * heads_local), inner_bias], axis=1
+    )
+    if whole_path:
+        out_qkv, out_out, gx_doc, gx_query, tensor_grads = finish_kernel(
+            jnp.concatenate([dot_tn(x_low, p).astype(BF) for p in pre], axis=1),
+            dot_tn(mixed, branch_low).astype(BF),
+            x_grad,
+            tensor_grads.reshape(ways, -1, 128),
         )
-        x_grad = x_grad + dot_nt(pre, full_qkv[j])
-    gx_doc, gx_query = rows_out(dot_nt(x_grad.astype(BF), turn).astype(BF))
-
-    grad_proj = dot_tn(output_low, proj_low)
-    for dr in [1] + chip_bits[::-1]:
-        size = grad_proj.shape[0] // 2
-        got = exchange(grad_proj[size:].astype(BF), dr=dr)
-        grad_proj = grad_proj[:size] + got.astype(F32)
-    for dt in (1, 2):
-        grad_proj = grad_proj + exchange(grad_proj, dt=dt)
-
-    vectors = jnp.stack(
-        [
-            jnp.sum(branch_low.astype(F32), axis=0),
-            gain_one_grad,
-            shift_one_grad,
-            jnp.sum(update_low.astype(F32), axis=0),
-            gain_two_grad,
-            shift_two_grad,
-        ]
-    )
-    vectors = lax.dot_general(
-        vectors, turn.astype(F32), (((1,), (1,)), ((), ())), precision=FULL_PRECISION
-    )
-    head_bias = []
-    for blocks, r in head_rights:
-        sums = jnp.sum(r.astype(F32), axis=0).reshape(3, blocks, heads_local)
-        head_bias.append(jnp.swapaxes(sums, 0, 1).reshape(blocks, 3 * heads_local))
-    tensor_grads = jnp.concatenate(
-        [
-            jnp.concatenate(head_bias, axis=0),
-            jnp.sum(inner_low.astype(F32), axis=0).reshape(ways, units_local),
-        ],
-        axis=1,
-    )
-    for dt in (2, 1):
-        tensor_grads = tensor_grads[:dt] + exchange(tensor_grads[dt:], dt=dt)
-        vectors = vectors + exchange(vectors, dt=dt)
-    for dr in [1] + chip_bits:
-        tensor_grads = tensor_grads + exchange(tensor_grads, dr=dr)
-        vectors = vectors + exchange(vectors, dr=dr)
-    tensor_grads = tensor_grads[0]
+        tensor_grads = tensor_grads.reshape(-1)
+    else:
+        gx_doc, gx_query = rows_out(x_grad)
+        gx_doc, gx_query = gx_doc.astype(F32), gx_query.astype(F32)
+        out_out = sum_out.finish()
+        out_qkv = functools.reduce(jnp.add, [item.finish() for item in head_sums])
+        for dr in [1] + chip_bits[::-1]:
+            size = grad_proj.shape[0] // 2
+            got = exchange(grad_proj[size:].astype(BF), dr=dr)
+            grad_proj = grad_proj[:size] + got.astype(F32)
+        for dt in (1, 2):
+            grad_proj = grad_proj + exchange(grad_proj, dt=dt)
+        for dt in (2, 1):
+            tensor_grads = tensor_grads[:dt] + exchange(tensor_grads[dt:], dt=dt)
+            vectors = vectors + exchange(vectors, dt=dt)
+        for dr in [1] + chip_bits:
+            tensor_grads = tensor_grads + exchange(tensor_grads, dr=dr)
+            vectors = vectors + exchange(vectors, dr=dr)
+        tensor_grads = tensor_grads[0]
     return (
         y_doc,
         y_query,
         loss_out,
-        gx_doc.astype(F32),
-        gx_query.astype(F32),
+        gx_doc,
+        gx_query,
         out_qkv,
         tensor_grads[: 3 * heads_local].reshape(3, heads_local),
         out_out,

time: 742 us -> 634 us (0.85)
  waiting for transfers between devices: 119 us -> 11.8 us
  Pallas kernels: 242 us -> 349 us
  starting transfers between devices: 82.3 us -> 32.5 us
  other arithmetic: 69.1 us -> 41 us
  local copies, waits for them, and re-layouts: 66.8 us -> 51.2 us
  matrix products: 148 us -> 135 us
    pallas_call x3 -> x2, Pallas kernels: 71.7 us -> 179 us  [the longest x1 121 us: attention_backward_kernel(): pl.pallas_call(kernel, grid=(pairs,), in_specs=[pl.BlockSpec((3, rows, 12...]
    ppermute x61 -> x13, waiting for transfers between devices: 96 us -> 6.91 us  [exchange(): return lax.ppermute(value, AXES, pairs)]
    ppermute x61 -> x13, starting transfers between devices: 59.5 us -> 12.3 us  [exchange(): return lax.ppermute(value, AXES, pairs)]
    add x28 -> x0, other arithmetic: 20.2 us -> none  [the longest x9 14 us: advance(): total = got if total is None else total + got]
    ppermute x6 -> x4, waiting for transfers between devices: 22.8 us -> 4.83 us  [quarters_out(): got.append(lax.ppermute(send, AXES, pairs))]
    dot_general x14 -> x8, matrix products: 47 us -> 33.7 us  [dot_tn(): lax.dot_general(a, b, (((0,), (0,)), ((), ())), preferred_element_type=F32)]
    slice x23 -> x1, local copies, waits for them, and re-layouts: 12.2 us -> 0.01 us  [body(): head_bias = head_bias[:3].reshape(3, ways, heads_local)]
    unnamed x292 -> x192, local copies, waits for them, and re-layouts: 20 us -> 19.6 us
  transfers between devices with their start and end apart: 69 -> 19, of which waited for: 23 -> 8; matrix products, arithmetic and copies ran while one was open for 28% -> 16% of each run, Pallas kernels for 9% -> 4%
where the time goes in v3:
time: 634 us; the launch traced here: 625 us
  Pallas kernels  349 us (55%)
  matrix products  135 us (21%)
  local copies, waits for them, and re-layouts  51.2 us (8%)
  other arithmetic  41 us (6%)
  starting transfers between devices  32.5 us (5%)
  waiting for transfers between devices  11.8 us (2%)
    pallas_call x1, Pallas kernels, gather_kernel(): pl.pallas_call(kernel, out_shape=out_shape, in_specs=[anywhere] * (5 + co...  133 us
    pallas_call x1, Pallas kernels, attention_backward_kernel(): pl.pallas_call(kernel, grid=(pairs,), in_specs=[pl.BlockSpec((3, rows, 12...  121 us
    pallas_call x1, Pallas kernels, finish_kernel(): pl.pallas_call(kernel, out_shape=out_shape, in_specs=[anywhere] * 3 + [wh...  57.4 us
    dot_general x9, matrix products, dot_nt(): lax.dot_general(a, b, (((1,), (1,)), ((), ())), preferred_element_type=F32)  49.7 us
    dot_general x7, matrix products, dot_nn(): lax.dot_general(a, b, (((1,), (0,)), ((), ())), preferred_element_type=F32)  41.8 us
    dot_general x8, matrix products, dot_tn(): lax.dot_general(a, b, (((0,), (0,)), ((), ())), preferred_element_type=F32)  33.7 us
    pallas_call x1, Pallas kernels, attention_forward(): pl.pallas_call(kernel, grid=(width // 128,), in_specs=[pl.BlockSpec((3, r...  27.4 us
    unnamed x192, local copies, waits for them, and re-layouts  19.6 us
  transfers between devices with their start and end apart: 19, of which 8 were waited for; matrix products, arithmetic and copies ran while one was open for 16% of the time, Pallas kernels for 4%

profile of v3, /device:TPU:0, one launch (start us, length us, event | category | flops | bytes accessed | tf_op | source)
XLA Modules:
  0.0 625.5 jit_solution(1475225268238414422)
XLA Ops:
  5.5 132.8 %gather_weights.1 = (bf16[576,1024]{1,0:T(8,128)(2,1)}, bf16[3,1024,1024]{2,1,0:T(8,128)(2,1)}, bf16[1024,1024]{1,0:T(8,128)(2,1)}, bf16[1024,4096]{1,0:T(8,128)...) custom-call(bf16[2,256,1024]{2,1,0:T(8,128)(2,1)} %refs_0_.1, ...), custom_call_target="tpu_custom_call" | custom-call | tf_op jit(solution)/shard_map/gather_weights/pallas_call | solution.py:585
  142.5 9.8 %project_heads.1.qkv_ref = bf16[3,576,1024]{2,1,0:T(8,128)(2,1)S(1)} custom-call(bf16[576,1024]{1,0:T(8,128)(2,1)S(1)} %fusion.30.x_ref, bf16[3,1024,1024]{2,1,0:T(8,128)(2,1)S(1)} %bitcast.146, f32[3,1,1024]{2,1,0:T(1,128)S(1)} %broadcast_in_dim.40.b_ref, f32[3,576,128]{2,1,0:T(8,128)S(1)} %maximum_maximum_fusion.c_ref, ...), custom_call_target="tpu_custom_call" | custom-call | flops 3623878656 | bytes 6291456 | tf_op jit(solution)/shard_map/project_heads/pallas_call | solution.py:66
  152.3 1.6 slice.308
  154.5 1.8 convert_element_type.157
  157.6 5.9 collective-permute-start.13
  163.6 7.2 %collective-permute-start.14 = (bf16[288,1024]{1,0:T(8,128)(2,1)}, bf16[288,1024]{1,0:T(8,128)(2,1)}, u32[]{:S(2)}, u32[]{:S(2)}) collective-permute-start(bf16[288,1024]{1,0:T(8,128)(2,1)} %get-tuple-element.97), channel_id=1, source_target_pairs={{0,2},{1,0},{2,6},{3,4},{4,3},{5,1},{6,7},{7,5},{8,10},{9,8},{10,1... | collective-permute-start | bytes 1769480 | tf_op jit(solution)/shard_map/ppermute | solution.py:1349
  180.8 2.1 fusion.10
  182.9 2.5 fusion.80
  186.4 27.4 %attend_forward.1 = bf16[576,1024]{1,0:T(8,128)(2,1)S(1)} custom-call(bf16[3,576,1024]{2,1,0:T(8,128)(2,1)S(1)} %project_heads.1.qkv_ref, bf16[2,512,1024]{2,1,0:T(8,128)(2,1)} %collective-permute-done.far_ref, s32[512,1]{1,0:T(8,128)S(1)} %copy-done.6, s32[1,512]{1,0:T(1,128)S(1)} %bitcast.141, s32[1,512]{1,0:T(1,128)S(1)} %bitcast.143), custom_call_target="tpu_custom_call" | custom-call | flops 19327352832 | bytes 6815744 | tf_op jit(solution)/shard_map/attend_forward/pallas_call | solution.py:130
  213.9 1.5 fusion.134
  216.7 2.0 slice-done.3
  218.6 29.8 %multiply_convert_fusion = (bf16[576,4096]{1,0:T(8,128)(2,1)S(1)}, f32[576,4096]{1,0:T(8,128)}, f32[576,4096]{1,0:T(8,128)}) fusion(f32[4096]{0:T(1024)S(1)} %pad_maximum_fusion.18, bf16[1024,4096]{1,0:T(8,128)(2,1)S(1)} %bitcast.193, f32[576,1024]{1,0:T(8,128)S(1)} %get-tuple-element.153, f32[1024]{0:T(1024)S(1)} %bitcast.174, f32[1024]{0:T(1024)S(1)} %bitcast.159, ...), kind=kOutput, calls=%fused_computation.4 | convolution fusion | flops 4990500864 | bytes 34370048 | tf_op jit(solution)/shard_map/dot_general | solution.py:38
  248.6 5.3 fusion.135
  262.7 2.3 pad_maximum_fusion.4.s_ref
  266.2 1.8 copy.80.c_ref
  268.1 1.7 copy.79
  269.8 1.6 tile.23
  271.3 1.8 copy.81.fc_ref
  273.9 1.6 collective-permute-start.5
  275.5 2.2 pad_maximum_fusion.7.fs_ref
  288.6 2.0 collective-permute-start.8
  290.7 1.7 collective-permute-done.8
  292.4 1.6 collective-permute-start.9
  294.0 2.4 collective-permute-done.9
  299.2 5.9 collective-permute-start.1
  306.2 1.7 concatenate.106
  307.8 1.7 concatenate.107
  315.4 2.9 multiply_convert_fusion.1
  324.3 1.6 collective-permute-start.16
  325.8 4.8 collective-permute-done.12
  339.0 2.6 multiply_reduce_fusion
  344.0 9.2 %convolution_convert_fusion.1.back_ref = bf16[4096,1024]{1,0:T(8,128)(2,1)} fusion(bf16[576,4096]{1,0:T(8,128)(2,1)S(1)} %bitcast.198, bf16[576,1024]{1,0:T(8,128)(2,1)S(1)} %get-tuple-element.83), kind=kOutput, calls=%fused_computation.19 | convolution fusion | flops 4836032512 | bytes 14286848 | tf_op jit(solution)/shard_map/dot_general | solution.py:46
  353.2 17.0 %convert_reduce_fusion = (f32[4096]{0:T(1024)}, bf16[576,4096]{1,0:T(8,128)(2,1)}) fusion(f32[576,4096]{1,0:T(8,128)} %get-tuple-element.93, f32[576,4096]{1,0:T(8,128)} %get-tuple-element.154, f32[4096]{0:T(1024)S(1)} %copy-done.61, bf16[576,1024]{1,0:T(8,128)(2,1)S(1)} %get-tuple-element.83, bf16[4096,1024]{1,0:T(8,128)(2,1)} %get-tuple-element.54), kind=kOutput, calls=%fused_computation.2 | convolution fusion | flops 4871942144 | bytes 33193984 | tf_op jit(solution)/shard_map/dot_general | solution.py:42
  370.2 10.5 %multiply_reduce_fusion.1 = (f32[1024]{0:T(1024)}, f32[576]{0:T(1024)S(1)}, f32[1024]{0:T(1024)}, f32[576,1024]{1,0:T(8,128)S(1)}) fusion(f32[576,1024]{1,0:T(8,128)S(1)} %copy-done.19, f32[576]{0:T(1024)S(1)} %copy-done.57, f32[576]{0:T(1024)S(1)} %broadcast_multiply_fusion.2, f32[1024]{0:T(1024)S(1)} %bitcast.161, f32[576,1024]{1,0:T(8,128)S(1)} %get-tuple-element.89, ...), kind=kOutput, calls=%fused_computation.33 | convolution fusion | flops 4837733888 | bytes 20206592 | tf_op jit(solution)/shard_map/dot_general | solution.py:42
  380.7 9.8 %convolution_convert_fusion.up_ref = bf16[1024,4096]{1,0:T(8,128)(2,1)} fusion(bf16[576,4096]{1,0:T(8,128)(2,1)S(1)} %copy-done.82, f32[576,1024]{1,0:T(8,128)S(1)} %copy-done.19, f32[1024]{0:T(1024)S(1)} %bitcast.176, f32[1024]{0:T(1024)S(1)} %bitcast.162, f32[576]{0:T(1024)S(1)} %copy-done.57, f32[576]{0:T(1024)S(1)} %broadcast_multiply_fusion.2), kind=kOutput, calls=%fused_computation.18 | convolution fusion | flops 4838981632 | bytes 15479296 | tf_op jit(solution)/shard_map/dot_general | solution.py:46
  393.3 3.3 fusion.7.vec_ref
  396.6 4.0 convolution_convert_fusion.6.g_ref
  400.7 121.3 %attend_backward_and_sum.1 = (bf16[3,576,1024]{2,1,0:T(8,128)(2,1)}, f32[8,1024]{1,0:T(8,128)}, f32[128,1024]{1,0:T(8,128)}, f32[1024,128]{1,0:T(8,128)}, f32[8,1024]{1,0:T(8,128)}, /*index=5*/f32[128,128]{1,0:T(8,128)}) custom-call(bf16[3,576,1024]{2,1,0:T(8,128)(2,1)} %copy-done.3, bf16[2,512,1024]{2,1,0:T(8,128)(2,1)} %collective-permute-done.far_ref, ...), custom_call_target="tpu_custom_call" | custom-call | flops 60397977600 | bytes 22544384 | tf_op jit(solution)/shard_map/attend_backward_and_sum/pallas_call | solution.py:1208
  522.0 4.9 fusion.14
  526.9 4.5 fusion.12
  531.4 3.2 convolution_convert_fusion.2.out_ref
  534.7 3.3 convolution_convert_fusion.5
  538.0 3.1 convolution_convert_fusion.4
  541.1 3.2 convolution_convert_fusion.3
  545.0 6.4 %fusion.32.rows_ref = bf16[576,1024]{1,0:T(8,128)(2,1)S(1)} fusion(s32[1024]{0:T(1024)} %copy-done.71, f32[576,1024]{1,0:T(8,128)} %fusion.12, f32[576,1024]{1,0:T(8,128)} %fusion.14, f32[576,1024]{1,0:T(8,128)S(1)} %get-tuple-element.87, f32[576]{0:T(1024)S(1)} %copy-done.59, bf16[3,1024,1024]{2,1,0:T(8,128)(2,1)} %get-tuple-element.50.w_ref, ...), kind=kOutput, calls=%fused_computation.72 | convolution fusion | flops 2420506624 | bytes 11540736 | tf_op jit(solution)/shard_map/dot_general | solution.py:42
  551.4 6.6 %pad_maximum_fusion.qkv_ref = bf16[1024,3072]{1,0:T(8,128)(2,1)} fusion(bf16[1024,1024]{1,0:T(8,128)(2,1)} %convolution_convert_fusion.3, bf16[1024,1024]{1,0:T(8,128)(2,1)} %convolution_convert_fusion.4, bf16[1024,1024]{1,0:T(8,128)(2,1)} %convolution_convert_fusion.5), kind=kLoop, calls=%fused_computation.20 | loop fusion | flops 18874368 | bytes 12582912 | tf_op jit(solution)/shard_map/concatenate | solution.py:1731
  558.0 57.4 %last_sums.1 = (f32[3,128,256]{2,1,0:T(8,128)S(1)}, f32[256,128]{1,0:T(8,128)S(1)}, f32[2,256,1024]{2,1,0:T(8,128)S(1)}, f32[2,32,1024]{2,1,0:T(8,128)S(1)}, f32[14,128]{1,0:T(8,128)S(1)}) custom-call(bf16[1024,3072]{1,0:T(8,128)(2,1)} %pad_maximum_fusion.qkv_ref, bf16[1024,1024]{1,0:T(8,128)(2,1)S(1)} %copy-done.2, bf16[576,1024]{1,0:T(8,128)(2,1)S(1)} %fusion.32.rows_ref, ...), custom_call_target="tpu_custom_call" | custom-call | tf_op jit(solution)/shard_map/last_sums/pallas_call | solution.py:968
  618.0 1.6 fusion.130
  (358 shorter events, 79.5 us)
Async XLA Ops:
  0.8 137.6 %copy-start.77 = (f32[32]{0:T(128)}, f32[32]{0:T(128)S(1)}, u32[]{:S(2)}) copy-start(f32[32]{0:T(128)S(1)} %multiply_power_fusion) | copy-start | bytes 388
  0.8 139.2 %copy-start.71 = (s32[1024]{0:T(1024)}, s32[1024]{0:T(1024)S(1)}, u32[]{:S(2)}) copy-start(s32[1024]{0:T(1024)S(1)} %fusion.94) | copy-start | bytes 12292
  1.9 183.5 %copy-start.11 = (s32[512]{0:T(512)}, s32[512]{0:T(512)S(1)}, u32[]{:S(2)}) copy-start(s32[512]{0:T(512)S(1)} %get-tuple-element.78) | copy-start | bytes 6148
  2.0 313.5 %copy-start.10 = (s32[512]{0:T(512)}, s32[512]{0:T(512)S(1)}, u32[]{:S(2)}) copy-start(s32[512]{0:T(512)S(1)} %get-tuple-element.79) | copy-start | bytes 6148
  3.8 135.8 %copy-start.23 = (f32[576,32]{1,0:T(8,128)}, f32[576,32]{1,0:T(8,128)S(1)}, u32[]{:S(2)}) copy-start(f32[576,32]{1,0:T(8,128)S(1)} %get-tuple-element.141) | copy-start | bytes 221188
  3.8 135.8 %copy-start.24 = (f32[576,32]{1,0:T(8,128)}, f32[576,32]{1,0:T(8,128)S(1)}, u32[]{:S(2)}) copy-start(f32[576,32]{1,0:T(8,128)S(1)} %get-tuple-element.143) | copy-start | bytes 221188
  3.9 135.9 %copy-start.22 = (f32[576,4,32]{0,2,1:T(8,128)}, f32[576,4,32]{0,2,1:T(8,128)S(1)}, u32[]{:S(2)}) copy-start(f32[576,4,32]{0,2,1:T(8,128)S(1)} %tile.20) | copy-start | bytes 884740
  141.5 10.8 %copy-start.12 = (bf16[576,1024]{1,0:T(8,128)(2,1)}, bf16[576,1024]{1,0:T(8,128)(2,1)S(1)}, u32[]{:S(2)}) copy-start(bf16[576,1024]{1,0:T(8,128)(2,1)S(1)} %fusion.30.x_ref) | copy-start | bytes 3538948
  152.3 33.2 %copy-start.3 = (bf16[3,576,1024]{2,1,0:T(8,128)(2,1)}, bf16[3,576,1024]{2,1,0:T(8,128)(2,1)S(1)}, u32[]{:S(2)}) copy-start(bf16[3,576,1024]{2,1,0:T(8,128)(2,1)S(1)} %project_heads.1.qkv_ref) | copy-start | bytes 10616836
  153.9 31.5 %collective-permute-start = (bf16[2,512,1024]{2,1,0:T(8,128)(2,1)}, bf16[2,512,1024]{2,1,0:T(8,128)(2,1)}, u32[]{:S(2)}, u32[]{:S(2)}) collective-permute-start(bf16[2,512,1024]{2,1,0:T(8,128)(2,1)} %slice.308), channel_id=1, source_target_pairs={{0,4},{1,5},{2,6},{3,7},{4,0},{5,1},{6,2},{7,3},{8,12},{9,13},{10,... | collective-permute-start | bytes 6291464 | tf_op jit(solution)/shard_map/ppermute | solution.py:1309
  157.6 121.3 %collective-permute-start.13 = (bf16[288,1024]{1,0:T(8,128)(2,1)}, bf16[288,1024]{1,0:T(8,128)(2,1)}, u32[]{:S(2)}, u32[]{:S(2)}) collective-permute-start(bf16[288,1024]{1,0:T(8,128)(2,1)} %get-tuple-element.96), channel_id=1, source_target_pairs={{0,0},{1,2},{2,4},{3,6},{4,1},{5,3},{6,5},{7,7},{8,8},{9,10},{10,1... | collective-permute-start | bytes 1769480 | tf_op jit(solution)/shard_map/ppermute | solution.py:1349
  163.6 115.4 %collective-permute-start.14 = (bf16[288,1024]{1,0:T(8,128)(2,1)}, bf16[288,1024]{1,0:T(8,128)(2,1)}, u32[]{:S(2)}, u32[]{:S(2)}) collective-permute-start(bf16[288,1024]{1,0:T(8,128)(2,1)} %get-tuple-element.97), channel_id=1, source_target_pairs={{0,2},{1,0},{2,6},{3,4},{4,3},{5,1},{6,7},{7,5},{8,10},{9,8},{10,1... | collective-permute-start | bytes 1769480 | tf_op jit(solution)/shard_map/ppermute | solution.py:1349
  179.5 36.5 %copy-start.60 = (f32[4096]{0:T(1024)}, f32[4096]{0:T(1024)S(1)}, u32[]{:S(2)}) copy-start(f32[4096]{0:T(1024)S(1)} %pad_maximum_fusion.18) | copy-start | bytes 49156
  182.9 65.6 %copy-start.54 = (f32[1,1024]{1,0:T(1,128)}, f32[1,1024]{1,0:T(1,128)S(1)}, u32[]{:S(2)}) copy-start(f32[1,1024]{1,0:T(1,128)S(1)} %get-tuple-element.130) | copy-start | bytes 12292
  182.9 65.6 %copy-start.69 = (f32[1,1024]{1,0:T(1,128)}, f32[1,1024]{1,0:T(1,128)S(1)}, u32[]{:S(2)}) copy-start(f32[1,1024]{1,0:T(1,128)S(1)} %get-tuple-element.129) | copy-start | bytes 12292
  186.4 27.5 %copy-start.13 = (bf16[576,1024]{1,0:T(8,128)(2,1)S(1)}, bf16[576,1024]{1,0:T(8,128)(2,1)}, u32[]{:S(2)}) copy-start(bf16[576,1024]{1,0:T(8,128)(2,1)} %copy-done.12) | copy-start | bytes 3538948
  186.4 27.5 %copy-start.79 = (bf16[1024,1024]{1,0:T(8,128)(2,1)S(1)}, bf16[1024,1024]{1,0:T(8,128)(2,1)}, u32[]{:S(2)}) copy-start(bf16[1024,1024]{1,0:T(8,128)(2,1)} %get-tuple-element.52) | copy-start | bytes 6291460
  213.9 34.6 %slice-start.4 = ((s8[8388608]{0:T(1024)(128)(4,1)}), s8[4194304]{0:T(1024)(128)(4,1)S(1)}, s32[]{:S(2)}) async-start(s8[8388608]{0:T(1024)(128)(4,1)} %bitcast.194), calls=%async_computation.4 | async-start | bytes 8388608
  215.5 33.0 %copy-start.18 = (f32[576,1024]{1,0:T(8,128)}, f32[576,1024]{1,0:T(8,128)S(1)}, u32[]{:S(2)}) copy-start(f32[576,1024]{1,0:T(8,128)S(1)} %get-tuple-element.153) | copy-start | bytes 7077892
  215.9 32.6 %copy-start.48 = (f32[576]{0:T(1024)}, f32[576]{0:T(1024)S(1)}, u32[]{:S(2)}) copy-start(f32[576]{0:T(1024)S(1)} %multiply_reduce_fusion.5) | copy-start | bytes 6916
  215.9 32.6 %copy-start.56 = (f32[576]{0:T(1024)}, f32[576]{0:T(1024)S(1)}, u32[]{:S(2)}) copy-start(f32[576]{0:T(1024)S(1)} %fusion.103) | copy-start | bytes 6916
  218.6 29.9 %slice-start.5 = ((s8[8388608]{0:T(1024)(128)(4,1)}), s8[4194304]{0:T(1024)(128)(4,1)S(1)}, s32[]{:S(2)}) async-start(s8[8388608]{0:T(1024)(128)(4,1)} %bitcast.194), calls=%async_computation.5 | async-start | bytes 8388608
  258.1 2.6 collective-permute-start.3
  262.7 10.4 %collective-permute-start.4 = (bf16[128,128]{1,0:T(8,128)(2,1)}, bf16[128,128]{1,0:T(8,128)(2,1)}, u32[]{:S(2)}, u32[]{:S(2)}) collective-permute-start(bf16[128,128]{1,0:T(8,128)(2,1)} %pad_maximum_fusion.14), channel_id=1, source_target_pairs={{0,1},{1,0},{2,3},{3,2},{4,5},{5,4},{6,7},{7,6},{8,9},{9,8},{10,11... | collective-permute-start | bytes 98312 | tf_op jit(solution)/shard_map/ppermute | solution.py:1309
  273.9 4.4 collective-permute-start.5
  278.4 5.0 collective-permute-start.6
  287.0 1.5 collective-permute-start.7
  288.6 3.8 collective-permute-start.8
  292.4 4.0 collective-permute-start.9
  296.4 9.1 %collective-permute-start.10 = (f32[16,1024]{1,0:T(8,128)S(1)}, f32[16,1024]{1,0:T(8,128)S(1)}, u32[]{:S(2)}, u32[]{:S(2)}) collective-permute-start(f32[16,1024]{1,0:T(8,128)S(1)} %pad_maximum_fusion.13), channel_id=1, source_target_pairs={{0,16},{1,17},{2,18},{3,19},{4,20},{5,21},{6,22},{7,23},{8,24},{9,... | collective-permute-start | bytes 196616 | tf_op jit(solution)/shard_map/ppermute | solution.py:1309
  299.2 32.9 %collective-permute-start.1 = (bf16[288,1024]{1,0:T(8,128)(2,1)}, bf16[288,1024]{1,0:T(8,128)(2,1)}, u32[]{:S(2)}, u32[]{:S(2)}) collective-permute-start(bf16[288,1024]{1,0:T(8,128)(2,1)} %get-tuple-element.101), channel_id=1, source_target_pairs={{0,0},{1,4},{2,1},{3,5},{4,2},{5,6},{6,3},{7,7},{8,8},{9,12},{10,9... | collective-permute-start | bytes 1769480 | tf_op jit(solution)/shard_map/ppermute | solution.py:1370
  305.1 27.0 %collective-permute-start.2 = (bf16[288,1024]{1,0:T(8,128)(2,1)}, bf16[288,1024]{1,0:T(8,128)(2,1)}, u32[]{:S(2)}, u32[]{:S(2)}) collective-permute-start(bf16[288,1024]{1,0:T(8,128)(2,1)} %get-tuple-element.100), channel_id=1, source_target_pairs={{0,1},{1,5},{2,0},{3,4},{4,3},{5,7},{6,2},{7,6},{8,9},{9,13},{10,8... | collective-permute-start | bytes 1769480 | tf_op jit(solution)/shard_map/ppermute | solution.py:1370
  315.4 8.3 %copy-start.29 = (bf16[512,128]{1,0:T(8,128)(2,1)S(1)}, bf16[512,128]{1,0:T(8,128)(2,1)}, u32[]{:S(2)}) copy-start(bf16[512,128]{1,0:T(8,128)(2,1)} %copy-done.28) | copy-start | bytes 393220
  315.4 8.3 %copy-start.31 = (bf16[512,128]{1,0:T(8,128)(2,1)S(1)}, bf16[512,128]{1,0:T(8,128)(2,1)}, u32[]{:S(2)}) copy-start(bf16[512,128]{1,0:T(8,128)(2,1)} %copy-done.30) | copy-start | bytes 393220
  318.9 5.3 collective-permute-start.15
  321.7 9.0 %collective-permute-start.12 = (f32[1,128]{1,0:T(1,128)S(1)}, f32[1,128]{1,0:T(1,128)S(1)}, u32[]{:S(2)}, u32[]{:S(2)}) collective-permute-start(f32[1,128]{1,0:T(1,128)S(1)} %broadcast_in_dim.47), channel_id=1, source_target_pairs={{0,1},{1,5},{2,0},{3,4},{4,3},{5,7},{6,2},{7,6},{8,9},{9,13},{10,8... | collective-permute-start | bytes 1544 | tf_op jit(solution)/shard_map/ppermute | solution.py:1370
  323.0 7.6 %collective-permute-start.11 = (f32[1,128]{1,0:T(1,128)S(1)}, f32[1,128]{1,0:T(1,128)S(1)}, u32[]{:S(2)}, u32[]{:S(2)}) collective-permute-start(f32[1,128]{1,0:T(1,128)S(1)} %broadcast_in_dim.46), channel_id=1, source_target_pairs={{0,0},{1,4},{2,1},{3,5},{4,2},{5,6},{6,3},{7,7},{8,8},{9,12},{10,9... | collective-permute-start | bytes 1544 | tf_op jit(solution)/shard_map/ppermute | solution.py:1370
  324.3 7.0 %collective-permute-start.16 = (bf16[256,128]{1,0:T(8,128)(2,1)S(1)}, bf16[256,128]{1,0:T(8,128)(2,1)S(1)}, u32[]{:S(2)}, u32[]{:S(2)}) collective-permute-start(bf16[256,128]{1,0:T(8,128)(2,1)S(1)} %select_convert_fusion.1), channel_id=1, source_target_pairs={{0,8},{1,9},{2,10},{3,11},{4,12},{5,13},{6,14},{7,15},{8,0},{9,1},... | collective-permute-start | bytes 196616 | tf_op jit(solution)/shard_map/ppermute | solution.py:1309
  331.3 4.0 collective-permute-start.17
  335.3 1.2 collective-permute-start.18
  344.0 9.2 %copy-start.61 = (f32[4096]{0:T(1024)S(1)}, f32[4096]{0:T(1024)}, u32[]{:S(2)}) copy-start(f32[4096]{0:T(1024)} %copy-done.60) | copy-start | bytes 49156
  353.2 17.0 %copy-start.19 = (f32[576,1024]{1,0:T(8,128)S(1)}, f32[576,1024]{1,0:T(8,128)}, u32[]{:S(2)}) copy-start(f32[576,1024]{1,0:T(8,128)} %copy-done.18) | copy-start | bytes 7077892
  353.2 17.0 %copy-start.55 = (f32[1,1024]{1,0:T(1,128)S(1)}, f32[1,1024]{1,0:T(1,128)}, u32[]{:S(2)}) copy-start(f32[1,1024]{1,0:T(1,128)} %copy-done.54) | copy-start | bytes 12292
  353.2 17.0 %copy-start.57 = (f32[576]{0:T(1024)S(1)}, f32[576]{0:T(1024)}, u32[]{:S(2)}) copy-start(f32[576]{0:T(1024)} %copy-done.56) | copy-start | bytes 6916
  370.2 10.5 %copy-start.70 = (f32[1,1024]{1,0:T(1,128)S(1)}, f32[1,1024]{1,0:T(1,128)}, u32[]{:S(2)}) copy-start(f32[1,1024]{1,0:T(1,128)} %copy-done.69) | copy-start | bytes 12292
  370.2 10.5 %copy-start.82 = (bf16[576,4096]{1,0:T(8,128)(2,1)S(1)}, bf16[576,4096]{1,0:T(8,128)(2,1)}, u32[]{:S(2)}) copy-start(bf16[576,4096]{1,0:T(8,128)(2,1)} %get-tuple-element.81) | copy-start | bytes 14155780
  380.7 9.8 %copy-start.49 = (f32[576]{0:T(1024)S(1)}, f32[576]{0:T(1024)}, u32[]{:S(2)}) copy-start(f32[576]{0:T(1024)} %copy-done.48) | copy-start | bytes 6916
  551.4 6.6 %copy-start.2 = (bf16[1024,1024]{1,0:T(8,128)(2,1)S(1)}, bf16[1024,1024]{1,0:T(8,128)(2,1)}, u32[]{:S(2)}) copy-start(bf16[1024,1024]{1,0:T(8,128)(2,1)} %convolution_convert_fusion.2.out_ref) | copy-start | bytes 6291460
  (63 other events, 167.2 us)

commit v4 on v3

--- a/solution.py
+++ b/solution.py
@@ -46,6 +46,141 @@
     return lax.dot_general(a, b, (((0,), (0,)), ((), ())), preferred_element_type=F32)
 
 
+def differing(a, b, bits):
+    total = 0
+    for bit in range(bits):
+        x, y = (a // 2**bit) % 2, (b // 2**bit) % 2
+        total = total + 2**bit * (x + y - 2 * x * y)
+    return total
+
+
+class Around:
+    def __init__(self):
+        self.rank = lax.axis_index("dp")
+        self.column = lax.axis_index("tensor")
+        self.core = self.rank % 2
+        self.base = self.rank - self.core
+
+    def other(self, bit):
+        rank = self.rank
+        return (rank + bit - 2 * bit * ((rank // bit) % 2), self.column)
+
+    def along(self, dt):
+        return (self.rank, differing(self.column, dt, 2))
+
+    def meet(self):
+        barrier = pltpu.get_barrier_semaphore()
+        for dc in range(2):
+            for dt in range(4):
+                if dc + dt > 0:
+                    pl.semaphore_signal(
+                        barrier,
+                        inc=1,
+                        device_id=(self.base + (self.core + dc) % 2, (self.column + dt) % 4),
+                        device_id_type=MESH,
+                    )
+        for bit in (2, 4):
+            pl.semaphore_signal(
+                barrier, inc=1, device_id=self.other(bit), device_id_type=MESH
+            )
+        pl.semaphore_wait(barrier, 9)
+
+
+class Sender:
+    def __init__(self, send_sem, recv_sem):
+        self.send_sem, self.recv_sem = send_sem, recv_sem
+        self.sent = []
+
+    def __call__(self, src, dst, to):
+        at = len(self.sent)
+        copy = pltpu.make_async_remote_copy(
+            src_ref=src,
+            dst_ref=dst,
+            send_sem=self.send_sem.at[at],
+            recv_sem=self.recv_sem.at[at],
+            device_id=to,
+            device_id_type=MESH,
+        )
+        self.sent.append(copy)
+        return copy
+
+    def drain(self):
+        for copy in self.sent:
+            copy.wait_send()
+
+
+class RowMoves:
+    def __init__(self, around, inward, docs, asked, packed, send_sem, recv_sem):
+        core, column, base = around.core, around.column, around.base
+        lonely = 3 * core == column
+        self.copies, self.arrivals = [], []
+        size, few = docs.shape[1], asked.shape[1]
+        for n in range(2):
+            q, m = (column % 2, n) if inward else (n, column // 2)
+            if inward:
+                mine = jnp.logical_and(lonely, column // 2 == n)
+                to = (base + column // 2, 2 * n + core)
+                here = jnp.logical_and(lonely, column % 2 == n)
+            else:
+                mine = jnp.logical_and(lonely, core == n)
+                to = (base + column % 2, 2 * core + n)
+                here = jnp.logical_and(lonely, column // 2 == n)
+            for kind, (ref, many, begin) in enumerate(((docs, size, 0), (asked, few, 2 * size))):
+                rows = packed.at[pl.ds(pl.multiple_of(begin + q * many, few), many), :]
+                src, dst = (ref.at[m], rows) if inward else (rows, ref.at[m])
+                away = pltpu.make_async_remote_copy(
+                    src_ref=src,
+                    dst_ref=dst,
+                    send_sem=send_sem.at[n, kind],
+                    recv_sem=recv_sem.at[q if inward else m, kind],
+                    device_id=to,
+                    device_id_type=MESH,
+                )
+                local = pltpu.make_async_copy(src, dst, send_sem.at[n, kind])
+                self.copies.append((mine, local, away))
+                if inward:
+                    land = packed.at[pl.ds(begin + n * many, many), :]
+                else:
+                    land = ref.at[n]
+                came = pltpu.make_async_remote_copy(
+                    src_ref=land,
+                    dst_ref=land,
+                    send_sem=send_sem.at[n, kind],
+                    recv_sem=recv_sem.at[n, kind],
+                    device_id=to,
+                    device_id_type=MESH,
+                )
+                self.arrivals.append((here, came))
+
+    def start(self):
+        for mine, local, away in self.copies:
+
+            @pl.when(mine)
+            def _(local=local):
+                local.start()
+
+            @pl.when(jnp.logical_not(mine))
+            def _(away=away):
+                away.start()
+
+    def wait(self):
+        for here, came in self.arrivals:
+
+            @pl.when(jnp.logical_not(here))
+            def _(came=came):
+                came.wait_recv()
+
+        for mine, local, away in self.copies:
+
+            @pl.when(mine)
+            def _(local=local):
+                local.wait()
+
+            @pl.when(jnp.logical_not(mine))
+            def _(away=away):
+                away.wait_send()
+
+
 def turned(values):
     lane = lax.broadcasted_iota(jnp.int32, (1, 128), 1)
     ahead = pltpu.roll(values, 96, 1)
@@ -53,43 +188,116 @@
     return jnp.where(lane % HEAD_WIDTH < HEAD_WIDTH // 2, ahead, behind)
 
 
-def project_heads(x, weights, bias, cosine, sine):
+def project_heads(x, weights, bias, cosine, sine, docs, remote):
     rows, width = x.shape
     columns = 256
-
-    def kernel(x_ref, w_ref, b_ref, c_ref, s_ref, o_ref):
+    steps = width // columns
+
+    def kernel(x_ref, w_ref, b_ref, c_ref, s_ref, o_ref, *rest):
+        j, n = pl.program_id(0), pl.program_id(1)
         got = dot_nn(x_ref[...], w_ref[0]) + b_ref[0]
+        low = []
         for at in range(0, columns, 128):
             piece = got[:, at : at + 128]
-            o_ref[0, :, at : at + 128] = (piece * c_ref[0] + turned(piece) * s_ref[0]).astype(BF)
-
+            low.append((piece * c_ref[0] + turned(piece) * s_ref[0]).astype(BF))
+            o_ref[0, :, at : at + 128] = low[-1]
+        if not remote:
+            return
+        far_ref, held, send_sem, recv_sem = rest
+        rank, column = lax.axis_index("dp"), lax.axis_index("tensor")
+        sibling = (rank + 1 - 2 * (rank % 2), column)
+        copies = [
+            pltpu.make_async_remote_copy(
+                src_ref=held.at[i, m],
+                dst_ref=far_ref.at[i, :, pl.ds(m * columns, columns)],
+                send_sem=send_sem.at[i, m],
+                recv_sem=recv_sem.at[i, m],
+                device_id=sibling,
+                device_id_type=MESH,
+            )
+            for i in range(2)
+            for m in range(steps)
+        ]
+
+        @pl.when(jnp.logical_and(j == 0, n == 0))
+        def _():
+            barrier = pltpu.get_barrier_semaphore()
+            pl.semaphore_signal(barrier, inc=1, device_id=sibling, device_id_type=MESH)
+            pl.semaphore_wait(barrier, 1)
+
+        for i in range(2):
+            for m in range(steps):
+
+                @pl.when(jnp.logical_and(j == i, n == m))
+                def _(i=i, m=m):
+                    for at, piece in enumerate(low):
+                        held[i, m, :, at * 128 : (at + 1) * 128] = piece[:docs]
+                    copies[i * steps + m].start()
+
+        @pl.when(jnp.logical_and(j == 2, n == steps - 1))
+        def _():
+            for copy in copies:
+                copy.wait()
+
+    order = lambda j: (j + 1) % 3
+    out_specs = [pl.BlockSpec((1, rows, columns), lambda j, n: (order(j), 0, n))]
+    out_shape = [jax.ShapeDtypeStruct((3, rows, width), BF)]
+    extra = {}
+    if remote:
+        out_specs.append(pl.BlockSpec(memory_space=pl.ANY))
+        out_shape.append(jax.ShapeDtypeStruct((2, docs, width), BF))
+        extra = dict(
+            scratch_shapes=[
+                pltpu.VMEM((2, steps, docs, columns), BF),
+                pltpu.SemaphoreType.DMA((2, steps)),
+                pltpu.SemaphoreType.DMA((2, steps)),
+            ]
+        )
+        params = pltpu.CompilerParams(
+            vmem_limit_bytes=40 << 20, collective_id=3, has_side_effects=True
+        )
+    else:
+        params = pltpu.CompilerParams(vmem_limit_bytes=40 << 20)
     return pl.pallas_call(
         kernel,
-        grid=(3, width // columns),
+        grid=(3, steps),
         in_specs=[
             pl.BlockSpec((rows, width), lambda j, n: (0, 0)),
-            pl.BlockSpec((1, width, columns), lambda j, n: (j, 0, n)),
-            pl.BlockSpec((1, 1, columns), lambda j, n: (j, 0, n)),
-            pl.BlockSpec((1, rows, 128), lambda j, n: (j, 0, 0)),
-            pl.BlockSpec((1, rows, 128), lambda j, n: (j, 0, 0)),
+            pl.BlockSpec((1, width, columns), lambda j, n: (order(j), 0, n)),
+            pl.BlockSpec((1, 1, columns), lambda j, n: (order(j), 0, n)),
+            pl.BlockSpec((1, rows, 128), lambda j, n: (order(j), 0, 0)),
+            pl.BlockSpec((1, rows, 128), lambda j, n: (order(j), 0, 0)),
         ],
-        out_specs=pl.BlockSpec((1, rows, columns), lambda j, n: (j, 0, n)),
-        out_shape=jax.ShapeDtypeStruct((3, rows, width), BF),
-        compiler_params=pltpu.CompilerParams(vmem_limit_bytes=40 << 20),
+        out_specs=out_specs,
+        out_shape=out_shape,
+        compiler_params=params,
         name="project_heads",
         cost_estimate=pl.CostEstimate(
             flops=6 * rows * width * width, bytes_accessed=6 * width * width, transcendentals=0
         ),
+        **extra,
     )(x, weights, bias[:, None, :], cosine, sine)
 
 
-def attention_forward(qkv, far_kv, col_labels, own_labels, far_labels):
+def attention_forward(qkv, far_kv, col_labels, own_labels, far_labels, cots=None):
     rows, width = qkv.shape[1:]
     docs = far_kv.shape[1]
     block = 128
     asked = rows - docs
 
-    def kernel(qkv_ref, far_ref, lc_ref, lo_ref, lf_ref, o_ref):
+    def kernel(qkv_ref, far_ref, lc_ref, lo_ref, lf_ref, *rest):
+        if cots is None:
+            (o_ref,) = rest
+        else:
+            cd_ref, cq_ref, o_ref, c_ref, send_sem, recv_sem = rest
+            around = Around()
+            moves = RowMoves(around, True, cd_ref, cq_ref, c_ref, send_sem, recv_sem)
+
+            @pl.when(pl.program_id(0) == 0)
+            def _():
+                around.meet()
+                moves.start()
+
         lane = lax.broadcasted_iota(jnp.int32, (1, 128), 1)
 
         def part(start, size, keys, sames):
@@ -125,6 +333,23 @@
         row = lax.broadcasted_iota(jnp.int32, (asked, asked), 0) // QLEN
         col = lax.broadcasted_iota(jnp.int32, (asked, asked), 1) // QLEN
         part(docs, asked, [(qkv_ref[1, docs:, :], qkv_ref[2, docs:, :])], [row == col])
+        if cots is not None:
+
+            @pl.when(pl.program_id(0) == width // 128 - 1)
+            def _():
+                moves.wait()
+
+    in_more, out_more, shape_more, extra = [], [], [], {}
+    params = pltpu.CompilerParams(vmem_limit_bytes=40 << 20)
+    if cots is not None:
+        anywhere = pl.BlockSpec(memory_space=pl.ANY)
+        in_more, out_more = [anywhere, anywhere], [anywhere]
+        shape_more = [jax.ShapeDtypeStruct((rows, cots[0].shape[2]), cots[0].dtype)]
+        dma = pltpu.SemaphoreType.DMA
+        extra = dict(scratch_shapes=[dma((2, 2)), dma((2, 2))])
+        params = pltpu.CompilerParams(
+            vmem_limit_bytes=40 << 20, collective_id=4, has_side_effects=True
+        )
 
     whole = lambda shape: pl.BlockSpec(shape, lambda h: (0, 0))
     return pl.pallas_call(
@@ -136,17 +361,19 @@
             whole((docs, 1)),
             whole((1, docs)),
             whole((1, docs)),
-        ],
-        out_specs=pl.BlockSpec((rows, 128), lambda h: (0, h)),
-        out_shape=jax.ShapeDtypeStruct((rows, width), BF),
-        compiler_params=pltpu.CompilerParams(vmem_limit_bytes=40 << 20),
+        ]
+        + in_more,
+        out_specs=[pl.BlockSpec((rows, 128), lambda h: (0, h))] + out_more,
+        out_shape=[jax.ShapeDtypeStruct((rows, width), BF)] + shape_more,
+        compiler_params=params,
         name="attend_forward",
         cost_estimate=pl.CostEstimate(
             flops=32 * rows * 2 * docs * width,
             bytes_accessed=2 * (4 * rows + 2 * docs) * width,
             transcendentals=rows * 2 * docs * width // 64,
         ),
-    )(qkv, far_kv, col_labels, own_labels, far_labels)
+        **extra,
+    )(qkv, far_kv, col_labels, own_labels, far_labels, *(cots or ()))
 
 
 def attention_backward(
@@ -271,14 +498,6 @@
     )
 
 
-def differing(a, b, bits):
-    total = 0
-    for bit in range(bits):
-        x, y = (a // 2**bit) % 2, (b // 2**bit) % 2
-        total = total + 2**bit * (x + y - 2 * x * y)
-    return total
-
-
 def gather_kernel(x_doc, x_query, qkv, out, up, back, proj, bias, picks):
     chips, ways = 4, 4
     groups = 2 * chips
@@ -601,59 +820,259 @@
     )(x_doc, x_query, *weights, proj, bias, picks)
 
 
-class Around:
-    def __init__(self):
-        self.rank = lax.axis_index("dp")
-        self.column = lax.axis_index("tensor")
-        self.core = self.rank % 2
-        self.base = self.rank - self.core
-
-    def other(self, bit):
-        rank = self.rank
-        return (rank + bit - 2 * bit * ((rank // bit) % 2), self.column)
-
-    def along(self, dt):
-        return (self.rank, differing(self.column, dt, 2))
-
-    def meet(self):
+def loss_kernel(projection, labels, log_counts, picks, y):
+    rows, columns = projection.shape
+    width = y.shape[1]
+    docs = labels.shape[0]
+    own = rows - docs
+    tokens = 16 * own
+    units, segments = 8, 4
+    chunk = 64
+
+    def kernel(
+        p_ref, lab_ref, cnt_ref, pick_ref, y_ref,
+        grad_ref, loss_ref, yd_ref, yq_ref,
+        asked_all, weight, sums, sums_all, coef_all, slope, part, part_low, got, tile, tile_got,
+        send_sem, recv_sem, row_send, row_recv, tile_send, tile_recv,
+    ):
+        around = Around()
+        rank, column, core, base = around.rank, around.column, around.core, around.base
+        chip, side = rank // 2, column % 2
+        mine = (chip * 2 + side) * 2 + core
+        unit = chip * 2 + side
+
+        def flip(value, bit, on):
+            return value + bit - 2 * bit * ((value // bit) % 2) if on else value
+
+        def peer(i):
+            to = flip(flip(flip(rank, 1, i & 1), 2, i & 4), 4, i & 8)
+            return (to, flip(column, 1, i & 2))
+
+        def index_of(i):
+            to, z = peer(i)
+            return ((to // 2) * 2 + z % 2) * 2 + to % 2
+
         barrier = pltpu.get_barrier_semaphore()
-        for dc in range(2):
-            for dt in range(4):
-                if dc + dt > 0:
-                    pl.semaphore_signal(
-                        barrier,
-                        inc=1,
-                        device_id=(self.base + (self.core + dc) % 2, (self.column + dt) % 4),
-                        device_id_type=MESH,
-                    )
-        for bit in (2, 4):
-            pl.semaphore_signal(
-                barrier, inc=1, device_id=self.other(bit), device_id_type=MESH
+        peers = [peer(i) for i in range(1, 16)]
+        for dt in (2, 3):
+            for dc in range(2):
+                away, z = around.along(dt)
+                peers.append((flip(rank, 1, dc), z))
+        for to in peers:
+            pl.semaphore_signal(barrier, inc=1, device_id=to, device_id_type=MESH)
+        pl.semaphore_wait(barrier, len(peers))
+
+        values = p_ref[...]
+        rate = lax.rsqrt(jnp.sum(values * values, axis=-1, keepdims=True) + 1e-06)
+        unit_wide = values * rate
+        unit_low = unit_wide.astype(BF)
+        own_at = pl.ds(pl.multiple_of(mine * own, own), own)
+        asked_all[own_at, :] = unit_low[docs:]
+
+        def all_to_all(kind, src, dst):
+            copies = []
+            for i in range(1, 16):
+                copy = pltpu.make_async_remote_copy(
+                    src_ref=src(i),
+                    dst_ref=dst(i),
+                    send_sem=send_sem.at[kind, i],
+                    recv_sem=recv_sem.at[kind, i],
+                    device_id=peer(i),
+                    device_id_type=MESH,
+                )
+                copy.start()
+                copies.append(copy)
+            return copies
+
+        first = all_to_all(0, lambda i: asked_all.at[own_at, :], lambda i: asked_all.at[own_at, :])
+        home = RowMoves(around, False, yd_ref, yq_ref, y_ref, row_send, row_recv)
+        doc_low = unit_low[:docs]
+        seg_of = lab_ref[...]
+        for copy in first:
+            copy.wait_recv()
+        queries = asked_all[...]
+        sums[...] = jnp.zeros_like(sums)
+        for at in range(0, docs, chunk):
+            cosines = dot_nt(doc_low[at : at + chunk], queries)
+            power = jnp.exp(TAU * (cosines - 1.0))
+            weight[at : at + chunk, :] = power
+            for s in range(segments):
+                chosen = seg_of[at : at + chunk] == s
+                sums[s : s + 1, :] += jnp.sum(
+                    jnp.where(chosen, power, 0.0), axis=0, keepdims=True
+                )
+        second = all_to_all(1, lambda i: sums, lambda i: sums_all.at[mine])
+        home.start()
+        sums_all[mine] = sums[...]
+        for copy in second:
+            copy.wait_recv()
+        row = lax.broadcasted_iota(jnp.int32, (8, tokens), 0)
+        lane = lax.broadcasted_iota(jnp.int32, (8, tokens), 1)
+        valid = row < segments
+        totals, logits = [], []
+        for n in range(units):
+            total = jnp.where(valid, sums_all[2 * n] + sums_all[2 * n + 1], 1.0)
+            best = (jnp.log(total) - cnt_ref[8 * n : 8 * n + 8, :]) / TAU + 1.0
+            for step in (1, 2, 4, 8, 16):
+                other = jnp.where(
+                    (lane // step) % 2 == 1,
+                    pltpu.roll(best, step, 1),
+                    pltpu.roll(best, tokens - step, 1),
+                )
+                best = best + other
+            totals.append(total)
+            logits.append(jnp.where(valid, LOGIT_SCALE * best, MASKED))
+        peak = functools.reduce(
+            jnp.maximum, [jnp.max(x, axis=0, keepdims=True) for x in logits]
+        )
+        powers = [jnp.exp(x - peak) for x in logits]
+        mass = functools.reduce(jnp.add, [jnp.sum(x, axis=0, keepdims=True) for x in powers])
+        picked = jnp.zeros_like(peak)
+        for n in range(units):
+            hit = jnp.logical_and(valid, pick_ref[...] == n * segments + row)
+            picked = picked + jnp.sum(jnp.where(hit, logits[n], 0.0), axis=0, keepdims=True)
+            slope_n = LOGIT_SCALE * (powers[n] / mass - jnp.where(hit, 1.0, 0.0))
+            coef_all[n] = slope_n / totals[n]
+        losses = peak + jnp.log(mass) - picked
+        tiles = []
+        for q in range(2):
+            at = mine * own + q * QLEN
+            value = jnp.sum(
+                jnp.where(lane[:1] == at, losses, 0.0), axis=1, keepdims=True
             )
-        pl.semaphore_wait(barrier, 9)
-
-
-class Sender:
-    def __init__(self, send_sem, recv_sem):
-        self.send_sem, self.recv_sem = send_sem, recv_sem
-        self.sent = []
-
-    def __call__(self, src, dst, to):
-        at = len(self.sent)
-        copy = pltpu.make_async_remote_copy(
-            src_ref=src,
-            dst_ref=dst,
-            send_sem=self.send_sem.at[at],
-            recv_sem=self.recv_sem.at[at],
-            device_id=to,
-            device_id_type=MESH,
-        )
-        self.sent.append(copy)
-        return copy
-
-    def drain(self):
-        for copy in self.sent:
+            tile[q, 0] = jnp.broadcast_to(value, (8, 128))
+            tile[q, 1] = jnp.zeros((8, 128), F32)
+        lonely = 3 * core == column
+        for q in range(2):
+            here = jnp.logical_and(lonely, core == q)
+            slot = column // 2
+            away = pltpu.make_async_remote_copy(
+                src_ref=tile.at[q],
+                dst_ref=tile_got.at[slot],
+                send_sem=tile_send.at[q],
+                recv_sem=tile_recv.at[slot],
+                device_id=(base + column % 2, 2 * core + q),
+                device_id_type=MESH,
+            )
+            tiles.append((here, away))
+
+            @pl.when(here)
+            def _(q=q):
+                tile_got[slot] = tile[q]
+
+            @pl.when(jnp.logical_not(here))
+            def _(away=away):
+                away.start()
+
+        coef = coef_all[unit]
+        doc_grads = []
+        part[...] = jnp.zeros_like(part)
+        for at in range(0, docs, chunk):
+            spread = jnp.zeros((chunk, tokens), F32)
+            for s in range(segments):
+                chosen = seg_of[at : at + chunk] == s
+                spread = jnp.where(chosen, coef[s : s + 1, :], spread)
+            low = (weight[at : at + chunk, :] * spread).astype(BF)
+            slope[at : at + chunk, :] = low
+            doc_grads.append(dot_nn(low, queries))
+        part[...] = dot_tn(slope[...], doc_low)
+        part_low[...] = part[...].astype(BF)
+
+        def theirs(i):
+            return part_low.at[pl.ds(pl.multiple_of(index_of(i) * own, own), own), :]
+
+        third = all_to_all(2, theirs, lambda i: got.at[i])
+
+        def pull(grad, begin, size):
+            v, r = unit_wide[begin : begin + size], rate[begin : begin + size]
+            inner = jnp.sum(v * grad, axis=-1, keepdims=True)
+            return ((grad - v * inner) * r).astype(BF)
+
+        for n, at in enumerate(range(0, docs, chunk)):
+            grad_ref[at : at + chunk, :] = pull(doc_grads[n], at, chunk)
+        total = part[own_at, :]
+        for copy in third:
+            copy.wait_recv()
+        for i in range(1, 16):
+            total = total + got[i].astype(F32)
+        grad_ref[docs:, :] = pull(total, docs, own)
+        for n in range(2):
+            here = jnp.logical_and(lonely, column // 2 == n)
+            came = pltpu.make_async_remote_copy(
+                src_ref=tile.at[n],
+                dst_ref=tile_got.at[n],
+                send_sem=tile_send.at[n],
+                recv_sem=tile_recv.at[n],
+                device_id=peer(1),
+                device_id_type=MESH,
+            )
+
+            @pl.when(jnp.logical_not(here))
+            def _(came=came):
+                came.wait_recv()
+
+        loss_ref[...] = tile_got[:, 0]
+        home.wait()
+        for here, away in tiles:
+
+            @pl.when(jnp.logical_not(here))
+            def _(away=away):
+                away.wait_send()
+
+        for copy in first + second + third:
             copy.wait_send()
+
+    def whole(shape):
+        return pl.BlockSpec(shape, lambda: (0,) * len(shape))
+
+    anywhere = pl.BlockSpec(memory_space=pl.ANY)
+    vmem = pltpu.VMEM
+    dma = pltpu.SemaphoreType.DMA
+    return pl.pallas_call(
+        kernel,
+        in_specs=[
+            whole(projection.shape),
+            whole(labels.shape),
+            whole(log_counts.shape),
+            whole(picks.shape),
+            anywhere,
+        ],
+        out_specs=[whole((rows, columns)), whole((2, 8, 128)), anywhere, anywhere],
+        out_shape=[
+            jax.ShapeDtypeStruct((rows, columns), BF),
+            jax.ShapeDtypeStruct((2, 8, 128), F32),
+            jax.ShapeDtypeStruct((2, docs // 2, width), BF),
+            jax.ShapeDtypeStruct((2, own // 2, width), BF),
+        ],
+        scratch_shapes=[
+            vmem((tokens, columns), BF),
+            vmem((docs, tokens), F32),
+            vmem((8, tokens), F32),
+            vmem((16, 8, tokens), F32),
+            vmem((units, 8, tokens), F32),
+            vmem((docs, tokens), BF),
+            vmem((tokens, columns), F32),
+            vmem((tokens, columns), BF),
+            vmem((16, own, columns), BF),
+            vmem((2, 2, 8, 128), F32),
+            vmem((2, 2, 8, 128), F32),
+            dma((3, 16)),
+            dma((3, 16)),
+            dma((2, 2)),
+            dma((2, 2)),
+            dma((2,)),
+            dma((2,)),
+        ],
+        compiler_params=pltpu.CompilerParams(
+            collective_id=5, has_side_effects=True, vmem_limit_bytes=40 << 20
+        ),
+        name="loss",
+        cost_estimate=pl.CostEstimate(
+            flops=100 * docs * tokens * columns,
+            bytes_accessed=2 * rows * width,
+            transcendentals=docs * tokens,
+        ),
+    )(projection, labels, log_counts, picks, y)
 
 
 class MatrixSum:
@@ -696,7 +1115,7 @@
             else:
                 at = pl.ds(pl.multiple_of(k * step, step), step)
                 to, fr = (at, pl.ds(n * block, block)), (at, pl.ds(m * block, block))
-            self.own[to] = (self.own[to].astype(F32) + ref[fr].astype(F32)).astype(BF)
+            self.own[to] = self.own[to] + ref[fr]
 
     def first_axis(self):
         for load in self.loads:
@@ -818,7 +1237,6 @@
         send_sem, recv_sem, local_sem, row_send, row_recv,
     ):
         around = Around()
-        rank, column, core, base = around.rank, around.column, around.core, around.base
         around.meet()
         send = Sender(send_sem, recv_sem)
         small = SmallSum(around, send, t_got, t_run, tensor=())
@@ -860,32 +1278,8 @@
         for item in items:
             item.begin()
 
-        lonely = 3 * core == column
-        row_copies = []
-        for q in range(2):
-            own = jnp.logical_and(lonely, core == q)
-            for kind, (begin, size, buf) in enumerate(((0, quarter, gd), (docs, asked, ga))):
-                src = rows_ref.at[pl.ds(begin + q * size, size), :]
-                dst = buf.at[column // 2]
-                away = pltpu.make_async_remote_copy(
-                    src_ref=src,
-                    dst_ref=dst,
-                    send_sem=row_send.at[q, kind],
-                    recv_sem=row_recv.at[column // 2, kind],
-                    device_id=(base + column % 2, 2 * core + q),
-                    device_id_type=MESH,
-                )
-                here = pltpu.make_async_copy(src, dst, row_send.at[q, kind])
-
-                @pl.when(own)
-                def _():
-                    here.start()
-
-                @pl.when(jnp.logical_not(own))
-                def _():
-                    away.start()
-
-                row_copies.append((own, here, away))
+        home = RowMoves(around, False, gd, ga, rows_ref, row_send, row_recv)
+        home.start()
 
         for n in range(0, len(items) + 4, 2):
             for item in items[n - 2 : n] if n >= 2 else []:
@@ -901,32 +1295,7 @@
                 if 0 <= m < len(items):
                     items[m].tensor()
 
-        for m in range(2):
-            own = jnp.logical_and(lonely, column // 2 == m)
-            for kind, buf in enumerate((gd, ga)):
-                copy = pltpu.make_async_remote_copy(
-                    src_ref=buf.at[m],
-                    dst_ref=buf.at[m],
-                    send_sem=row_send.at[m, kind],
-                    recv_sem=row_recv.at[m, kind],
-                    device_id=(rank, column),
-                    device_id_type=MESH,
-                )
-
-                @pl.when(jnp.logical_not(own))
-                def _():
-                    copy.wait_recv()
-
-        for own, here, away in row_copies:
-
-            @pl.when(own)
-            def _():
-                here.wait()
-
-            @pl.when(jnp.logical_not(own))
-            def _():
-                away.wait_send()
-
+        home.wait()
         for m in range(2):
 
             @pl.loop(0, quarter // chunk)
@@ -1011,6 +1380,7 @@
     ways = 4
     half, own_block = width // 2, width // 8
     share = up.shape[1] // ways
+    count, piece = 2 * ways, share // 2
     assert pairs == 8
 
     def kernel(
@@ -1025,15 +1395,16 @@
         around = Around()
         send = Sender(send_sem, recv_sem)
         ups, backs = [], []
-        for n in range(ways):
-            span = pl.ds(n * share, share)
+        for n in range(count):
+            span = pl.ds(n * piece, piece)
+            dt, side = n // 2, pl.ds(n % 2 * piece, piece)
             ups.append(
                 MatrixSum(
                     around, send, 0, False, ua.at[n], u0.at[n], u1.at[n], u2.at[n],
                     [(up_ref.at[half:, span], u0.at[n])],
                     [(up_ref.at[:half, span], ua.at[n])],
                     [local_sem.at[n]],
-                    [(n, (slice(0, own_block), slice(None)), u3.at[n - 1])] if n > 0 else [],
+                    [(dt, (slice(0, own_block), slice(None)), u3.at[dt - 1, :, side])] if dt else [],
                 )
             )
             backs.append(
@@ -1041,11 +1412,11 @@
                     around, send, 1, True, ba.at[n], b0.at[n], b1.at[n], b2.at[n],
                     [(back_ref.at[span, half:], b0.at[n])],
                     [(back_ref.at[span, :half], ba.at[n])],
-                    [local_sem.at[ways + n]],
-                    [(n, (slice(None), slice(0, own_block)), b3.at[n - 1])] if n > 0 else [],
+                    [local_sem.at[count + n]],
+                    [(dt, (slice(None), slice(0, own_block)), b3.at[dt - 1, side, :])] if dt else [],
                 )
             )
-        couples = [(ups[n], backs[n]) for n in (2, 3, 1, 0)]
+        couples = [(ups[n], backs[n]) for n in (4, 5, 6, 7, 2, 3, 0, 1)]
         small = SmallSum(around, send, v_got, v_run)
         mean_proj = ProjSum(around, send, proj_ref, p_run, p_got)
         gives = [send(give.at[n], got_kv.at[n], around.other(1)) for n in range(pairs)]
@@ -1075,16 +1446,16 @@
                         for item in couple:
                             item.begin()
                 else:
-                    if 0 <= step - 2 < 4:
+                    if step >= 2:
                         for item in couples[step - 2]:
                             item.second_axis()
-                    if 0 <= step - 1 < 4:
-                        for item in couples[step - 1]:
+                    for couple in couples[:2] if step == 1 else [couples[step]]:
+                        for item in couple:
                             item.first_axis()
                     if step <= 5:
                         small.hop(step - 1)
                         mean_proj.hop(step - 1)
-                    if 0 <= step - 3 < 4:
+                    if step >= 3:
                         for item in couples[step - 3]:
                             item.tensor()
                     finish(step - 1)
@@ -1170,21 +1541,25 @@
         @pl.when(h == pairs - 1)
         def _():
             finish(pairs - 1)
+            for couple in couples[6:]:
+                for item in couple:
+                    item.second_axis()
+            for couple in couples[5:]:
+                for item in couple:
+                    item.tensor()
             for couple in couples:
                 for item in couple:
                     item.settle()
-            up_o[...] = (
-                ua[0, :own_block, :].astype(F32)
-                + u3[0].astype(F32)
-                + u3[1].astype(F32)
-                + u3[2].astype(F32)
-            )
-            back_o[...] = (
-                ba[0, :, :own_block].astype(F32)
-                + b3[0].astype(F32)
-                + b3[1].astype(F32)
-                + b3[2].astype(F32)
-            )
+            for n in range(2):
+                at = pl.ds(n * piece, piece)
+                total = ua[n, :own_block, :].astype(F32)
+                for dt in range(ways - 1):
+                    total = total + u3[dt, :, at].astype(F32)
+                up_o[:, at] = total
+                total = ba[n, :, :own_block].astype(F32)
+                for dt in range(ways - 1):
+                    total = total + b3[dt, at, :].astype(F32)
+                back_o[at, :] = total
             vec_o[...] = v_run[5]
             proj_o[...] = mean_proj.result()
             send.drain()
@@ -1204,7 +1579,7 @@
         jax.ShapeDtypeStruct(vectors.shape, F32),
         jax.ShapeDtypeStruct((own_block, columns), F32),
     ]
-    count = 2 * (ways * 4 + 3) + 5 + 5 + pairs
+    slots = 2 * (count * 4 + 6) + 5 + 5 + pairs
     return pl.pallas_call(
         kernel,
         grid=(pairs,),
@@ -1232,23 +1607,23 @@
             vmem((pairs, 2, docs, 128), BF),
             vmem((2, 2, rows, 128), F32),
             vmem((pairs, 2, docs, 128), BF),
-            vmem((ways, half, share), BF),
-            vmem((ways, half, share), BF),
-            vmem((ways, 2 * own_block, share), BF),
-            vmem((ways, own_block, share), BF),
+            vmem((count, half, piece), BF),
+            vmem((count, half, piece), BF),
+            vmem((count, 2 * own_block, piece), BF),
+            vmem((count, own_block, piece), BF),
             vmem((ways - 1, own_block, share), BF),
-            vmem((ways, share, half), BF),
-            vmem((ways, share, half), BF),
-            vmem((ways, share, 2 * own_block), BF),
-            vmem((ways, share, own_block), BF),
+            vmem((count, piece, half), BF),
+            vmem((count, piece, half), BF),
+            vmem((count, piece, 2 * own_block), BF),
+            vmem((count, piece, own_block), BF),
             vmem((ways - 1, share, own_block), BF),
             vmem((5,) + vectors.shape, F32),
             vmem((6,) + vectors.shape, F32),
             vmem((width, columns), F32),
             vmem((width + 2 * own_block, columns), F32),
-            dma((count,)),
-            dma((count,)),
-            dma((2 * ways,)),
+            dma((slots,)),
+            dma((slots,)),
+            dma((2 * count,)),
         ],
         compiler_params=pltpu.CompilerParams(
             collective_id=2, has_side_effects=True, vmem_limit_bytes=60 << 20
@@ -1402,7 +1777,9 @@
         picks_rel = gather_proj(own_picks[None])
         biases = [bias_pack] + [exchange(bias_pack[None], dt=j)[0] for j in range(1, ways)]
     picks_rel = picks_rel[:, :micro, : positives.shape[1]].astype(F32)
-    own_cot = rows_in(doc_cot.astype(BF), query_cot.astype(BF))
+    cots = (doc_cot.astype(BF), query_cot.astype(BF))
+    if chips != 4:
+        own_cot = rows_in(*cots)
     bias_qkv = jnp.concatenate(
         [b[: 3 * heads_local].reshape(3, heads_local) for b in biases], axis=1
     )
@@ -1447,10 +1824,16 @@
     sines_three = jnp.stack([sine * 0.125, sine, jnp.zeros_like(sine)])
 
     x_low = dot_nn(own_x, turn).astype(BF)
-    qkv = project_heads(x_low, full_qkv, bias_qkv, cosines_three, sines_three)
-    far_kv = exchange(qkv[1:, :docs], dr=1)
+    projected = project_heads(
+        x_low, full_qkv, bias_qkv, cosines_three, sines_three, docs, chips == 4
+    )
+    qkv = projected[0]
+    far_kv = projected[1] if chips == 4 else exchange(qkv[1:, :docs], dr=1)
     label_args = (own_labels[:, None], own_labels[None, :], far_labels[None, :])
-    mixed = attention_forward(qkv, far_kv, *label_args)
+    if chips == 4:
+        mixed, own_cot = attention_forward(qkv, far_kv, *label_args, cots)
+    else:
+        (mixed,) = attention_forward(qkv, far_kv, *label_args)
     branch = dot_nn(mixed, full_out)
     resid_one = x_low.astype(F32) + branch + b_out
     normed, norm_one_pull = jax.vjp(layer_norm, resid_one, gain_one, shift_one)
@@ -1461,74 +1844,89 @@
     resid_two = normed + dot_nn(active_low, full_back) + b_back
     output, norm_two_pull = jax.vjp(layer_norm, resid_two, gain_two, shift_two)
     output_low = output.astype(BF)
-    y_doc, y_query = rows_out(dot_nt(output_low, turn).astype(BF))
+    y_low = dot_nt(output_low, turn).astype(BF)
     projection = dot_nn(output_low, full_proj)
-    unit, unit_pull = jax.vjp(normalize, projection)
-    unit_low = unit.astype(BF)
-
-    doc_unit = unit_low[:docs]
-    query_unit = unit_low[docs:]
-
-    def bit_of(dr, dt):
-        return (rank // dr) % 2 == 1 if dr else (column // dt) % 2 == 1
-
-    def join(value, dr, dt, axis=0):
-        got = exchange(value, dr=dr, dt=dt)
-        on = bit_of(dr, dt)
-        low = jnp.where(on, got, value)
-        high = jnp.where(on, value, got)
-        return jnp.concatenate([low, high], axis=axis)
-
-    def split_sum(value, dr, dt):
-        on = bit_of(dr, dt)
-        size = value.shape[0] // 2
-        send = jnp.where(on, value[:size], value[size:])
-        keep = jnp.where(on, value[size:], value[:size])
-        return keep + exchange(send.astype(BF), dr=dr, dt=dt).astype(F32)
-
-    steps = [(1, 0), (0, 1)] + [(dr, 0) for dr in chip_bits]
-    all_queries = query_unit
-    for dr, dt in steps:
-        all_queries = join(all_queries, dr, dt)
     held = jnp.arange(groups, dtype=jnp.int32)
     held = rank ^ (2 * (held % chips) + held // chips)
     order = (jnp.arange(groups, dtype=jnp.int32)[:, None] == held[None, :]).astype(F32)
     picks = jnp.where(unit_micro == 0, picks_rel[:, 0], picks_rel[:, 1])
     picks = jnp.dot(order, picks, precision=FULL_PRECISION).astype(jnp.int32).reshape(-1)
-    seg_labels = jnp.arange(segments, dtype=jnp.int32)
-    member = (own_labels[:, None] == seg_labels[None, :]).astype(F32)
-    cosines = dot_nt(doc_unit, all_queries)
-    weight = jnp.exp(TAU * (cosines - 1.0))
-    totals = jnp.einsum("js,ji->si", member, weight, precision=FULL_PRECISION)
-    totals = totals + exchange(totals, dr=1)
-    for dr, dt in steps[1:]:
-        totals = join(totals, dr, dt)
     counts = sizes_all[:, :segments].reshape(-1).astype(F32)
-    best = (jnp.log(totals) - jnp.log(counts)[:, None]) / TAU + 1.0
-    score = jnp.sum(best.reshape(best.shape[0], -1, QLEN), axis=-1)
-    logits = LOGIT_SCALE * score
-    documents = jnp.arange(logits.shape[0], dtype=jnp.int32)
-    chosen = (documents[:, None] == picks[None, :]).astype(F32)
-    peak = jnp.max(logits, axis=0, keepdims=True)
-    powers = jnp.exp(logits - peak)
-    mass = jnp.sum(powers, axis=0, keepdims=True)
-    losses = (peak + jnp.log(mass))[0] - jnp.sum(chosen * logits, axis=0)
-    logit_grad = LOGIT_SCALE * (powers / mass - chosen)
-    own_grad = lax.dynamic_slice_in_dim(logit_grad, unit_row * segments, segments, axis=0)
-    own_total = lax.dynamic_slice_in_dim(totals, unit_row * segments, segments, axis=0)
-    coef = jnp.repeat(own_grad, QLEN, axis=1) / own_total
-    spread = jnp.einsum("js,si->ji", member, coef, precision=FULL_PRECISION)
-    cosine_grad = (weight * spread).astype(BF)
-    doc_grad = dot_nn(cosine_grad, all_queries)
-    query_grad = dot_tn(cosine_grad, doc_unit)
-    for dr, dt in steps[::-1]:
-        query_grad = split_sum(query_grad, dr, dt)
-    own_losses = lax.dynamic_slice_in_dim(losses, unit_row * (4 * asked // QLEN) + core * 2 * (asked // QLEN), 2 * (asked // QLEN))
-    per = asked // QLEN
-    loss_tiles = [
-        jnp.broadcast_to(own_losses[i * per : (i + 1) * per, None], (per, 128)) for i in range(2)
-    ]
-    loss_out = quarters_out(loss_tiles[0], loss_tiles[1])[:, :, 0]
+
+    if chips == 4:
+        log_counts = jnp.pad(
+            jnp.log(counts).reshape(-1, segments), ((0, 0), (0, 8 - segments))
+        ).reshape(-1, 1)
+        proj_low, loss_out, y_doc, y_query = loss_kernel(
+            projection, own_labels[:, None], log_counts, jnp.repeat(picks, QLEN)[None], y_low
+        )
+        loss_out = loss_out[:, : asked // QLEN, 0]
+    else:
+        y_doc, y_query = rows_out(y_low)
+        unit, unit_pull = jax.vjp(normalize, projection)
+        unit_low = unit.astype(BF)
+
+        doc_unit = unit_low[:docs]
+        query_unit = unit_low[docs:]
+
+        def bit_of(dr, dt):
+            return (rank // dr) % 2 == 1 if dr else (column // dt) % 2 == 1
+
+        def join(value, dr, dt, axis=0):
+            got = exchange(value, dr=dr, dt=dt)
+            on = bit_of(dr, dt)
+            low = jnp.where(on, got, value)
+            high = jnp.where(on, value, got)
+            return jnp.concatenate([low, high], axis=axis)
+
+        def split_sum(value, dr, dt):
+            on = bit_of(dr, dt)
+            size = value.shape[0] // 2
+            send = jnp.where(on, value[:size], value[size:])
+            keep = jnp.where(on, value[size:], value[:size])
+            return keep + exchange(send.astype(BF), dr=dr, dt=dt).astype(F32)
+
+        steps = [(1, 0), (0, 1)] + [(dr, 0) for dr in chip_bits]
+        all_queries = query_unit
+        for dr, dt in steps:
+            all_queries = join(all_queries, dr, dt)
+        seg_labels = jnp.arange(segments, dtype=jnp.int32)
+        member = (own_labels[:, None] == seg_labels[None, :]).astype(F32)
+        cosines = dot_nt(doc_unit, all_queries)
+        weight = jnp.exp(TAU * (cosines - 1.0))
+        totals = jnp.einsum("js,ji->si", member, weight, precision=FULL_PRECISION)
+        totals = totals + exchange(totals, dr=1)
+        for dr, dt in steps[1:]:
+            totals = join(totals, dr, dt)
+        best = (jnp.log(totals) - jnp.log(counts)[:, None]) / TAU + 1.0
+        score = jnp.sum(best.reshape(best.shape[0], -1, QLEN), axis=-1)
+        logits = LOGIT_SCALE * score
+        documents = jnp.arange(logits.shape[0], dtype=jnp.int32)
+        chosen = (documents[:, None] == picks[None, :]).astype(F32)
+        peak = jnp.max(logits, axis=0, keepdims=True)
+        powers = jnp.exp(logits - peak)
+        mass = jnp.sum(powers, axis=0, keepdims=True)
+        losses = (peak + jnp.log(mass))[0] - jnp.sum(chosen * logits, axis=0)
+        logit_grad = LOGIT_SCALE * (powers / mass - chosen)
+        own_grad = lax.dynamic_slice_in_dim(logit_grad, unit_row * segments, segments, axis=0)
+        own_total = lax.dynamic_slice_in_dim(totals, unit_row * segments, segments, axis=0)
+        coef = jnp.repeat(own_grad, QLEN, axis=1) / own_total
+        spread = jnp.einsum("js,si->ji", member, coef, precision=FULL_PRECISION)
+        cosine_grad = (weight * spread).astype(BF)
+        doc_grad = dot_nn(cosine_grad, all_queries)
+        query_grad = dot_tn(cosine_grad, doc_unit)
+        for dr, dt in steps[::-1]:
+            query_grad = split_sum(query_grad, dr, dt)
+        own_losses = lax.dynamic_slice_in_dim(losses, unit_row * (4 * asked // QLEN) + core * 2 * (asked // QLEN), 2 * (asked // QLEN))
+        per = asked // QLEN
+        loss_tiles = [
+            jnp.broadcast_to(own_losses[i * per : (i + 1) * per, None], (per, 128)) for i in range(2)
+        ]
+        loss_out = quarters_out(loss_tiles[0], loss_tiles[1])[:, :, 0]
+
+        unit_grad = jnp.concatenate([doc_grad, query_grad], axis=0)
+        (proj_grad,) = unit_pull(unit_grad)
+        proj_low = proj_grad.astype(BF)
 
     class Reduction:
         def __init__(self, half, axis, reverse, last):
@@ -1603,9 +2001,6 @@
             r.sends = s
         return value
 
-    unit_grad = jnp.concatenate([doc_grad, query_grad], axis=0)
-    (proj_grad,) = unit_pull(unit_grad)
-    proj_low = proj_grad.astype(BF)
     out_grad = own_cot_turned = dot_nn(own_cot, turn) + dot_nt(proj_low, full_proj)
     resid_two_grad, gain_two_grad, shift_two_grad = norm_two_pull(out_grad)
     update_low = resid_two_grad.astype(BF)

time: 634 us -> 578 us (0.912)
  Pallas kernels: 349 us -> 387 us
  starting transfers between devices: 32.5 us -> 0 us
  other arithmetic: 41 us -> 17.1 us
  local copies, waits for them, and re-layouts: 51.2 us -> 32.9 us
  waiting for transfers between devices: 11.8 us -> 0 us
    pallas_call x1 -> x2, Pallas kernels: 9.82 us -> 53.9 us  [the longest x1 40.6 us: loss_kernel(): pl.pallas_call(kernel, in_specs=[whole(projection.shape), whole(labels.sh...]
    ppermute x19 -> x0, starting transfers between devices: 32.5 us -> none  [the longest x2 13.2 us: rows_in(): got.append(lax.ppermute(send, AXES, pairs))]
    pallas_call x1, Pallas kernels: 121 us -> 104 us  [attention_backward_kernel(): pl.pallas_call(kernel, grid=(pairs,), in_specs=[pl.BlockSpec((3, rows, 12...]
    ppermute x19 -> x0, waiting for transfers between devices: 11.8 us -> none  [the longest x13 6.91 us: exchange(): return lax.ppermute(value, AXES, pairs)]
    pallas_call x1, Pallas kernels: 27.4 us -> 38.9 us  [attention_forward(): pl.pallas_call(kernel, grid=(width // 128,), in_specs=[pl.BlockSpec((3, r...]
    dot_general x7 -> x6, matrix products: 41.8 us -> 47.5 us  [dot_nn(): lax.dot_general(a, b, (((1,), (0,)), ((), ())), preferred_element_type=F32)]
    dot_general x8 -> x7, matrix products: 33.7 us -> 29.5 us  [dot_tn(): lax.dot_general(a, b, (((0,), (0,)), ((), ())), preferred_element_type=F32)]
    unnamed x192 -> x152, local copies, waits for them, and re-layouts: 19.6 us -> 21.4 us
  transfers between devices with their start and end apart: 19 -> 0, of which waited for: 8 -> 0; matrix products, arithmetic and copies ran while one was open for 16% -> 0% of each run, Pallas kernels for 4% -> 0%
where the time goes in v4:
time: 578 us; the launch traced here: 572 us
  Pallas kernels  387 us (67%)
  matrix products  133 us (23%)
  local copies, waits for them, and re-layouts  32.9 us (6%)
  other arithmetic  17.1 us (3%)
    pallas_call x1, Pallas kernels, gather_kernel(): pl.pallas_call(kernel, out_shape=out_shape, in_specs=[anywhere] * (5 + co...  133 us
    pallas_call x1, Pallas kernels, attention_backward_kernel(): pl.pallas_call(kernel, grid=(pairs,), in_specs=[pl.BlockSpec((3, rows, 12...  104 us
    pallas_call x1, Pallas kernels, finish_kernel(): pl.pallas_call(kernel, out_shape=out_shape, in_specs=[anywhere] * 3 + [wh...  57.9 us
    dot_general x8, matrix products, dot_nt(): lax.dot_general(a, b, (((1,), (1,)), ((), ())), preferred_element_type=F32)  50.7 us
    dot_general x6, matrix products, dot_nn(): lax.dot_general(a, b, (((1,), (0,)), ((), ())), preferred_element_type=F32)  47.5 us
    pallas_call x1, Pallas kernels, loss_kernel(): pl.pallas_call(kernel, in_specs=[whole(projection.shape), whole(labels.sh...  40.6 us
    pallas_call x1, Pallas kernels, attention_forward(): pl.pallas_call(kernel, grid=(width // 128,), in_specs=[pl.BlockSpec((3, r...  38.9 us
    dot_general x7, matrix products, dot_tn(): lax.dot_general(a, b, (((0,), (0,)), ((), ())), preferred_element_type=F32)  29.5 us

profile of v4, /device:TPU:0, one launch (start us, length us, event | category | flops | bytes accessed | tf_op | source)
XLA Modules:
  0.0 572.0 jit_solution(11147460817897834612)
XLA Ops:
  2.7 1.1 fusion.54
  6.5 132.8 %gather_weights.1 = (bf16[576,1024]{1,0:T(8,128)(2,1)}, bf16[3,1024,1024]{2,1,0:T(8,128)(2,1)}, bf16[1024,1024]{1,0:T(8,128)(2,1)}, bf16[1024,4096]{1,0:T(8,128)...) custom-call(bf16[2,256,1024]{2,1,0:T(8,128)(2,1)} %refs_0_.1, ...), custom_call_target="tpu_custom_call" | custom-call | tf_op jit(solution)/shard_map/gather_weights/pallas_call | solution.py:804
  140.2 2.7 fusion.28.x_ref
  142.9 13.3 %project_heads.1 = (bf16[3,576,1024]{2,1,0:T(8,128)(2,1)S(1)}, bf16[2,512,1024]{2,1,0:T(8,128)(2,1)S(1)}) custom-call(bf16[576,1024]{1,0:T(8,128)(2,1)S(1)} %fusion.28.x_ref, bf16[3,1024,1024]{2,1,0:T(8,128)(2,1)} %get-tuple-element.58.w_ref, f32[3,1,1024]{2,1,0:T(1,128)S(1)} %broadcast_in_dim.34.b_ref, f32[3,576,128]{2,1,0:T(8,128)S(1)} %maximum_maximum_fusion.c_ref, ...), custom_call_target="tpu_custom_call" | custom-call | flops 3623878656 | bytes 6291456 | tf_op jit(solution)/shard_map/project_heads/pallas_call | solution.py:261
  156.2 1.8 copy-done.12
  158.0 1.3 copy-done.14
  159.5 1.9 convert_element_type.110.rest_0_
  162.3 1.6 copy-done.15
  163.9 38.9 %attend_forward.1 = (bf16[576,1024]{1,0:T(8,128)(2,1)S(1)}, bf16[576,1024]{1,0:T(8,128)(2,1)S(1)}) custom-call(bf16[3,576,1024]{2,1,0:T(8,128)(2,1)S(1)} %copy-done.13, bf16[2,512,1024]{2,1,0:T(8,128)(2,1)S(1)} %copy-done.15, s32[512,1]{1,0:T(8,128)S(1)} %copy.79.lc_ref.lab_ref, s32[1,512]{1,0:T(1,128)S(1)} %bitcast.124, s32[1,512]{1,0:T(1,128)S(1)} %bitcast.126, ...), custom_call_target="tpu_custom_call" | custom-call | flops 19327352832 | bytes 6815744 | tf_op jit(solution)/shard_map/attend_forward/pallas_call | solution.py:355
  202.8 1.0 copy-done.20
  203.9 1.4 fusion.10
  205.3 3.6 fusion.91
  209.8 29.8 %multiply_convert_fusion = (bf16[576,4096]{1,0:T(8,128)(2,1)S(1)}, f32[576,4096]{1,0:T(8,128)}, f32[576,4096]{1,0:T(8,128)}) fusion(f32[4096]{0:T(1024)S(1)} %pad_maximum_fusion.5, bf16[1024,4096]{1,0:T(8,128)(2,1)S(1)} %bitcast.174, f32[576,1024]{1,0:T(8,128)S(1)} %get-tuple-element.135, f32[1024]{0:T(1024)S(1)} %bitcast.157, f32[1024]{0:T(1024)S(1)} %bitcast.140, ...), kind=kOutput, calls=%fused_computation.4 | convolution fusion | flops 4990500864 | bytes 34370048 | tf_op jit(solution)/shard_map/dot_general | solution.py:38
  239.5 9.5 %fusion.92 = (f32[576]{0:T(1024)S(1)}, f32[576,1024]{1,0:T(8,128)S(1)}) fusion(f32[1024]{0:T(1024)S(1)} %bitcast.166, bf16[576,4096]{1,0:T(8,128)(2,1)S(1)} %get-tuple-element.104, bf16[4096,1024]{1,0:T(8,128)(2,1)} %get-tuple-element.65, f32[1024]{0:T(1024)S(1)} %bitcast.158, f32[1024]{0:T(1024)S(1)} %bitcast.141, f32[576]{0:T(1024)S(1)} %fusion.75, ...), kind=kOutput, calls=%fused_computation.183 | convolution fusion | flops 4835966464 | bytes 17844992 | tf_op jit(solution)/shard_map/dot_general | solution.py:38
  250.4 1.5 fusion.29.y_ref
  253.9 40.6 %loss.1 = (bf16[576,128]{1,0:T(8,128)(2,1)S(1)}, f32[2,8,128]{2,1,0:T(8,128)S(1)}, bf16[2,256,1024]{2,1,0:T(8,128)(2,1)S(1)}, bf16[2,32,1024]{2,1,0:T(8,128)(2,1)S(1)}) custom-call(f32[576,128]{1,0:T(8,128)S(1)} %fusion.93.p_ref, s32[512,1]{1,0:T(8,128)S(1)} %copy.79.lc_ref.lab_ref, f32[64,1]{1,0:T(8,128)S(1)} %reshape.578.cnt_ref, ...), custom_call_target="tpu_custom_call" | custom-call | flops 6710886400 | bytes 1179648 | tf_op jit(solution)/shard_map/loss/pallas_call | solution.py:1031
  294.5 1.4 fusion.94.proj_ref
  295.8 1.4 fusion.8
  297.5 1.6 multiply_reduce_fusion
  300.0 0.9 convert_reduce_fusion.1
  300.9 17.9 %convert_reduce_fusion = (f32[4096]{0:T(1024)}, bf16[576,4096]{1,0:T(8,128)(2,1)}) fusion(f32[576,4096]{1,0:T(8,128)} %get-tuple-element.105, f32[576,4096]{1,0:T(8,128)} %get-tuple-element.136, f32[4096]{0:T(1024)S(1)} %pad_maximum_fusion.5, bf16[576,1024]{1,0:T(8,128)(2,1)S(1)} %get-tuple-element.97, bf16[4096,1024]{1,0:T(8,128)(2,1)} %get-tuple-element.65), kind=kOutput, calls=%fused_computation.2 | convolution fusion | flops 4871942144 | bytes 33193984 | tf_op jit(solution)/shard_map/dot_general | solution.py:42
  318.8 10.4 %multiply_reduce_fusion.1 = (f32[1024]{0:T(1024)}, f32[576]{0:T(1024)S(1)}, f32[1024]{0:T(1024)}, f32[576,1024]{1,0:T(8,128)S(1)}) fusion(f32[576,1024]{1,0:T(8,128)S(1)} %copy-done.25, f32[576]{0:T(1024)S(1)} %fusion.75, f32[576]{0:T(1024)S(1)} %broadcast_multiply_fusion.2, f32[1024]{0:T(1024)S(1)} %bitcast.142, f32[576,1024]{1,0:T(8,128)S(1)} %get-tuple-element.103, ...), kind=kOutput, calls=%fused_computation.33 | convolution fusion | flops 4837733888 | bytes 20206592 | tf_op jit(solution)/shard_map/dot_general | solution.py:42
  330.1 1.4 copy-done.26
  331.5 0.9 convert_reduce_fusion.2
  333.0 1.4 stack.63
  334.5 3.5 fusion.7.vec_ref
  337.9 11.2 %convolution_convert_fusion.1.back_ref = bf16[4096,1024]{1,0:T(8,128)(2,1)} fusion(bf16[576,4096]{1,0:T(8,128)(2,1)} %copy-done.66, bf16[576,1024]{1,0:T(8,128)(2,1)} %copy-done.35), kind=kOutput, calls=%fused_computation.19 | convolution fusion | flops 4836032512 | bytes 14286848 | tf_op jit(solution)/shard_map/dot_general | solution.py:46
  349.1 9.6 %convolution_convert_fusion.up_ref = bf16[1024,4096]{1,0:T(8,128)(2,1)} fusion(bf16[576,4096]{1,0:T(8,128)(2,1)S(1)} %bitcast.177, f32[576,1024]{1,0:T(8,128)S(1)} %copy-done.25, f32[1024]{0:T(1024)S(1)} %bitcast.159, f32[1024]{0:T(1024)S(1)} %bitcast.144, f32[576]{0:T(1024)S(1)} %copy-done.44, f32[576]{0:T(1024)S(1)} %broadcast_multiply_fusion.2), kind=kOutput, calls=%fused_computation.18 | convolution fusion | flops 4838981632 | bytes 15479296 | tf_op jit(solution)/shard_map/dot_general | solution.py:46
  358.8 2.5 convolution_convert_fusion.6.g_ref
  361.3 1.0 pad_maximum_fusion.1.s_ref
  362.4 1.0 fusion.55
  363.3 1.0 pad_maximum_fusion.2.fs_ref
  364.3 0.9 copy.87.c_ref
  365.3 0.8 copy.88.fc_ref
  366.2 103.7 %attend_backward_and_sum.1 = (bf16[3,576,1024]{2,1,0:T(8,128)(2,1)}, f32[8,1024]{1,0:T(8,128)}, f32[128,1024]{1,0:T(8,128)}, f32[1024,128]{1,0:T(8,128)}, f32[8,1024]{1,0:T(8,128)}, /*index=5*/f32[128,128]{1,0:T(8,128)}) custom-call(bf16[3,576,1024]{2,1,0:T(8,128)(2,1)} %copy-done.12, bf16[2,512,1024]{2,1,0:T(8,128)(2,1)} %copy-done.14, ...), custom_call_target="tpu_custom_call" | custom-call | flops 60397977600 | bytes 22544384 | tf_op jit(solution)/shard_map/attend_backward_and_sum/pallas_call | solution.py:1583
  471.3 4.8 fusion.14
  476.2 4.8 fusion.12
  481.0 7.1 %fusion.30.rows_ref = bf16[576,1024]{1,0:T(8,128)(2,1)S(1)} fusion(s32[1024]{0:T(1024)S(1)} %copy-done.58, f32[576,1024]{1,0:T(8,128)} %fusion.12, f32[576,1024]{1,0:T(8,128)} %fusion.14, f32[576,1024]{1,0:T(8,128)} %copy-done.26, f32[576]{0:T(1024)S(1)} %copy-done.46, bf16[3,1024,1024]{2,1,0:T(8,128)(2,1)} %get-tuple-element.58.w_ref, ...), kind=kOutput, calls=%fused_computation.69 | convolution fusion | flops 2420506624 | bytes 11540736 | tf_op jit(solution)/shard_map/dot_general | solution.py:42
  488.2 1.8 convolution_convert_fusion.2.out_ref
  490.5 1.8 convolution_convert_fusion.5
  492.4 1.8 convolution_convert_fusion.4
  494.2 1.8 convolution_convert_fusion.3
  496.1 3.1 pad_maximum_fusion.qkv_ref
  499.2 57.9 %last_sums.1 = (f32[3,128,256]{2,1,0:T(8,128)S(1)}, f32[256,128]{1,0:T(8,128)S(1)}, f32[2,256,1024]{2,1,0:T(8,128)S(1)}, f32[2,32,1024]{2,1,0:T(8,128)S(1)}, f32[14,128]{1,0:T(8,128)S(1)}) custom-call(bf16[1024,3072]{1,0:T(8,128)(2,1)} %pad_maximum_fusion.qkv_ref, bf16[1024,1024]{1,0:T(8,128)(2,1)S(1)} %convolution_convert_fusion.2.out_ref, ...), custom_call_target="tpu_custom_call" | custom-call | tf_op jit(solution)/shard_map/last_sums/pallas_call | solution.py:1337
  559.7 1.7 fusion.88
  562.0 2.3 copy.106
  564.3 1.6 copy.107
  565.9 1.3 copy.108
  (222 shorter events, 22.8 us)
Async XLA Ops:
  1.9 159.6 %copy-start.10 = (s32[512]{0:T(512)}, s32[512]{0:T(512)S(1)}, u32[]{:S(2)}) copy-start(s32[512]{0:T(512)S(1)} %get-tuple-element.93) | copy-start | bytes 6148
  1.9 159.6 %copy-start.11 = (s32[512]{0:T(512)}, s32[512]{0:T(512)S(1)}, u32[]{:S(2)}) copy-start(s32[512]{0:T(512)S(1)} %get-tuple-element.92) | copy-start | bytes 6148
  4.9 134.5 %copy-start.27 = (f32[576,4,32]{0,2,1:T(8,128)}, f32[576,4,32]{0,2,1:T(8,128)S(1)}, u32[]{:S(2)}) copy-start(f32[576,4,32]{0,2,1:T(8,128)S(1)} %tile.20) | copy-start | bytes 884740
  140.2 63.7 %copy-start.56 = (s32[1024]{0:T(1024)}, s32[1024]{0:T(1024)S(1)}, u32[]{:S(2)}) copy-start(s32[1024]{0:T(1024)S(1)} %fusion.66) | copy-start | bytes 12292
  142.9 62.4 %copy-start.16 = (bf16[576,1024]{1,0:T(8,128)(2,1)}, bf16[576,1024]{1,0:T(8,128)(2,1)S(1)}, u32[]{:S(2)}) copy-start(bf16[576,1024]{1,0:T(8,128)(2,1)S(1)} %fusion.28.x_ref) | copy-start | bytes 3538948
  159.5 94.4 %copy-start.5 = (s32[512,1]{1,0:T(8,128)}, s32[512,1]{1,0:T(8,128)S(1)}, u32[]{:S(2)}) copy-start(s32[512,1]{1,0:T(8,128)S(1)} %copy.79.lc_ref.lab_ref) | copy-start | bytes 6148
  159.5 2.7 copy-start.13
  163.8 39.9 %copy-start.41 = (f32[1024]{0:T(1024)S(1)}, f32[1024]{0:T(1024)}, u32[]{:S(2)}) copy-start(f32[1024]{0:T(1024)} %param.30) | copy-start | bytes 12292
  163.8 39.9 %copy-start.49 = (f32[1024]{0:T(1024)S(1)}, f32[1024]{0:T(1024)}, u32[]{:S(2)}) copy-start(f32[1024]{0:T(1024)} %param.31) | copy-start | bytes 12292
  163.9 39.9 %copy-start.50 = (f32[1024]{0:T(1024)S(1)}, f32[1024]{0:T(1024)}, u32[]{:S(2)}) copy-start(f32[1024]{0:T(1024)} %param.32) | copy-start | bytes 12292
  163.9 39.9 %copy-start.51 = (f32[1024]{0:T(1024)S(1)}, f32[1024]{0:T(1024)}, u32[]{:S(2)}) copy-start(f32[1024]{0:T(1024)} %param.36) | copy-start | bytes 12292
  163.9 39.9 %copy-start.52 = (f32[1024]{0:T(1024)S(1)}, f32[1024]{0:T(1024)}, u32[]{:S(2)}) copy-start(f32[1024]{0:T(1024)} %param.37) | copy-start | bytes 12292
  163.9 39.9 %copy-start.53 = (f32[1024]{0:T(1024)S(1)}, f32[1024]{0:T(1024)}, u32[]{:S(2)}) copy-start(f32[1024]{0:T(1024)} %param.38) | copy-start | bytes 12292
  203.8 5.2 copy-start.18
  205.3 34.3 %copy-start.54 = (f32[1,1024]{1,0:T(1,128)}, f32[1,1024]{1,0:T(1,128)S(1)}, u32[]{:S(2)}) copy-start(f32[1,1024]{1,0:T(1,128)S(1)} %get-tuple-element.115) | copy-start | bytes 12292
  205.3 4.5 slice-start
  205.3 4.4 slice-start.1
  208.9 30.6 %copy-start.24 = (f32[576,1024]{1,0:T(8,128)}, f32[576,1024]{1,0:T(8,128)S(1)}, u32[]{:S(2)}) copy-start(f32[576,1024]{1,0:T(8,128)S(1)} %get-tuple-element.135) | copy-start | bytes 7077892
  209.7 119.5 %copy-start.43 = (f32[576]{0:T(1024)}, f32[576]{0:T(1024)S(1)}, u32[]{:S(2)}) copy-start(f32[576]{0:T(1024)S(1)} %fusion.75) | copy-start | bytes 6916
  239.5 9.5 %copy-start.66 = (bf16[576,4096]{1,0:T(8,128)(2,1)}, bf16[576,4096]{1,0:T(8,128)(2,1)S(1)}, u32[]{:S(2)}) copy-start(bf16[576,4096]{1,0:T(8,128)(2,1)S(1)} %get-tuple-element.104) | copy-start | bytes 14155780
  253.9 42.0 %copy-start.19 = (bf16[576,1024]{1,0:T(8,128)(2,1)S(1)}, bf16[576,1024]{1,0:T(8,128)(2,1)}, u32[]{:S(2)}) copy-start(bf16[576,1024]{1,0:T(8,128)(2,1)} %copy-done.18) | copy-start | bytes 3538948
  294.5 2.8 copy-start.2
  294.5 2.8 copy-start.7
  300.9 17.9 %copy-start.35 = (bf16[576,1024]{1,0:T(8,128)(2,1)}, bf16[576,1024]{1,0:T(8,128)(2,1)S(1)}, u32[]{:S(2)}) copy-start(bf16[576,1024]{1,0:T(8,128)(2,1)S(1)} %get-tuple-element.97) | copy-start | bytes 3538948
  300.9 17.9 %copy-start.25 = (f32[576,1024]{1,0:T(8,128)S(1)}, f32[576,1024]{1,0:T(8,128)}, u32[]{:S(2)}) copy-start(f32[576,1024]{1,0:T(8,128)} %copy-done.24) | copy-start | bytes 7077892
  332.4 26.4 %copy-start.33 = (bf16[576,1024]{1,0:T(8,128)(2,1)}, bf16[576,1024]{1,0:T(8,128)(2,1)S(1)}, u32[]{:S(2)}) copy-start(bf16[576,1024]{1,0:T(8,128)(2,1)S(1)} %get-tuple-element.99) | copy-start | bytes 3538948
  334.5 14.6 %slice-start.2 = ((s8[4718592]{0:T(1024)(128)(4,1)}), s8[4194304]{0:T(1024)(128)(4,1)S(1)}, s32[]{:S(2)}) async-start(s8[4718592]{0:T(1024)(128)(4,1)} %bitcast.176), calls=%async_computation.2 | async-start | bytes 8388608
  337.9 11.2 %copy-start.44 = (f32[576]{0:T(1024)S(1)}, f32[576]{0:T(1024)}, u32[]{:S(2)}) copy-start(f32[576]{0:T(1024)} %copy-done.43) | copy-start | bytes 6916
  337.9 11.2 %copy-start.55 = (f32[1,1024]{1,0:T(1,128)S(1)}, f32[1,1024]{1,0:T(1,128)}, u32[]{:S(2)}) copy-start(f32[1,1024]{1,0:T(1,128)} %copy-done.54) | copy-start | bytes 12292
  337.9 11.2 %slice-start.3 = ((s8[4718592]{0:T(1024)(128)(4,1)}), s8[524288]{0:T(1024)(128)(4,1)S(1)}, s32[]{:S(2)}) async-start(s8[4718592]{0:T(1024)(128)(4,1)} %bitcast.176), calls=%async_computation.3 | async-start | bytes 1048576
  349.1 9.6 %copy-start.64 = (bf16[1024,1024]{1,0:T(8,128)(2,1)S(1)}, bf16[1024,1024]{1,0:T(8,128)(2,1)}, u32[]{:S(2)}) copy-start(bf16[1024,1024]{1,0:T(8,128)(2,1)} %get-tuple-element.63) | copy-start | bytes 6291460
  358.8 2.5 copy-start.30
  358.8 2.5 copy-start.32
  358.8 3.6 copy-start.48
  358.8 3.6 copy-start.62
  361.3 3.0 copy-start.28
  366.2 104.5 %copy-start.47 = (f32[4096]{0:T(1024)S(1)}, f32[4096]{0:T(1024)}, u32[]{:S(2)}) copy-start(f32[4096]{0:T(1024)} %get-tuple-element.94) | copy-start | bytes 49156
  476.2 4.8 copy-start.46
  476.2 4.8 copy-start.58
  481.0 7.2 %copy-start.21 = (bf16[576,1024]{1,0:T(8,128)(2,1)S(1)}, bf16[576,1024]{1,0:T(8,128)(2,1)}, u32[]{:S(2)}) copy-start(bf16[576,1024]{1,0:T(8,128)(2,1)} %copy-done.20) | copy-start | bytes 3538948
  481.0 7.2 %copy-start.34 = (bf16[576,1024]{1,0:T(8,128)(2,1)S(1)}, bf16[576,1024]{1,0:T(8,128)(2,1)}, u32[]{:S(2)}) copy-start(bf16[576,1024]{1,0:T(8,128)(2,1)} %copy-done.33) | copy-start | bytes 3538948
  488.2 2.4 copy-start.65
  496.1 3.1 copy-start.6
  565.9 2.8 copy-start.9
  565.9 3.5 copy-start.38
  565.9 4.2 copy-start.37
  565.9 5.7 copy-start.1
  567.2 3.7 copy-start.40
  (23 other events, 29.9 us)

commit v5 on v4

--- a/solution.py
+++ b/solution.py
@@ -68,7 +68,7 @@
     def along(self, dt):
         return (self.rank, differing(self.column, dt, 2))
 
-    def meet(self):
+    def greet(self):
         barrier = pltpu.get_barrier_semaphore()
         for dc in range(2):
             for dt in range(4):
@@ -83,7 +83,17 @@
             pl.semaphore_signal(
                 barrier, inc=1, device_id=self.other(bit), device_id_type=MESH
             )
-        pl.semaphore_wait(barrier, 9)
+
+    def await_all(self):
+        pl.semaphore_wait(pltpu.get_barrier_semaphore(), 9)
+
+    def meet(self):
+        self.greet()
+        self.await_all()
+
+
+def feature_block(rank, p):
+    return differing(rank, 2 * (p % 4) + p // 4, 3)
 
 
 class Sender:
@@ -114,30 +124,46 @@
         core, column, base = around.core, around.column, around.base
         lonely = 3 * core == column
         self.copies, self.arrivals = [], []
-        size, few = docs.shape[1], asked.shape[1]
+        size, few, width = docs.shape[1], asked.shape[1], docs.shape[2]
+        block = width // 8
         for n in range(2):
             q, m = (column % 2, n) if inward else (n, column // 2)
             if inward:
                 mine = jnp.logical_and(lonely, column // 2 == n)
                 to = (base + column // 2, 2 * n + core)
                 here = jnp.logical_and(lonely, column % 2 == n)
+                holder = base + column // 2
             else:
                 mine = jnp.logical_and(lonely, core == n)
                 to = (base + column % 2, 2 * core + n)
                 here = jnp.logical_and(lonely, column // 2 == n)
+                holder = around.rank
+            wheres = [
+                pl.ds(pl.multiple_of(feature_block(holder, p) * block, block), block)
+                for p in range(8)
+            ]
             for kind, (ref, many, begin) in enumerate(((docs, size, 0), (asked, few, 2 * size))):
-                rows = packed.at[pl.ds(pl.multiple_of(begin + q * many, few), many), :]
-                src, dst = (ref.at[m], rows) if inward else (rows, ref.at[m])
-                away = pltpu.make_async_remote_copy(
-                    src_ref=src,
-                    dst_ref=dst,
-                    send_sem=send_sem.at[n, kind],
-                    recv_sem=recv_sem.at[q if inward else m, kind],
-                    device_id=to,
-                    device_id_type=MESH,
-                )
-                local = pltpu.make_async_copy(src, dst, send_sem.at[n, kind])
-                self.copies.append((mine, local, away))
+                span = pl.ds(pl.multiple_of(begin + q * many, few), many)
+                aways, locals_ = [], []
+                for p in list(range(8)) + [None]:
+                    if p is None:
+                        rows, flat = packed.at[span, :], ref.at[m]
+                    else:
+                        rows = packed.at[span, pl.ds(p * block, block)]
+                        flat = ref.at[m, :, wheres[p]]
+                    src, dst = (flat, rows) if inward else (rows, flat)
+                    aways.append(
+                        pltpu.make_async_remote_copy(
+                            src_ref=src,
+                            dst_ref=dst,
+                            send_sem=send_sem.at[n, kind],
+                            recv_sem=recv_sem.at[q if inward else m, kind],
+                            device_id=to,
+                            device_id_type=MESH,
+                        )
+                    )
+                    locals_.append(pltpu.make_async_copy(src, dst, send_sem.at[n, kind]))
+                self.copies.append((mine, locals_, aways))
                 if inward:
                     land = packed.at[pl.ds(begin + n * many, many), :]
                 else:
@@ -153,15 +179,17 @@
                 self.arrivals.append((here, came))
 
     def start(self):
-        for mine, local, away in self.copies:
+        for mine, locals_, aways in self.copies:
 
             @pl.when(mine)
-            def _(local=local):
-                local.start()
+            def _(locals_=locals_):
+                for copy in locals_[:8]:
+                    copy.start()
 
             @pl.when(jnp.logical_not(mine))
-            def _(away=away):
-                away.start()
+            def _(aways=aways):
+                for copy in aways[:8]:
+                    copy.start()
 
     def wait(self):
         for here, came in self.arrivals:
@@ -170,15 +198,269 @@
             def _(came=came):
                 came.wait_recv()
 
-        for mine, local, away in self.copies:
+        for mine, locals_, aways in self.copies:
 
             @pl.when(mine)
-            def _(local=local):
-                local.wait()
+            def _(locals_=locals_):
+                locals_[8].wait()
 
             @pl.when(jnp.logical_not(mine))
-            def _(away=away):
-                away.wait_send()
+            def _(aways=aways):
+                aways[8].wait_send()
+
+
+class WeightGather:
+    slots = 31
+
+    def __init__(
+        self, around, sources, outs, feature_axis, tensor_axis, bits, send_sem, recv_sem, local_sem
+    ):
+        self.around, self.sources, self.outs = around, sources, outs
+        self.feature_axis, self.tensor_axis, self.bits = feature_axis, tensor_axis, bits
+        self.send_sem, self.recv_sem, self.local_sem = send_sem, recv_sem, local_sem
+        self.all = range(len(sources))
+
+    def place(self, j):
+        return (j & 1) * 4 + (j >> 1)
+
+    def line(self, a, j):
+        index = [slice(None)] * len(self.sources[a].shape)
+        size = self.sources[a].shape[self.feature_axis[a]]
+        index[self.feature_axis[a]] = pl.ds(self.place(j) * size, size)
+        return self.outs[a].at[tuple(index)]
+
+    def piece(self, a, j, source, column=None):
+        column = self.around.column if column is None else column
+        index = [slice(None)] * len(self.sources[a].shape)
+        size = self.sources[a].shape[self.feature_axis[a]]
+        index[self.feature_axis[a]] = pl.ds(self.place(j) * size, size)
+        size = self.sources[a].shape[self.tensor_axis[a]]
+        offset = pl.multiple_of(differing(column, source, 2) * size, size)
+        index[self.tensor_axis[a]] = pl.ds(offset, size)
+        return self.outs[a].at[tuple(index)]
+
+    def origin(self, kind):
+        column = self.around.column
+        if kind == 0:
+            return column, None
+        if kind <= 3:
+            return column - kind, column >= kind
+        return column + (kind - 3), column + (kind - 3) <= 3
+
+    def describe(self, a, slot):
+        around, column = self.around, self.around.column
+        first, second = self.bits[a]
+        if slot >= 27:
+            j = (0, first, second, first | second)[slot - 27]
+            return None, self.line(a, j), self.line(a, j | 1), around.other(1)
+        if slot < 6:
+            kind = slot if slot < 3 else (0 if slot == 3 else slot)
+            to = column + 1 if slot < 3 else column - 1
+            edge = column < 3 if slot < 3 else column > 0
+            source, there = self.origin(kind)
+            there = edge if there is None else jnp.logical_and(there, edge)
+            src = self.sources[a] if kind == 0 else self.piece(a, 0, source)
+            return there, src, self.piece(a, 0, source, to), (around.rank, to)
+        kind = (slot - 6) % 7
+        source, there = self.origin(kind)
+        if slot < 20:
+            bit = first if slot < 13 else second
+            src = self.sources[a] if kind == 0 else self.piece(a, 0, source)
+            return there, src, self.piece(a, bit, source), around.other(bit)
+        src, dst = self.piece(a, first, source), self.piece(a, first | second, source)
+        return there, src, dst, around.other(second)
+
+    def landing(self, a, slot):
+        first, second = self.bits[a]
+        if slot >= 27:
+            return None, self.line(a, (0, first, second, first | second)[slot - 27] | 1)
+        if slot < 6:
+            kind, j = (slot + 1, 0)
+        else:
+            kind, j = (slot - 6) % 7, (first, second, first | second)[(slot - 6) // 7]
+        source, there = self.origin(kind)
+        return there, self.piece(a, j, source)
+
+    def copy(self, a, slot, src, dst, to):
+        return pltpu.make_async_remote_copy(
+            src_ref=src,
+            dst_ref=dst,
+            send_sem=self.send_sem.at[a, slot],
+            recv_sem=self.recv_sem.at[a, slot],
+            device_id=to,
+            device_id_type=MESH,
+        )
+
+    def when(self, condition, act):
+        if condition is None:
+            act()
+        else:
+            pl.when(condition)(act)
+
+    def start(self, a, slot):
+        condition, src, dst, to = self.describe(a, slot)
+        self.when(condition, lambda: self.copy(a, slot, src, dst, to).start())
+
+    def sent(self, a, slot):
+        condition, src, dst, to = self.describe(a, slot)
+        self.when(condition, lambda: self.copy(a, slot, src, dst, to).wait_send())
+
+    def arrived(self, a, slot):
+        condition, dst = self.landing(a, slot)
+        to = self.around.other(1)
+        self.when(condition, lambda: self.copy(a, slot, dst, dst, to).wait_recv())
+
+    def home(self, a):
+        return pltpu.make_async_copy(
+            self.sources[a], self.piece(a, 0, self.around.column), self.local_sem.at[a]
+        )
+
+    def begin(self):
+        for a in self.all:
+            for slot in (0, 3, 6, 13):
+                self.start(a, slot)
+        for a in self.all:
+            self.home(a).start()
+
+    def onward(self, a, kind):
+        self.arrived(a, 6 + kind)
+        self.start(a, 20 + kind)
+
+    def hop(self, n):
+        for a in self.all:
+            for kind, slot in ((n, n - 1), (n + 3, n + 2)):
+                self.arrived(a, slot)
+                if n < 3:
+                    self.start(a, slot + 1)
+                self.start(a, 6 + kind)
+                self.start(a, 13 + kind)
+        for a in self.all:
+            for kind in (0,) if n == 1 else (n - 1, n + 2):
+                self.onward(a, kind)
+
+    def finish(self):
+        for a in self.all:
+            self.home(a).wait()
+            self.start(a, 27)
+        for a in self.all:
+            for kind in (3, 6):
+                self.onward(a, kind)
+            self.start(a, 28)
+        for begin, slot in ((13, 29), (20, 30)):
+            for a in self.all:
+                for kind in range(7):
+                    self.arrived(a, begin + kind)
+                self.start(a, slot)
+        for a in self.all:
+            for slot in range(27, 31):
+                self.arrived(a, slot)
+            for slot in range(31):
+                self.sent(a, slot)
+
+
+def gathered(weight, feature_axis, tensor_axis):
+    shape = list(weight.shape)
+    shape[feature_axis] *= 8
+    shape[tensor_axis] *= 4
+    return jax.ShapeDtypeStruct(tuple(shape), weight.dtype)
+
+
+def gather_kernel(x_doc, x_query, qkv, out, proj, bias, picks):
+    ways, groups = 4, 8
+    quarter, width = x_doc.shape[1:]
+    asked = x_query.shape[1]
+
+    def kernel(
+        xd_ref, xq_ref, qkv_ref, out_ref, proj_ref, bias_ref, picks_ref,
+        x_o, qkv_o, out_o, proj_o, bias_o, picks_o,
+        send_sem, recv_sem, small_send, small_recv, x_send, x_recv, local_sem,
+    ):
+        around = Around()
+        around.meet()
+        other, along = around.other, around.along
+        gather = WeightGather(
+            around,
+            [qkv_ref.at[0:2], qkv_ref.at[2:3], out_ref],
+            [qkv_o.at[0:2], qkv_o.at[2:3], out_o],
+            [1, 1, 1],
+            [2, 2, 0],
+            [(2, 4), (4, 2), (4, 2)],
+            send_sem,
+            recv_sem,
+            local_sem,
+        )
+        moves = RowMoves(around, True, xd_ref, xq_ref, x_o, x_send, x_recv)
+        send = Sender(small_send, small_recv)
+        gather.begin()
+        place = gather.place
+        small = [send(bias_ref, bias_o.at[dt], along(dt)) for dt in range(1, ways)]
+        local = [pltpu.make_async_copy(bias_ref, bias_o.at[0], local_sem.at[3])]
+        flat = []
+        for n, (ref, o) in enumerate(((proj_ref, proj_o), (picks_ref, picks_o))):
+            local.append(pltpu.make_async_copy(ref, o.at[0], local_sem.at[4 + n]))
+            flat.append(
+                (
+                    send(ref, o.at[place(2)], other(2)),
+                    send(ref, o.at[place(4)], other(4)),
+                    send(ref, o.at[place(1)], other(1)),
+                    send(o.at[place(2)], o.at[place(6)], other(4)),
+                    send(o.at[place(2)], o.at[place(3)], other(1)),
+                    send(o.at[place(4)], o.at[place(5)], other(1)),
+                    send(o.at[place(6)], o.at[place(7)], other(1)),
+                )
+            )
+        for copy in small + local + [c for f in flat for c in f[:3]]:
+            copy.start()
+        gather.hop(1)
+        moves.start()
+        for f in flat:
+            f[0].wait_recv()
+            f[3].start()
+            f[4].start()
+            f[1].wait_recv()
+            f[5].start()
+        gather.hop(2)
+        gather.hop(3)
+        for f in flat:
+            f[3].wait_recv()
+            f[6].start()
+        gather.finish()
+        for f in flat:
+            for n in (2, 4, 5, 6):
+                f[n].wait_recv()
+        for copy in small:
+            copy.wait_recv()
+        for copy in local:
+            copy.wait()
+        moves.wait()
+        send.drain()
+
+    anywhere = pl.BlockSpec(memory_space=pl.ANY)
+    dma = pltpu.SemaphoreType.DMA
+    return pl.pallas_call(
+        kernel,
+        out_shape=[
+            jax.ShapeDtypeStruct((2 * (quarter + asked), width), x_doc.dtype),
+            gathered(qkv, 1, 2),
+            gathered(out, 1, 0),
+            jax.ShapeDtypeStruct((groups,) + proj.shape, proj.dtype),
+            jax.ShapeDtypeStruct((ways,) + bias.shape, bias.dtype),
+            jax.ShapeDtypeStruct((groups,) + picks.shape, picks.dtype),
+        ],
+        in_specs=[anywhere] * 7,
+        out_specs=[anywhere] * 6,
+        scratch_shapes=[
+            dma((3, WeightGather.slots)),
+            dma((3, WeightGather.slots)),
+            dma((17,)),
+            dma((17,)),
+            dma((2, 2)),
+            dma((2, 2)),
+            dma((6,)),
+        ],
+        compiler_params=pltpu.CompilerParams(collective_id=0, has_side_effects=True),
+        name="gather_weights",
+    )(x_doc, x_query, qkv, out, proj, bias, picks)
 
 
 def turned(values):
@@ -188,116 +470,41 @@
     return jnp.where(lane % HEAD_WIDTH < HEAD_WIDTH // 2, ahead, behind)
 
 
-def project_heads(x, weights, bias, cosine, sine, docs, remote):
+def project_heads(x, weights, bias, cosine, sine):
     rows, width = x.shape
     columns = 256
     steps = width // columns
 
-    def kernel(x_ref, w_ref, b_ref, c_ref, s_ref, o_ref, *rest):
-        j, n = pl.program_id(0), pl.program_id(1)
+    def kernel(x_ref, w_ref, b_ref, c_ref, s_ref, o_ref):
         got = dot_nn(x_ref[...], w_ref[0]) + b_ref[0]
-        low = []
         for at in range(0, columns, 128):
             piece = got[:, at : at + 128]
-            low.append((piece * c_ref[0] + turned(piece) * s_ref[0]).astype(BF))
-            o_ref[0, :, at : at + 128] = low[-1]
-        if not remote:
-            return
-        far_ref, held, send_sem, recv_sem = rest
-        rank, column = lax.axis_index("dp"), lax.axis_index("tensor")
-        sibling = (rank + 1 - 2 * (rank % 2), column)
-        copies = [
-            pltpu.make_async_remote_copy(
-                src_ref=held.at[i, m],
-                dst_ref=far_ref.at[i, :, pl.ds(m * columns, columns)],
-                send_sem=send_sem.at[i, m],
-                recv_sem=recv_sem.at[i, m],
-                device_id=sibling,
-                device_id_type=MESH,
-            )
-            for i in range(2)
-            for m in range(steps)
-        ]
-
-        @pl.when(jnp.logical_and(j == 0, n == 0))
-        def _():
-            barrier = pltpu.get_barrier_semaphore()
-            pl.semaphore_signal(barrier, inc=1, device_id=sibling, device_id_type=MESH)
-            pl.semaphore_wait(barrier, 1)
-
-        for i in range(2):
-            for m in range(steps):
-
-                @pl.when(jnp.logical_and(j == i, n == m))
-                def _(i=i, m=m):
-                    for at, piece in enumerate(low):
-                        held[i, m, :, at * 128 : (at + 1) * 128] = piece[:docs]
-                    copies[i * steps + m].start()
-
-        @pl.when(jnp.logical_and(j == 2, n == steps - 1))
-        def _():
-            for copy in copies:
-                copy.wait()
-
-    order = lambda j: (j + 1) % 3
-    out_specs = [pl.BlockSpec((1, rows, columns), lambda j, n: (order(j), 0, n))]
-    out_shape = [jax.ShapeDtypeStruct((3, rows, width), BF)]
-    extra = {}
-    if remote:
-        out_specs.append(pl.BlockSpec(memory_space=pl.ANY))
-        out_shape.append(jax.ShapeDtypeStruct((2, docs, width), BF))
-        extra = dict(
-            scratch_shapes=[
-                pltpu.VMEM((2, steps, docs, columns), BF),
-                pltpu.SemaphoreType.DMA((2, steps)),
-                pltpu.SemaphoreType.DMA((2, steps)),
-            ]
-        )
-        params = pltpu.CompilerParams(
-            vmem_limit_bytes=40 << 20, collective_id=3, has_side_effects=True
-        )
-    else:
-        params = pltpu.CompilerParams(vmem_limit_bytes=40 << 20)
+            o_ref[0, :, at : at + 128] = (piece * c_ref[0] + turned(piece) * s_ref[0]).astype(BF)
+
     return pl.pallas_call(
         kernel,
         grid=(3, steps),
         in_specs=[
             pl.BlockSpec((rows, width), lambda j, n: (0, 0)),
-            pl.BlockSpec((1, width, columns), lambda j, n: (order(j), 0, n)),
-            pl.BlockSpec((1, 1, columns), lambda j, n: (order(j), 0, n)),
-            pl.BlockSpec((1, rows, 128), lambda j, n: (order(j), 0, 0)),
-            pl.BlockSpec((1, rows, 128), lambda j, n: (order(j), 0, 0)),
+            pl.BlockSpec((1, width, columns), lambda j, n: (j, 0, n)),
+            pl.BlockSpec((1, 1, columns), lambda j, n: (j, 0, n)),
+            pl.BlockSpec((1, rows, 128), lambda j, n: (j, 0, 0)),
+            pl.BlockSpec((1, rows, 128), lambda j, n: (j, 0, 0)),
         ],
-        out_specs=out_specs,
-        out_shape=out_shape,
-        compiler_params=params,
+        out_specs=pl.BlockSpec((1, rows, columns), lambda j, n: (j, 0, n)),
+        out_shape=jax.ShapeDtypeStruct((3, rows, width), BF),
+        compiler_params=pltpu.CompilerParams(vmem_limit_bytes=40 << 20),
         name="project_heads",
-        cost_estimate=pl.CostEstimate(
-            flops=6 * rows * width * width, bytes_accessed=6 * width * width, transcendentals=0
-        ),
-        **extra,
     )(x, weights, bias[:, None, :], cosine, sine)
 
 
-def attention_forward(qkv, far_kv, col_labels, own_labels, far_labels, cots=None):
+def attention_forward(qkv, far_kv, col_labels, own_labels, far_labels):
     rows, width = qkv.shape[1:]
     docs = far_kv.shape[1]
     block = 128
     asked = rows - docs
 
-    def kernel(qkv_ref, far_ref, lc_ref, lo_ref, lf_ref, *rest):
-        if cots is None:
-            (o_ref,) = rest
-        else:
-            cd_ref, cq_ref, o_ref, c_ref, send_sem, recv_sem = rest
-            around = Around()
-            moves = RowMoves(around, True, cd_ref, cq_ref, c_ref, send_sem, recv_sem)
-
-            @pl.when(pl.program_id(0) == 0)
-            def _():
-                around.meet()
-                moves.start()
-
+    def kernel(qkv_ref, far_ref, lc_ref, lo_ref, lf_ref, o_ref):
         lane = lax.broadcasted_iota(jnp.int32, (1, 128), 1)
 
         def part(start, size, keys, sames):
@@ -333,23 +540,6 @@
         row = lax.broadcasted_iota(jnp.int32, (asked, asked), 0) // QLEN
         col = lax.broadcasted_iota(jnp.int32, (asked, asked), 1) // QLEN
         part(docs, asked, [(qkv_ref[1, docs:, :], qkv_ref[2, docs:, :])], [row == col])
-        if cots is not None:
-
-            @pl.when(pl.program_id(0) == width // 128 - 1)
-            def _():
-                moves.wait()
-
-    in_more, out_more, shape_more, extra = [], [], [], {}
-    params = pltpu.CompilerParams(vmem_limit_bytes=40 << 20)
-    if cots is not None:
-        anywhere = pl.BlockSpec(memory_space=pl.ANY)
-        in_more, out_more = [anywhere, anywhere], [anywhere]
-        shape_more = [jax.ShapeDtypeStruct((rows, cots[0].shape[2]), cots[0].dtype)]
-        dma = pltpu.SemaphoreType.DMA
-        extra = dict(scratch_shapes=[dma((2, 2)), dma((2, 2))])
-        params = pltpu.CompilerParams(
-            vmem_limit_bytes=40 << 20, collective_id=4, has_side_effects=True
-        )
 
     whole = lambda shape: pl.BlockSpec(shape, lambda h: (0, 0))
     return pl.pallas_call(
@@ -361,19 +551,17 @@
             whole((docs, 1)),
             whole((1, docs)),
             whole((1, docs)),
-        ]
-        + in_more,
-        out_specs=[pl.BlockSpec((rows, 128), lambda h: (0, h))] + out_more,
-        out_shape=[jax.ShapeDtypeStruct((rows, width), BF)] + shape_more,
-        compiler_params=params,
+        ],
+        out_specs=pl.BlockSpec((rows, 128), lambda h: (0, h)),
+        out_shape=jax.ShapeDtypeStruct((rows, width), BF),
+        compiler_params=pltpu.CompilerParams(vmem_limit_bytes=40 << 20),
         name="attend_forward",
         cost_estimate=pl.CostEstimate(
             flops=32 * rows * 2 * docs * width,
             bytes_accessed=2 * (4 * rows + 2 * docs) * width,
             transcendentals=rows * 2 * docs * width // 64,
         ),
-        **extra,
-    )(qkv, far_kv, col_labels, own_labels, far_labels, *(cots or ()))
+    )(qkv, far_kv, col_labels, own_labels, far_labels)
 
 
 def attention_backward(
@@ -498,331 +686,289 @@
     )
 
 
-def gather_kernel(x_doc, x_query, qkv, out, up, back, proj, bias, picks):
-    chips, ways = 4, 4
-    groups = 2 * chips
-    weights = [qkv, out, up, back]
-    feature_axis = [1, 1, 0, 1]
-    tensor_axis = [2, 0, 1, 0]
-    first_bits = [(2, 4), (4, 2), (2, 4), (4, 2)]
-    count = len(weights)
-    quarter, width = x_doc.shape[1:]
-    asked = x_query.shape[1]
-    docs = 2 * quarter
-    slots = 32
-
-    def place(j):
-        return (j & 1) * chips + (j >> 1)
-
-    def kernel(*refs):
-        xd_ref, xq_ref = refs[:2]
-        sources = refs[2 : 2 + count]
-        proj_ref, bias_ref, picks_ref = refs[2 + count : 5 + count]
-        x_out = refs[5 + count]
-        outs = refs[6 + count : 6 + 2 * count]
-        proj_out, bias_out, picks_out = refs[6 + 2 * count : 9 + 2 * count]
-        send_sem, recv_sem, small_send, small_recv, x_send, x_recv, local_sem = refs[9 + 2 * count :]
-        rank = lax.axis_index("dp")
-        column = lax.axis_index("tensor")
-        core = rank % 2
-        base = rank - core
-
-        def other(bit):
-            return rank + bit - 2 * bit * ((rank // bit) % 2)
-
-        barrier = pltpu.get_barrier_semaphore()
-        for dc in range(2):
-            for dt in range(4):
-                if dc + dt > 0:
-                    pl.semaphore_signal(
-                        barrier,
-                        inc=1,
-                        device_id=(base + (core + dc) % 2, (column + dt) % 4),
-                        device_id_type=MESH,
-                    )
-        for bit in (2, 4):
-            pl.semaphore_signal(
-                barrier, inc=1, device_id=(other(bit), column), device_id_type=MESH
+def project_and_attend(
+    x, weights, bias, cosines, sines, col_labels, own_labels, far_labels,
+    doc_cot, query_cot, up, back,
+):
+    rows, width = x.shape
+    docs = col_labels.shape[0]
+    asked = rows - docs
+    pairs = width // 128
+    block = 256
+    columns = 256
+    steps = width // columns
+    assert pairs == 8
+
+    def kernel(
+        x_ref, w_ref, b_ref, c_ref, s_ref, lc_ref, lo_ref, lf_ref,
+        cd_ref, cq_ref, up_ref, back_ref,
+        qkv_o, far_o, o_ref, cot_o, up_o, back_o,
+        held, far, load_sem, far_send, far_recv, row_send, row_recv, send_sem, recv_sem, local_sem,
+    ):
+        h = pl.program_id(0)
+
+        def parts():
+            around = Around()
+            moves = RowMoves(around, True, cd_ref, cq_ref, cot_o, row_send, row_recv)
+            gather = WeightGather(
+                around,
+                [up_ref, back_ref],
+                [up_o, back_o],
+                [0, 1],
+                [1, 0],
+                [(2, 4), (4, 2)],
+                send_sem,
+                recv_sem,
+                local_sem,
             )
-        pl.semaphore_wait(barrier, 9)
-
-        local = []
-
-        def keep(src, dst):
-            copy = pltpu.make_async_copy(src, dst, local_sem.at[len(local)])
-            copy.start()
-            local.append(copy)
-
-        lonely = 3 * core == column
-        x_copies = []
-        for m in range(2):
-            mine = jnp.logical_and(lonely, column // 2 == m)
-            q = column % 2
-            for kind, (ref, size, begin) in enumerate(((xd_ref, quarter, 0), (xq_ref, asked, docs))):
-                src = ref.at[m]
-                dst = x_out.at[pl.ds(pl.multiple_of(begin + q * size, 32), size), :]
-                away = pltpu.make_async_remote_copy(
-                    src_ref=src,
-                    dst_ref=dst,
-                    send_sem=x_send.at[m, kind],
-                    recv_sem=x_recv.at[q, kind],
-                    device_id=(base + column // 2, 2 * m + core),
-                    device_id_type=MESH,
+            return around, moves, gather
+
+        @pl.when(h == 0)
+        def _():
+            loads = [pltpu.make_async_copy(w_ref.at[j], held.at[j], load_sem.at[j]) for j in range(3)]
+            for j in (1, 2, 0):
+                loads[j].start()
+            around, _, gather = parts()
+            around.meet()
+            gather.begin()
+            copies = []
+            for j in (1, 2, 0):
+                loads[j].wait()
+                for n in range(steps):
+                    at = pl.ds(n * columns, columns)
+                    got = dot_nn(x_ref[...], held[j, :, at]) + b_ref[j : j + 1, at]
+                    for m in range(columns // 128):
+                        piece = got[:, m * 128 : (m + 1) * 128]
+                        low = piece * c_ref[j] + turned(piece) * s_ref[j]
+                        qkv_o[j, :, n * columns + m * 128 : n * columns + (m + 1) * 128] = low.astype(BF)
+                    if j > 0:
+                        copy = pltpu.make_async_remote_copy(
+                            src_ref=qkv_o.at[j, pl.ds(0, docs), at],
+                            dst_ref=far.at[j - 1, :, at],
+                            send_sem=far_send.at[j - 1, n],
+                            recv_sem=far_recv.at[j - 1, n],
+                            device_id=around.other(1),
+                            device_id_type=MESH,
+                        )
+                        copy.start()
+                        copies.append(copy)
+            for copy in copies:
+                copy.wait()
+            pltpu.make_async_copy(far, far_o, load_sem.at[3]).start()
+
+        @pl.when(h == 1)
+        def _():
+            parts()[2].hop(1)
+
+        @pl.when(h == 4)
+        def _():
+            _, moves, gather = parts()
+            gather.hop(2)
+            moves.start()
+
+        @pl.when(h == 7)
+        def _():
+            parts()[2].hop(3)
+
+        lane = lax.broadcasted_iota(jnp.int32, (1, 128), 1)
+        pair = pl.ds(pl.multiple_of(h * 128, 128), 128)
+
+        def part(start, size, keys, sames):
+            q_block = qkv_o[0, pl.ds(start, size), pair]
+            outs = []
+            for head in range(2):
+                mask = (lane // HEAD_WIDTH) == head
+                q_head = jnp.where(mask, q_block, jnp.zeros_like(q_block))
+                scores = [
+                    jnp.where(same, dot_nt(q_head, key), MASKED)
+                    for (key, _), same in zip(keys, sames)
+                ]
+                top = functools.reduce(
+                    jnp.maximum, [jnp.max(s, axis=-1, keepdims=True) for s in scores]
                 )
-                here = pltpu.make_async_copy(src, dst, x_send.at[m, kind])
-
-                @pl.when(mine)
-                def _():
-                    here.start()
-
-                @pl.when(jnp.logical_not(mine))
-                def _():
-                    away.start()
-
-                x_copies.append((mine, here, away))
-
-        waits = []
-
-        def remote(a, slot, src, dst, to):
-            return pltpu.make_async_remote_copy(
-                src_ref=src,
-                dst_ref=dst,
-                send_sem=send_sem.at[a, slot],
-                recv_sem=recv_sem.at[a, slot],
-                device_id=to,
-                device_id_type=MESH,
-            )
-
-        def piece(a, j, source, at=None):
-            at = column if at is None else at
-            index = [slice(None)] * len(sources[a].shape)
-            size = sources[a].shape[feature_axis[a]]
-            index[feature_axis[a]] = pl.ds(place(j) * size, size)
-            size = sources[a].shape[tensor_axis[a]]
-            offset = pl.multiple_of(differing(at, source, 2) * size, size)
-            index[tensor_axis[a]] = pl.ds(offset, size)
-            return outs[a].at[tuple(index)]
-
-        def line(a, j):
-            index = [slice(None)] * len(sources[a].shape)
-            size = sources[a].shape[feature_axis[a]]
-            index[feature_axis[a]] = pl.ds(place(j) * size, size)
-            return outs[a].at[tuple(index)]
-
-        def go(copy, condition):
-            if condition is None:
-                copy.start()
-            else:
-
-                @pl.when(condition)
-                def _():
-                    copy.start()
-
-            waits.append((condition, copy))
-
-        def origin(kind):
-            if kind == 0:
-                return column, None
-            if kind <= 3:
-                return column - kind, column >= kind
-            return column + (kind - 3), column + (kind - 3) <= 3
-
-        def both(x, y):
-            if x is None:
-                return y
-            return x if y is None else jnp.logical_and(x, y)
-
-        def spread(a, kind):
-            source, there = origin(kind)
-            first, second = first_bits[a]
-            src = sources[a] if kind == 0 else piece(a, 0, source)
-            go(remote(a, 6 + kind, src, piece(a, first, source), (other(first), column)), there)
-            go(remote(a, 13 + kind, src, piece(a, second, source), (other(second), column)), there)
-
-        def along(a, kind):
-            source, there = origin(kind)
-            src = sources[a] if kind == 0 else piece(a, 0, source)
-            hops = kind if kind <= 3 else kind - 3
-            if kind <= 3 and hops < 3:
-                dst = piece(a, 0, source, column + 1)
-                go(remote(a, hops, src, dst, (rank, column + 1)), both(there, column < 3))
-            if (kind == 0 or kind > 3) and hops < 3:
-                dst = piece(a, 0, source, column - 1)
-                go(remote(a, 3 + hops, src, dst, (rank, column - 1)), both(there, column > 0))
-
-        def arrived(a, slot, dst, condition):
-            copy = remote(a, slot, dst, dst, (rank, column))
-            if condition is None:
-                copy.wait_recv()
-            else:
-
-                @pl.when(condition)
-                def _():
-                    copy.wait_recv()
-
-        def onward(a, kind):
-            source, there = origin(kind)
-            first, second = first_bits[a]
-            src = piece(a, first, source)
-            arrived(a, 6 + kind, src, there)
-            dst = piece(a, first | second, source)
-            go(remote(a, 20 + kind, src, dst, (other(second), column)), there)
-
-        small = []
-
-        def tiny(src, dst, to):
-            at = len(small)
-            copy = pltpu.make_async_remote_copy(
-                src_ref=src,
-                dst_ref=dst,
-                send_sem=small_send.at[at],
-                recv_sem=small_recv.at[at],
-                device_id=to,
-                device_id_type=MESH,
-            )
-            copy.start()
-            small.append(copy)
-            return copy
-
-        for a in range(count):
-            along(a, 0)
-            spread(a, 0)
-        for a in range(count):
-            keep(sources[a], piece(a, 0, column))
-        keep(bias_ref, bias_out.at[0])
-        for dt in range(1, 4):
-            to = differing(column, dt, 2)
-            tiny(bias_ref, bias_out.at[dt], (rank, to))
-        flat = []
-        for ref, out_ref in ((proj_ref, proj_out), (picks_ref, picks_out)):
-            keep(ref, out_ref.at[0])
-            flat.append(
-                (
-                    tiny(ref, out_ref.at[place(2)], (other(2), column)),
-                    tiny(ref, out_ref.at[place(4)], (other(4), column)),
-                    tiny(ref, out_ref.at[place(1)], (other(1), column)),
-                    out_ref,
+                powers = [jnp.exp(s - top) for s in scores]
+                total = functools.reduce(
+                    jnp.add, [jnp.sum(p, axis=-1, keepdims=True) for p in powers]
                 )
-            )
-
-        for hops in range(1, 4):
-            for a in range(count):
-                for kind in (hops, hops + 3):
-                    source, there = origin(kind)
-                    slot = hops - 1 if kind <= 3 else 2 + hops
-                    arrived(a, slot, piece(a, 0, source), there)
-                    along(a, kind)
-                    spread(a, kind)
-            kinds = (0,) if hops == 1 else (hops - 1, hops + 2)
-            for a in range(count):
-                for kind in kinds:
-                    onward(a, kind)
-        for copy in local:
-            copy.wait()
-
-        def sibling(a, slot, j):
-            go(remote(a, slot, line(a, j), line(a, j | 1), (other(1), column)), None)
-
-        for a in range(count):
-            sibling(a, 27, 0)
-        for by_two, by_four, _, out_ref in flat:
-            by_two.wait_recv()
-            tiny(out_ref.at[place(2)], out_ref.at[place(6)], (other(4), column))
-            tiny(out_ref.at[place(2)], out_ref.at[place(3)], (other(1), column))
-            by_four.wait_recv()
-            tiny(out_ref.at[place(4)], out_ref.at[place(5)], (other(1), column))
-        for a in range(count):
-            for kind in (3, 6):
-                onward(a, kind)
-            sibling(a, 28, first_bits[a][0])
-        for n, (_, _, _, out_ref) in enumerate(flat):
-            small[9 + 3 * n].wait_recv()
-            tiny(out_ref.at[place(6)], out_ref.at[place(7)], (other(1), column))
-        for a in range(count):
-            first, second = first_bits[a]
-            for base_slot, j, slot in ((13, second, 29), (20, first | second, 30)):
-                for kind in range(7):
-                    source, there = origin(kind)
-                    arrived(a, base_slot + kind, piece(a, j, source), there)
-                sibling(a, slot, j)
-        for n, copy in enumerate(small):
-            if n not in (3, 4, 6, 7, 9, 12):
-                copy.wait_recv()
-            copy.wait_send()
-        for q in range(2):
-            mine = jnp.logical_and(lonely, column % 2 == q)
-            for kind, (size, begin) in enumerate(((quarter, 0), (asked, docs))):
-                dst = x_out.at[pl.ds(begin + q * size, size), :]
-                copy = pltpu.make_async_remote_copy(
-                    src_ref=dst,
-                    dst_ref=dst,
-                    send_sem=x_send.at[q, kind],
-                    recv_sem=x_recv.at[q, kind],
-                    device_id=(rank, column),
-                    device_id_type=MESH,
+                mixed = functools.reduce(
+                    jnp.add, [dot_nn(p.astype(BF), value) for p, (_, value) in zip(powers, keys)]
                 )
-
-                @pl.when(jnp.logical_not(mine))
-                def _():
-                    copy.wait_recv()
-
-        for mine, here, away in x_copies:
-
-            @pl.when(mine)
-            def _():
-                here.wait()
-
-            @pl.when(jnp.logical_not(mine))
-            def _():
-                away.wait_send()
-
-        for a in range(count):
-            for slot, j in ((27, 1), (28, first_bits[a][0] | 1), (29, first_bits[a][1] | 1), (30, 7)):
-                arrived(a, slot, line(a, j), None)
-        for condition, copy in waits:
-            if condition is None:
-                copy.wait_send()
-            else:
-
-                @pl.when(condition)
-                def _():
-                    copy.wait_send()
-
-    out_shape = [jax.ShapeDtypeStruct((docs + 2 * asked, width), x_doc.dtype)]
-    for w, f, t in zip(weights, feature_axis, tensor_axis):
-        shape = list(w.shape)
-        shape[f] *= groups
-        shape[t] *= ways
-        out_shape.append(jax.ShapeDtypeStruct(tuple(shape), w.dtype))
-    out_shape += [
-        jax.ShapeDtypeStruct((groups,) + proj.shape, proj.dtype),
-        jax.ShapeDtypeStruct((ways,) + bias.shape, bias.dtype),
-        jax.ShapeDtypeStruct((groups,) + picks.shape, picks.dtype),
-    ]
+                outs.append(mixed * (1.0 / total))
+            o_ref[pl.ds(start, size), :] = jnp.where(lane < HEAD_WIDTH, outs[0], outs[1]).astype(BF)
+
+        doc_keys = [
+            (qkv_o[1, :docs, pair], qkv_o[2, :docs, pair]),
+            (far[0, :, pair], far[1, :, pair]),
+        ]
+        for at in range(docs // block):
+            labels = lc_ref[pl.ds(at * block, block), :]
+            part(at * block, block, doc_keys, [labels == lo_ref[...], labels == lf_ref[...]])
+        row = lax.broadcasted_iota(jnp.int32, (asked, asked), 0) // QLEN
+        col = lax.broadcasted_iota(jnp.int32, (asked, asked), 1) // QLEN
+        part(docs, asked, [(qkv_o[1, docs:, pair], qkv_o[2, docs:, pair])], [row == col])
+
+        @pl.when(h == pairs - 1)
+        def _():
+            _, moves, gather = parts()
+            gather.finish()
+            moves.wait()
+            pltpu.make_async_copy(far, far_o, load_sem.at[3]).wait()
+
+    def whole(shape):
+        return pl.BlockSpec(shape, lambda h: (0,) * len(shape))
+
     anywhere = pl.BlockSpec(memory_space=pl.ANY)
     dma = pltpu.SemaphoreType.DMA
     return pl.pallas_call(
         kernel,
-        out_shape=out_shape,
-        in_specs=[anywhere] * (5 + count),
-        out_specs=[anywhere] * (4 + count),
+        grid=(pairs,),
+        in_specs=[
+            whole((rows, width)),
+            anywhere,
+            whole((3, width)),
+            whole((3, rows, 128)),
+            whole((3, rows, 128)),
+            whole((docs, 1)),
+            whole((1, docs)),
+            whole((1, docs)),
+        ]
+        + [anywhere] * 4,
+        out_specs=[
+            whole((3, rows, width)),
+            anywhere,
+            pl.BlockSpec((rows, 128), lambda h: (0, h)),
+        ]
+        + [anywhere] * 3,
+        out_shape=[
+            jax.ShapeDtypeStruct((3, rows, width), BF),
+            jax.ShapeDtypeStruct((2, docs, width), BF),
+            jax.ShapeDtypeStruct((rows, width), BF),
+            jax.ShapeDtypeStruct((rows, width), doc_cot.dtype),
+            gathered(up, 0, 1),
+            gathered(back, 1, 0),
+        ],
         scratch_shapes=[
-            dma((count, slots)),
-            dma((count, slots)),
-            dma((17,)),
-            dma((17,)),
+            pltpu.VMEM((3, width, width), BF),
+            pltpu.VMEM((2, docs, width), BF),
+            dma((4,)),
+            dma((2, steps)),
+            dma((2, steps)),
             dma((2, 2)),
             dma((2, 2)),
-            dma((count + 3,)),
+            dma((2, WeightGather.slots)),
+            dma((2, WeightGather.slots)),
+            dma((2,)),
         ],
-        compiler_params=pltpu.CompilerParams(collective_id=0, has_side_effects=True),
-        name="gather_weights",
-    )(x_doc, x_query, *weights, proj, bias, picks)
-
-
-def loss_kernel(projection, labels, log_counts, picks, y):
+        compiler_params=pltpu.CompilerParams(
+            vmem_limit_bytes=56 << 20, collective_id=4, has_side_effects=True
+        ),
+        name="project_and_attend",
+        cost_estimate=pl.CostEstimate(
+            flops=64 * rows * 2 * docs * width,
+            bytes_accessed=2 * (4 * rows + 2 * docs) * width,
+            transcendentals=rows * 2 * docs * width // 64,
+        ),
+    )(
+        x, weights, bias, cosines, sines, col_labels, own_labels, far_labels,
+        doc_cot, query_cot, up, back,
+    )
+
+
+def feed_forward(hidden, up, bias, back):
+    rows, width = hidden.shape
+    units = up.shape[1]
+    columns, piece = 512, 256
+
+    def kernel(h_ref, u_ref, b_ref, w_ref, a_ref, d_ref, o_ref):
+        @pl.when(pl.program_id(0) == 0)
+        def _():
+            o_ref[...] = jnp.zeros_like(o_ref)
+
+        for at in range(0, columns, piece):
+            z = dot_nn(h_ref[...], u_ref[:, at : at + piece]) + b_ref[:, at : at + piece]
+            bell = jnp.exp(-0.5 * z * z)
+            t = 1.0 / (1.0 + 0.23164189 * jnp.abs(z))
+            tail = 0.5 * t * (
+                0.254829592
+                + t * (-0.284496736 + t * (1.421413741 + t * (-1.453152027 + t * 1.061405429)))
+            ) * bell
+            below = jnp.where(z < 0.0, tail, 1.0 - tail)
+            low = (z * below).astype(BF)
+            a_ref[:, at : at + piece] = low
+            d_ref[:, at : at + piece] = (below + z * (bell * 0.3989422804014327)).astype(BF)
+            o_ref[...] += dot_nn(low, w_ref[at : at + piece, :])
+
+    return pl.pallas_call(
+        kernel,
+        grid=(units // columns,),
+        in_specs=[
+            pl.BlockSpec((rows, width), lambda n: (0, 0)),
+            pl.BlockSpec((width, columns), lambda n: (0, n)),
+            pl.BlockSpec((1, columns), lambda n: (0, n)),
+            pl.BlockSpec((columns, width), lambda n: (n, 0)),
+        ],
+        out_specs=[
+            pl.BlockSpec((rows, columns), lambda n: (0, n)),
+            pl.BlockSpec((rows, columns), lambda n: (0, n)),
+            pl.BlockSpec((rows, width), lambda n: (0, 0)),
+        ],
+        out_shape=[
+            jax.ShapeDtypeStruct((rows, units), BF),
+            jax.ShapeDtypeStruct((rows, units), BF),
+            jax.ShapeDtypeStruct((rows, width), F32),
+        ],
+        compiler_params=pltpu.CompilerParams(vmem_limit_bytes=40 << 20),
+        name="feed_forward",
+    )(hidden, up, bias[None], back)
+
+
+def feed_forward_backward(grad, back, slope, up, hidden, active):
+    rows, width = grad.shape
+    units = up.shape[1]
+    columns = 512
+
+    def kernel(g_ref, w_ref, d_ref, u_ref, h_ref, a_ref, o_ref, du_ref, dw_ref, db_ref):
+        @pl.when(pl.program_id(0) == 0)
+        def _():
+            o_ref[...] = jnp.zeros_like(o_ref)
+
+        g = g_ref[...]
+        dw_ref[...] = dot_tn(a_ref[...], g).astype(BF)
+        low = (dot_nt(g, w_ref[...]) * d_ref[...].astype(F32)).astype(BF)
+        db_ref[...] = jnp.sum(low.astype(F32), axis=0, keepdims=True)
+        o_ref[...] += dot_nt(low, u_ref[...])
+        du_ref[...] = dot_tn(h_ref[...], low).astype(BF)
+
+    return pl.pallas_call(
+        kernel,
+        grid=(units // columns,),
+        in_specs=[
+            pl.BlockSpec((rows, width), lambda n: (0, 0)),
+            pl.BlockSpec((columns, width), lambda n: (n, 0)),
+            pl.BlockSpec((rows, columns), lambda n: (0, n)),
+            pl.BlockSpec((width, columns), lambda n: (0, n)),
+            pl.BlockSpec((rows, width), lambda n: (0, 0)),
+            pl.BlockSpec((rows, columns), lambda n: (0, n)),
+        ],
+        out_specs=[
+            pl.BlockSpec((rows, width), lambda n: (0, 0)),
+            pl.BlockSpec((width, columns), lambda n: (0, n)),
+            pl.BlockSpec((columns, width), lambda n: (n, 0)),
+            pl.BlockSpec((1, columns), lambda n: (0, n)),
+        ],
+        out_shape=[
+            jax.ShapeDtypeStruct((rows, width), F32),
+            jax.ShapeDtypeStruct((width, units), BF),
+            jax.ShapeDtypeStruct((units, width), BF),
+            jax.ShapeDtypeStruct((1, units), F32),
+        ],
+        compiler_params=pltpu.CompilerParams(vmem_limit_bytes=48 << 20),
+        name="feed_forward_backward",
+    )(grad, back, slope, up, hidden, active)
+
+
+def loss_kernel(projection, labels, log_counts, picks):
     rows, columns = projection.shape
-    width = y.shape[1]
     docs = labels.shape[0]
     own = rows - docs
     tokens = 16 * own
@@ -830,10 +976,10 @@
     chunk = 64
 
     def kernel(
-        p_ref, lab_ref, cnt_ref, pick_ref, y_ref,
-        grad_ref, loss_ref, yd_ref, yq_ref,
+        p_ref, lab_ref, cnt_ref, pick_ref,
+        grad_ref, loss_ref,
         asked_all, weight, sums, sums_all, coef_all, slope, part, part_low, got, tile, tile_got,
-        send_sem, recv_sem, row_send, row_recv, tile_send, tile_recv,
+        send_sem, recv_sem, tile_send, tile_recv,
     ):
         around = Around()
         rank, column, core, base = around.rank, around.column, around.core, around.base
@@ -885,7 +1031,6 @@
             return copies
 
         first = all_to_all(0, lambda i: asked_all.at[own_at, :], lambda i: asked_all.at[own_at, :])
-        home = RowMoves(around, False, yd_ref, yq_ref, y_ref, row_send, row_recv)
         doc_low = unit_low[:docs]
         seg_of = lab_ref[...]
         for copy in first:
@@ -902,7 +1047,6 @@
                     jnp.where(chosen, power, 0.0), axis=0, keepdims=True
                 )
         second = all_to_all(1, lambda i: sums, lambda i: sums_all.at[mine])
-        home.start()
         sums_all[mine] = sums[...]
         for copy in second:
             copy.wait_recv()
@@ -1012,7 +1156,6 @@
                 came.wait_recv()
 
         loss_ref[...] = tile_got[:, 0]
-        home.wait()
         for here, away in tiles:
 
             @pl.when(jnp.logical_not(here))
@@ -1025,7 +1168,6 @@
     def whole(shape):
         return pl.BlockSpec(shape, lambda: (0,) * len(shape))
 
-    anywhere = pl.BlockSpec(memory_space=pl.ANY)
     vmem = pltpu.VMEM
     dma = pltpu.SemaphoreType.DMA
     return pl.pallas_call(
@@ -1035,14 +1177,11 @@
             whole(labels.shape),
             whole(log_counts.shape),
             whole(picks.shape),
-            anywhere,
         ],
-        out_specs=[whole((rows, columns)), whole((2, 8, 128)), anywhere, anywhere],
+        out_specs=[whole((rows, columns)), whole((2, 8, 128))],
         out_shape=[
             jax.ShapeDtypeStruct((rows, columns), BF),
             jax.ShapeDtypeStruct((2, 8, 128), F32),
-            jax.ShapeDtypeStruct((2, docs // 2, width), BF),
-            jax.ShapeDtypeStruct((2, own // 2, width), BF),
         ],
         scratch_shapes=[
             vmem((tokens, columns), BF),
@@ -1058,8 +1197,6 @@
             vmem((2, 2, 8, 128), F32),
             dma((3, 16)),
             dma((3, 16)),
-            dma((2, 2)),
-            dma((2, 2)),
             dma((2,)),
             dma((2,)),
         ],
@@ -1069,15 +1206,16 @@
         name="loss",
         cost_estimate=pl.CostEstimate(
             flops=100 * docs * tokens * columns,
-            bytes_accessed=2 * rows * width,
+            bytes_accessed=8 * rows * columns,
             transcendentals=docs * tokens,
         ),
-    )(projection, labels, log_counts, picks, y)
+    )(projection, labels, log_counts, picks)
 
 
 class MatrixSum:
     def __init__(
-        self, around, send, axis, across, own, got, next_, near, far, home, local_sems, pieces
+        self, around, send, axis, across, own, got, next_, near, far, home, local_sems,
+        away=None, extras=(),
     ):
         self.axis, self.own, self.got, self.next, self.near = axis, own, got, next_, near
         self.block = own.shape[axis] // 4
@@ -1092,7 +1230,10 @@
             for slot, n in enumerate(self.gone)
         ]
         self.second = send(self.at(own, self.later), near, around.other(second))
-        self.pieces = [send(own.at[index], dst, around.along(dt)) for dt, index, dst in pieces]
+        self.extras = extras
+        self.away = None
+        if away is not None:
+            self.away = send(self.at(own, 0), away[1], around.along(away[0]))
 
     def at(self, ref, n):
         span = pl.ds(n * self.block, self.block)
@@ -1138,12 +1279,11 @@
     def tensor(self):
         self.second.wait_recv()
         self.add(0, self.near, 0)
-        for copy in self.pieces:
-            copy.start()
-
-    def settle(self):
-        for copy in self.pieces:
+        for buffer, copy in self.extras:
             copy.wait_recv()
+            self.add(0, buffer, 0)
+        if self.away is not None:
+            self.away.start()
 
 
 class SmallSum:
@@ -1152,8 +1292,7 @@
         tos = [around.other(bit) for bit in bits] + [around.along(dt) for dt in tensor]
         self.copies = [send(run.at[n], got.at[n], to) for n, to in enumerate(tos)]
 
-    def begin(self, value):
-        self.run[0] = value
+    def begin(self):
         self.copies[0].start()
 
     def hop(self, n):
@@ -1219,105 +1358,115 @@
         return self.run[pl.ds(self.ref.shape[0] // 2 + 2 * self.last, self.last), :]
 
 
-def finish_kernel(qkv, out, rows, tensor_sums):
+def finish_kernel(x, weights, pre, mixed, branch, resid, tensor_sums):
     ways = 4
-    width = qkv.shape[0]
+    rows, width = x.shape
     half, block = width // 2, width // 8
     share = width // ways
-    docs = rows.shape[0] // 9 * 8
-    quarter, asked = docs // 2, (rows.shape[0] - docs) // 2
-    chunk = 16
-    parts = 4
+    docs = rows // 9 * 8
+    quarter, asked = docs // 2, (rows - docs) // 2
     part = 3 * share
 
     def kernel(
-        qkv_ref, out_ref, rows_ref, ten_ref,
+        x_ref, w_ref, p_ref, m_ref, g_ref, r_ref, ten_ref,
         qkv_o, out_o, doc_o, ask_o, ten_o,
-        qa, q0, q1, q2, q3, oa, o0, o1, o2, o3, gd, ga, t_got, t_run, tz,
-        send_sem, recv_sem, local_sem, row_send, row_recv,
+        xs, ws, ps, ms, gs, rs, low, qf, qa, q0, q1, q2, q3, of, oa, o0, o1, o2, o3,
+        t_got, t_run, tz, send_sem, recv_sem, local_sem, row_send, row_recv,
     ):
         around = Around()
-        around.meet()
+        around.greet()
+        loads = {}
+        for n, (name, src, dst) in enumerate(
+            [("p", p_ref, ps), ("r", r_ref, rs)]
+            + [(j, w_ref.at[j], ws.at[j]) for j in range(3)]
+            + [("x", x_ref, xs), ("m", m_ref, ms), ("g", g_ref, gs)]
+        ):
+            loads[name] = pltpu.make_async_copy(src, dst, local_sem.at[n])
+            loads[name].start()
         send = Sender(send_sem, recv_sem)
         small = SmallSum(around, send, t_got, t_run, tensor=())
         spread = [send(t_run.at[3, dt], tz.at[dt - 1], around.along(dt)) for dt in range(1, ways)]
-        across = (True, False, False, True)
-        heads, feats = [], []
-        for n in range(parts):
-            spans = [(pl.ds(j * width + n * share, share), pl.ds(j * share, share)) for j in range(3)]
-            heads.append(
-                MatrixSum(
-                    around, send, 0, across[n], qa.at[n], q0.at[n], q1.at[n], q2.at[n],
-                    [(qkv_ref.at[half:, fr], q0.at[n, :, to]) for fr, to in spans],
-                    [(qkv_ref.at[:half, fr], qa.at[n, :, to]) for fr, to in spans],
-                    [local_sem.at[3 * n + j] for j in range(3)],
-                    [
-                        (n, (slice(0, block), pl.ds(j * share, share)), q3.at[n - 1, j])
-                        for j in range(3)
-                        if n > 0
-                    ],
-                )
+        heads, feats = [None] * ways, [None] * ways
+        for n in (3, 2, 1, 0):
+            step = {3: (1, 1), 2: (2, 2), 1: (1, 0), 0: None}[n]
+            heads[n] = MatrixSum(
+                around, send, 0, n % 2 == 0, qa.at[n], q0.at[n], q1.at[n], q2.at[n],
+                [(qf.at[n], q0.at[n])], [], [],
+                None if step is None else (step[0], q3.at[step[1]]),
+                [(q3.at[1], heads[3].away)] if n == 2 else [],
             )
-        for n in range(2):
-            span = pl.ds(n * half, half)
-            feats.append(
-                MatrixSum(
-                    around, send, 1, n == 0, oa.at[n], o0.at[n], o1.at[n], o2.at[n],
-                    [(out_ref.at[span, half:], o0.at[n])],
-                    [(out_ref.at[span, :half], oa.at[n])],
-                    [local_sem.at[3 * parts + n]],
-                    [
-                        (dt, (pl.ds((dt % 2) * share, share), slice(0, block)), o3.at[dt - 1])
-                        for dt in (2 * n, 2 * n + 1)
-                        if dt > 0
-                    ],
-                )
+            feats[n] = MatrixSum(
+                around, send, 1, n % 2 == 0, oa.at[n], o0.at[n], o1.at[n], o2.at[n],
+                [(of.at[n], o0.at[n])], [], [],
+                None if step is None else (step[0], o3.at[step[1]]),
+                [(o3.at[1], feats[3].away)] if n == 2 else [],
             )
-        items = [heads[2], heads[3], feats[1], heads[0], heads[1], feats[0]]
-        small.begin(ten_ref[...])
-        for item in items:
-            item.begin()
-
-        home = RowMoves(around, False, gd, ga, rows_ref, row_send, row_recv)
+        names = [("h", 3), ("h", 2), ("f", 3), ("f", 2), ("h", 1), ("h", 0), ("f", 1), ("f", 0)]
+        items = [(heads if kind == "h" else feats)[n] for kind, n in names]
+
+        def compute(k):
+            kind, n = names[k]
+            at = pl.ds(n * share, share)
+            for side, to in ((1, qf if kind == "h" else of), (0, qa if kind == "h" else oa)):
+                span = pl.ds(side * half, half)
+                if kind == "h":
+                    for j in range(3):
+                        to[n, :, j * share : (j + 1) * share] = dot_tn(
+                            xs[:, span], ps[j, :, at]
+                        ).astype(BF)
+                else:
+                    to[n] = dot_tn(ms[:, at], gs[:, span]).astype(BF)
+                if side == 1:
+                    items[k].begin()
+
+        loads["p"].wait()
+        loads["r"].wait()
+        for j in range(3):
+            loads[j].wait()
+        for at in range(0, width, share):
+            total = rs[:, at : at + share]
+            for j in range(3):
+                total = total + dot_nt(ps[j], ws[j, at : at + share, :])
+            low[:, at : at + share] = total.astype(BF)
+        around.await_all()
+        t_run[0] = ten_ref[...]
+        small.begin()
+        home = RowMoves(around, False, doc_o, ask_o, low, row_send, row_recv)
         home.start()
-
+        for name in ("x", "m", "g"):
+            loads[name].wait()
+        compute(0)
+        compute(1)
         for n in range(0, len(items) + 4, 2):
+            if 0 < n < 8:
+                small.hop(n // 2 - 1)
+            if n == 6:
+                for copy in spread:
+                    copy.start()
             for item in items[n - 2 : n] if n >= 2 else []:
                 item.second_axis()
             for item in items[n : n + 2]:
                 item.first_axis()
-            if n // 2 < 3:
-                small.hop(n // 2)
-            if n // 2 == 2:
-                for copy in spread:
-                    copy.start()
+            for k in (n + 2, n + 3):
+                if k < len(items):
+                    compute(k)
             for m in (n - 4, n - 3):
                 if 0 <= m < len(items):
                     items[m].tensor()
 
         home.wait()
-        for m in range(2):
-
-            @pl.loop(0, quarter // chunk)
-            def _(n):
-                at = pl.ds(pl.multiple_of(n * chunk, chunk), chunk)
-                doc_o[m, at, :] = gd[m, at, :].astype(F32)
-
-        ask_o[...] = ga[...].astype(F32)
         for copy in spread:
             copy.wait_recv()
         ten_o[...] = t_run[3, 0] + tz[0] + tz[1] + tz[2]
-        for item in items:
-            item.settle()
+        for group in (heads, feats):
+            group[1].away.wait_recv()
+            group[2].away.wait_recv()
         for j in range(3):
-            total = qa[0, :block, pl.ds(j * share, share)].astype(F32)
-            for dt in range(ways - 1):
-                total = total + q3[dt, j].astype(F32)
-            qkv_o[j] = total
-        total = oa[0, :share, :block].astype(F32)
-        for dt in range(ways - 1):
-            total = total + o3[dt].astype(F32)
-        out_o[...] = total
+            at = pl.ds(j * share, share)
+            total = qa[0, :block, at].astype(F32) + q3[0, :, at].astype(F32)
+            qkv_o[j] = total + q3[2, :, at].astype(F32)
+        total = oa[0, :, :block].astype(F32) + o3[0].astype(F32)
+        out_o[...] = total + o3[2].astype(F32)
         send.drain()
 
     def whole(x):
@@ -1326,56 +1475,69 @@
     out_shape = [
         jax.ShapeDtypeStruct((3, block, share), F32),
         jax.ShapeDtypeStruct((share, block), F32),
-        jax.ShapeDtypeStruct((2, quarter, width), F32),
-        jax.ShapeDtypeStruct((2, asked, width), F32),
+        jax.ShapeDtypeStruct((2, quarter, width), BF),
+        jax.ShapeDtypeStruct((2, asked, width), BF),
         jax.ShapeDtypeStruct(tensor_sums.shape[1:], F32),
     ]
     anywhere = pl.BlockSpec(memory_space=pl.ANY)
     vmem = pltpu.VMEM
     dma = pltpu.SemaphoreType.DMA
-    count = 6 + parts * 6 + 9 + 2 * 4 + 3
+    count = 6 + 2 * (ways * 4 + 3)
     return pl.pallas_call(
         kernel,
         out_shape=out_shape,
-        in_specs=[anywhere] * 3 + [whole(tensor_sums)],
-        out_specs=[whole(x) for x in out_shape],
+        in_specs=[anywhere] * 6 + [whole(tensor_sums)],
+        out_specs=[
+            whole(out_shape[0]),
+            whole(out_shape[1]),
+            anywhere,
+            anywhere,
+            whole(out_shape[4]),
+        ],
         scratch_shapes=[
-            vmem((parts, half, part), BF),
-            vmem((parts, half, part), BF),
-            vmem((parts, 2 * block, part), BF),
-            vmem((parts, block, part), BF),
-            vmem((ways - 1, 3, block, share), BF),
-            vmem((2, half, half), BF),
-            vmem((2, half, half), BF),
-            vmem((2, half, 2 * block), BF),
-            vmem((2, half, block), BF),
+            vmem((rows, width), BF),
+            vmem((3, width, width), BF),
+            vmem((3, rows, width), BF),
+            vmem((rows, width), BF),
+            vmem((rows, width), BF),
+            vmem((rows, width), F32),
+            vmem((rows, width), BF),
+            vmem((ways, half, part), BF),
+            vmem((ways, half, part), BF),
+            vmem((ways, half, part), BF),
+            vmem((ways, 2 * block, part), BF),
+            vmem((ways, block, part), BF),
+            vmem((ways - 1, block, part), BF),
+            vmem((ways, share, half), BF),
+            vmem((ways, share, half), BF),
+            vmem((ways, share, half), BF),
+            vmem((ways, share, 2 * block), BF),
+            vmem((ways, share, block), BF),
             vmem((ways - 1, share, block), BF),
-            vmem((2, quarter, width), BF),
-            vmem((2, asked, width), BF),
             vmem((3,) + tensor_sums.shape, F32),
             vmem((4,) + tensor_sums.shape, F32),
             vmem((ways - 1,) + tensor_sums.shape[1:], F32),
             dma((count,)),
             dma((count,)),
-            dma((3 * parts + 2,)),
+            dma((8,)),
             dma((2, 2)),
             dma((2, 2)),
         ],
         compiler_params=pltpu.CompilerParams(
-            collective_id=1, has_side_effects=True, vmem_limit_bytes=48 << 20
+            collective_id=1, has_side_effects=True, vmem_limit_bytes=60 << 20
         ),
         name="last_sums",
-    )(qkv, out, rows, tensor_sums)
+    )(x, weights, pre, mixed, branch, resid, tensor_sums)
 
 
 def attention_backward_kernel(
-    qkv, far_kv, grad, cosine, sine, far_cosine, far_sine, col_labels, own_labels, far_labels,
-    up, back, vectors, proj,
+    qkv, far_kv, grad, cosines, sines, col_labels, own_labels, far_labels,
+    up, back, vectors, proj, y,
 ):
     rows, width = qkv.shape[1:]
     docs = far_kv.shape[1]
     pairs = width // 128
-    block = 128
+    block = docs
     asked = rows - docs
     ways = 4
     half, own_block = width // 2, width // 8
@@ -1384,53 +1546,57 @@
     assert pairs == 8
 
     def kernel(
-        qkv_ref, far_ref, g_ref, c_ref, s_ref, fc_ref, fs_ref, lc_ref, lo_ref, lf_ref,
-        up_ref, back_ref, vec_ref, proj_ref,
-        pre_ref, bias_ref, up_o, back_o, vec_o, proj_o,
+        qkv_ref, far_ref, g_ref, c_ref, s_ref, lc_ref, lo_ref, lf_ref,
+        up_ref, back_ref, vec_ref, proj_ref, y_ref,
+        pre_ref, bias_ref, up_o, back_o, vec_o, proj_o, yd_ref, yq_ref,
         sums_own, sums_far, give, kept, got_kv,
         ua, u0, u1, u2, u3, ba, b0, b1, b2, b3, v_got, v_run, p_run, p_got,
-        send_sem, recv_sem, local_sem,
+        send_sem, recv_sem, local_sem, row_send, row_recv,
     ):
         h = pl.program_id(0)
         around = Around()
         send = Sender(send_sem, recv_sem)
-        ups, backs = [], []
-        for n in range(count):
+        ups, backs = [None] * count, [None] * count
+        for n in range(count - 1, -1, -1):
             span = pl.ds(n * piece, piece)
-            dt, side = n // 2, pl.ds(n % 2 * piece, piece)
-            ups.append(
-                MatrixSum(
-                    around, send, 0, False, ua.at[n], u0.at[n], u1.at[n], u2.at[n],
-                    [(up_ref.at[half:, span], u0.at[n])],
-                    [(up_ref.at[:half, span], ua.at[n])],
-                    [local_sem.at[n]],
-                    [(dt, (slice(0, own_block), slice(None)), u3.at[dt - 1, :, side])] if dt else [],
-                )
+            dt, side = n // 2, n % 2
+            step = {3: (1, 1), 2: (2, 2), 1: (1, 0), 0: None}[dt]
+            ups[n] = MatrixSum(
+                around, send, 0, False, ua.at[n], u0.at[n], u1.at[n], u2.at[n],
+                [(up_ref.at[half:, span], u0.at[n])],
+                [(up_ref.at[:half, span], ua.at[n])],
+                [local_sem.at[n]],
+                None if step is None else (step[0], u3.at[step[1], side]),
+                [(u3.at[1, side], ups[n + 2].away)] if dt == 2 else [],
             )
-            backs.append(
-                MatrixSum(
-                    around, send, 1, True, ba.at[n], b0.at[n], b1.at[n], b2.at[n],
-                    [(back_ref.at[span, half:], b0.at[n])],
-                    [(back_ref.at[span, :half], ba.at[n])],
-                    [local_sem.at[count + n]],
-                    [(dt, (slice(None), slice(0, own_block)), b3.at[dt - 1, side, :])] if dt else [],
-                )
+            backs[n] = MatrixSum(
+                around, send, 1, True, ba.at[n], b0.at[n], b1.at[n], b2.at[n],
+                [(back_ref.at[span, half:], b0.at[n])],
+                [(back_ref.at[span, :half], ba.at[n])],
+                [local_sem.at[count + n]],
+                None if step is None else (step[0], b3.at[step[1], side]),
+                [(b3.at[1, side], backs[n + 2].away)] if dt == 2 else [],
             )
-        couples = [(ups[n], backs[n]) for n in (4, 5, 6, 7, 2, 3, 0, 1)]
+        couples = [(ups[n], backs[n]) for n in (6, 7, 4, 5, 2, 3, 0, 1)]
         small = SmallSum(around, send, v_got, v_run)
         mean_proj = ProjSum(around, send, proj_ref, p_run, p_got)
         gives = [send(give.at[n], got_kv.at[n], around.other(1)) for n in range(pairs)]
+        home = RowMoves(around, False, yd_ref, yq_ref, y_ref, row_send, row_recv)
         lane = lax.broadcasted_iota(jnp.int32, (1, 128), 1)
 
         def finish(n):
             gives[n].wait_recv()
             at = pl.ds(n * 128, 128)
             for i in range(2):
-                low = (kept[n % 2, i, :docs, :] + got_kv[n, i].astype(F32)).astype(BF)
-                tail = kept[n % 2, i, docs:, :].astype(BF)
-                pre_ref[i + 1, :docs, at] = low
+                head = kept[n % 2, i, :docs, :] + got_kv[n, i].astype(F32)
+                tail = kept[n % 2, i, docs:, :]
+                if i == 0:
+                    head = head * c_ref[0, :docs, :] - turned(head) * s_ref[0, :docs, :]
+                    tail = tail * c_ref[0, docs:, :] - turned(tail) * s_ref[0, docs:, :]
+                head, tail = head.astype(BF), tail.astype(BF)
+                pre_ref[i + 1, :docs, at] = head
                 pre_ref[i + 1, docs:, at] = tail
-                total = jnp.sum(low.astype(F32), axis=0, keepdims=True)
+                total = jnp.sum(head.astype(F32), axis=0, keepdims=True)
                 total = total + jnp.sum(tail.astype(F32), axis=0, keepdims=True)
                 bias_ref[i + 1 : i + 2, at] = total
 
@@ -1440,23 +1606,35 @@
             def _(step=step):
                 if step == 0:
                     around.meet()
-                    small.begin(vec_ref[...])
+                    for p in range(8):
+                        to = feature_block(around.rank, p) * own_block
+                        at = pl.ds(pl.multiple_of(to, own_block), own_block)
+                        v_run[0, :, at] = vec_ref[:, p * own_block : (p + 1) * own_block]
+                    small.begin()
                     mean_proj.begin()
-                    for couple in couples:
-                        for item in couple:
-                            item.begin()
+                    for n, many in ((0, 2), (2, 4), (4, 8)):
+                        for couple in couples[n:many]:
+                            for item in couple:
+                                item.begin()
+                        if n < 4:
+                            for item in couples[n // 2]:
+                                item.first_axis()
+                    home.start()
                 else:
-                    if step >= 2:
-                        for item in couples[step - 2]:
-                            item.second_axis()
-                    for couple in couples[:2] if step == 1 else [couples[step]]:
-                        for item in couple:
-                            item.first_axis()
+                    firsts = {1: (2,), 2: (3, 4), 3: (5,), 4: (6,), 5: (7,)}
+                    seconds = {1: (0,), 2: (1,), 3: (2,), 4: (3, 4), 5: (5,), 6: (6,), 7: (7,)}
+                    tensors = {3: (0, 1), 4: (2,), 5: (3,), 6: (4,), 7: (5, 6)}
                     if step <= 5:
                         small.hop(step - 1)
                         mean_proj.hop(step - 1)
-                    if step >= 3:
-                        for item in couples[step - 3]:
+                    for n in seconds.get(step, ()):
+                        for item in couples[n]:
+                            item.second_axis()
+                    for n in firsts.get(step, ()):
+                        for item in couples[n]:
+                            item.first_axis()
+                    for n in tensors.get(step, ()):
+                        for item in couples[n]:
                             item.tensor()
                     finish(step - 1)
 
@@ -1499,7 +1677,7 @@
                     ref[1, pl.ds(begin, many), :] += dot_tn(p.astype(BF), g_head)
             total = jnp.where(lane < HEAD_WIDTH, grads[0], grads[1])
             at = pl.ds(start, size)
-            low = (total * c_ref[at, :] - turned(total) * s_ref[at, :]).astype(BF)
+            low = (total * c_ref[0, at, :] - turned(total) * s_ref[0, at, :]).astype(BF)
             pre_ref[0, at, pl.ds(pl.multiple_of(h * 128, 128), 128)] = low
             return jnp.sum(low.astype(F32), axis=0, keepdims=True)
 
@@ -1528,10 +1706,8 @@
         )
         bias_ref[0:1, pl.ds(pl.multiple_of(h * 128, 128), 128)] = bias
         side = h % 2
-        kept[side, 0] = sums_own[0] * c_ref[...] - turned(sums_own[0]) * s_ref[...]
-        kept[side, 1] = sums_own[1]
-        give[h, 0] = (sums_far[0] * fc_ref[...] - turned(sums_far[0]) * fs_ref[...]).astype(BF)
-        give[h, 1] = sums_far[1].astype(BF)
+        kept[side] = sums_own[...]
+        give[h] = sums_far[...].astype(BF)
         for step in range(pairs):
 
             @pl.when(h == step)
@@ -1541,27 +1717,26 @@
         @pl.when(h == pairs - 1)
         def _():
             finish(pairs - 1)
-            for couple in couples[6:]:
-                for item in couple:
-                    item.second_axis()
-            for couple in couples[5:]:
+            for couple in couples[7:]:
                 for item in couple:
                     item.tensor()
-            for couple in couples:
-                for item in couple:
-                    item.settle()
-            for n in range(2):
-                at = pl.ds(n * piece, piece)
-                total = ua[n, :own_block, :].astype(F32)
-                for dt in range(ways - 1):
-                    total = total + u3[dt, :, at].astype(F32)
-                up_o[:, at] = total
-                total = ba[n, :, :own_block].astype(F32)
-                for dt in range(ways - 1):
-                    total = total + b3[dt, at, :].astype(F32)
-                back_o[at, :] = total
+            for group, acc, came, o in ((ups, ua, u3, up_o), (backs, ba, b3, back_o)):
+                for n in range(2):
+                    group[n + 2].away.wait_recv()
+                    group[n + 4].away.wait_recv()
+                    at = pl.ds(n * piece, piece)
+                    if acc is ua:
+                        total = acc[n, :own_block, :].astype(F32)
+                    else:
+                        total = acc[n, :, :own_block].astype(F32)
+                    total = total + came[0, n].astype(F32) + came[2, n].astype(F32)
+                    if acc is ua:
+                        o[:, at] = total
+                    else:
+                        o[at, :] = total
             vec_o[...] = v_run[5]
             proj_o[...] = mean_proj.result()
+            home.wait()
             send.drain()
 
     def whole(shape):
@@ -1587,10 +1762,8 @@
             pl.BlockSpec((3, rows, 128), lambda h: (0, 0, h)),
             pl.BlockSpec((2, docs, 128), lambda h: (0, 0, h)),
             pl.BlockSpec((rows, 128), lambda h: (0, h)),
-            whole((rows, 128)),
-            whole((rows, 128)),
-            whole((docs, 128)),
-            whole((docs, 128)),
+            pl.BlockSpec((1, rows, 128), lambda h: (1, 0, 0)),
+            pl.BlockSpec((1, rows, 128), lambda h: (1, 0, 0)),
             whole((docs, 1)),
             whole((1, docs)),
             whole((1, docs)),
@@ -1598,9 +1771,14 @@
             anywhere,
             whole(vectors.shape),
             whole(proj.shape),
+            anywhere,
         ],
-        out_specs=[whole(x.shape) for x in out_shape],
-        out_shape=out_shape,
+        out_specs=[whole(x.shape) for x in out_shape] + [anywhere, anywhere],
+        out_shape=out_shape
+        + [
+            jax.ShapeDtypeStruct((2, docs // 2, width), BF),
+            jax.ShapeDtypeStruct((2, asked // 2, width), BF),
+        ],
         scratch_shapes=[
             vmem((2, rows, 128), F32),
             vmem((2, docs, 128), F32),
@@ -1611,12 +1789,12 @@
             vmem((count, half, piece), BF),
             vmem((count, 2 * own_block, piece), BF),
             vmem((count, own_block, piece), BF),
-            vmem((ways - 1, own_block, share), BF),
+            vmem((ways - 1, 2, own_block, piece), BF),
             vmem((count, piece, half), BF),
             vmem((count, piece, half), BF),
             vmem((count, piece, 2 * own_block), BF),
             vmem((count, piece, own_block), BF),
-            vmem((ways - 1, share, own_block), BF),
+            vmem((ways - 1, 2, piece, own_block), BF),
             vmem((5,) + vectors.shape, F32),
             vmem((6,) + vectors.shape, F32),
             vmem((width, columns), F32),
@@ -1624,6 +1802,8 @@
             dma((slots,)),
             dma((slots,)),
             dma((2 * count,)),
+            dma((2, 2)),
+            dma((2, 2)),
         ],
         compiler_params=pltpu.CompilerParams(
             collective_id=2, has_side_effects=True, vmem_limit_bytes=60 << 20
@@ -1635,8 +1815,8 @@
             transcendentals=rows * 2 * docs * width // 64,
         ),
     )(
-        qkv, far_kv, grad, cosine, sine, far_cosine, far_sine, col_labels, own_labels, far_labels,
-        up, back, vectors, proj,
+        qkv, far_kv, grad, cosines, sines, col_labels, own_labels, far_labels,
+        up, back, vectors, proj, y,
     )
 
 
@@ -1762,8 +1942,8 @@
     bias_pack = jnp.concatenate([b_qkv.reshape(-1), b_in])
     own_picks = jnp.zeros((8, 128), jnp.int32).at[:micro, : positives.shape[1]].set(positives)
     if chips == 4:
-        own_x, full_qkv, full_out, full_in, full_back, full_proj, biases, picks_rel = gather_kernel(
-            x_doc, x_query, w_qkv, w_out, w_in, w_back, w_proj, bias_pack.reshape(-1, 128), own_picks
+        own_x, full_qkv, full_out, full_proj, biases, picks_rel = gather_kernel(
+            x_doc, x_query, w_qkv, w_out, w_proj, bias_pack.reshape(-1, 128), own_picks
         )
         biases = [biases[j].reshape(-1) for j in range(ways)]
         full_proj = full_proj.reshape(width, proj_width)
@@ -1823,28 +2003,33 @@
     cosines_three = jnp.stack([cosine * 0.125, cosine, jnp.ones_like(cosine)])
     sines_three = jnp.stack([sine * 0.125, sine, jnp.zeros_like(sine)])
 
-    x_low = dot_nn(own_x, turn).astype(BF)
-    projected = project_heads(
-        x_low, full_qkv, bias_qkv, cosines_three, sines_three, docs, chips == 4
-    )
-    qkv = projected[0]
-    far_kv = projected[1] if chips == 4 else exchange(qkv[1:, :docs], dr=1)
     label_args = (own_labels[:, None], own_labels[None, :], far_labels[None, :])
     if chips == 4:
-        mixed, own_cot = attention_forward(qkv, far_kv, *label_args, cots)
+        x_low = own_x
+        qkv, far_kv, mixed, own_cot, full_in, full_back = project_and_attend(
+            own_x, full_qkv, bias_qkv, cosines_three, sines_three, *label_args,
+            *cots, w_in, w_back,
+        )
     else:
-        (mixed,) = attention_forward(qkv, far_kv, *label_args)
+        x_low = dot_nn(own_x, turn).astype(BF)
+        qkv = project_heads(x_low, full_qkv, bias_qkv, cosines_three, sines_three)
+        far_kv = exchange(qkv[1:, :docs], dr=1)
+        mixed = attention_forward(qkv, far_kv, *label_args)
     branch = dot_nn(mixed, full_out)
     resid_one = x_low.astype(F32) + branch + b_out
     normed, norm_one_pull = jax.vjp(layer_norm, resid_one, gain_one, shift_one)
     normed_low = normed.astype(BF)
-    inner = dot_nn(normed_low, full_in) + bias_in
-    active, gelu_pull = jax.vjp(gelu_exact, inner)
-    active_low = active.astype(BF)
-    resid_two = normed + dot_nn(active_low, full_back) + b_back
+    if chips == 4:
+        active_low, active_slope, update = feed_forward(normed_low, full_in, bias_in, full_back)
+    else:
+        inner = dot_nn(normed_low, full_in) + bias_in
+        active, gelu_pull = jax.vjp(gelu_exact, inner)
+        active_low = active.astype(BF)
+        update = dot_nn(active_low, full_back)
+    resid_two = normed + update + b_back
     output, norm_two_pull = jax.vjp(layer_norm, resid_two, gain_two, shift_two)
     output_low = output.astype(BF)
-    y_low = dot_nt(output_low, turn).astype(BF)
+    y_low = output_low if chips == 4 else dot_nt(output_low, turn).astype(BF)
     projection = dot_nn(output_low, full_proj)
     held = jnp.arange(groups, dtype=jnp.int32)
     held = rank ^ (2 * (held % chips) + held // chips)
@@ -1857,8 +2042,8 @@
         log_counts = jnp.pad(
             jnp.log(counts).reshape(-1, segments), ((0, 0), (0, 8 - segments))
         ).reshape(-1, 1)
-        proj_low, loss_out, y_doc, y_query = loss_kernel(
-            projection, own_labels[:, None], log_counts, jnp.repeat(picks, QLEN)[None], y_low
+        proj_low, loss_out = loss_kernel(
+            projection, own_labels[:, None], log_counts, jnp.repeat(picks, QLEN)[None]
         )
         loss_out = loss_out[:, : asked // QLEN, 0]
     else:
@@ -2001,22 +2186,26 @@
             r.sends = s
         return value
 
-    out_grad = own_cot_turned = dot_nn(own_cot, turn) + dot_nt(proj_low, full_proj)
+    if chips == 4:
+        out_cot = own_cot.astype(F32)
+    else:
+        out_cot = dot_nn(own_cot, turn)
+    out_grad = out_cot + dot_nt(proj_low, full_proj)
     resid_two_grad, gain_two_grad, shift_two_grad = norm_two_pull(out_grad)
     update_low = resid_two_grad.astype(BF)
     whole_path = chips == 4
     if whole_path:
-        back_grad = dot_tn(active_low, update_low).astype(BF)
+        hidden_grad, in_grad, back_grad, inner_bias = feed_forward_backward(
+            update_low, full_back, active_slope, full_in, normed_low, active_low
+        )
     else:
         sum_back = weight_sum(active_low, update_low, 1, True)
-    active_grad = dot_nt(update_low, full_back)
-    (inner_grad,) = gelu_pull(active_grad)
-    inner_low = inner_grad.astype(BF)
-    if whole_path:
-        in_grad = dot_tn(normed_low, inner_low).astype(BF)
-    else:
+        (inner_grad,) = gelu_pull(dot_nt(update_low, full_back))
+        inner_low = inner_grad.astype(BF)
         sum_in = weight_sum(normed_low, inner_low, 0, False)
-    normed_grad = dot_nt(inner_low, full_in) + resid_two_grad
+        hidden_grad = dot_nt(inner_low, full_in)
+        inner_bias = jnp.sum(inner_low.astype(F32), axis=0)
+    normed_grad = hidden_grad + resid_two_grad
     resid_one_grad, gain_one_grad, shift_one_grad = norm_one_pull(normed_grad)
     branch_low = resid_one_grad.astype(BF)
     mixed_grad = dot_nt(branch_low, full_out).astype(BF)
@@ -2034,9 +2223,10 @@
             zero,
         ]
     )
-    vectors = lax.dot_general(
-        vectors, turn.astype(F32), (((1,), (1,)), ((), ())), precision=FULL_PRECISION
-    )
+    if not whole_path:
+        vectors = lax.dot_general(
+            vectors, turn.astype(F32), (((1,), (1,)), ((), ())), precision=FULL_PRECISION
+        )
 
     def heads_sum(rights, first_block, blocks, reverse):
         size = width // 2
@@ -2059,24 +2249,24 @@
 
         return Reduction(half, 0, reverse, last)
 
-    inner_bias = jnp.sum(inner_low.astype(F32), axis=0).reshape(ways, units_local)
+    inner_bias = inner_bias.reshape(ways, units_local)
     if whole_path:
-        pre, head_bias, out_in, out_back, vectors, grad_proj = attention_backward_kernel(
-            qkv,
-            far_kv,
-            mixed_grad,
-            cosine,
-            sine,
-            far_cosine,
-            far_sine,
-            *label_args,
-            in_grad,
-            back_grad,
-            vectors,
-            grad_proj,
+        pre, head_bias, out_in, out_back, vectors, grad_proj, y_doc, y_query = (
+            attention_backward_kernel(
+                qkv,
+                far_kv,
+                mixed_grad,
+                cosines_three,
+                sines_three,
+                *label_args,
+                in_grad,
+                back_grad,
+                vectors,
+                grad_proj,
+                y_low,
+            )
         )
         head_bias = head_bias[:3].reshape(3, ways, heads_local)
-        pre = [pre[j] for j in range(3)]
     else:
         head_sums, head_rights = [], []
         running = [sum_back, sum_in]
@@ -2114,22 +2304,26 @@
         pre = [jnp.concatenate([part[j] for part in head_rights], axis=1) for j in range(3)]
         head_bias = jnp.stack([jnp.sum(p.astype(F32), axis=0) for p in pre])
         head_bias = head_bias.reshape(3, ways, heads_local)
-    x_grad = resid_one_grad
-    for j in range(3):
-        x_grad = x_grad + dot_nt(pre[j], full_qkv[j])
-    x_grad = dot_nt(x_grad.astype(BF), turn).astype(BF)
     tensor_grads = jnp.concatenate(
         [jnp.swapaxes(head_bias, 0, 1).reshape(ways, 3 * heads_local), inner_bias], axis=1
     )
     if whole_path:
         out_qkv, out_out, gx_doc, gx_query, tensor_grads = finish_kernel(
-            jnp.concatenate([dot_tn(x_low, p).astype(BF) for p in pre], axis=1),
-            dot_tn(mixed, branch_low).astype(BF),
-            x_grad,
+            x_low,
+            full_qkv,
+            pre,
+            mixed,
+            branch_low,
+            resid_one_grad,
             tensor_grads.reshape(ways, -1, 128),
         )
+        gx_doc, gx_query = gx_doc.astype(F32), gx_query.astype(F32)
         tensor_grads = tensor_grads.reshape(-1)
     else:
+        x_grad = resid_one_grad
+        for j in range(3):
+            x_grad = x_grad + dot_nt(pre[j], full_qkv[j])
+        x_grad = dot_nt(x_grad.astype(BF), turn).astype(BF)
         gx_doc, gx_query = rows_out(x_grad)
         gx_doc, gx_query = gx_doc.astype(F32), gx_query.astype(F32)
         out_out = sum_out.finish()

time: 578 us -> 429 us (0.74)
  matrix products: 133 us -> 9.75 us
  Pallas kernels: 387 us -> 369 us
  local copies, waits for them, and re-layouts: 32.9 us -> 20.4 us
  other arithmetic: 17.1 us -> 22.9 us
    dot_general x8 -> x2, matrix products: 50.7 us -> 3.56 us  [dot_nt(): lax.dot_general(a, b, (((1,), (1,)), ((), ())), preferred_element_type=F32)]
    dot_general x6 -> x2, matrix products: 47.5 us -> 3.28 us  [dot_nn(): lax.dot_general(a, b, (((1,), (0,)), ((), ())), preferred_element_type=F32)]
    dot_general x7 -> x1, matrix products: 29.5 us -> 1.35 us  [dot_tn(): lax.dot_general(a, b, (((0,), (0,)), ((), ())), preferred_element_type=F32)]
    pallas_call x1, Pallas kernels: 104 us -> 87.8 us  [attention_backward_kernel(): pl.pallas_call(kernel, grid=(pairs,), in_specs=[pl.BlockSpec((3, rows, 12...]
    pallas_call x1, Pallas kernels: 40.6 us -> 28.1 us  [loss_kernel(): pl.pallas_call(kernel, in_specs=[whole(projection.shape), whole(labels.sh...]
    unnamed x152 -> x80, local copies, waits for them, and re-layouts: 21.4 us -> 10.6 us
    pallas_call x4 -> x5, Pallas kernels: 243 us -> 253 us  [the longest x1 82.5 us: project_and_attend(): pl.pallas_call(kernel, grid=(pairs,), in_specs=[whole((rows, width)), any...]
where the time goes in v5:
time: 429 us; the launch traced here: 424 us
  Pallas kernels  369 us (86%)
  other arithmetic  22.9 us (5%)
  local copies, waits for them, and re-layouts  20.4 us (5%)
  matrix products  9.75 us (2%)
    pallas_call x1, Pallas kernels, attention_backward_kernel(): pl.pallas_call(kernel, grid=(pairs,), in_specs=[pl.BlockSpec((3, rows, 12...  87.8 us
    pallas_call x1, Pallas kernels, project_and_attend(): pl.pallas_call(kernel, grid=(pairs,), in_specs=[whole((rows, width)), any...  82.5 us
    pallas_call x1, Pallas kernels, finish_kernel(): pl.pallas_call(kernel, out_shape=out_shape, in_specs=[anywhere] * 6 + [wh...  61.7 us
    pallas_call x1, Pallas kernels, gather_kernel(): pl.pallas_call(kernel, out_shape=[jax.ShapeDtypeStruct((2 * (quarter + as...  56 us
    pallas_call x1, Pallas kernels, feed_forward_backward(): pl.pallas_call(kernel, grid=(units // columns,), in_specs=[pl.BlockSpec((...  28.3 us
    pallas_call x1, Pallas kernels, loss_kernel(): pl.pallas_call(kernel, in_specs=[whole(projection.shape), whole(labels.sh...  28.1 us
    pallas_call x1, Pallas kernels, feed_forward(): pl.pallas_call(kernel, grid=(units // columns,), in_specs=[pl.BlockSpec((...  24.9 us
    unnamed x80, local copies, waits for them, and re-layouts  10.6 us

profile of v5, /device:TPU:0, one launch (start us, length us, event | category | flops | bytes accessed | tf_op | source)
XLA Modules:
  0.0 424.1 jit_solution(13328251966659022499)
XLA Ops:
  0.7 0.7 reshape.519
  1.4 1.3 maximum_bitcast_fusion.1.bias_ref
  2.7 1.3 scatter.4.picks_ref
  3.9 56.0 %gather_weights.1 = (bf16[576,1024]{1,0:T(8,128)(2,1)}, bf16[3,1024,1024]{2,1,0:T(8,128)(2,1)}, bf16[1024,1024]{1,0:T(8,128)(2,1)}, bf16[8,128,128]{2,1,0:T(8,12...) custom-call(bf16[2,256,1024]{2,1,0:T(8,128)(2,1)} %xd_ref.1, bf16[2,32,1024]{2,1,0:T(8,128)(2,1)} %xq_ref.1, ...), custom_call_target="tpu_custom_call" | custom-call | tf_op jit(solution)/shard_map/gather_weights/pallas_call | solution.py:440
  60.0 0.7 fusion.37
  60.7 0.6 pad_maximum_fusion.1.b_ref
  61.9 0.7 convert_reduce_fusion.2
  62.7 1.9 fusion.5
  65.0 1.1 maximum_maximum_fusion.c_ref
  66.1 1.3 maximum_bitcast_fusion
  67.8 1.1 maximum_maximum_fusion.1.s_ref
  68.9 0.9 copy.54.lc_ref.lab_ref
  69.8 1.1 convert_element_type.70.cd_ref
  70.9 0.7 convert_element_type.71.cq_ref
  71.6 82.5 %project_and_attend.1 = (bf16[3,576,1024]{2,1,0:T(8,128)(2,1)}, bf16[2,512,1024]{2,1,0:T(8,128)(2,1)}, bf16[576,1024]{1,0:T(8,128)(2,1)}, bf16[576,1024]{1,0:T(8...) custom-call(bf16[576,1024]{1,0:T(8,128)(2,1)} %get-tuple-element.64.x_ref, ...), custom_call_target="tpu_custom_call" | custom-call | flops 38654705664 | bytes 6815744 | tf_op jit(solution)/shard_map/project_and_attend/pallas_call | solution.py:822
  154.2 1.4 fusion
  155.6 2.8 fusion.38
  159.7 24.9 %feed_forward.1 = (bf16[576,4096]{1,0:T(8,128)(2,1)S(1)}, bf16[576,4096]{1,0:T(8,128)(2,1)S(1)}, f32[576,1024]{1,0:T(8,128)S(1)}) custom-call(bf16[576,1024]{1,0:T(8,128)(2,1)S(1)} %fusion.2.h_ref, bf16[1024,4096]{1,0:T(8,128)(2,1)} %get-tuple-element.72.u_ref, f32[1,4096]{1,0:T(1,128)S(1)} %bitcast.71, bf16[4096,1024]{1,0:T(8,128)(2,1)} %get-tuple-element.73.w_ref), custom_call_target="tpu_custom_call" | custom-call | tf_op jit(solution)/shard_map/feed_forward/pallas_call | solution.py:901
  184.5 2.1 copy-done.3
  186.7 0.8 fusion.34
  187.5 1.4 copy-done.2
  191.1 0.8 slice_convert_fusion
  192.4 28.1 %loss.1 = (bf16[576,128]{1,0:T(8,128)(2,1)S(1)}, f32[2,8,128]{2,1,0:T(8,128)S(1)}) custom-call(f32[576,128]{1,0:T(8,128)S(1)} %fusion.39.p_ref, s32[512,1]{1,0:T(8,128)S(1)} %copy-done.4, f32[64,1]{1,0:T(8,128)S(1)} %reshape.539.cnt_ref, s32[1,1024]{1,0:T(1,128)S(1)} %broadcast_in_dim_reshape.3.pick_ref), custom_call_target="tpu_custom_call" | custom-call | flops 6710886400 | bytes 589824 | tf_op jit(solution)/shard_map/loss/pallas_call | solution.py:1173
  220.5 1.1 multiply_reduce_fusion
  221.7 0.8 fusion.33
  222.8 28.3 %feed_forward_backward.1 = (f32[576,1024]{1,0:T(8,128)S(1)}, bf16[1024,4096]{1,0:T(8,128)(2,1)}, bf16[4096,1024]{1,0:T(8,128)(2,1)}, f32[1,4096]{1,0:T(1,128)S(1)}) custom-call(bf16[576,1024]{1,0:T(8,128)(2,1)S(1)} %get-tuple-element.107.g_ref, bf16[4096,1024]{1,0:T(8,128)(2,1)} %get-tuple-element.73.w_ref, bf16[576,4096]{1,0:T(8,128)(2,1)} %copy-done.3, ...), custom_call_target="tpu_custom_call" | custom-call | tf_op jit(solution)/shard_map/feed_forward_backward/pallas_call | solution.py:942
  251.1 1.2 multiply_reduce_fusion.1
  252.3 0.8 fusion.32
  253.2 1.7 convert_reduce_fusion.1
  254.8 0.7 copy-done.35
  255.5 2.4 convolution_convert_fusion.g_ref
  257.9 0.7 stack.63.vec_ref
  258.6 1.4 fusion.40.proj_ref
  259.9 87.8 %attend_backward_and_sum.1 = (bf16[3,576,1024]{2,1,0:T(8,128)(2,1)}, f32[8,1024]{1,0:T(8,128)}, f32[128,1024]{1,0:T(8,128)}, f32[1024,128]{1,0:T(8,128)}, f32[8,...) custom-call(bf16[3,576,1024]{2,1,0:T(8,128)(2,1)} %get-tuple-element.67.qkv_ref,, ...), custom_call_target="tpu_custom_call" | custom-call | flops 60397977600 | bytes 22544384 | tf_op jit(solution)/shard_map/attend_backward_and_sum/pallas_call | solution.py:1758
  348.9 0.7 reduce.9
  349.6 0.8 slice.164
  350.4 0.6 reshape.537.ten_ref
  351.1 61.7 %last_sums.1 = (f32[3,128,256]{2,1,0:T(8,128)}, f32[256,128]{1,0:T(8,128)}, bf16[2,256,1024]{2,1,0:T(8,128)(2,1)}, bf16[2,32,1024]{2,1,0:T(8,128)(2,1)}, f32[14,128]{1,0:T(8,128)}) custom-call(bf16[576,1024]{1,0:T(8,128)(2,1)} %get-tuple-element.64.x_ref, bf16[3,1024,1024]{2,1,0:T(8,128)(2,1)} %get-tuple-element.65.w_ref, ...), custom_call_target="tpu_custom_call" | custom-call | tf_op jit(solution)/shard_map/last_sums/pallas_call | solution.py:1486
  412.9 2.9 convert_element_type.84
  415.8 0.7 convert_element_type.85
  417.1 0.6 fusion.35
  418.3 1.0 copy.69
  419.3 0.7 copy.70
  420.0 0.7 copy.71
  420.7 0.7 copy.72
  421.4 0.8 copy.73
  422.2 0.8 copy.74
  423.0 0.6 copy.75
  (129 shorter events, 8.2 us)
Async XLA Ops:
  0.7 60.7 %copy-start = (s32[2,8,5]{1,0,2:T(2,128)S(1)}, s32[2,8,5]{1,0,2:T(2,128)}, u32[]{:S(2)}) copy-start(s32[2,8,5]{1,0,2:T(2,128)} %param.25) | copy-start | bytes 964
  62.6 6.3 %copy-start.26 = (s32[512]{0:T(512)}, s32[512]{0:T(512)S(1)}, u32[]{:S(2)}) copy-start(s32[512]{0:T(512)S(1)} %get-tuple-element.105) | copy-start | bytes 6148
  65.0 4.8 %copy-start.11 = (f32[2,256,1024]{2,1,0:T(8,128)S(1)}, f32[2,256,1024]{2,1,0:T(8,128)}, u32[]{:S(2)}) copy-start(f32[2,256,1024]{2,1,0:T(8,128)} %param.23) | copy-start | bytes 6291460
  67.8 3.1 copy-start.19
  71.6 82.5 %copy-start.24 = (f32[1024]{0:T(1024)S(1)}, f32[1024]{0:T(1024)}, u32[]{:S(2)}) copy-start(f32[1024]{0:T(1024)} %param.30) | copy-start | bytes 12292
  71.6 82.5 %copy-start.29 = (f32[1024]{0:T(1024)S(1)}, f32[1024]{0:T(1024)}, u32[]{:S(2)}) copy-start(f32[1024]{0:T(1024)} %param.31) | copy-start | bytes 12292
  71.6 82.5 %copy-start.30 = (f32[1024]{0:T(1024)S(1)}, f32[1024]{0:T(1024)}, u32[]{:S(2)}) copy-start(f32[1024]{0:T(1024)} %param.32) | copy-start | bytes 12292
  71.6 82.6 %copy-start.31 = (f32[1024]{0:T(1024)S(1)}, f32[1024]{0:T(1024)}, u32[]{:S(2)}) copy-start(f32[1024]{0:T(1024)} %param.36) | copy-start | bytes 12292
  71.6 82.6 %copy-start.32 = (f32[1024]{0:T(1024)S(1)}, f32[1024]{0:T(1024)}, u32[]{:S(2)}) copy-start(f32[1024]{0:T(1024)} %param.37) | copy-start | bytes 12292
  71.6 82.6 %copy-start.33 = (f32[1024]{0:T(1024)S(1)}, f32[1024]{0:T(1024)}, u32[]{:S(2)}) copy-start(f32[1024]{0:T(1024)} %param.38) | copy-start | bytes 12292
  71.6 84.0 %copy-start.13 = (bf16[576,1024]{1,0:T(8,128)(2,1)S(1)}, bf16[576,1024]{1,0:T(8,128)(2,1)}, u32[]{:S(2)}) copy-start(bf16[576,1024]{1,0:T(8,128)(2,1)} %get-tuple-element.64.x_ref) | copy-start | bytes 3538948
  71.6 84.0 %copy-start.34 = (bf16[1024,1024]{1,0:T(8,128)(2,1)S(1)}, bf16[1024,1024]{1,0:T(8,128)(2,1)}, u32[]{:S(2)}) copy-start(bf16[1024,1024]{1,0:T(8,128)(2,1)} %get-tuple-element.71) | copy-start | bytes 6291460
  158.5 28.2 %copy-start.5 = (f32[576,1024]{1,0:T(8,128)}, f32[576,1024]{1,0:T(8,128)S(1)}, u32[]{:S(2)}) copy-start(f32[576,1024]{1,0:T(8,128)S(1)} %get-tuple-element.144) | copy-start | bytes 7077892
  158.9 0.8 copy-start.25
  184.5 2.1 copy-start.3
  186.7 2.2 copy-start.2
  188.9 1.4 copy-start.7
  189.3 1.2 copy-start.15
  189.3 3.1 copy-start.4
  190.3 68.3 %copy-start.9 = (bf16[576,1024]{1,0:T(8,128)(2,1)}, bf16[576,1024]{1,0:T(8,128)(2,1)S(1)}, u32[]{:S(2)}) copy-start(bf16[576,1024]{1,0:T(8,128)(2,1)S(1)} %add_convert_fusion.y_ref) | copy-start | bytes 3538948
  192.4 28.1 %copy-start.8 = (f32[576,1024]{1,0:T(8,128)S(1)}, f32[576,1024]{1,0:T(8,128)}, u32[]{:S(2)}) copy-start(f32[576,1024]{1,0:T(8,128)} %copy-done.7) | copy-start | bytes 7077892
  192.4 28.1 %copy-start.12 = (bf16[576,1024]{1,0:T(8,128)(2,1)S(1)}, bf16[576,1024]{1,0:T(8,128)(2,1)}, u32[]{:S(2)}) copy-start(bf16[576,1024]{1,0:T(8,128)(2,1)} %get-tuple-element.69) | copy-start | bytes 3538948
  222.7 28.4 %copy-start.6 = (f32[576,1024]{1,0:T(8,128)S(1)}, f32[576,1024]{1,0:T(8,128)}, u32[]{:S(2)}) copy-start(f32[576,1024]{1,0:T(8,128)} %copy-done.5) | copy-start | bytes 7077892
  253.2 2.3 copy-start.35
  254.8 3.1 copy-start.10
  412.8 3.0 copy-start.20
  412.8 3.7 copy-start.28
  412.8 4.3 %copy-start.27 = (f32[8,1024]{1,0:T(8,128)S(1)}, f32[8,1024]{1,0:T(8,128)}, u32[]{:S(2)}) copy-start(f32[8,1024]{1,0:T(8,128)} %get-tuple-element.94) | copy-start | bytes 98308
  412.8 5.5 %copy-start.14 = (bf16[2,256,1024]{2,1,0:T(8,128)(2,1)S(1)}, bf16[2,256,1024]{2,1,0:T(8,128)(2,1)}, u32[]{:S(2)}) copy-start(bf16[2,256,1024]{2,1,0:T(8,128)(2,1)} %get-tuple-element.166) | copy-start | bytes 3145732
  412.8 6.5 %copy-start.21 = (bf16[2,32,1024]{2,1,0:T(8,128)(2,1)S(1)}, bf16[2,32,1024]{2,1,0:T(8,128)(2,1)}, u32[]{:S(2)}) copy-start(bf16[2,32,1024]{2,1,0:T(8,128)(2,1)} %get-tuple-element.167) | copy-start | bytes 393220
  412.9 7.1 %copy-start.18 = (f32[3,128,256]{2,1,0:T(8,128)S(1)}, f32[3,128,256]{2,1,0:T(8,128)}, u32[]{:S(2)}) copy-start(f32[3,128,256]{2,1,0:T(8,128)} %get-tuple-element.171) | copy-start | bytes 1179652
  415.8 4.9 %copy-start.22 = (f32[256,128]{1,0:T(8,128)S(1)}, f32[256,128]{1,0:T(8,128)}, u32[]{:S(2)}) copy-start(f32[256,128]{1,0:T(8,128)} %get-tuple-element.173) | copy-start | bytes 393220
  415.8 5.6 %copy-start.17 = (f32[128,1024]{1,0:T(8,128)S(1)}, f32[128,1024]{1,0:T(8,128)}, u32[]{:S(2)}) copy-start(f32[128,1024]{1,0:T(8,128)} %get-tuple-element.177) | copy-start | bytes 1572868
  416.5 5.7 %copy-start.16 = (f32[1024,128]{1,0:T(8,128)S(1)}, f32[1024,128]{1,0:T(8,128)}, u32[]{:S(2)}) copy-start(f32[1024,128]{1,0:T(8,128)} %get-tuple-element.179) | copy-start | bytes 1572868
  418.3 5.3 %copy-start.1 = (s32[2,8,5]{1,0,2:T(2,128)S(1)}, s32[2,8,5]{1,0,2:T(2,128)}, u32[]{:S(2)}) copy-start(s32[2,8,5]{1,0,2:T(2,128)} %param.25) | copy-start | bytes 964
  418.3 4.6 %copy-start.23 = (f32[128,128]{1,0:T(8,128)S(1)}, f32[128,128]{1,0:T(8,128)}, u32[]{:S(2)}) copy-start(f32[128,128]{1,0:T(8,128)} %get-tuple-element.183) | copy-start | bytes 196612

commit v6 on v5

--- a/solution.py
+++ b/solution.py
@@ -365,16 +365,28 @@
     return jax.ShapeDtypeStruct(tuple(shape), weight.dtype)
 
 
-def gather_kernel(x_doc, x_query, qkv, out, proj, bias, picks):
+def gather_kernel(
+    x_doc, x_query, qkv, out, proj, b_qkv, b_in, picks, doc_cot, query_cot, ends, rates, params
+):
     ways, groups = 4, 8
     quarter, width = x_doc.shape[1:]
     asked = x_query.shape[1]
-
-    def kernel(
-        xd_ref, xq_ref, qkv_ref, out_ref, proj_ref, bias_ref, picks_ref,
-        x_o, qkv_o, out_o, proj_o, bias_o, picks_o,
-        send_sem, recv_sem, small_send, small_recv, x_send, x_recv, local_sem,
-    ):
+    docs, queries = 2 * quarter, 2 * asked
+    rows = docs + queries
+    share, units = b_qkv.shape[1], b_in.shape[1]
+    block = width // groups
+    marks = ends.shape[0]
+    count = len(params)
+
+    def kernel(*refs):
+        xd_ref, xq_ref, qkv_ref, out_ref, proj_ref, bq_ref, bi_ref, picks_ref = refs[:8]
+        cd_ref, cq_ref, ends_ref, rates_ref = refs[8:12]
+        param_refs = refs[12 : 12 + count]
+        x_o, qkv_o, out_o, proj_o, picks_o = refs[12 + count : 17 + count]
+        bq_o, bi_o, cos_o, sin_o, col_o, row_o, cd_o, cq_o, param_o = refs[17 + count : 26 + count]
+        (
+            bq, bi, send_sem, recv_sem, small_send, small_recv, x_send, x_recv, local_sem,
+        ) = refs[26 + count :]
         around = Around()
         around.meet()
         other, along = around.other, around.along
@@ -393,11 +405,12 @@
         send = Sender(small_send, small_recv)
         gather.begin()
         place = gather.place
-        small = [send(bias_ref, bias_o.at[dt], along(dt)) for dt in range(1, ways)]
-        local = [pltpu.make_async_copy(bias_ref, bias_o.at[0], local_sem.at[3])]
+        small = [send(bq_ref, bq.at[dt], along(dt)) for dt in range(1, ways)]
+        small += [send(bi_ref, bi.at[dt], along(dt)) for dt in range(1, ways)]
+        local = []
         flat = []
         for n, (ref, o) in enumerate(((proj_ref, proj_o), (picks_ref, picks_o))):
-            local.append(pltpu.make_async_copy(ref, o.at[0], local_sem.at[4 + n]))
+            local.append(pltpu.make_async_copy(ref, o.at[0], local_sem.at[3 + n]))
             flat.append(
                 (
                     send(ref, o.at[place(2)], other(2)),
@@ -411,8 +424,34 @@
             )
         for copy in small + local + [c for f in flat for c in f[:3]]:
             copy.start()
+
+        def layout(first, shape, axis):
+            index = lax.broadcasted_iota(jnp.int32, shape, axis) + first
+            segment = jnp.zeros(shape, jnp.int32)
+            begin = jnp.zeros(shape, jnp.int32)
+            for n in range(marks):
+                after = index >= ends_ref[n]
+                segment = segment + jnp.where(after, 1, 0)
+                begin = jnp.where(after, ends_ref[n], begin)
+            return segment, index - begin
+
+        segment, places = layout(around.core * docs, (docs, 1), 0)
+        col_o[...] = segment
+        row_o[0:1, :] = layout(around.core * docs, (1, docs), 1)[0]
+        row_o[1:2, :] = layout((1 - around.core) * docs, (1, docs), 1)[0]
+        lane = lax.broadcasted_iota(jnp.int32, (1, 128), 1)
+        first_half = lane % HEAD_WIDTH < HEAD_WIDTH // 2
+        asked_places = lax.broadcasted_iota(jnp.int32, (queries, 1), 0) % QLEN
+        for begin, at in ((0, places), (docs, asked_places)):
+            span = pl.ds(begin, at.shape[0])
+            angle = at.astype(F32) * rates_ref[...]
+            sine = jnp.sin(angle)
+            cos_o[span, :] = jnp.cos(angle)
+            sin_o[span, :] = jnp.where(first_half, -sine, sine)
         gather.hop(1)
-        moves.start()
+        for m in range(2):
+            cd_o[m] = cd_ref[m].astype(BF)
+            cq_o[m] = cq_ref[m].astype(BF)
         for f in flat:
             f[0].wait_recv()
             f[3].start()
@@ -420,47 +459,82 @@
             f[1].wait_recv()
             f[5].start()
         gather.hop(2)
+        moves.start()
+        for p in range(groups):
+            fr = pl.ds(pl.multiple_of(feature_block(around.rank, p) * block, block), block)
+            for n in range(count):
+                param_o[n : n + 1, p * block : (p + 1) * block] = param_refs[n][:, fr]
+        bq[0] = bq_ref[...]
+        bi[0] = bi_ref[...]
         gather.hop(3)
         for f in flat:
             f[3].wait_recv()
             f[6].start()
+        for copy in small:
+            copy.wait_recv()
+        for dt in range(ways):
+            bq_o[:, dt * share : (dt + 1) * share] = bq[dt]
+            bi_o[:, dt * units : (dt + 1) * units] = bi[dt]
         gather.finish()
         for f in flat:
             for n in (2, 4, 5, 6):
                 f[n].wait_recv()
-        for copy in small:
-            copy.wait_recv()
         for copy in local:
             copy.wait()
         moves.wait()
         send.drain()
 
+    def whole(shape):
+        return pl.BlockSpec(shape, lambda: (0,) * len(shape))
+
     anywhere = pl.BlockSpec(memory_space=pl.ANY)
     dma = pltpu.SemaphoreType.DMA
+    tables = [
+        jax.ShapeDtypeStruct((3, ways * share), F32),
+        jax.ShapeDtypeStruct((1, ways * units), F32),
+        jax.ShapeDtypeStruct((rows, 128), F32),
+        jax.ShapeDtypeStruct((rows, 128), F32),
+        jax.ShapeDtypeStruct((docs, 1), jnp.int32),
+        jax.ShapeDtypeStruct((2, docs), jnp.int32),
+        jax.ShapeDtypeStruct(doc_cot.shape, BF),
+        jax.ShapeDtypeStruct(query_cot.shape, BF),
+        jax.ShapeDtypeStruct((8, width), F32),
+    ]
     return pl.pallas_call(
         kernel,
         out_shape=[
-            jax.ShapeDtypeStruct((2 * (quarter + asked), width), x_doc.dtype),
+            jax.ShapeDtypeStruct((rows, width), x_doc.dtype),
             gathered(qkv, 1, 2),
             gathered(out, 1, 0),
             jax.ShapeDtypeStruct((groups,) + proj.shape, proj.dtype),
-            jax.ShapeDtypeStruct((ways,) + bias.shape, bias.dtype),
             jax.ShapeDtypeStruct((groups,) + picks.shape, picks.dtype),
-        ],
-        in_specs=[anywhere] * 7,
-        out_specs=[anywhere] * 6,
+        ]
+        + tables,
+        in_specs=[anywhere] * 5
+        + [whole(b_qkv.shape), whole(b_in.shape), anywhere]
+        + [whole(doc_cot.shape), whole(query_cot.shape)]
+        + [pl.BlockSpec(memory_space=pltpu.SMEM), whole(rates.shape)]
+        + [whole((1, width))] * count,
+        out_specs=[anywhere] * 5 + [whole(x.shape) for x in tables],
         scratch_shapes=[
+            pltpu.VMEM((ways,) + b_qkv.shape, F32),
+            pltpu.VMEM((ways,) + b_in.shape, F32),
             dma((3, WeightGather.slots)),
             dma((3, WeightGather.slots)),
-            dma((17,)),
-            dma((17,)),
+            dma((20,)),
+            dma((20,)),
             dma((2, 2)),
             dma((2, 2)),
-            dma((6,)),
+            dma((5,)),
         ],
-        compiler_params=pltpu.CompilerParams(collective_id=0, has_side_effects=True),
+        compiler_params=pltpu.CompilerParams(
+            collective_id=0, has_side_effects=True, vmem_limit_bytes=60 << 20
+        ),
         name="gather_weights",
-    )(x_doc, x_query, qkv, out, proj, bias, picks)
+    )(
+        x_doc, x_query, qkv, out, proj, b_qkv, b_in, picks, doc_cot, query_cot, ends, rates,
+        *[p[None] for p in params],
+    )
 
 
 def turned(values):
@@ -687,7 +761,7 @@
 
 
 def project_and_attend(
-    x, weights, bias, cosines, sines, col_labels, own_labels, far_labels,
+    x, weights, bias, cosine, sine, col_labels, row_labels, out, params,
     doc_cot, query_cot, up, back,
 ):
     rows, width = x.shape
@@ -700,10 +774,10 @@
     assert pairs == 8
 
     def kernel(
-        x_ref, w_ref, b_ref, c_ref, s_ref, lc_ref, lo_ref, lf_ref,
+        x_ref, w_ref, b_ref, c_ref, s_ref, lc_ref, lr_ref, ow_ref, par_ref,
         cd_ref, cq_ref, up_ref, back_ref,
-        qkv_o, far_o, o_ref, cot_o, up_o, back_o,
-        held, far, load_sem, far_send, far_recv, row_send, row_recv, send_sem, recv_sem, local_sem,
+        qkv_o, far_o, mixed_o, resid_o, norm_o, low_o, cot_o, up_o, back_o,
+        held, far, qkv, mixed, out_w, resid, norm, low, load_sem, far_send, far_recv, row_send, row_recv, send_sem, recv_sem, local_sem,
     ):
         h = pl.program_id(0)
 
@@ -728,6 +802,7 @@
             loads = [pltpu.make_async_copy(w_ref.at[j], held.at[j], load_sem.at[j]) for j in range(3)]
             for j in (1, 2, 0):
                 loads[j].start()
+            pltpu.make_async_copy(ow_ref, out_w, load_sem.at[4]).start()
             around, _, gather = parts()
             around.meet()
             gather.begin()
@@ -739,11 +814,14 @@
                     got = dot_nn(x_ref[...], held[j, :, at]) + b_ref[j : j + 1, at]
                     for m in range(columns // 128):
                         piece = got[:, m * 128 : (m + 1) * 128]
-                        low = piece * c_ref[j] + turned(piece) * s_ref[j]
-                        qkv_o[j, :, n * columns + m * 128 : n * columns + (m + 1) * 128] = low.astype(BF)
+                        if j < 2:
+                            piece = piece * c_ref[...] + turned(piece) * s_ref[...]
+                        if j == 0:
+                            piece = piece * 0.125
+                        qkv[j, :, n * columns + m * 128 : n * columns + (m + 1) * 128] = piece.astype(BF)
                     if j > 0:
                         copy = pltpu.make_async_remote_copy(
-                            src_ref=qkv_o.at[j, pl.ds(0, docs), at],
+                            src_ref=qkv.at[j, pl.ds(0, docs), at],
                             dst_ref=far.at[j - 1, :, at],
                             send_sem=far_send.at[j - 1, n],
                             recv_sem=far_recv.at[j - 1, n],
@@ -755,6 +833,7 @@
             for copy in copies:
                 copy.wait()
             pltpu.make_async_copy(far, far_o, load_sem.at[3]).start()
+            pltpu.make_async_copy(qkv, qkv_o, load_sem.at[5]).start()
 
         @pl.when(h == 1)
         def _():
@@ -774,7 +853,7 @@
         pair = pl.ds(pl.multiple_of(h * 128, 128), 128)
 
         def part(start, size, keys, sames):
-            q_block = qkv_o[0, pl.ds(start, size), pair]
+            q_block = qkv[0, pl.ds(start, size), pair]
             outs = []
             for head in range(2):
                 mask = (lane // HEAD_WIDTH) == head
@@ -790,29 +869,50 @@
                 total = functools.reduce(
                     jnp.add, [jnp.sum(p, axis=-1, keepdims=True) for p in powers]
                 )
-                mixed = functools.reduce(
+                blend = functools.reduce(
                     jnp.add, [dot_nn(p.astype(BF), value) for p, (_, value) in zip(powers, keys)]
                 )
-                outs.append(mixed * (1.0 / total))
-            o_ref[pl.ds(start, size), :] = jnp.where(lane < HEAD_WIDTH, outs[0], outs[1]).astype(BF)
+                outs.append(blend * (1.0 / total))
+            both = jnp.where(lane < HEAD_WIDTH, outs[0], outs[1]).astype(BF)
+            mixed[pl.ds(start, size), pair] = both
 
         doc_keys = [
-            (qkv_o[1, :docs, pair], qkv_o[2, :docs, pair]),
+            (qkv[1, :docs, pair], qkv[2, :docs, pair]),
             (far[0, :, pair], far[1, :, pair]),
         ]
         for at in range(docs // block):
             labels = lc_ref[pl.ds(at * block, block), :]
-            part(at * block, block, doc_keys, [labels == lo_ref[...], labels == lf_ref[...]])
+            part(at * block, block, doc_keys, [labels == lr_ref[0:1, :], labels == lr_ref[1:2, :]])
         row = lax.broadcasted_iota(jnp.int32, (asked, asked), 0) // QLEN
         col = lax.broadcasted_iota(jnp.int32, (asked, asked), 1) // QLEN
-        part(docs, asked, [(qkv_o[1, docs:, pair], qkv_o[2, docs:, pair])], [row == col])
+        part(docs, asked, [(qkv[1, docs:, pair], qkv[2, docs:, pair])], [row == col])
 
         @pl.when(h == pairs - 1)
         def _():
             _, moves, gather = parts()
+            pltpu.make_async_copy(ow_ref, out_w, load_sem.at[4]).wait()
+            for at in range(0, rows, rows // 4):
+                span = pl.ds(at, rows // 4)
+                total = x_ref[span, :].astype(F32) + dot_nn(mixed[span, :], out_w[...])
+                total = total + par_ref[0:1, :]
+                resid[span, :] = total
+                total = layer_norm(total, par_ref[1:2, :], par_ref[2:3, :])
+                norm[span, :] = total
+                low[span, :] = total.astype(BF)
+            stores = [
+                pltpu.make_async_copy(src, dst, load_sem.at[6 + n])
+                for n, (src, dst) in enumerate(
+                    ((mixed, mixed_o), (resid, resid_o), (norm, norm_o), (low, low_o))
+                )
+            ]
+            for store in stores:
+                store.start()
             gather.finish()
             moves.wait()
             pltpu.make_async_copy(far, far_o, load_sem.at[3]).wait()
+            pltpu.make_async_copy(qkv, qkv_o, load_sem.at[5]).wait()
+            for store in stores:
+                store.wait()
 
     def whole(shape):
         return pl.BlockSpec(shape, lambda h: (0,) * len(shape))
@@ -826,22 +926,21 @@
             whole((rows, width)),
             anywhere,
             whole((3, width)),
-            whole((3, rows, 128)),
-            whole((3, rows, 128)),
+            whole((rows, 128)),
+            whole((rows, 128)),
             whole((docs, 1)),
-            whole((1, docs)),
-            whole((1, docs)),
+            whole((2, docs)),
+            anywhere,
+            whole(params.shape),
         ]
         + [anywhere] * 4,
-        out_specs=[
-            whole((3, rows, width)),
-            anywhere,
-            pl.BlockSpec((rows, 128), lambda h: (0, h)),
-        ]
-        + [anywhere] * 3,
+        out_specs=[anywhere] * 9,
         out_shape=[
             jax.ShapeDtypeStruct((3, rows, width), BF),
             jax.ShapeDtypeStruct((2, docs, width), BF),
+            jax.ShapeDtypeStruct((rows, width), BF),
+            jax.ShapeDtypeStruct((rows, width), F32),
+            jax.ShapeDtypeStruct((rows, width), F32),
             jax.ShapeDtypeStruct((rows, width), BF),
             jax.ShapeDtypeStruct((rows, width), doc_cot.dtype),
             gathered(up, 0, 1),
@@ -850,7 +949,13 @@
         scratch_shapes=[
             pltpu.VMEM((3, width, width), BF),
             pltpu.VMEM((2, docs, width), BF),
-            dma((4,)),
+            pltpu.VMEM((3, rows, width), BF),
+            pltpu.VMEM((rows, width), BF),
+            pltpu.VMEM((width, width), BF),
+            pltpu.VMEM((rows, width), F32),
+            pltpu.VMEM((rows, width), F32),
+            pltpu.VMEM((rows, width), BF),
+            dma((10,)),
             dma((2, steps)),
             dma((2, steps)),
             dma((2, 2)),
@@ -860,7 +965,7 @@
             dma((2,)),
         ],
         compiler_params=pltpu.CompilerParams(
-            vmem_limit_bytes=56 << 20, collective_id=4, has_side_effects=True
+            vmem_limit_bytes=60 << 20, collective_id=4, has_side_effects=True
         ),
         name="project_and_attend",
         cost_estimate=pl.CostEstimate(
@@ -869,17 +974,19 @@
             transcendentals=rows * 2 * docs * width // 64,
         ),
     )(
-        x, weights, bias, cosines, sines, col_labels, own_labels, far_labels,
+        x, weights, bias, cosine, sine, col_labels, row_labels, out, params,
         doc_cot, query_cot, up, back,
     )
 
 
-def feed_forward(hidden, up, bias, back):
+def feed_forward(hidden, up, bias, back, normed, params, proj):
     rows, width = hidden.shape
     units = up.shape[1]
     columns, piece = 512, 256
 
-    def kernel(h_ref, u_ref, b_ref, w_ref, a_ref, d_ref, o_ref):
+    def kernel(
+        h_ref, u_ref, b_ref, w_ref, n_ref, par_ref, p_ref, a_ref, d_ref, o_ref, y_ref, q_ref
+    ):
         @pl.when(pl.program_id(0) == 0)
         def _():
             o_ref[...] = jnp.zeros_like(o_ref)
@@ -898,6 +1005,16 @@
             d_ref[:, at : at + piece] = (below + z * (bell * 0.3989422804014327)).astype(BF)
             o_ref[...] += dot_nn(low, w_ref[at : at + piece, :])
 
+        @pl.when(pl.program_id(0) == units // columns - 1)
+        def _():
+            for at in range(0, rows, rows // 4):
+                span = pl.ds(at, rows // 4)
+                total = n_ref[span, :] + o_ref[span, :] + par_ref[3:4, :]
+                o_ref[span, :] = total
+                low = layer_norm(total, par_ref[4:5, :], par_ref[5:6, :]).astype(BF)
+                y_ref[span, :] = low
+                q_ref[span, :] = dot_nn(low, p_ref[...])
+
     return pl.pallas_call(
         kernel,
         grid=(units // columns,),
@@ -906,65 +1023,176 @@
             pl.BlockSpec((width, columns), lambda n: (0, n)),
             pl.BlockSpec((1, columns), lambda n: (0, n)),
             pl.BlockSpec((columns, width), lambda n: (n, 0)),
+            pl.BlockSpec((rows, width), lambda n: (0, 0)),
+            pl.BlockSpec(params.shape, lambda n: (0, 0)),
+            pl.BlockSpec(proj.shape, lambda n: (0, 0)),
         ],
         out_specs=[
             pl.BlockSpec((rows, columns), lambda n: (0, n)),
             pl.BlockSpec((rows, columns), lambda n: (0, n)),
             pl.BlockSpec((rows, width), lambda n: (0, 0)),
+            pl.BlockSpec((rows, width), lambda n: (0, 0)),
+            pl.BlockSpec((rows, proj.shape[1]), lambda n: (0, 0)),
         ],
         out_shape=[
             jax.ShapeDtypeStruct((rows, units), BF),
             jax.ShapeDtypeStruct((rows, units), BF),
             jax.ShapeDtypeStruct((rows, width), F32),
+            jax.ShapeDtypeStruct((rows, width), BF),
+            jax.ShapeDtypeStruct((rows, proj.shape[1]), F32),
         ],
-        compiler_params=pltpu.CompilerParams(vmem_limit_bytes=40 << 20),
+        compiler_params=pltpu.CompilerParams(vmem_limit_bytes=60 << 20),
         name="feed_forward",
-    )(hidden, up, bias[None], back)
-
-
-def feed_forward_backward(grad, back, slope, up, hidden, active):
-    rows, width = grad.shape
+    )(hidden, up, bias, back, normed, params, proj)
+
+
+def norm_backward(values, gain, grad):
+    center = values - jnp.mean(values, axis=-1, keepdims=True)
+    rate = lax.rsqrt(jnp.mean(center * center, axis=-1, keepdims=True) + EPS)
+    unit = center * rate
+    inner = grad * gain
+    pull = inner - jnp.mean(inner, axis=-1, keepdims=True)
+    pull = pull - unit * jnp.mean(inner * unit, axis=-1, keepdims=True)
+    return (
+        pull * rate,
+        jnp.sum(grad * unit, axis=0, keepdims=True),
+        jnp.sum(grad, axis=0, keepdims=True),
+    )
+
+
+def feed_forward_backward(
+    cot, proj_low, proj, resid_two, output_low, params, back, slope, up, hidden, active,
+    resid_one, out,
+):
+    rows, width = cot.shape
     units = up.shape[1]
     columns = 512
-
-    def kernel(g_ref, w_ref, d_ref, u_ref, h_ref, a_ref, o_ref, du_ref, dw_ref, db_ref):
-        @pl.when(pl.program_id(0) == 0)
+    steps = units // columns
+    piece = rows // 4
+
+    def kernel(
+        c_ref, pl_ref, p_ref, r2_ref, y_ref, par_ref, w_ref, d_ref, u_ref, h_ref, a_ref,
+        r1_ref, out_ref,
+        one_ref, low_ref, mix_ref, du_ref, dw_ref, db_ref, dp_ref, vec_ref,
+        two, g, total, r1, out_w, sem,
+    ):
+        step = pl.program_id(0)
+
+        @pl.when(step == 0)
         def _():
-            o_ref[...] = jnp.zeros_like(o_ref)
-
-        g = g_ref[...]
-        dw_ref[...] = dot_tn(a_ref[...], g).astype(BF)
-        low = (dot_nt(g, w_ref[...]) * d_ref[...].astype(F32)).astype(BF)
+            pltpu.make_async_copy(r1_ref, r1, sem.at[0]).start()
+            pltpu.make_async_copy(out_ref, out_w, sem.at[1]).start()
+            total[...] = jnp.zeros_like(total)
+            vec_ref[...] = jnp.zeros_like(vec_ref)
+            for at in range(0, rows, piece):
+                span = pl.ds(at, piece)
+                grad = c_ref[span, :].astype(F32) + dot_nt(pl_ref[span, :], p_ref[...])
+                pull, gain, shift = norm_backward(r2_ref[span, :], par_ref[4:5, :], grad)
+                two[span, :] = pull
+                low = pull.astype(BF)
+                g[span, :] = low
+                vec_ref[3:4, :] += jnp.sum(low.astype(F32), axis=0, keepdims=True)
+                vec_ref[4:5, :] += gain
+                vec_ref[5:6, :] += shift
+            dp_ref[...] = dot_tn(y_ref[...], pl_ref[...])
+
+        dw_ref[...] = dot_tn(a_ref[...], g[...]).astype(BF)
+        low = (dot_nt(g[...], w_ref[...]) * d_ref[...].astype(F32)).astype(BF)
         db_ref[...] = jnp.sum(low.astype(F32), axis=0, keepdims=True)
-        o_ref[...] += dot_nt(low, u_ref[...])
+        total[...] += dot_nt(low, u_ref[...])
         du_ref[...] = dot_tn(h_ref[...], low).astype(BF)
 
+        @pl.when(step == steps - 1)
+        def _():
+            pltpu.make_async_copy(r1_ref, r1, sem.at[0]).wait()
+            pltpu.make_async_copy(out_ref, out_w, sem.at[1]).wait()
+            for at in range(0, rows, piece):
+                span = pl.ds(at, piece)
+                grad = total[span, :] + two[span, :]
+                pull, gain, shift = norm_backward(r1[span, :], par_ref[1:2, :], grad)
+                one_ref[span, :] = pull
+                low = pull.astype(BF)
+                low_ref[span, :] = low
+                vec_ref[0:1, :] += jnp.sum(low.astype(F32), axis=0, keepdims=True)
+                vec_ref[1:2, :] += gain
+                vec_ref[2:3, :] += shift
+                mix_ref[span, :] = dot_nt(low, out_w[...]).astype(BF)
+
+    def whole(shape):
+        return pl.BlockSpec(shape, lambda n: (0,) * len(shape))
+
+    anywhere = pl.BlockSpec(memory_space=pl.ANY)
+    vmem = pltpu.VMEM
     return pl.pallas_call(
         kernel,
-        grid=(units // columns,),
+        grid=(steps,),
         in_specs=[
-            pl.BlockSpec((rows, width), lambda n: (0, 0)),
+            whole((rows, width)),
+            whole(proj_low.shape),
+            whole(proj.shape),
+            whole((rows, width)),
+            whole((rows, width)),
+            whole(params.shape),
             pl.BlockSpec((columns, width), lambda n: (n, 0)),
             pl.BlockSpec((rows, columns), lambda n: (0, n)),
             pl.BlockSpec((width, columns), lambda n: (0, n)),
-            pl.BlockSpec((rows, width), lambda n: (0, 0)),
+            whole((rows, width)),
             pl.BlockSpec((rows, columns), lambda n: (0, n)),
+            anywhere,
+            anywhere,
         ],
         out_specs=[
-            pl.BlockSpec((rows, width), lambda n: (0, 0)),
+            whole((rows, width)),
+            whole((rows, width)),
+            whole((rows, width)),
             pl.BlockSpec((width, columns), lambda n: (0, n)),
             pl.BlockSpec((columns, width), lambda n: (n, 0)),
             pl.BlockSpec((1, columns), lambda n: (0, n)),
+            whole(proj.shape),
+            whole((8, width)),
         ],
         out_shape=[
             jax.ShapeDtypeStruct((rows, width), F32),
+            jax.ShapeDtypeStruct((rows, width), BF),
+            jax.ShapeDtypeStruct((rows, width), BF),
             jax.ShapeDtypeStruct((width, units), BF),
             jax.ShapeDtypeStruct((units, width), BF),
             jax.ShapeDtypeStruct((1, units), F32),
+            jax.ShapeDtypeStruct(proj.shape, F32),
+            jax.ShapeDtypeStruct((8, width), F32),
         ],
-        compiler_params=pltpu.CompilerParams(vmem_limit_bytes=48 << 20),
+        scratch_shapes=[
+            vmem((rows, width), F32),
+            vmem((rows, width), BF),
+            vmem((rows, width), F32),
+            vmem((rows, width), F32),
+            vmem((width, width), BF),
+            pltpu.SemaphoreType.DMA((2,)),
+        ],
+        compiler_params=pltpu.CompilerParams(vmem_limit_bytes=60 << 20),
         name="feed_forward_backward",
-    )(grad, back, slope, up, hidden, active)
+    )(
+        cot, proj_low, proj, resid_two, output_low, params, back, slope, up, hidden, active,
+        resid_one, out,
+    )
+
+
+def emit_kernel(arrays, dtypes):
+    def kernel(*refs):
+        for src, dst in zip(refs[: len(arrays)], refs[len(arrays) :]):
+            dst[...] = src[...].astype(dst.dtype)
+
+    def whole(x):
+        return pl.BlockSpec(x.shape, lambda: (0,) * len(x.shape))
+
+    return pl.pallas_call(
+        kernel,
+        in_specs=[whole(x) for x in arrays],
+        out_specs=[whole(x) for x in arrays],
+        out_shape=[jax.ShapeDtypeStruct(x.shape, t) for x, t in zip(arrays, dtypes)],
+        compiler_params=pltpu.CompilerParams(vmem_limit_bytes=60 << 20),
+        name="emit",
+    )(*arrays)
 
 
 def loss_kernel(projection, labels, log_counts, picks):
@@ -1201,7 +1429,7 @@
             dma((2,)),
         ],
         compiler_params=pltpu.CompilerParams(
-            collective_id=5, has_side_effects=True, vmem_limit_bytes=40 << 20
+            collective_id=5, has_side_effects=True, vmem_limit_bytes=60 << 20
         ),
         name="loss",
         cost_estimate=pl.CostEstimate(
@@ -1531,7 +1759,7 @@
 
 
 def attention_backward_kernel(
-    qkv, far_kv, grad, cosines, sines, col_labels, own_labels, far_labels,
+    qkv, far_kv, grad, cosine, sine, col_labels, row_labels,
     up, back, vectors, proj, y,
 ):
     rows, width = qkv.shape[1:]
@@ -1546,7 +1774,7 @@
     assert pairs == 8
 
     def kernel(
-        qkv_ref, far_ref, g_ref, c_ref, s_ref, lc_ref, lo_ref, lf_ref,
+        qkv_ref, far_ref, g_ref, c_ref, s_ref, lc_ref, lr_ref,
         up_ref, back_ref, vec_ref, proj_ref, y_ref,
         pre_ref, bias_ref, up_o, back_o, vec_o, proj_o, yd_ref, yq_ref,
         sums_own, sums_far, give, kept, got_kv,
@@ -1591,8 +1819,8 @@
                 head = kept[n % 2, i, :docs, :] + got_kv[n, i].astype(F32)
                 tail = kept[n % 2, i, docs:, :]
                 if i == 0:
-                    head = head * c_ref[0, :docs, :] - turned(head) * s_ref[0, :docs, :]
-                    tail = tail * c_ref[0, docs:, :] - turned(tail) * s_ref[0, docs:, :]
+                    head = head * c_ref[:docs, :] - turned(head) * s_ref[:docs, :]
+                    tail = tail * c_ref[docs:, :] - turned(tail) * s_ref[docs:, :]
                 head, tail = head.astype(BF), tail.astype(BF)
                 pre_ref[i + 1, :docs, at] = head
                 pre_ref[i + 1, docs:, at] = tail
@@ -1677,7 +1905,7 @@
                     ref[1, pl.ds(begin, many), :] += dot_tn(p.astype(BF), g_head)
             total = jnp.where(lane < HEAD_WIDTH, grads[0], grads[1])
             at = pl.ds(start, size)
-            low = (total * c_ref[0, at, :] - turned(total) * s_ref[0, at, :]).astype(BF)
+            low = (total * c_ref[at, :] - turned(total) * s_ref[at, :]).astype(BF)
             pre_ref[0, at, pl.ds(pl.multiple_of(h * 128, 128), 128)] = low
             return jnp.sum(low.astype(F32), axis=0, keepdims=True)
 
@@ -1692,7 +1920,7 @@
                 at * block,
                 block,
                 doc_keys,
-                [labels == lo_ref[...], labels == lf_ref[...]],
+                [labels == lr_ref[0:1, :], labels == lr_ref[1:2, :]],
                 [(sums_own, 0, docs), (sums_far, 0, docs)],
             )
         row = lax.broadcasted_iota(jnp.int32, (asked, asked), 0) // QLEN
@@ -1762,11 +1990,10 @@
             pl.BlockSpec((3, rows, 128), lambda h: (0, 0, h)),
             pl.BlockSpec((2, docs, 128), lambda h: (0, 0, h)),
             pl.BlockSpec((rows, 128), lambda h: (0, h)),
-            pl.BlockSpec((1, rows, 128), lambda h: (1, 0, 0)),
-            pl.BlockSpec((1, rows, 128), lambda h: (1, 0, 0)),
+            whole((rows, 128)),
+            whole((rows, 128)),
             whole((docs, 1)),
-            whole((1, docs)),
-            whole((1, docs)),
+            whole((2, docs)),
             anywhere,
             anywhere,
             whole(vectors.shape),
@@ -1815,7 +2042,7 @@
             transcendentals=rows * 2 * docs * width // 64,
         ),
     )(
-        qkv, far_kv, grad, cosines, sines, col_labels, own_labels, far_labels,
+        qkv, far_kv, grad, cosine, sine, col_labels, row_labels,
         up, back, vectors, proj, y,
     )
 
@@ -1939,98 +2166,105 @@
     actual = (rank ^ (2 * (step % chips) + step // chips)) * block + place % block
     turn = (place[:, None] == actual[None, :]).astype(BF)
 
-    bias_pack = jnp.concatenate([b_qkv.reshape(-1), b_in])
+    docs = 2 * quarter
+    queries = 2 * asked
+    rows = docs + queries
+    sizes_all = lengths[unit_micro]
+    sizes = sizes_all[unit_row]
+    ends = jnp.cumsum(sizes[:-1])
+    half = HEAD_WIDTH // 2
+    rates = 10000.0 ** (-(2.0 * jnp.arange(half, dtype=F32)) / HEAD_WIDTH)
     own_picks = jnp.zeros((8, 128), jnp.int32).at[:micro, : positives.shape[1]].set(positives)
+    params = [b_out, gain_one, shift_one, b_back, gain_two, shift_two]
     if chips == 4:
-        own_x, full_qkv, full_out, full_proj, biases, picks_rel = gather_kernel(
-            x_doc, x_query, w_qkv, w_out, w_proj, bias_pack.reshape(-1, 128), own_picks
+        (
+            own_x, full_qkv, full_out, full_proj, picks_rel,
+            bias_qkv, bias_in, cosine, sine, col_labels, row_labels, *cots, params,
+        ) = gather_kernel(
+            x_doc, x_query, w_qkv, w_out, w_proj, b_qkv, b_in[None], own_picks,
+            doc_cot, query_cot, ends, jnp.tile(rates, 4)[None], params,
         )
-        biases = [biases[j].reshape(-1) for j in range(ways)]
         full_proj = full_proj.reshape(width, proj_width)
     else:
         own_x = rows_in(x_doc, x_query)
+        own_cot = rows_in(doc_cot.astype(BF), query_cot.astype(BF))
         full_qkv = gather_weights(w_qkv, False)
         full_out = gather_weights(w_out.T, False).T
         full_in = gather_weights(w_in, False)
         full_back = gather_weights(w_back.T, False).T
         full_proj = gather_proj(w_proj)
         picks_rel = gather_proj(own_picks[None])
+        bias_pack = jnp.concatenate([b_qkv.reshape(-1), b_in])
         biases = [bias_pack] + [exchange(bias_pack[None], dt=j)[0] for j in range(1, ways)]
+        bias_qkv = jnp.concatenate(
+            [b[: 3 * heads_local].reshape(3, heads_local) for b in biases], axis=1
+        )
+        bias_in = jnp.concatenate([b[3 * heads_local :] for b in biases])
+        params = jnp.dot(
+            jnp.stack(params + [b_out, b_out]), turn.astype(F32), precision=FULL_PRECISION
+        )
+        starts = jnp.concatenate([jnp.zeros((1,), jnp.int32), ends])
+
+        def layout(first):
+            index = first + jnp.arange(docs, dtype=jnp.int32)
+            segment = jnp.sum((index[:, None] >= ends[None, :]).astype(jnp.int32), axis=1)
+            labels = jnp.arange(starts.shape[0], dtype=jnp.int32)
+            begin = jnp.sum(
+                jnp.where(segment[:, None] == labels[None, :], starts[None, :], 0), axis=1
+            )
+            return segment, index - begin
+
+        def rotation(places):
+            angle = places.astype(F32)[:, None] * rates[None, :]
+            turned_sine = jnp.sin(angle)
+            return (
+                jnp.tile(jnp.cos(angle), (1, 4)),
+                jnp.concatenate([-turned_sine, turned_sine] * 2, axis=1),
+            )
+
+        own_labels, own_places = layout(core * docs)
+        far_labels, far_places = layout((1 - core) * docs)
+        own_places = jnp.concatenate([own_places, jnp.arange(queries, dtype=jnp.int32) % QLEN])
+        cosine, sine = rotation(own_places)
+        far_cosine, far_sine = rotation(far_places)
+        label_args = (own_labels[:, None], own_labels[None, :], far_labels[None, :])
     picks_rel = picks_rel[:, :micro, : positives.shape[1]].astype(F32)
-    cots = (doc_cot.astype(BF), query_cot.astype(BF))
-    if chips != 4:
-        own_cot = rows_in(*cots)
-    bias_qkv = jnp.concatenate(
-        [b[: 3 * heads_local].reshape(3, heads_local) for b in biases], axis=1
-    )
-    bias_in = jnp.concatenate([b[3 * heads_local :] for b in biases])
-    params = jnp.stack(
-        [b_out, gain_one, shift_one, b_back, gain_two, shift_two, b_out, b_out]
-    )
-    params = jnp.dot(params, turn.astype(F32), precision=FULL_PRECISION)
-    b_out, gain_one, shift_one, b_back, gain_two, shift_two = [params[i] for i in range(6)]
-
-    docs = 2 * quarter
-    queries = 2 * asked
-    rows = docs + queries
-    sizes_all = lengths[unit_micro]
-    sizes = sizes_all[unit_row]
-    ends = jnp.cumsum(sizes[:-1])
-    starts = jnp.concatenate([jnp.zeros((1,), jnp.int32), ends])
-
-    def layout(first):
-        index = first + jnp.arange(docs, dtype=jnp.int32)
-        segment = jnp.sum((index[:, None] >= ends[None, :]).astype(jnp.int32), axis=1)
-        labels = jnp.arange(starts.shape[0], dtype=jnp.int32)
-        begin = jnp.sum(
-            jnp.where(segment[:, None] == labels[None, :], starts[None, :], 0), axis=1
-        )
-        return segment, index - begin
-
-    own_labels, own_places = layout(core * docs)
-    far_labels, far_places = layout((1 - core) * docs)
-    own_places = jnp.concatenate([own_places, jnp.arange(queries, dtype=jnp.int32) % QLEN])
-    half = HEAD_WIDTH // 2
-    rates = 10000.0 ** (-(2.0 * jnp.arange(half, dtype=F32)) / HEAD_WIDTH)
-
-    def rotation(places):
-        angle = places.astype(F32)[:, None] * rates[None, :]
-        sine = jnp.sin(angle)
-        return jnp.tile(jnp.cos(angle), (1, 4)), jnp.concatenate([-sine, sine] * 2, axis=1)
-
-    cosine, sine = rotation(own_places)
-    far_cosine, far_sine = rotation(far_places)
-    cosines_three = jnp.stack([cosine * 0.125, cosine, jnp.ones_like(cosine)])
-    sines_three = jnp.stack([sine * 0.125, sine, jnp.zeros_like(sine)])
-
-    label_args = (own_labels[:, None], own_labels[None, :], far_labels[None, :])
+    b_out, gain_one, shift_one, b_back, gain_two, shift_two = [params[n] for n in range(6)]
+
     if chips == 4:
         x_low = own_x
-        qkv, far_kv, mixed, own_cot, full_in, full_back = project_and_attend(
-            own_x, full_qkv, bias_qkv, cosines_three, sines_three, *label_args,
-            *cots, w_in, w_back,
+        qkv, far_kv, mixed, resid_one, normed, normed_low, own_cot, full_in, full_back = (
+            project_and_attend(
+                own_x, full_qkv, bias_qkv, cosine, sine, col_labels, row_labels, full_out, params,
+                *cots, w_in, w_back,
+            )
         )
+        active_low, active_slope, resid_two, output_low, projection = feed_forward(
+            normed_low, full_in, bias_in, full_back, normed, params, full_proj
+        )
+        y_low = output_low
     else:
         x_low = dot_nn(own_x, turn).astype(BF)
-        qkv = project_heads(x_low, full_qkv, bias_qkv, cosines_three, sines_three)
+        qkv = project_heads(
+            x_low,
+            full_qkv,
+            bias_qkv,
+            jnp.stack([cosine * 0.125, cosine, jnp.ones_like(cosine)]),
+            jnp.stack([sine * 0.125, sine, jnp.zeros_like(sine)]),
+        )
         far_kv = exchange(qkv[1:, :docs], dr=1)
         mixed = attention_forward(qkv, far_kv, *label_args)
-    branch = dot_nn(mixed, full_out)
-    resid_one = x_low.astype(F32) + branch + b_out
-    normed, norm_one_pull = jax.vjp(layer_norm, resid_one, gain_one, shift_one)
-    normed_low = normed.astype(BF)
-    if chips == 4:
-        active_low, active_slope, update = feed_forward(normed_low, full_in, bias_in, full_back)
-    else:
+        resid_one = x_low.astype(F32) + dot_nn(mixed, full_out) + b_out
+        normed, norm_one_pull = jax.vjp(layer_norm, resid_one, gain_one, shift_one)
+        normed_low = normed.astype(BF)
         inner = dot_nn(normed_low, full_in) + bias_in
         active, gelu_pull = jax.vjp(gelu_exact, inner)
         active_low = active.astype(BF)
-        update = dot_nn(active_low, full_back)
-    resid_two = normed + update + b_back
-    output, norm_two_pull = jax.vjp(layer_norm, resid_two, gain_two, shift_two)
-    output_low = output.astype(BF)
-    y_low = output_low if chips == 4 else dot_nt(output_low, turn).astype(BF)
-    projection = dot_nn(output_low, full_proj)
+        resid_two = normed + dot_nn(active_low, full_back) + b_back
+        output, norm_two_pull = jax.vjp(layer_norm, resid_two, gain_two, shift_two)
+        output_low = output.astype(BF)
+        y_low = dot_nt(output_low, turn).astype(BF)
+        projection = dot_nn(output_low, full_proj)
     held = jnp.arange(groups, dtype=jnp.int32)
     held = rank ^ (2 * (held % chips) + held // chips)
     order = (jnp.arange(groups, dtype=jnp.int32)[:, None] == held[None, :]).astype(F32)
@@ -2043,7 +2277,7 @@
             jnp.log(counts).reshape(-1, segments), ((0, 0), (0, 8 - segments))
         ).reshape(-1, 1)
         proj_low, loss_out = loss_kernel(
-            projection, own_labels[:, None], log_counts, jnp.repeat(picks, QLEN)[None]
+            projection, col_labels, log_counts, jnp.repeat(picks, QLEN)[None]
         )
         loss_out = loss_out[:, : asked // QLEN, 0]
     else:
@@ -2186,44 +2420,41 @@
             r.sends = s
         return value
 
-    if chips == 4:
-        out_cot = own_cot.astype(F32)
-    else:
-        out_cot = dot_nn(own_cot, turn)
-    out_grad = out_cot + dot_nt(proj_low, full_proj)
-    resid_two_grad, gain_two_grad, shift_two_grad = norm_two_pull(out_grad)
-    update_low = resid_two_grad.astype(BF)
     whole_path = chips == 4
     if whole_path:
-        hidden_grad, in_grad, back_grad, inner_bias = feed_forward_backward(
-            update_low, full_back, active_slope, full_in, normed_low, active_low
+        (
+            resid_one_grad, branch_low, mixed_grad, in_grad, back_grad, inner_bias, grad_proj, vectors,
+        ) = feed_forward_backward(
+            own_cot, proj_low, full_proj, resid_two, output_low, params, full_back, active_slope,
+            full_in, normed_low, active_low, resid_one, full_out,
         )
     else:
+        out_grad = dot_nn(own_cot, turn) + dot_nt(proj_low, full_proj)
+        resid_two_grad, gain_two_grad, shift_two_grad = norm_two_pull(out_grad)
+        update_low = resid_two_grad.astype(BF)
         sum_back = weight_sum(active_low, update_low, 1, True)
         (inner_grad,) = gelu_pull(dot_nt(update_low, full_back))
         inner_low = inner_grad.astype(BF)
         sum_in = weight_sum(normed_low, inner_low, 0, False)
-        hidden_grad = dot_nt(inner_low, full_in)
         inner_bias = jnp.sum(inner_low.astype(F32), axis=0)
-    normed_grad = hidden_grad + resid_two_grad
-    resid_one_grad, gain_one_grad, shift_one_grad = norm_one_pull(normed_grad)
-    branch_low = resid_one_grad.astype(BF)
-    mixed_grad = dot_nt(branch_low, full_out).astype(BF)
-    grad_proj = dot_tn(output_low, proj_low)
-    zero = jnp.zeros((width,), F32)
-    vectors = jnp.stack(
-        [
-            jnp.sum(branch_low.astype(F32), axis=0),
-            gain_one_grad,
-            shift_one_grad,
-            jnp.sum(update_low.astype(F32), axis=0),
-            gain_two_grad,
-            shift_two_grad,
-            zero,
-            zero,
-        ]
-    )
-    if not whole_path:
+        normed_grad = dot_nt(inner_low, full_in) + resid_two_grad
+        resid_one_grad, gain_one_grad, shift_one_grad = norm_one_pull(normed_grad)
+        branch_low = resid_one_grad.astype(BF)
+        mixed_grad = dot_nt(branch_low, full_out).astype(BF)
+        grad_proj = dot_tn(output_low, proj_low)
+        zero = jnp.zeros((width,), F32)
+        vectors = jnp.stack(
+            [
+                jnp.sum(branch_low.astype(F32), axis=0),
+                gain_one_grad,
+                shift_one_grad,
+                jnp.sum(update_low.astype(F32), axis=0),
+                gain_two_grad,
+                shift_two_grad,
+                zero,
+                zero,
+            ]
+        )
         vectors = lax.dot_general(
             vectors, turn.astype(F32), (((1,), (1,)), ((), ())), precision=FULL_PRECISION
         )
@@ -2256,9 +2487,10 @@
                 qkv,
                 far_kv,
                 mixed_grad,
-                cosines_three,
-                sines_three,
-                *label_args,
+                cosine,
+                sine,
+                col_labels,
+                row_labels,
                 in_grad,
                 back_grad,
                 vectors,
@@ -2317,7 +2549,10 @@
             resid_one_grad,
             tensor_grads.reshape(ways, -1, 128),
         )
-        gx_doc, gx_query = gx_doc.astype(F32), gx_query.astype(F32)
+        y_doc, y_query, gx_doc, gx_query, out_qkv, out_out, out_in, out_back, grad_proj = emit_kernel(
+            [y_doc, y_query, gx_doc, gx_query, out_qkv, out_out, out_in, out_back, grad_proj],
+            [BF, BF] + [F32] * 7,
+        )
         tensor_grads = tensor_grads.reshape(-1)
     else:
         x_grad = resid_one_grad

time: 429 us -> 403 us (0.939)
  other arithmetic: 22.9 us -> 2.18 us
  Pallas kernels: 369 us -> 386 us
  local copies, waits for them, and re-layouts: 20.4 us -> 9.56 us
  matrix products: 9.75 us -> 0.18 us
    pallas_call x2 -> x3, Pallas kernels: 84.4 us -> 94.8 us  [the longest x1 51.2 us: gather_kernel(): pl.pallas_call(kernel, out_shape=[jax.ShapeDtypeStruct((rows, width), x_d...]
    unnamed x80 -> x11, local copies, waits for them, and re-layouts: 10.6 us -> 0.75 us
    dot_general x6 -> x0, matrix products: 9.57 us -> none  [the longest x2 3.56 us: dot_nt(): lax.dot_general(a, b, (((1,), (1,)), ((), ())), preferred_element_type=F32)]
    reduce_sum x10 -> x0, other arithmetic: 7.11 us -> none  [the longest x3 2.42 us: layer_norm(): center = values - jnp.mean(values, axis=-1, keepdims=True)]
    convert_element_type x7 -> x0, other arithmetic: 6.32 us -> none  [the longest x2 3.63 us: body(): gx_doc, gx_query = (gx_doc.astype(F32), gx_query.astype(F32))]
where the time goes in v6:
time: 403 us; the launch traced here: 399 us
  Pallas kernels  386 us (96%)
  local copies, waits for them, and re-layouts  9.56 us (2%)
    pallas_call x1, Pallas kernels, attention_backward_kernel(): pl.pallas_call(kernel, grid=(pairs,), in_specs=[pl.BlockSpec((3, rows, 12...  87.9 us
    pallas_call x1, Pallas kernels, project_and_attend(): pl.pallas_call(kernel, grid=(pairs,), in_specs=[whole((rows, width)), any...  83.6 us
    pallas_call x1, Pallas kernels, finish_kernel(): pl.pallas_call(kernel, out_shape=out_shape, in_specs=[anywhere] * 6 + [wh...  62 us
    pallas_call x1, Pallas kernels, gather_kernel(): pl.pallas_call(kernel, out_shape=[jax.ShapeDtypeStruct((rows, width), x_d...  51.2 us
    pallas_call x1, Pallas kernels, feed_forward_backward(): pl.pallas_call(kernel, grid=(steps,), in_specs=[whole((rows, width)), who...  39.1 us
    pallas_call x1, Pallas kernels, loss_kernel(): pl.pallas_call(kernel, in_specs=[whole(projection.shape), whole(labels.sh...  29.1 us
    pallas_call x1, Pallas kernels, feed_forward(): pl.pallas_call(kernel, grid=(units // columns,), in_specs=[pl.BlockSpec((...  28.7 us

profile of v6, /device:TPU:0, one launch (start us, length us, event | category | flops | bytes accessed | tf_op | source)
XLA Modules:
  0.0 399.1 jit_solution(16220210649062912073)
XLA Ops:
  0.7 0.0 copy-start
  0.7 0.6 copy-done
  1.4 0.2 dynamic-slice_reduce_fusion
  1.6 0.7 reduce-window.9
  2.3 1.3 scatter.4.refs_7_
  3.6 0.6 broadcast_in_dim_tile.3.refs_11_
  4.2 51.2 %gather_weights.1 = (bf16[576,1024]{1,0:T(8,128)(2,1)}, bf16[3,1024,1024]{2,1,0:T(8,128)(2,1)}, bf16[1024,1024]{1,0:T(8,128)(2,1)}, bf16[8,128,128]{2,1,0:T(8,12...) custom-call(bf16[2,256,1024]{2,1,0:T(8,128)(2,1)} %refs_0_.1, ...), custom_call_target="tpu_custom_call" | custom-call | tf_op jit(solution)/shard_map/gather_weights/pallas_call | solution.py:503
  55.4 83.6 %project_and_attend.1 = (bf16[3,576,1024]{2,1,0:T(8,128)(2,1)}, bf16[2,512,1024]{2,1,0:T(8,128)(2,1)}, bf16[576,1024]{1,0:T(8,128)(2,1)}, f32[576,1024]{1,0:T(8,...) custom-call(bf16[576,1024]{1,0:T(8,128)(2,1)} %get-tuple-element.90., ...), custom_call_target="tpu_custom_call" | custom-call | flops 38654705664 | bytes 6815744 | tf_op jit(solution)/shard_map/project_and_attend/pallas_call | solution.py:922
  139.0 28.7 %feed_forward.1 = (bf16[576,4096]{1,0:T(8,128)(2,1)}, bf16[576,4096]{1,0:T(8,128)(2,1)}, f32[576,1024]{1,0:T(8,128)}, bf16[576,1024]{1,0:T(8,128)(2,1)}, f32[576,128]{1,0:T(8,128)}) custom-call(bf16[576,1024]{1,0:T(8,128)(2,1)} %get-tuple-element.104.h_ref, bf16[1024,4096]{1,0:T(8,128)(2,1)} %get-tuple-element.105.u_ref, ...), custom_call_target="tpu_custom_call" | custom-call | tf_op jit(solution)/shard_map/feed_forward/pallas_call | solution.py:1018
  167.7 0.8 slice_convert_fusion
  168.5 0.2 convolution_convert_fusion
  168.7 0.1 copy.43
  168.8 0.1 reshape.163
  168.9 0.1 broadcast_in_dim.34
  168.9 0.7 broadcast_in_dim_reshape.3.pick_ref
  169.6 0.1 copy.45
  169.7 0.7 reshape.169.cnt_ref
  170.4 29.1 %loss.1 = (bf16[576,128]{1,0:T(8,128)(2,1)}, f32[2,8,128]{2,1,0:T(8,128)}) custom-call(f32[576,128]{1,0:T(8,128)} %get-tuple-element.110.p_ref, s32[512,1]{1,0:T(8,128)} %get-tuple-element.95.lc_ref.lab_ref, f32[64,1]{1,0:T(8,128)} %reshape.169.cnt_ref, s32[1,1024]{1,0:T(1,128)} %broadcast_in_dim_reshape.3.pick_ref), custom_call_target="tpu_custom_call" | custom-call | flops 6710886400 | bytes 589824 | tf_op jit(solution)/shard_map/loss/pallas_call | solution.py:1401
  199.6 39.1 %feed_forward_backward.1 = (f32[576,1024]{1,0:T(8,128)}, bf16[576,1024]{1,0:T(8,128)(2,1)}, bf16[576,1024]{1,0:T(8,128)(2,1)}, bf16[1024,4096]{1,0:T(8,128)(2,1)...) custom-call(bf16[576,1024]{1,0:T(8,128)(2,1)} %get-tuple-element.103.c_ref, ...), custom_call_target="tpu_custom_call" | custom-call | tf_op jit(solution)/shard_map/feed_forward_backward/pallas_call | solution.py:1126
  238.7 0.0 copy-start.3
  238.7 87.9 %attend_backward_and_sum.1 = (bf16[3,576,1024]{2,1,0:T(8,128)(2,1)}, f32[8,1024]{1,0:T(8,128)}, f32[128,1024]{1,0:T(8,128)}, f32[1024,128]{1,0:T(8,128)}, f32[8,...) custom-call(bf16[3,576,1024]{2,1,0:T(8,128)(2,1)} %get-tuple-element.101.qkv_ref, ...), custom_call_target="tpu_custom_call" | custom-call | flops 60397977600 | bytes 22544384 | tf_op jit(solution)/shard_map/attend_backward_and_sum/pallas_call | solution.py:1986
  326.6 0.8 slice.75
  327.4 0.5 broadcast.121
  327.9 0.0 copy-done.3
  327.9 0.7 reduce.9
  328.6 0.6 reshape.167.ten_ref
  329.2 0.0 copy-start.1
  329.2 62.0 %last_sums.1 = (f32[3,128,256]{2,1,0:T(8,128)}, f32[256,128]{1,0:T(8,128)}, bf16[2,256,1024]{2,1,0:T(8,128)(2,1)}, bf16[2,32,1024]{2,1,0:T(8,128)(2,1)}, f32[14,128]{1,0:T(8,128)}) custom-call(bf16[576,1024]{1,0:T(8,128)(2,1)} %get-tuple-element.90.x_ref, bf16[3,1024,1024]{2,1,0:T(8,128)(2,1)} %get-tuple-element.91.w_ref, ...), custom_call_target="tpu_custom_call" | custom-call | tf_op jit(solution)/shard_map/last_sums/pallas_call | solution.py:1714
  391.2 0.0 copy-start.4
  391.2 0.0 copy-start.2
  391.2 4.5 %emit.1 = (bf16[2,256,1024]{2,1,0:T(8,128)(2,1)}, bf16[2,32,1024]{2,1,0:T(8,128)(2,1)}, f32[2,256,1024]{2,1,0:T(8,128)}, f32[2,32,1024]{2,1,0:T(8,128)}, f32[3,1...) custom-call(bf16[2,256,1024]{2,1,0:T(8,128)(2,1)} %get-tuple-element, ...), custom_call_target="tpu_custom_call" | custom-call | tf_op jit(solution)/shard_map/emit/pallas_call | solution.py:1188
  395.7 0.0 copy-done.4
  395.7 0.6 reshape.168
  396.3 0.6 slice_bitcast_fusion
  396.9 0.0 copy-done.2
  396.9 0.6 fusion.4
  397.5 1.3 slice_reduce_fusion
  398.8 0.0 copy-done.1
  (11 shorter events, 0.1 us)
Async XLA Ops:
  0.7 0.7 copy-start
  238.7 89.2 %copy-start.3 = (f32[1,4096]{1,0:T(1,128)S(1)}, f32[1,4096]{1,0:T(1,128)}, u32[]{:S(2)}) copy-start(f32[1,4096]{1,0:T(1,128)} %get-tuple-element.130) | copy-start | bytes 49156
  329.2 69.6 %copy-start.1 = (s32[2,8,5]{1,0,2:T(2,128)S(1)}, s32[2,8,5]{1,0,2:T(2,128)}, u32[]{:S(2)}) copy-start(s32[2,8,5]{1,0,2:T(2,128)} %param.25) | copy-start | bytes 964
  391.2 4.5 %copy-start.4 = (f32[14,128]{1,0:T(8,128)S(1)}, f32[14,128]{1,0:T(8,128)}, u32[]{:S(2)}) copy-start(f32[14,128]{1,0:T(8,128)} %get-tuple-element.144) | copy-start | bytes 21508
  391.2 5.7 %copy-start.2 = (f32[8,1024]{1,0:T(8,128)S(1)}, f32[8,1024]{1,0:T(8,128)}, u32[]{:S(2)}) copy-start(f32[8,1024]{1,0:T(8,128)} %get-tuple-element.146) | copy-start | bytes 98308

commit v7 on v6

--- a/solution.py
+++ b/solution.py
@@ -178,8 +178,8 @@
                 )
                 self.arrivals.append((here, came))
 
-    def start(self):
-        for mine, locals_, aways in self.copies:
+    def start(self, n=None):
+        for mine, locals_, aways in self.copies if n is None else self.copies[2 * n : 2 * n + 2]:
 
             @pl.when(mine)
             def _(locals_=locals_):
@@ -982,7 +982,7 @@
 def feed_forward(hidden, up, bias, back, normed, params, proj):
     rows, width = hidden.shape
     units = up.shape[1]
-    columns, piece = 512, 256
+    columns, piece = 1024, 1024
 
     def kernel(
         h_ref, u_ref, b_ref, w_ref, n_ref, par_ref, p_ref, a_ref, d_ref, o_ref, y_ref, q_ref
@@ -1586,7 +1586,7 @@
         return self.run[pl.ds(self.ref.shape[0] // 2 + 2 * self.last, self.last), :]
 
 
-def finish_kernel(x, weights, pre, mixed, branch, resid, tensor_sums):
+def finish_kernel(x, weights, pre, mixed, branch, resid, head_bias, inner_bias):
     ways = 4
     rows, width = x.shape
     half, block = width // 2, width // 8
@@ -1594,9 +1594,12 @@
     docs = rows // 9 * 8
     quarter, asked = docs // 2, (rows - docs) // 2
     part = 3 * share
+    units = inner_bias.shape[1] // ways
+    lines = 16
+    assert (3 * share + units) // 128 <= lines
 
     def kernel(
-        x_ref, w_ref, p_ref, m_ref, g_ref, r_ref, ten_ref,
+        x_ref, w_ref, p_ref, m_ref, g_ref, r_ref, hb_ref, ib_ref,
         qkv_o, out_o, doc_o, ask_o, ten_o,
         xs, ws, ps, ms, gs, rs, low, qf, qa, q0, q1, q2, q3, of, oa, o0, o1, o2, o3,
         t_got, t_run, tz, send_sem, recv_sem, local_sem, row_send, row_recv,
@@ -1651,16 +1654,27 @@
         loads["r"].wait()
         for j in range(3):
             loads[j].wait()
+        t_run[0] = jnp.zeros((ways, lines, 128), F32)
+        for dt in range(ways):
+            for j in range(3):
+                for m in range(share // 128):
+                    fr = dt * share + m * 128
+                    row = j * (share // 128) + m
+                    t_run[0, dt, row : row + 1, :] = hb_ref[j : j + 1, fr : fr + 128]
+            for m in range(units // 128):
+                fr = dt * units + m * 128
+                row = 3 * share // 128 + m
+                t_run[0, dt, row : row + 1, :] = ib_ref[:, fr : fr + 128]
+
         for at in range(0, width, share):
             total = rs[:, at : at + share]
             for j in range(3):
                 total = total + dot_nt(ps[j], ws[j, at : at + share, :])
             low[:, at : at + share] = total.astype(BF)
         around.await_all()
-        t_run[0] = ten_ref[...]
-        small.begin()
         home = RowMoves(around, False, doc_o, ask_o, low, row_send, row_recv)
         home.start()
+        small.begin()
         for name in ("x", "m", "g"):
             loads[name].wait()
         compute(0)
@@ -1705,7 +1719,7 @@
         jax.ShapeDtypeStruct((share, block), F32),
         jax.ShapeDtypeStruct((2, quarter, width), BF),
         jax.ShapeDtypeStruct((2, asked, width), BF),
-        jax.ShapeDtypeStruct(tensor_sums.shape[1:], F32),
+        jax.ShapeDtypeStruct((lines, 128), F32),
     ]
     anywhere = pl.BlockSpec(memory_space=pl.ANY)
     vmem = pltpu.VMEM
@@ -1714,7 +1728,7 @@
     return pl.pallas_call(
         kernel,
         out_shape=out_shape,
-        in_specs=[anywhere] * 6 + [whole(tensor_sums)],
+        in_specs=[anywhere] * 6 + [whole(head_bias), whole(inner_bias)],
         out_specs=[
             whole(out_shape[0]),
             whole(out_shape[1]),
@@ -1742,9 +1756,9 @@
             vmem((ways, share, 2 * block), BF),
             vmem((ways, share, block), BF),
             vmem((ways - 1, share, block), BF),
-            vmem((3,) + tensor_sums.shape, F32),
-            vmem((4,) + tensor_sums.shape, F32),
-            vmem((ways - 1,) + tensor_sums.shape[1:], F32),
+            vmem((3, ways, lines, 128), F32),
+            vmem((4, ways, lines, 128), F32),
+            vmem((ways - 1, lines, 128), F32),
             dma((count,)),
             dma((count,)),
             dma((8,)),
@@ -1755,7 +1769,7 @@
             collective_id=1, has_side_effects=True, vmem_limit_bytes=60 << 20
         ),
         name="last_sums",
-    )(x, weights, pre, mixed, branch, resid, tensor_sums)
+    )(x, weights, pre, mixed, branch, resid, head_bias, inner_bias)
 
 
 def attention_backward_kernel(
@@ -2480,7 +2494,6 @@
 
         return Reduction(half, 0, reverse, last)
 
-    inner_bias = inner_bias.reshape(ways, units_local)
     if whole_path:
         pre, head_bias, out_in, out_back, vectors, grad_proj, y_doc, y_query = (
             attention_backward_kernel(
@@ -2498,7 +2511,6 @@
                 y_low,
             )
         )
-        head_bias = head_bias[:3].reshape(3, ways, heads_local)
     else:
         head_sums, head_rights = [], []
         running = [sum_back, sum_in]
@@ -2536,9 +2548,6 @@
         pre = [jnp.concatenate([part[j] for part in head_rights], axis=1) for j in range(3)]
         head_bias = jnp.stack([jnp.sum(p.astype(F32), axis=0) for p in pre])
         head_bias = head_bias.reshape(3, ways, heads_local)
-    tensor_grads = jnp.concatenate(
-        [jnp.swapaxes(head_bias, 0, 1).reshape(ways, 3 * heads_local), inner_bias], axis=1
-    )
     if whole_path:
         out_qkv, out_out, gx_doc, gx_query, tensor_grads = finish_kernel(
             x_low,
@@ -2547,14 +2556,22 @@
             mixed,
             branch_low,
             resid_one_grad,
-            tensor_grads.reshape(ways, -1, 128),
+            head_bias,
+            inner_bias,
         )
         y_doc, y_query, gx_doc, gx_query, out_qkv, out_out, out_in, out_back, grad_proj = emit_kernel(
             [y_doc, y_query, gx_doc, gx_query, out_qkv, out_out, out_in, out_back, grad_proj],
             [BF, BF] + [F32] * 7,
         )
-        tensor_grads = tensor_grads.reshape(-1)
+        tensor_grads = tensor_grads[: (3 * heads_local + units_local) // 128].reshape(-1)
     else:
+        tensor_grads = jnp.concatenate(
+            [
+                jnp.swapaxes(head_bias, 0, 1).reshape(ways, 3 * heads_local),
+                inner_bias.reshape(ways, units_local),
+            ],
+            axis=1,
+        )
         x_grad = resid_one_grad
         for j in range(3):
             x_grad = x_grad + dot_nt(pre[j], full_qkv[j])

time: 403 us -> 396 us (0.983)
  Pallas kernels: 386 us -> 380 us
    pallas_call x1, Pallas kernels: 28.7 us -> 22.9 us  [feed_forward(): pl.pallas_call(kernel, grid=(units // columns,), in_specs=[pl.BlockSpec((...]
where the time goes in v7:
time: 396 us; the launch traced here: 392 us
  Pallas kernels  380 us (96%)
  local copies, waits for them, and re-layouts  8.99 us (2%)
    pallas_call x1, Pallas kernels, attention_backward_kernel(): pl.pallas_call(kernel, grid=(pairs,), in_specs=[pl.BlockSpec((3, rows, 12...  87.9 us
    pallas_call x1, Pallas kernels, project_and_attend(): pl.pallas_call(kernel, grid=(pairs,), in_specs=[whole((rows, width)), any...  83.5 us
    pallas_call x1, Pallas kernels, finish_kernel(): pl.pallas_call(kernel, out_shape=out_shape, in_specs=[anywhere] * 6 + [wh...  62 us
    pallas_call x1, Pallas kernels, gather_kernel(): pl.pallas_call(kernel, out_shape=[jax.ShapeDtypeStruct((rows, width), x_d...  51.2 us
    pallas_call x1, Pallas kernels, feed_forward_backward(): pl.pallas_call(kernel, grid=(steps,), in_specs=[whole((rows, width)), who...  39.2 us
    pallas_call x1, Pallas kernels, loss_kernel(): pl.pallas_call(kernel, in_specs=[whole(projection.shape), whole(labels.sh...  29.2 us
    pallas_call x1, Pallas kernels, feed_forward(): pl.pallas_call(kernel, grid=(units // columns,), in_specs=[pl.BlockSpec((...  22.9 us

profile of v7, /device:TPU:0, one launch (start us, length us, event | category | flops | bytes accessed | tf_op | source)
XLA Modules:
  0.0 392.1 jit_solution(12030339613734119353)
XLA Ops:
  0.7 0.0 copy-start
  0.7 0.6 copy-done
  1.4 0.2 dynamic-slice_reduce_fusion
  1.6 0.7 reduce-window.9
  2.3 0.6 broadcast_in_dim_tile.3.refs_11_
  2.9 0.1 copy.45
  3.0 1.3 scatter.4.refs_7_
  4.3 0.7 reshape.153.cnt_ref
  5.0 51.2 %gather_weights.1 = (bf16[576,1024]{1,0:T(8,128)(2,1)}, bf16[3,1024,1024]{2,1,0:T(8,128)(2,1)}, bf16[1024,1024]{1,0:T(8,128)(2,1)}, bf16[8,128,128]{2,1,0:T(8,12...) custom-call(bf16[2,256,1024]{2,1,0:T(8,128)(2,1)} %refs_0_.1, ...), custom_call_target="tpu_custom_call" | custom-call | tf_op jit(solution)/shard_map/gather_weights/pallas_call | solution.py:503
  56.2 0.8 slice_convert_fusion
  57.0 0.2 convolution_convert_fusion
  57.2 0.1 copy.43
  57.3 0.1 reshape.151
  57.4 0.1 broadcast_in_dim.34
  57.4 0.7 broadcast_in_dim_reshape.3.pick_ref
  58.1 83.5 %project_and_attend.1 = (bf16[3,576,1024]{2,1,0:T(8,128)(2,1)}, bf16[2,512,1024]{2,1,0:T(8,128)(2,1)}, bf16[576,1024]{1,0:T(8,128)(2,1)}, f32[576,1024]{1,0:T(8,...) custom-call(bf16[576,1024]{1,0:T(8,128)(2,1)} %get-tuple-element.90., ...), custom_call_target="tpu_custom_call" | custom-call | flops 38654705664 | bytes 6815744 | tf_op jit(solution)/shard_map/project_and_attend/pallas_call | solution.py:922
  141.6 22.9 %feed_forward.1 = (bf16[576,4096]{1,0:T(8,128)(2,1)}, bf16[576,4096]{1,0:T(8,128)(2,1)}, f32[576,1024]{1,0:T(8,128)}, bf16[576,1024]{1,0:T(8,128)(2,1)}, f32[576,128]{1,0:T(8,128)}) custom-call(bf16[576,1024]{1,0:T(8,128)(2,1)} %get-tuple-element.104.h_ref, bf16[1024,4096]{1,0:T(8,128)(2,1)} %get-tuple-element.105.u_ref, ...), custom_call_target="tpu_custom_call" | custom-call | tf_op jit(solution)/shard_map/feed_forward/pallas_call | solution.py:1018
  164.5 29.2 %loss.1 = (bf16[576,128]{1,0:T(8,128)(2,1)}, f32[2,8,128]{2,1,0:T(8,128)}) custom-call(f32[576,128]{1,0:T(8,128)} %get-tuple-element.110.p_ref, s32[512,1]{1,0:T(8,128)} %get-tuple-element.95.lc_ref.lab_ref, f32[64,1]{1,0:T(8,128)} %reshape.153.cnt_ref, s32[1,1024]{1,0:T(1,128)} %broadcast_in_dim_reshape.3.pick_ref), custom_call_target="tpu_custom_call" | custom-call | flops 6710886400 | bytes 589824 | tf_op jit(solution)/shard_map/loss/pallas_call | solution.py:1401
  193.7 39.2 %feed_forward_backward.1 = (f32[576,1024]{1,0:T(8,128)}, bf16[576,1024]{1,0:T(8,128)(2,1)}, bf16[576,1024]{1,0:T(8,128)(2,1)}, bf16[1024,4096]{1,0:T(8,128)(2,1)...) custom-call(bf16[576,1024]{1,0:T(8,128)(2,1)} %get-tuple-element.103.c_ref, ...), custom_call_target="tpu_custom_call" | custom-call | tf_op jit(solution)/shard_map/feed_forward_backward/pallas_call | solution.py:1126
  232.9 87.9 %attend_backward_and_sum.1 = (bf16[3,576,1024]{2,1,0:T(8,128)(2,1)}, f32[8,1024]{1,0:T(8,128)}, f32[128,1024]{1,0:T(8,128)}, f32[1024,128]{1,0:T(8,128)}, f32[8,...) custom-call(bf16[3,576,1024]{2,1,0:T(8,128)(2,1)} %get-tuple-element.101.qkv_ref, ...), custom_call_target="tpu_custom_call" | custom-call | flops 60397977600 | bytes 22544384 | tf_op jit(solution)/shard_map/attend_backward_and_sum/pallas_call | solution.py:2000
  320.8 0.0 copy-start.2
  320.8 0.0 copy-start.1
  320.8 62.0 %last_sums.1 = (f32[3,128,256]{2,1,0:T(8,128)}, f32[256,128]{1,0:T(8,128)}, bf16[2,256,1024]{2,1,0:T(8,128)(2,1)}, bf16[2,32,1024]{2,1,0:T(8,128)(2,1)}, f32[16,128]{1,0:T(8,128)}) custom-call(bf16[576,1024]{1,0:T(8,128)(2,1)} %get-tuple-element.90.x_ref, bf16[3,1024,1024]{2,1,0:T(8,128)(2,1)} %get-tuple-element.91.w_ref, ...), custom_call_target="tpu_custom_call" | custom-call | tf_op jit(solution)/shard_map/last_sums/pallas_call | solution.py:1728
  382.8 1.3 slice_reduce_fusion
  384.1 1.3 slice_bitcast_fusion
  385.4 0.7 slice.76
  386.1 0.6 reshape.152
  386.7 0.0 copy-done.2
  386.7 0.6 fusion.4
  387.3 4.5 %emit.1 = (bf16[2,256,1024]{2,1,0:T(8,128)(2,1)}, bf16[2,32,1024]{2,1,0:T(8,128)(2,1)}, f32[2,256,1024]{2,1,0:T(8,128)}, f32[2,32,1024]{2,1,0:T(8,128)}, f32[3,1...) custom-call(bf16[2,256,1024]{2,1,0:T(8,128)(2,1)} %get-tuple-element, ...), custom_call_target="tpu_custom_call" | custom-call | tf_op jit(solution)/shard_map/emit/pallas_call | solution.py:1188
  391.8 0.0 copy-done.1
  (7 shorter events, 0.1 us)
Async XLA Ops:
  0.7 0.7 copy-start
  320.8 65.9 %copy-start.2 = (f32[8,1024]{1,0:T(8,128)S(1)}, f32[8,1024]{1,0:T(8,128)}, u32[]{:S(2)}) copy-start(f32[8,1024]{1,0:T(8,128)} %get-tuple-element.146) | copy-start | bytes 98308
  320.8 71.0 %copy-start.1 = (s32[2,8,5]{1,0,2:T(2,128)S(1)}, s32[2,8,5]{1,0,2:T(2,128)}, u32[]{:S(2)}) copy-start(s32[2,8,5]{1,0,2:T(2,128)} %param.25) | copy-start | bytes 964
